TPU v7x, 32 devices: a whole 2x2x4 slice. The times are simulated.
32 devices in a mesh: seq: 4 (over y, core), fsdp: 8 (over z, x).
Axes of the slice: x: 2, y: 2, z: 4, core: 2. Of those that a mesh axis runs over, the one named last changes fastest.
Arguments:
- tokens: bfloat16 [2, 8, 512, 2048], P(None, 'fsdp', 'seq'), may hold values from -6 to 6
- norm_gains: float32 [2, 2048], replicated, may hold values from 0.5 to 1.5
- w_query: bfloat16 [2048, 2048], P('fsdp', 'seq'), may hold values from -0.125 to 0.125
- w_key: bfloat16 [2048, 2048], P('fsdp', 'seq'), may hold values from -0.125 to 0.125
- w_value: bfloat16 [2048, 4096], P('fsdp', 'seq'), may hold values from -0.125 to 0.125
- w_gate: bfloat16 [2048, 4096], P('fsdp', 'seq'), may hold values from -0.125 to 0.125
- w_out: bfloat16 [4096, 2048], P('seq', 'fsdp'), may hold values from -0.1875 to 0.1875
- w_up: bfloat16 [2048, 4096], P('fsdp', 'seq'), may hold values from -0.125 to 0.125
- w_down: bfloat16 [4096, 2048], P('seq', 'fsdp'), may hold values from -0.125 to 0.125
- segments: int32 [2, 8, 512], P(None, 'fsdp'), may hold values from 0 to 3, never falling along the last dimension, each value on 1 to 256 neighbouring positions
- d_output: bfloat16 [2, 8, 512, 2048], P(None, 'fsdp', 'seq'), may hold values from -6 to 6
Outputs:
- output: bfloat16 [2, 8, 512, 2048], P(None, 'fsdp', 'seq')
- d_input: float32 [2, 8, 512, 2048], P(None, 'fsdp', 'seq')
- grad_norms: float32 [2, 2048], replicated
- grad_query: float32 [2048, 2048], P('fsdp', 'seq')
- grad_key: float32 [2048, 2048], P('fsdp', 'seq')
- grad_value: float32 [2048, 4096], P('fsdp', 'seq')
- grad_gate: float32 [2048, 4096], P('fsdp', 'seq')
- grad_out: float32 [4096, 2048], P('seq', 'fsdp')
- grad_up: float32 [2048, 4096], P('fsdp', 'seq')
- grad_down: float32 [4096, 2048], P('seq', 'fsdp')
Inputs may be any that keep to these rules, and one draw needn't show every extreme that they name: `segments`: within a sequence the document numbers never fall; each document has 1 to 256 positions, and one has exactly 256.
All inputs are finite; a program needn't handle non-finite values.
Results may differ from a plain program's by a relative error of at most 0.02.
Values may be sent and summed in bfloat16 or wider, within the bound.
No kernel may reach another device: no remote copies, remote signals or barrier semaphores. Data moves between devices by JAX's collectives and lax.ppermute only.
A program may use at most 192 MiB of HBM per device.

v0:
```python
from functools import partial

import jax
import jax.numpy as jnp
from jax import lax
from jax.sharding import PartitionSpec as P

KEY_HEAD = 256
VAL_HEAD = 512


eps_norm = 1e-05
eps_group = 1.0


def plain_product(left, right):
    return jnp.dot(left, right, preferred_element_type=jnp.float32)


def product_back(left, right):
    return lax.dot_general(
        left, right, (((1,), (1,)), ((), ())), preferred_element_type=jnp.float32
    )


def token_sum(left, right):
    return lax.dot_general(
        left, right, (((0,), (0,)), ((), ())), preferred_element_type=jnp.float32
    )


def layer_norm_parts(inputs, gain_row):
    center = inputs - jnp.mean(inputs, axis=-1, keepdims=True)
    inverse = lax.rsqrt(jnp.mean(center * center, axis=-1, keepdims=True) + eps_norm)
    scaled = center * inverse
    return (scaled * gain_row, scaled, inverse)


def layer_norm_back(incoming, scaled, inverse, gain_row):
    upstream = incoming * gain_row
    centered_grad = (
        upstream
        - jnp.mean(upstream, axis=-1, keepdims=True)
        - scaled * jnp.mean(upstream * scaled, axis=-1, keepdims=True)
    )
    return (centered_grad * inverse, jnp.sum(incoming * scaled, axis=0))


def rotation_tables(length, head_dim):
    half_dim = head_dim // 2
    positions = jnp.arange(length, dtype=jnp.float32)[:, None]
    frequency = jnp.exp(
        -jnp.log(10000.0) * 2.0 * jnp.arange(half_dim, dtype=jnp.float32) / head_dim
    )
    angles = positions * frequency[None, :]
    return (jnp.cos(angles), jnp.sin(angles))


def rotate(inputs, cos_table, sin_table):
    half_dim = inputs.shape[-1] // 2
    first_half = inputs[..., :half_dim]
    second_half = inputs[..., half_dim:]
    cos_part = cos_table[:, None, :]
    sin_part = sin_table[:, None, :]
    return jnp.concatenate(
        [
            first_half * cos_part - second_half * sin_part,
            second_half * cos_part + first_half * sin_part,
        ],
        axis=-1,
    )


def rotate_back(inputs, cos_table, sin_table):
    half_dim = inputs.shape[-1] // 2
    first_half = inputs[..., :half_dim]
    second_half = inputs[..., half_dim:]
    cos_part = cos_table[:, None, :]
    sin_part = sin_table[:, None, :]
    return jnp.concatenate(
        [
            first_half * cos_part + second_half * sin_part,
            second_half * cos_part - first_half * sin_part,
        ],
        axis=-1,
    )


def decay_masks(segment_row, head_ids):
    length = segment_row.shape[0]
    positions = jnp.arange(length, dtype=jnp.int32)
    distance = positions[:, None] - positions[None, :]
    allowed = (distance >= 0) & (segment_row[:, None] == segment_row[None, :])
    log_decay = jnp.log1p(-jnp.exp2(-5.0 - head_ids.astype(jnp.float32)))
    steps_back = jnp.maximum(distance, 0).astype(jnp.float32)
    score_scale = 1.0 / jnp.sqrt(jnp.float32(KEY_HEAD))
    return jnp.where(
        allowed[None], jnp.exp(steps_back[None] * log_decay[:, None, None]) * score_scale, 0.0
    )


def fetch_weights(w_query, w_key, w_value, w_gate, w_up, w_out, w_down):
    row_parts = (
        lax.all_gather(w_query, "fsdp", axis=0, tiled=True),
        lax.all_gather(w_key, "fsdp", axis=0, tiled=True),
        lax.all_gather(w_value, "fsdp", axis=0, tiled=True),
        lax.all_gather(w_gate, "fsdp", axis=0, tiled=True),
        lax.all_gather(w_up, "fsdp", axis=0, tiled=True),
    )
    col_parts = (
        lax.all_gather(w_out, "fsdp", axis=1, tiled=True),
        lax.all_gather(w_down, "fsdp", axis=1, tiled=True),
    )
    return tuple(row_parts) + tuple(col_parts)


def reduce_grads(local_grads):
    row_sums = (
        lax.psum_scatter(
            local_grads[0].astype(jnp.bfloat16), "fsdp", scatter_dimension=0, tiled=True
        ).astype(jnp.float32),
        lax.psum_scatter(
            local_grads[1].astype(jnp.bfloat16), "fsdp", scatter_dimension=0, tiled=True
        ).astype(jnp.float32),
        lax.psum_scatter(
            local_grads[2].astype(jnp.bfloat16), "fsdp", scatter_dimension=0, tiled=True
        ).astype(jnp.float32),
        lax.psum_scatter(
            local_grads[3].astype(jnp.bfloat16), "fsdp", scatter_dimension=0, tiled=True
        ).astype(jnp.float32),
        lax.psum_scatter(
            local_grads[4].astype(jnp.bfloat16), "fsdp", scatter_dimension=0, tiled=True
        ).astype(jnp.float32),
    )
    col_sums = (
        lax.psum_scatter(
            local_grads[5].astype(jnp.bfloat16), "fsdp", scatter_dimension=1, tiled=True
        ).astype(jnp.float32),
        lax.psum_scatter(
            local_grads[6].astype(jnp.bfloat16), "fsdp", scatter_dimension=1, tiled=True
        ).astype(jnp.float32),
    )
    return tuple(row_sums) + tuple(col_sums)


def add_tuples(running, latest):
    if running is None:
        return latest
    return tuple((accumulated + increment for accumulated, increment in zip(running, latest)))


def on_device(
    tokens, norm_gains, w_query, w_key, w_value, w_gate, w_out, w_up, w_down, segments, d_output
):
    micro_count = tokens.shape[0]
    heads_here = w_query.shape[1] // KEY_HEAD
    head_ids = lax.axis_index("seq") * heads_here + jnp.arange(heads_here, dtype=jnp.int32)
    gain_in = norm_gains[0]
    gain_mid = norm_gains[1]
    full_grads = None
    shard_grads = None
    gain_grads = None
    result_list = []
    input_grads = []
    gelu_plain = partial(jax.nn.gelu, approximate=True)
    for batch_index in range(micro_count):
        gathered = fetch_weights(w_query, w_key, w_value, w_gate, w_up, w_out, w_down)
        full_query, full_key, full_value, full_gate, full_up, full_out, full_down = gathered
        x_piece = tokens[batch_index, 0].astype(jnp.float32)
        segment_row = segments[batch_index, 0]
        normed_piece, scaled_in, inverse_in = layer_norm_parts(x_piece, gain_in)
        normed_in = lax.all_gather(normed_piece.astype(jnp.bfloat16), "seq", axis=0, tiled=True)
        length = normed_in.shape[0]
        cos_table, sin_table = rotation_tables(length, KEY_HEAD)
        query_rot = rotate(
            plain_product(normed_in, full_query).reshape(length, heads_here, KEY_HEAD),
            cos_table,
            sin_table,
        ).astype(jnp.bfloat16)
        key_rot = rotate(
            plain_product(normed_in, full_key).reshape(length, heads_here, KEY_HEAD),
            cos_table,
            sin_table,
        ).astype(jnp.bfloat16)
        values = (
            plain_product(normed_in, full_value)
            .astype(jnp.bfloat16)
            .reshape(length, heads_here, VAL_HEAD)
        )
        gate_raw = plain_product(normed_in, full_gate)
        decay = decay_masks(segment_row, head_ids)
        scores = jnp.einsum("nhk,mhk->hnm", query_rot, key_rot, preferred_element_type=jnp.float32)
        weights = (scores * decay).astype(jnp.bfloat16)
        retained = jnp.einsum("hnm,mhv->nhv", weights, values, preferred_element_type=jnp.float32)
        inverse_group = lax.rsqrt(jnp.mean(retained * retained, axis=-1, keepdims=True) + eps_group)
        group_normed = retained * inverse_group
        flat_normed = group_normed.reshape(length, heads_here * VAL_HEAD)
        swish, swish_pull = jax.vjp(jax.nn.silu, gate_raw)
        gated = (swish * flat_normed).astype(jnp.bfloat16)
        mixed = lax.psum_scatter(
            plain_product(gated, full_out).astype(jnp.bfloat16),
            "seq",
            scatter_dimension=0,
            tiled=True,
        ).astype(jnp.float32)
        resid_mid = x_piece + mixed
        normed_mid_piece, scaled_mid, inverse_mid = layer_norm_parts(resid_mid, gain_mid)
        normed_mid = lax.all_gather(
            normed_mid_piece.astype(jnp.bfloat16), "seq", axis=0, tiled=True
        )
        up_input = plain_product(normed_mid, full_up)
        activated_raw, gelu_pull = jax.vjp(gelu_plain, up_input)
        activated = activated_raw.astype(jnp.bfloat16)
        ffn_out = lax.psum_scatter(
            plain_product(activated, full_down).astype(jnp.bfloat16),
            "seq",
            scatter_dimension=0,
            tiled=True,
        ).astype(jnp.float32)
        result_list.append((resid_mid + ffn_out).astype(jnp.bfloat16))
        back_weights = fetch_weights(w_query, w_key, w_value, w_gate, w_up, w_out, w_down)
        back_query, back_key, back_value, back_gate, back_up, back_out, back_down = back_weights
        cot_piece = d_output[batch_index, 0]
        cot_whole = lax.all_gather(cot_piece, "seq", axis=0, tiled=True)
        d_activated = product_back(cot_whole, back_down)
        grad_down_local = token_sum(activated, cot_whole)
        d_up = gelu_pull(d_activated)[0].astype(jnp.bfloat16)
        grad_up_local = token_sum(normed_mid, d_up)
        d_normed_mid = lax.psum_scatter(
            product_back(d_up, back_up).astype(jnp.bfloat16), "seq", scatter_dimension=0, tiled=True
        ).astype(jnp.float32)
        d_resid_ln, gain_mid_grad = layer_norm_back(d_normed_mid, scaled_mid, inverse_mid, gain_mid)
        d_resid = cot_piece.astype(jnp.float32) + d_resid_ln
        d_mixed = lax.all_gather(d_resid.astype(jnp.bfloat16), "seq", axis=0, tiled=True)
        d_gated = product_back(d_mixed, back_out)
        grad_out_local = token_sum(gated, d_mixed)
        d_gate = swish_pull(d_gated * flat_normed)[0].astype(jnp.bfloat16)
        d_group = (d_gated * swish).reshape(length, heads_here, VAL_HEAD)
        d_retained = (
            (d_group - group_normed * jnp.mean(d_group * group_normed, axis=-1, keepdims=True))
            * inverse_group
        ).astype(jnp.bfloat16)
        scores_again = jnp.einsum(
            "nhk,mhk->hnm", query_rot, key_rot, preferred_element_type=jnp.float32
        )
        weights_again = (scores_again * decay).astype(jnp.bfloat16)
        d_weights = jnp.einsum(
            "nhv,mhv->hnm", d_retained, values, preferred_element_type=jnp.float32
        )
        d_values = (
            jnp.einsum(
                "hnm,nhv->mhv", weights_again, d_retained, preferred_element_type=jnp.float32
            )
            .astype(jnp.bfloat16)
            .reshape(length, heads_here * VAL_HEAD)
        )
        d_scores = (d_weights * decay).astype(jnp.bfloat16)
        d_query_rot = jnp.einsum(
            "hnm,mhk->nhk", d_scores, key_rot, preferred_element_type=jnp.float32
        )
        d_key_rot = jnp.einsum(
            "hnm,nhk->mhk", d_scores, query_rot, preferred_element_type=jnp.float32
        )
        d_query = (
            rotate_back(d_query_rot, cos_table, sin_table)
            .astype(jnp.bfloat16)
            .reshape(length, heads_here * KEY_HEAD)
        )
        d_key = (
            rotate_back(d_key_rot, cos_table, sin_table)
            .astype(jnp.bfloat16)
            .reshape(length, heads_here * KEY_HEAD)
        )
        d_normed_sum = (
            product_back(d_query, back_query)
            + product_back(d_key, back_key)
            + product_back(d_values, back_value)
            + product_back(d_gate, back_gate)
        )
        d_normed_in = lax.psum_scatter(
            d_normed_sum.astype(jnp.bfloat16), "seq", scatter_dimension=0, tiled=True
        ).astype(jnp.float32)
        d_input_ln, gain_in_grad = layer_norm_back(d_normed_in, scaled_in, inverse_in, gain_in)
        input_grads.append(d_resid + d_input_ln)
        local_grads = (
            token_sum(normed_in, d_query),
            token_sum(normed_in, d_key),
            token_sum(normed_in, d_values),
            token_sum(normed_in, d_gate),
            grad_up_local,
            grad_out_local,
            grad_down_local,
        )
        gain_grads = add_tuples(gain_grads, (jnp.stack([gain_in_grad, gain_mid_grad]),))
        full_grads = add_tuples(full_grads, local_grads)
    shard_grads = reduce_grads(full_grads)
    grad_norms = lax.psum(gain_grads[0], ("seq", "fsdp"))
    output = jnp.stack(result_list)[:, None]
    d_input = jnp.stack(input_grads)[:, None]
    return (
        output,
        d_input,
        grad_norms,
        shard_grads[0],
        shard_grads[1],
        shard_grads[2],
        shard_grads[3],
        shard_grads[5],
        shard_grads[4],
        shard_grads[6],
    )


def solution(mesh):
    placed = (
        P(None, "fsdp", "seq", None),
        P(),
        P("fsdp", "seq"),
        P("fsdp", "seq"),
        P("fsdp", "seq"),
        P("fsdp", "seq"),
        P("seq", "fsdp"),
        P("fsdp", "seq"),
        P("seq", "fsdp"),
        P(None, "fsdp", None),
        P(None, "fsdp", "seq", None),
    )
    return jax.shard_map(
        on_device,
        mesh=mesh,
        in_specs=placed,
        out_specs=(
            P(None, "fsdp", "seq", None),
            P(None, "fsdp", "seq", None),
            P(),
            P("fsdp", "seq"),
            P("fsdp", "seq"),
            P("fsdp", "seq"),
            P("fsdp", "seq"),
            P("seq", "fsdp"),
            P("fsdp", "seq"),
            P("seq", "fsdp"),
        ),
        check_vma=False,
    )
```

profile of v0, /device:TPU:1, one launch (start us, length us, event | category | flops | bytes accessed | tf_op | source)
XLA Modules:
  0.0 1610.0 jit_solution(138930825966965992)
XLA Ops:
  19.4 18.9 %all-gather.18.cloned.1.call-done = bf16[512,2048]{1,0:T(8,128)(2,1)} async-done(((bf16[128,2048]{1,0:T(8,128)(2,1)}), bf16[512,2048]{1,0:T(8,128)(2,1)}) %all-gather.18.cloned.1.call-update) | async-done | bytes 2097168 | tf_op jit(solution)/shard_map/all_gather | solution.py:172
  38.3 49.9 %all-gather.26.cloned.1.call-done = bf16[2048,512]{1,0:T(8,128)(2,1)} async-done(((bf16[256,512]{1,0:T(8,128)(2,1)}), bf16[2048,512]{1,0:T(8,128)(2,1)}) %all-gather.26.cloned.1.call-update) | async-done | bytes 2097168 | tf_op jit(solution)/shard_map/all_gather | solution.py:105
  96.1 42.1 %all-gather.24.cloned.1.call-done = bf16[2048,512]{1,0:T(8,128)(2,1)} async-done(((bf16[256,512]{1,0:T(8,128)(2,1)}), bf16[2048,512]{1,0:T(8,128)(2,1)}) %all-gather.24.cloned.1.call-update) | async-done | bytes 2097168 | tf_op jit(solution)/shard_map/all_gather | solution.py:104
  150.7 61.3 %all-gather.22.cloned.1.call-done = bf16[2048,1024]{1,0:T(8,128)(2,1)} async-done(((bf16[256,1024]{1,0:T(8,128)(2,1)}), bf16[2048,1024]{1,0:T(8,128)(2,1)}) %all-gather.22.cloned.1.call-update) | async-done | bytes 4194320 | tf_op jit(solution)/shard_map/all_gather | solution.py:106
  222.6 63.1 %all-gather.20.cloned.1.call-done = bf16[2048,1024]{1,0:T(8,128)(2,1)} async-done(((bf16[256,1024]{1,0:T(8,128)(2,1)}), bf16[2048,1024]{1,0:T(8,128)(2,1)}) %all-gather.20.cloned.1.call-update) | async-done | bytes 4194320 | tf_op jit(solution)/shard_map/all_gather | solution.py:107
  285.7 7.3 multiply_convert_fusion.8
  293.0 68.7 %all-gather.28.cloned.1.call-done = bf16[1024,2048]{1,0:T(8,128)(2,1)} async-done(((bf16[1024,256]{1,0:T(8,128)(2,1)}), bf16[1024,2048]{1,0:T(8,128)(2,1)}) %all-gather.28.cloned.1.call-update) | async-done | bytes 4194320 | tf_op jit(solution)/shard_map/all_gather | solution.py:111
  367.6 30.1 %reduce-scatter.16.cloned.1.call-done = bf16[128,2048]{1,0:T(8,128)(2,1)} async-done(((bf16[512,2048]{1,0:T(8,128)(2,1)}), bf16[128,2048]{1,0:T(8,128)(2,1)}) %reduce-scatter.16.cloned.1.call-update) | async-done | bytes 524304 | tf_op jit(solution)/shard_map/reduce_scatter | solution.py:200
  401.9 22.2 %all-gather.36.cloned.1.call-done = bf16[512,2048]{1,0:T(8,128)(2,1)} async-done(((bf16[128,2048]{1,0:T(8,128)(2,1)}), bf16[512,2048]{1,0:T(8,128)(2,1)}) %all-gather.36.cloned.1.call-update) | async-done | bytes 2097168 | tf_op jit(solution)/shard_map/all_gather | solution.py:172
  454.1 7.5 multiply_convert_fusion.5
  467.0 30.3 %reduce-scatter.20.cloned.1.call-done = bf16[128,2048]{1,0:T(8,128)(2,1)} async-done(((bf16[512,2048]{1,0:T(8,128)(2,1)}), bf16[128,2048]{1,0:T(8,128)(2,1)}) %reduce-scatter.20.cloned.1.call-update) | async-done | bytes 524304 | tf_op jit(solution)/shard_map/reduce_scatter | solution.py:200
  505.2 66.4 %all-gather.32.cloned.1.call-done = bf16[2048,1024]{1,0:T(8,128)(2,1)} async-done(((bf16[256,1024]{1,0:T(8,128)(2,1)}), bf16[2048,1024]{1,0:T(8,128)(2,1)}) %all-gather.32.cloned.1.call-update) | async-done | bytes 4194320 | tf_op jit(solution)/shard_map/all_gather | solution.py:108
  571.6 24.6 %all-gather.38.cloned.1.call-done = bf16[512,2048]{1,0:T(8,128)(2,1)} async-done(((bf16[128,2048]{1,0:T(8,128)(2,1)}), bf16[512,2048]{1,0:T(8,128)(2,1)}) %all-gather.38.cloned.1.call-update) | async-done | bytes 2097168 | tf_op jit(solution)/shard_map/all_gather | solution.py:208
  602.7 18.2 %all-gather.46.cloned.1.call-done = bf16[1,1,512,2048]{3,2,1,0:T(8,128)(2,1)} async-done(((bf16[1,1,128,2048]{3,2,1,0:T(8,128)(2,1)}), bf16[1,1,512,2048]{3,2,1,0:T(8,128)(2,1)}) %all-gather.46.cloned.1.call-update) | async-done | bytes 2097168 | tf_op jit(solution)/shard_map/all_gather | solution.py:224
  620.8 76.3 %all-gather.34.cloned.1.call-done = bf16[1024,2048]{1,0:T(8,128)(2,1)} async-done(((bf16[1024,256]{1,0:T(8,128)(2,1)}), bf16[1024,2048]{1,0:T(8,128)(2,1)}) %all-gather.34.cloned.1.call-update) | async-done | bytes 4194320 | tf_op jit(solution)/shard_map/all_gather | solution.py:112
  709.1 11.6 all-gather.30.cloned.1.call-done
  727.3 18.0 %all-gather.44.cloned.1.call-done = bf16[1,1,512,2048]{3,2,1,0:T(8,128)(2,1)} async-done(((bf16[1,1,128,2048]{3,2,1,0:T(8,128)(2,1)}), bf16[1,1,512,2048]{3,2,1,0:T(8,128)(2,1)}) %all-gather.44.cloned.1.call-update) | async-done | bytes 2097168 | tf_op jit(solution)/shard_map/all_gather | solution.py:224
  763.9 14.9 reduce-scatter.28.cloned.1.call-done
  778.8 34.0 %reduce-scatter.24.cloned.1.call-done = bf16[128,2048]{1,0:T(8,128)(2,1)} async-done(((bf16[512,2048]{1,0:T(8,128)(2,1)}), bf16[128,2048]{1,0:T(8,128)(2,1)}) %reduce-scatter.24.cloned.1.call-update) | async-done | bytes 524304 | tf_op jit(solution)/shard_map/reduce_scatter | solution.py:229
  815.5 31.1 %reduce-scatter.22.cloned.1.call-done = bf16[128,2048]{1,0:T(8,128)(2,1)} async-done(((bf16[512,2048]{1,0:T(8,128)(2,1)}), bf16[128,2048]{1,0:T(8,128)(2,1)}) %reduce-scatter.22.cloned.1.call-update) | async-done | bytes 524304 | tf_op jit(solution)/shard_map/reduce_scatter | solution.py:214
  874.1 8.7 fusion.104
  885.7 13.0 all-gather.42.cloned.1.call-done
  898.8 8.7 fusion.105
  1012.8 69.3 %reduce-scatter.42.cloned.1.call-done = bf16[256,1024]{1,0:T(8,128)(2,1)} async-done(((bf16[2048,1024]{1,0:T(8,128)(2,1)}), bf16[256,1024]{1,0:T(8,128)(2,1)}) %reduce-scatter.42.cloned.1.call-update) | async-done | bytes 524304 | tf_op jit(solution)/shard_map/reduce_scatter | solution.py:131
  1084.2 67.3 %reduce-scatter.32.cloned.1.call-done = bf16[256,512]{1,0:T(8,128)(2,1)} async-done(((bf16[2048,512]{1,0:T(8,128)(2,1)}), bf16[256,512]{1,0:T(8,128)(2,1)}) %reduce-scatter.32.cloned.1.call-update) | async-done | bytes 262160 | tf_op jit(solution)/shard_map/reduce_scatter | solution.py:119
  1153.4 68.6 %reduce-scatter.34.cloned.1.call-done = bf16[256,512]{1,0:T(8,128)(2,1)} async-done(((bf16[2048,512]{1,0:T(8,128)(2,1)}), bf16[256,512]{1,0:T(8,128)(2,1)}) %reduce-scatter.34.cloned.1.call-update) | async-done | bytes 262160 | tf_op jit(solution)/shard_map/reduce_scatter | solution.py:122
  1223.8 33.7 %reduce-scatter.26.cloned.1.call-done = bf16[128,2048]{1,0:T(8,128)(2,1)} async-done(((bf16[512,2048]{1,0:T(8,128)(2,1)}), bf16[128,2048]{1,0:T(8,128)(2,1)}) %reduce-scatter.26.cloned.1.call-update) | async-done | bytes 524304 | tf_op jit(solution)/shard_map/reduce_scatter | solution.py:280
  1257.5 33.9 %reduce-scatter.30.cloned.1.call-done = bf16[128,2048]{1,0:T(8,128)(2,1)} async-done(((bf16[512,2048]{1,0:T(8,128)(2,1)}), bf16[128,2048]{1,0:T(8,128)(2,1)}) %reduce-scatter.30.cloned.1.call-update) | async-done | bytes 524304 | tf_op jit(solution)/shard_map/reduce_scatter | solution.py:280
  1293.6 39.2 %psum.7 = f32[2,2048]{1,0:T(2,128)} all-reduce(f32[2,2048]{1,0:T(2,128)S(1)} %maximum_add_fusion), channel_id=1, replica_groups=mesh['seq'=4,'fsdp'=8] {'seq','fsdp'}, use_global_device_ids=true, to_apply=%region_32.33 | all-reduce | flops 4096 | bytes 32768 | tf_op jit(solution)/shard_map/psum | solution.py:297
  1339.8 77.8 %reduce-scatter.40.cloned.1.call-done = bf16[1024,256]{1,0:T(8,128)(2,1)} async-done(((bf16[1024,2048]{1,0:T(8,128)(2,1)}), bf16[1024,256]{1,0:T(8,128)(2,1)}) %reduce-scatter.40.cloned.1.call-update) | async-done | bytes 524304 | tf_op jit(solution)/shard_map/reduce_scatter | solution.py:136
  1419.7 89.9 %reduce-scatter.38.cloned.1.call-done = bf16[256,1024]{1,0:T(8,128)(2,1)} async-done(((bf16[2048,1024]{1,0:T(8,128)(2,1)}), bf16[256,1024]{1,0:T(8,128)(2,1)}) %reduce-scatter.38.cloned.1.call-update) | async-done | bytes 524304 | tf_op jit(solution)/shard_map/reduce_scatter | solution.py:128
  1511.7 89.2 %reduce-scatter.36.cloned.1.call-done = bf16[256,1024]{1,0:T(8,128)(2,1)} async-done(((bf16[2048,1024]{1,0:T(8,128)(2,1)}), bf16[256,1024]{1,0:T(8,128)(2,1)}) %reduce-scatter.36.cloned.1.call-update) | async-done | bytes 524304 | tf_op jit(solution)/shard_map/reduce_scatter | solution.py:125
  (399 shorter events, 298.4 us)
Async XLA Ops:
  7.2 31.1 %all-gather.18.cloned.1.call-start = ((), (), s32[]{:S(2)}) async-start(), calls=%async_computation.15 | async-start | bytes 2621440 | tf_op jit(solution)/shard_map/all_gather | solution.py:172
  10.8 388.3 %copy-start.56 = (f32[1,2048]{1,0:T(1,128)}, f32[1,2048]{1,0:T(1,128)S(1)}, u32[]{:S(2)}) copy-start(f32[1,2048]{1,0:T(1,128)S(1)} %get-tuple-element.99) | copy-start | bytes 24580
  13.1 75.2 %all-gather.26.cloned.1.call-start = ((), (), s32[]{:S(2)}) async-start(), calls=%async_computation.19 | async-start | bytes 2359296 | tf_op jit(solution)/shard_map/all_gather | solution.py:105
  13.8 124.4 %all-gather.24.cloned.1.call-start = ((), (), s32[]{:S(2)}) async-start(), calls=%async_computation.18 | async-start | bytes 2359296 | tf_op jit(solution)/shard_map/all_gather | solution.py:104
  14.6 197.4 %all-gather.22.cloned.1.call-start = ((), (), s32[]{:S(2)}) async-start(), calls=%async_computation.17 | async-start | bytes 4718592 | tf_op jit(solution)/shard_map/all_gather | solution.py:106
  15.1 270.5 %all-gather.20.cloned.1.call-start = ((), (), s32[]{:S(2)}) async-start(), calls=%async_computation.16 | async-start | bytes 4718592 | tf_op jit(solution)/shard_map/all_gather | solution.py:107
  15.7 345.9 %all-gather.28.cloned.1.call-start = ((), (), s32[]{:S(2)}) async-start(), calls=%async_computation.20 | async-start | bytes 4718592 | tf_op jit(solution)/shard_map/all_gather | solution.py:111
  16.3 381.5 %reduce-scatter.16.cloned.1.call-start = ((), (), s32[]{:S(2)}) async-start(), calls=%async_computation.21 | async-start | bytes 2621440 | tf_op jit(solution)/shard_map/reduce_scatter | solution.py:200
  367.6 56.5 %all-gather.36.cloned.1.call-start = ((), (), s32[]{:S(2)}) async-start(), calls=%async_computation.26 | async-start | bytes 2621440 | tf_op jit(solution)/shard_map/all_gather | solution.py:172
  400.9 96.4 %reduce-scatter.20.cloned.1.call-start = ((), (), s32[]{:S(2)}) async-start(), calls=%async_computation.27 | async-start | bytes 2621440 | tf_op jit(solution)/shard_map/reduce_scatter | solution.py:200
  466.2 105.4 %all-gather.32.cloned.1.call-start = ((), (), s32[]{:S(2)}) async-start(), calls=%async_computation.23 | async-start | bytes 4718592 | tf_op jit(solution)/shard_map/all_gather | solution.py:108
  466.8 129.4 %all-gather.38.cloned.1.call-start = ((), (), s32[]{:S(2)}) async-start(), calls=%async_computation.28 | async-start | bytes 2621440 | tf_op jit(solution)/shard_map/all_gather | solution.py:208
  500.9 120.0 %all-gather.46.cloned.1.call-start = ((), (), s32[]{:S(2)}) async-start(), calls=%async_computation.44 | async-start | bytes 2621440 | tf_op jit(solution)/shard_map/all_gather | solution.py:224
  503.2 193.9 %all-gather.34.cloned.1.call-start = ((), (), s32[]{:S(2)}) async-start(), calls=%async_computation.24 | async-start | bytes 4718592 | tf_op jit(solution)/shard_map/all_gather | solution.py:112
  504.0 216.7 %all-gather.30.cloned.1.call-start = ((), (), s32[]{:S(2)}) async-start(), calls=%async_computation.22 | async-start | bytes 2621440 | tf_op jit(solution)/shard_map/all_gather | solution.py:208
  504.6 240.8 %all-gather.44.cloned.1.call-start = ((), (), s32[]{:S(2)}) async-start(), calls=%async_computation.43 | async-start | bytes 2621440 | tf_op jit(solution)/shard_map/all_gather | solution.py:224
  505.2 273.6 %reduce-scatter.28.cloned.1.call-start = ((), (), s32[]{:S(2)}) async-start(), calls=%async_computation.33 | async-start | bytes 2621440 | tf_op jit(solution)/shard_map/reduce_scatter | solution.py:229
  708.9 103.9 %reduce-scatter.24.cloned.1.call-start = ((), (), s32[]{:S(2)}) async-start(), calls=%async_computation.30 | async-start | bytes 2621440 | tf_op jit(solution)/shard_map/reduce_scatter | solution.py:229
  757.1 89.5 %reduce-scatter.22.cloned.1.call-start = ((), (), s32[]{:S(2)}) async-start(), calls=%async_computation.29 | async-start | bytes 2621440 | tf_op jit(solution)/shard_map/reduce_scatter | solution.py:214
  763.8 110.2 %all-gather.40.cloned.1.call-start = ((), (), s32[]{:S(2)}) async-start(), calls=%async_computation.31 | async-start | bytes 2621440 | tf_op jit(solution)/shard_map/all_gather | solution.py:234
  850.9 47.8 %all-gather.42.cloned.1.call-start = ((), (), s32[]{:S(2)}) async-start(), calls=%async_computation.34 | async-start | bytes 2621440 | tf_op jit(solution)/shard_map/all_gather | solution.py:234
  851.5 159.2 %reduce-scatter.44.cloned.1.call-start = ((), (), s32[]{:S(2)}) async-start(), calls=%async_computation.42 | async-start | bytes 4718592 | tf_op jit(solution)/shard_map/reduce_scatter | solution.py:139
  861.9 220.2 %reduce-scatter.42.cloned.1.call-start = ((), (), s32[]{:S(2)}) async-start(), calls=%async_computation.41 | async-start | bytes 4718592 | tf_op jit(solution)/shard_map/reduce_scatter | solution.py:131
  871.0 280.5 %reduce-scatter.32.cloned.1.call-start = ((), (), s32[]{:S(2)}) async-start(), calls=%async_computation.36 | async-start | bytes 2359296 | tf_op jit(solution)/shard_map/reduce_scatter | solution.py:119
  937.4 284.6 %reduce-scatter.34.cloned.1.call-start = ((), (), s32[]{:S(2)}) async-start(), calls=%async_computation.37 | async-start | bytes 2359296 | tf_op jit(solution)/shard_map/reduce_scatter | solution.py:122
  950.8 306.7 %reduce-scatter.26.cloned.1.call-start = ((), (), s32[]{:S(2)}) async-start(), calls=%async_computation.32 | async-start | bytes 2621440 | tf_op jit(solution)/shard_map/reduce_scatter | solution.py:280
  963.6 327.8 %reduce-scatter.30.cloned.1.call-start = ((), (), s32[]{:S(2)}) async-start(), calls=%async_computation.35 | async-start | bytes 2621440 | tf_op jit(solution)/shard_map/reduce_scatter | solution.py:280
  977.0 355.9 %reduce-scatter.18.cloned.1.call-start = ((), (), s32[]{:S(2)}) async-start(), calls=%async_computation.25 | async-start | bytes 2621440 | tf_op jit(solution)/shard_map/reduce_scatter | solution.py:214
  983.7 433.9 %reduce-scatter.40.cloned.1.call-start = ((), (), s32[]{:S(2)}) async-start(), calls=%async_computation.40 | async-start | bytes 4718592 | tf_op jit(solution)/shard_map/reduce_scatter | solution.py:136
  993.3 516.3 %reduce-scatter.38.cloned.1.call-start = ((), (), s32[]{:S(2)}) async-start(), calls=%async_computation.39 | async-start | bytes 4718592 | tf_op jit(solution)/shard_map/reduce_scatter | solution.py:128
  1001.8 599.0 %reduce-scatter.36.cloned.1.call-start = ((), (), s32[]{:S(2)}) async-start(), calls=%async_computation.38 | async-start | bytes 4718592 | tf_op jit(solution)/shard_map/reduce_scatter | solution.py:125
  1010.6 280.7 %copy-start.57 = (f32[1,2048]{1,0:T(1,128)S(1)}, f32[1,2048]{1,0:T(1,128)}, u32[]{:S(2)}) copy-start(f32[1,2048]{1,0:T(1,128)} %copy-done.56) | copy-start | bytes 24580
  (99 other events, 2427.7 us)
Sparse Core Ops, SparseCore 0:
  13.2 25.0 all-gather.17
  40.4 47.7 all-gather.25
  90.4 47.7 all-gather.23
  140.1 71.7 all-gather.21
  214.0 71.6 all-gather.19
  287.6 74.0 all-gather.27
  367.7 30.0 reduce-scatter.15
  401.0 22.9 all-gather.35
  466.3 31.0 reduce-scatter.19
  499.3 72.2 all-gather.31
  573.8 22.4 all-gather.37
  598.2 22.5 all-gather.45
  622.9 74.1 all-gather.33
  699.1 21.5 all-gather.29
  722.7 22.5 all-gather.43
  747.7 31.0 reduce-scatter.27
  781.3 31.3 reduce-scatter.23
  815.1 31.4 reduce-scatter.21
  851.1 22.9 all-gather.39
  876.1 22.5 all-gather.41
  902.8 87.9 reduce-scatter.43
  994.4 87.6 reduce-scatter.41
  1086.1 65.4 reduce-scatter.31
  1155.4 66.5 reduce-scatter.33
  1225.2 32.2 reduce-scatter.25
  1259.9 31.4 reduce-scatter.29
  1293.9 31.5 reduce-scatter.17
  1329.1 88.4 reduce-scatter.39
  1421.7 87.8 reduce-scatter.37
  1513.0 87.7 reduce-scatter.35
where the time goes:
time: 1620 us; the launch traced here: 1610 us
  waiting for transfers between devices  1230 us (76%)
  matrix products  196 us (12%)
  other arithmetic  64.2 us (4%)
  local copies, waits for them, and re-layouts  57.7 us (4%)
  blocking collectives  39.2 us (2%)
    reduce_scatter x1, waiting for transfers between devices, reduce_grads(): lax.psum_scatter(local_grads[3].astype(jnp.bfloat16), 'fsdp', scatter_dim...  89.9 us
    reduce_scatter x1, waiting for transfers between devices, reduce_grads(): lax.psum_scatter(local_grads[2].astype(jnp.bfloat16), 'fsdp', scatter_dim...  89.2 us
    reduce_scatter x1, waiting for transfers between devices, reduce_grads(): lax.psum_scatter(local_grads[5].astype(jnp.bfloat16), 'fsdp', scatter_dim...  77.8 us
    all_gather x1, waiting for transfers between devices, fetch_weights(): lax.all_gather(w_down, 'fsdp', axis=1, tiled=True)  76.3 us
    dot_general x14, matrix products, plain_product(): return jnp.dot(left, right, preferred_element_type=jnp.float32)  71.1 us
    reduce_scatter x1, waiting for transfers between devices, reduce_grads(): lax.psum_scatter(local_grads[4].astype(jnp.bfloat16), 'fsdp', scatter_dim...  69.3 us
    all_gather x1, waiting for transfers between devices, fetch_weights(): lax.all_gather(w_out, 'fsdp', axis=1, tiled=True)  68.7 us
    reduce_scatter x1, waiting for transfers between devices, reduce_grads(): lax.psum_scatter(local_grads[1].astype(jnp.bfloat16), 'fsdp', scatter_dim...  68.6 us
  transfers between devices with their start and end apart: 30, of which 28 were waited for; matrix products, arithmetic and copies ran while one was open for 15% of the time, Pallas kernels for 0%

commit v1 on v0

v1 whole, which is shorter than its diff:
```python
import jax
import jax.numpy as jnp
from jax import lax
from jax.sharding import PartitionSpec as P

KEY_HEAD = 256
VAL_HEAD = 512
eps_norm = 1e-05
eps_group = 1.0
BF = jnp.bfloat16
F32 = jnp.float32
AXES = ("seq", "fsdp")


def mm(left, right):
    return jnp.dot(left, right, preferred_element_type=F32)


def mm_t(left, right):
    return lax.dot_general(left, right, (((1,), (1,)), ((), ())), preferred_element_type=F32)


def mm_tok(left, right):
    return lax.dot_general(left, right, (((0,), (0,)), ((), ())), preferred_element_type=F32)


class Grid:
    def __init__(self, n_seq, n_fsdp):
        self.n_seq, self.n_fsdp = n_seq, n_fsdp
        self.ny, self.nz = n_seq // 2, n_fsdp // 2
        self.masks = [0]
        bit = self.nz // 2
        self.z_bits = []
        while bit:
            self.z_bits.append(bit)
            self.masks = self.masks + [m ^ bit for m in self.masks]
            bit //= 2
        self.y_bits = []
        bit = self.ny // 2
        while bit:
            self.y_bits.append(bit)
            bit //= 2

    def pairs(self, move):
        found = []
        for y in range(self.ny):
            for c in range(2):
                for z in range(self.nz):
                    for x in range(2):
                        y2, c2, z2, x2 = move(y, c, z, x)
                        src = (y * 2 + c) * self.n_fsdp + z * 2 + x
                        dst = (y2 * 2 + c2) * self.n_fsdp + z2 * 2 + x2
                        if src != dst:
                            found.append((src, dst))
        return found

    def send(self, value, move):
        return lax.ppermute(value, AXES, self.pairs(move))

    def flip_z(self, value, bit):
        return self.send(value, lambda y, c, z, x: (y, c, z ^ bit, x))

    def flip_c(self, value):
        return self.send(value, lambda y, c, z, x: (y, 1 - c, z, x))

    def flip_y(self, value, bit):
        return self.send(value, lambda y, c, z, x: (y ^ bit, c, z, x))

    def flip_x(self, value):
        return self.send(value, lambda y, c, z, x: (y, c, z, 1 - x))

    def swap(self, value, same):
        other = self.send(value, lambda y, c, z, x: (y, x, z, c))
        return jnp.where(same, value, other)


def gather_weight(grid, shard):
    held = shard
    for bit in grid.z_bits:
        held = jnp.concatenate([held, grid.flip_z(held, bit)], axis=0)
    return jnp.concatenate([held, grid.flip_c(held)], axis=0)


def scatter_grad(grid, grad, same):
    half = grad.shape[0] // 2
    held = grad[:half] + grid.flip_c(grad[half:].astype(BF)).astype(F32)
    for bit in reversed(grid.z_bits):
        half = held.shape[0] // 2
        held = held[:half] + grid.flip_z(held[half:].astype(BF), bit).astype(F32)
    return held


def gather_tokens(grid, block):
    held = block
    for bit in grid.y_bits:
        held = jnp.concatenate([held, grid.flip_y(held, bit)], axis=0)
    return jnp.concatenate([held, grid.flip_x(held)], axis=0)


def scatter_tokens(grid, partial):
    half = partial.shape[0] // 2
    held = partial[:half] + grid.flip_x(partial[half:].astype(BF)).astype(F32)
    for bit in reversed(grid.y_bits):
        half = held.shape[0] // 2
        held = held[:half] + grid.flip_y(held[half:].astype(BF), bit).astype(F32)
    return held


def layer_norm_parts(inputs, gain_row):
    center = inputs - jnp.mean(inputs, axis=-1, keepdims=True)
    inverse = lax.rsqrt(jnp.mean(center * center, axis=-1, keepdims=True) + eps_norm)
    scaled = center * inverse
    return (scaled * gain_row, scaled, inverse)


def layer_norm_back(incoming, scaled, inverse, gain_row):
    upstream = incoming * gain_row
    centered_grad = (
        upstream
        - jnp.mean(upstream, axis=-1, keepdims=True)
        - scaled * jnp.mean(upstream * scaled, axis=-1, keepdims=True)
    )
    return (centered_grad * inverse, jnp.sum(incoming * scaled, axis=0))


def rotate(inputs, cos_table, sin_table, sign):
    pieces = []
    half = KEY_HEAD // 2
    for start in range(0, inputs.shape[-1], KEY_HEAD):
        first = inputs[:, start : start + half]
        second = inputs[:, start + half : start + KEY_HEAD]
        pieces.append(first * cos_table - sign * (second * sin_table))
        pieces.append(second * cos_table + sign * (first * sin_table))
    return jnp.concatenate(pieces, axis=-1)


def decay_masks(segment_row, positions, head_ids):
    distance = positions[:, None] - positions[None, :]
    allowed = (distance >= 0) & (segment_row[:, None] == segment_row[None, :])
    log_decay = jnp.log1p(-jnp.exp2(-5.0 - head_ids.astype(F32)))
    steps_back = jnp.maximum(distance, 0).astype(F32)
    score_scale = 1.0 / jnp.sqrt(F32(KEY_HEAD))
    return jnp.where(
        allowed[None], jnp.exp(steps_back[None] * log_decay[:, None, None]) * score_scale, 0.0
    )


def make_on_device(grid):
    n_slots = grid.n_fsdp

    def on_device(
        tokens, norm_gains, w_query, w_key, w_value, w_gate, w_out, w_up, w_down, segments, d_output
    ):
        micro = tokens.shape[0]
        piece = tokens.shape[2]
        width = tokens.shape[3]
        col = width // n_slots
        heads_here = w_query.shape[1] // KEY_HEAD
        dk = heads_here * KEY_HEAD
        seq_id = lax.axis_index("seq")
        fsdp_id = lax.axis_index("fsdp")
        y, c = seq_id // 2, seq_id % 2
        z, x = fsdp_id // 2, fsdp_id % 2
        same = x == c
        place = y * 2 + x
        head_ids = place * heads_here + jnp.arange(heads_here, dtype=jnp.int32)

        slot_block = [2 * (z ^ m) + (c ^ p) for p in range(2) for m in grid.masks]
        back = jnp.asarray([grid.masks.index(m) for m in range(grid.nz)], jnp.int32)
        block_slot = [
            (p ^ c) * grid.nz + back[zb ^ z] for zb in range(grid.nz) for p in range(2)
        ]

        def pick(value, blocks):
            return jnp.concatenate(
                [lax.dynamic_slice_in_dim(value, b * col, col, axis=-1) for b in blocks], axis=-1
            )

        shards = [
            jnp.concatenate([w_query, w_key], axis=1),
            w_value,
            w_gate,
            w_out.T,
            w_up,
            w_down.T,
        ]
        toks = grid.swap(tokens.reshape(micro * piece, width), same)
        segs = grid.swap(segments.reshape(micro, -1), same)
        shards = [grid.swap(s, same) for s in shards]
        full_qk, full_v, full_g, full_o, full_u, full_d = [gather_weight(grid, s) for s in shards]
        cots = grid.swap(d_output.reshape(micro * piece, width), same)

        gains = pick(norm_gains, slot_block)
        gain_in, gain_mid = gains[0], gains[1]
        xin = pick(toks, slot_block).astype(F32)
        cot_own = pick(cots, slot_block)

        y_masks = [0]
        for bit in grid.y_bits:
            y_masks = y_masks + [m ^ bit for m in y_masks]
        ranks = [2 * (y ^ m) + (x ^ p) for p in range(2) for m in y_masks]
        positions = jnp.concatenate(
            [r * piece + jnp.arange(piece, dtype=jnp.int32) for r in ranks]
        )
        half = KEY_HEAD // 2
        frequency = jnp.exp(
            -jnp.log(10000.0) * 2.0 * jnp.arange(half, dtype=F32) / KEY_HEAD
        )
        angles = positions.astype(F32)[:, None] * frequency[None, :]
        cos_table, sin_table = jnp.cos(angles), jnp.sin(angles)
        segs_order = [
            jnp.concatenate(
                [lax.dynamic_slice_in_dim(segs[b], r * piece, piece) for r in ranks]
            )
            for b in range(micro)
        ]

        def rows(value, b):
            return value[b * piece : (b + 1) * piece]

        normed, scaled_in, inverse_in = layer_norm_parts(xin, gain_in)
        normed = normed.astype(BF)
        saved = []
        outs = []
        for b in range(micro):
            h1 = gather_tokens(grid, rows(normed, b))
            qk = mm(h1, full_qk)
            qr = rotate(qk[:, :dk], cos_table, sin_table, 1.0).astype(BF)
            kr = rotate(qk[:, dk:], cos_table, sin_table, 1.0).astype(BF)
            values = mm(h1, full_v).astype(BF)
            gate = mm(h1, full_g)
            decay = decay_masks(segs_order[b], positions, head_ids)
            weights, retained = [], []
            for h in range(heads_here):
                ks = slice(h * KEY_HEAD, (h + 1) * KEY_HEAD)
                vs = slice(h * VAL_HEAD, (h + 1) * VAL_HEAD)
                w = (mm_t(qr[:, ks], kr[:, ks]) * decay[h]).astype(BF)
                weights.append(w)
                retained.append(mm(w, values[:, vs]))
            rgroup = [
                lax.rsqrt(jnp.mean(r * r, axis=-1, keepdims=True) + eps_group) for r in retained
            ]
            ynorm = jnp.concatenate([r * g for r, g in zip(retained, rgroup)], axis=-1)
            sig = jax.nn.sigmoid(gate)
            swish = gate * sig
            gated = (swish * ynorm).astype(BF)
            mixed = scatter_tokens(grid, mm_t(gated, full_o))
            x1 = rows(xin, b) + mixed
            normed_mid, scaled_mid, inverse_mid = layer_norm_parts(x1, gain_mid)
            h2 = gather_tokens(grid, normed_mid.astype(BF))
            up = mm(h2, full_u)
            act, gelu_pull = jax.vjp(lambda t: jax.nn.gelu(t, approximate=True), up)
            act = act.astype(BF)
            ffn = scatter_tokens(grid, mm_t(act, full_d))
            outs.append((x1 + ffn).astype(BF))
            saved.append(
                (h1, qr, kr, values, gate, sig, swish, decay, weights, rgroup, ynorm, gated)
                + (scaled_mid, inverse_mid, h2, gelu_pull, act)
            )

        sums = [None] * 6
        gain_grads = None
        d_inputs = []
        stage = []
        for b in range(micro):
            act, gelu_pull, h2 = saved[b][16], saved[b][15], saved[b][14]
            cot = gather_tokens(grid, rows(cot_own, b))
            g_down = mm_tok(cot, act)
            d_act = mm(cot, full_d)
            d_up = gelu_pull(d_act)[0].astype(BF)
            g_up = mm_tok(h2, d_up)
            d_h2 = scatter_tokens(grid, mm_t(d_up, full_u))
            stage.append((g_down, g_up, d_h2))
        rest = []
        for b in range(micro):
            (h1, qr, kr, values, gate, sig, swish, decay, weights, rgroup, ynorm, gated) = saved[b][:12]
            scaled_mid, inverse_mid = saved[b][12:14]
            g_down, g_up, d_h2 = stage[b]
            d_ln, gain_mid_grad = layer_norm_back(d_h2, scaled_mid, inverse_mid, gain_mid)
            d_x1 = rows(cot_own, b).astype(F32) + d_ln
            d_mix = gather_tokens(grid, d_x1.astype(BF))
            d_gated = mm(d_mix, full_o)
            g_out = mm_tok(d_mix, gated)
            d_gate = (d_gated * ynorm * sig * (1.0 + gate * (1.0 - sig))).astype(BF)
            d_yn = d_gated * swish
            d_q, d_k, d_v = [], [], []
            for h in range(heads_here):
                ks = slice(h * KEY_HEAD, (h + 1) * KEY_HEAD)
                vs = slice(h * VAL_HEAD, (h + 1) * VAL_HEAD)
                dy_h, yn_h = d_yn[:, vs], ynorm[:, vs]
                d_ret = (
                    (dy_h - yn_h * jnp.mean(dy_h * yn_h, axis=-1, keepdims=True)) * rgroup[h]
                ).astype(BF)
                d_w = mm_t(d_ret, values[:, vs])
                d_v.append(mm_tok(weights[h], d_ret).astype(BF))
                d_s = (d_w * decay[h]).astype(BF)
                d_q.append(mm(d_s, kr[:, ks]))
                d_k.append(mm_tok(d_s, qr[:, ks]))
            d_qk = rotate(
                jnp.concatenate(d_q + d_k, axis=-1), cos_table, sin_table, -1.0
            ).astype(BF)
            d_v = jnp.concatenate(d_v, axis=-1)
            d_h1 = mm_t(d_qk, full_qk) + mm_t(d_v, full_v) + mm_t(d_gate, full_g)
            d_h1 = scatter_tokens(grid, d_h1)
            d_ln1, gain_in_grad = layer_norm_back(
                d_h1, rows(scaled_in, b), rows(inverse_in, b), gain_in
            )
            d_inputs.append(d_x1 + d_ln1)
            grads = (
                mm_tok(h1, d_qk),
                mm_tok(h1, d_v),
                mm_tok(h1, d_gate),
                g_out,
                g_up,
                g_down,
            )
            sums = [g if s is None else s + g for s, g in zip(sums, grads)]
            both = jnp.stack([gain_in_grad, gain_mid_grad])
            gain_grads = both if gain_grads is None else gain_grads + both

        def finish(value):
            moved = grid.send(value.astype(BF), lambda y, c, z, x: (y, x, z, c))
            return jnp.where(same, value, moved.astype(value.dtype))

        done = [finish(scatter_grad(grid, g, same)) for g in sums]
        grad_norms = lax.psum(pick(gain_grads, block_slot), AXES)
        output = finish(pick(jnp.concatenate(outs), block_slot))
        d_input = finish(pick(jnp.concatenate(d_inputs), block_slot))
        shape = (micro, 1, piece, width)
        return (
            output.reshape(shape),
            d_input.reshape(shape),
            grad_norms,
            done[0][:, :dk],
            done[0][:, dk:],
            done[1],
            done[2],
            done[3].T,
            done[4],
            done[5].T,
        )

    return on_device


def solution(mesh):
    grid = Grid(mesh.shape["seq"], mesh.shape["fsdp"])
    rows = P("fsdp", "seq")
    cols = P("seq", "fsdp")
    tok = P(None, "fsdp", "seq", None)
    return jax.shard_map(
        make_on_device(grid),
        mesh=mesh,
        in_specs=(tok, P(), rows, rows, rows, rows, cols, rows, cols, P(None, "fsdp", None), tok),
        out_specs=(tok, tok, P(), rows, rows, rows, rows, cols, rows, cols),
        check_vma=False,
    )
```

time: 1620 us -> 1090 us (0.67)
  waiting for transfers between devices: 1230 us -> 530 us
  starting transfers between devices: 3.07 us -> 143 us
  other arithmetic: 64.2 us -> 102 us
  matrix products: 196 us -> 178 us
  local copies, waits for them, and re-layouts: 57.7 us -> 74.4 us
    reduce_scatter x15 -> x0, waiting for transfers between devices: 670 us -> none  [the longest x1 89.9 us: reduce_grads(): lax.psum_scatter(local_grads[3].astype(jnp.bfloat16), 'fsdp', scatter_dim...]
    all_gather x15 -> x0, waiting for transfers between devices: 557 us -> none  [the longest x1 76.3 us: fetch_weights(): lax.all_gather(w_down, 'fsdp', axis=1, tiled=True)]
    ppermute x0 -> x85, waiting for transfers between devices: none -> 530 us  [send(): return lax.ppermute(value, AXES, self.pairs(move))]
    ppermute x0 -> x85, starting transfers between devices: none -> 143 us  [send(): return lax.ppermute(value, AXES, self.pairs(move))]
    add x1 -> x24, other arithmetic: 0.03 us -> 30 us  [the longest x6 16.5 us: scatter_grad(): held = grad[:half] + grid.flip_c(grad[half:].astype(BF)).astype(F32)]
    select_n x0 -> x16, other arithmetic: none -> 20.6 us  [the longest x6 13.1 us: finish(): return jnp.where(same, value, moved.astype(value.dtype))]
    slice x7 -> x40, local copies, waits for them, and re-layouts: 7.36 us -> 26.2 us  [the longest x6 10.3 us: scatter_grad(): held = grad[:half] + grid.flip_c(grad[half:].astype(BF)).astype(F32)]
    dot_general x54 -> x60, matrix products: 196 us -> 178 us  [the longest x20 69.6 us: mm_t(): lax.dot_general(left, right, (((1,), (1,)), ((), ())), preferred_element_...]
  transfers between devices with their start and end apart: 30 -> 85, of which waited for: 28 -> 37; matrix products, arithmetic and copies ran while one was open for 15% -> 30% of each run, Pallas kernels for 0% -> 0%
where the time goes in v1:
time: 1090 us; the launch traced here: 1080 us
  waiting for transfers between devices  530 us (49%)
  matrix products  178 us (16%)
  starting transfers between devices  143 us (13%)
  other arithmetic  102 us (9%)
  local copies, waits for them, and re-layouts  74.4 us (7%)
  blocking collectives  44.6 us (4%)
    ppermute x85, waiting for transfers between devices, send(): return lax.ppermute(value, AXES, self.pairs(move))  530 us
    ppermute x85, starting transfers between devices, send(): return lax.ppermute(value, AXES, self.pairs(move))  143 us
    dot_general x20, matrix products, mm_t(): lax.dot_general(left, right, (((1,), (1,)), ((), ())), preferred_element_...  69.6 us
    dot_general x20, matrix products, mm(): return jnp.dot(left, right, preferred_element_type=F32)  65.1 us
    psum x1, blocking collectives, on_device(): grad_norms = lax.psum(pick(gain_grads, block_slot), AXES)  44.6 us
    dot_general x20, matrix products, mm_tok(): lax.dot_general(left, right, (((0,), (0,)), ((), ())), preferred_element_...  42.8 us
    unnamed x528, local copies, waits for them, and re-layouts  35.9 us
  transfers between devices with their start and end apart: 85, of which 37 were waited for; matrix products, arithmetic and copies ran while one was open for 30% of the time, Pallas kernels for 0%

profile of v1, /device:TPU:1, one launch (start us, length us, event | category | flops | bytes accessed | tf_op | source)
XLA Modules:
  0.0 1082.7 jit_solution(6825428028961947795)
XLA Ops:
  52.8 24.9 %collective-permute-done.8 = bf16[256,1024]{1,0:T(8,128)(2,1)S(1)} collective-permute-done((bf16[256,1024]{1,0:T(8,128)(2,1)S(1)}, bf16[256,1024]{1,0:T(8,128)(2,1)S(1)}, u32[]{:S(2)}, u32[]{:S(2)}) %collective-permute-start.8) | collective-permute-done | bytes 524320 | tf_op jit(solution)/shard_map/ppermute | solution.py:58
  78.1 22.2 %collective-permute-done.13 = bf16[256,1024]{1,0:T(8,128)(2,1)S(1)} collective-permute-done((bf16[256,1024]{1,0:T(8,128)(2,1)S(1)}, bf16[256,1024]{1,0:T(8,128)(2,1)S(1)}, u32[]{:S(2)}, u32[]{:S(2)}) %collective-permute-start.13) | collective-permute-done | bytes 524320 | tf_op jit(solution)/shard_map/ppermute | solution.py:58
  102.5 41.1 %collective-permute-done.9 = bf16[512,1024]{1,0:T(8,128)(2,1)S(1)} collective-permute-done((bf16[512,1024]{1,0:T(8,128)(2,1)S(1)}, bf16[512,1024]{1,0:T(8,128)(2,1)S(1)}, u32[]{:S(2)}, u32[]{:S(2)}) %collective-permute-start.9) | collective-permute-done | bytes 1048608 | tf_op jit(solution)/shard_map/ppermute | solution.py:58
  158.5 18.7 %collective-permute-done.25 = bf16[256,1024]{1,0:T(8,128)(2,1)S(1)} collective-permute-done((bf16[256,1024]{1,0:T(8,128)(2,1)S(1)}, bf16[256,1024]{1,0:T(8,128)(2,1)S(1)}, u32[]{:S(2)}, u32[]{:S(2)}) %collective-permute-start.25) | collective-permute-done | bytes 524320 | tf_op jit(solution)/shard_map/ppermute | solution.py:58
  184.7 8.8 collective-permute-done.1
  205.9 29.4 %collective-permute-done.18 = bf16[512,1024]{1,0:T(8,128)(2,1)S(1)} collective-permute-done((bf16[512,1024]{1,0:T(8,128)(2,1)S(1)}, bf16[512,1024]{1,0:T(8,128)(2,1)S(1)}, u32[]{:S(2)}, u32[]{:S(2)}) %collective-permute-start.18) | collective-permute-done | bytes 1048608 | tf_op jit(solution)/shard_map/ppermute | solution.py:58
  312.2 17.6 %collective-permute-done.20 = bf16[256,2048]{1,0:T(8,128)(2,1)S(1)} collective-permute-done((bf16[256,2048]{1,0:T(8,128)(2,1)S(1)}, bf16[256,2048]{1,0:T(8,128)(2,1)S(1)}, u32[]{:S(2)}, u32[]{:S(2)}) %collective-permute-start.20) | collective-permute-done | bytes 1048608 | tf_op jit(solution)/shard_map/ppermute | solution.py:58
  359.8 7.8 collective-permute-done.52
  370.3 8.4 collective-permute-done.44
  382.1 7.9 collective-permute-done.22
  404.7 40.8 %collective-permute-done.23 = bf16[256,2048]{1,0:T(8,128)(2,1)S(1)} collective-permute-done((bf16[256,2048]{1,0:T(8,128)(2,1)S(1)}, bf16[256,2048]{1,0:T(8,128)(2,1)S(1)}, u32[]{:S(2)}, u32[]{:S(2)}) %collective-permute-start.23) | collective-permute-done | bytes 1048608 | tf_op jit(solution)/shard_map/ppermute | solution.py:58
  510.6 23.9 %collective-permute-done.46 = bf16[256,2048]{1,0:T(8,128)(2,1)} collective-permute-done((bf16[256,2048]{1,0:T(8,128)(2,1)}, bf16[256,2048]{1,0:T(8,128)(2,1)}, u32[]{:S(2)}, u32[]{:S(2)}) %collective-permute-start.46) | collective-permute-done | bytes 1048608 | tf_op jit(solution)/shard_map/ppermute | solution.py:58
  537.6 19.2 %collective-permute-done.40 = bf16[256,2048]{1,0:T(8,128)(2,1)S(1)} collective-permute-done((bf16[256,2048]{1,0:T(8,128)(2,1)}, bf16[256,2048]{1,0:T(8,128)(2,1)S(1)}, u32[]{:S(2)}, u32[]{:S(2)}) %collective-permute-start.40) | collective-permute-done | bytes 1048608 | tf_op jit(solution)/shard_map/ppermute | solution.py:58
  558.7 20.6 %collective-permute-done.54 = bf16[256,2048]{1,0:T(8,128)(2,1)S(1)} collective-permute-done((bf16[256,2048]{1,0:T(8,128)(2,1)S(1)}, bf16[256,2048]{1,0:T(8,128)(2,1)S(1)}, u32[]{:S(2)}, u32[]{:S(2)}) %collective-permute-start.54) | collective-permute-done | bytes 1048608 | tf_op jit(solution)/shard_map/ppermute | solution.py:58
  583.2 8.0 collective-permute-done.41
  591.2 11.2 %collective-permute-done.55 = bf16[128,2048]{1,0:T(8,128)(2,1)S(1)} collective-permute-done((bf16[128,2048]{1,0:T(8,128)(2,1)S(1)}, bf16[128,2048]{1,0:T(8,128)(2,1)S(1)}, u32[]{:S(2)}, u32[]{:S(2)}) %collective-permute-start.55) | collective-permute-done | bytes 524320 | tf_op jit(solution)/shard_map/ppermute | solution.py:58
  604.1 9.6 collective-permute-done.33
  618.1 6.5 collective-permute-start.42
  631.8 6.8 collective-permute-done.48
  643.4 14.9 %collective-permute-done.57 = bf16[256,2048]{1,0:T(8,128)(2,1)S(1)} collective-permute-done((bf16[256,2048]{1,0:T(8,128)(2,1)S(1)}, bf16[256,2048]{1,0:T(8,128)(2,1)S(1)}, u32[]{:S(2)}, u32[]{:S(2)}) %collective-permute-start.57) | collective-permute-done | bytes 1048608 | tf_op jit(solution)/shard_map/ppermute | solution.py:58
  668.8 11.9 %collective-permute-done.49 = bf16[256,2048]{1,0:T(8,128)(2,1)S(1)} collective-permute-done((bf16[256,2048]{1,0:T(8,128)(2,1)S(1)}, bf16[256,2048]{1,0:T(8,128)(2,1)S(1)}, u32[]{:S(2)}, u32[]{:S(2)}) %collective-permute-start.49) | collective-permute-done | bytes 1048608 | tf_op jit(solution)/shard_map/ppermute | solution.py:58
  681.8 6.6 multiply_convert_fusion.1
  758.5 7.8 fusion.292
  770.0 12.2 %add_add_fusion = f32[512,2048]{1,0:T(8,128)} fusion(f32[512,2048]{1,0:T(8,128)} %fusion.292, f32[512,2048]{1,0:T(8,128)} %fusion.45, bf16[512,1024]{1,0:T(8,128)(2,1)} %get-tuple-element.49, bf16[1024,1024]{1,0:T(8,128)(2,1)} %collective-permute-done.6, bf16[512,1024]{1,0:T(8,128)(2,1)} %copy-done.151, bf16[256,1024]{1,0:T(8,128)(2,1)} %copy-done.99, ...), kind=kOutput, calls=%fused_computation.34 | convolution fusion | flops 2166358016 | bytes 17825792 | tf_op jit(solution)/shard_map/dot_general | solution.py:20
  804.7 11.5 %collective-permute-done.58 = bf16[256,2048]{1,0:T(8,128)(2,1)S(1)} collective-permute-done((bf16[256,2048]{1,0:T(8,128)(2,1)S(1)}, bf16[256,2048]{1,0:T(8,128)(2,1)S(1)}, u32[]{:S(2)}, u32[]{:S(2)}) %collective-permute-start.58) | collective-permute-done | bytes 1048608 | tf_op jit(solution)/shard_map/ppermute | solution.py:58
  832.3 7.9 collective-permute-done.59
  851.8 44.6 %psum.7 = f32[2,2048]{1,0:T(2,128)} all-reduce(f32[2,2048]{1,0:T(2,128)S(1)} %constant_dynamic-update-slice_fusion.50), channel_id=1, replica_groups=mesh['seq'=4,'fsdp'=8] {'seq','fsdp'}, use_global_device_ids=true, to_apply=%region_26.27 | all-reduce | flops 4096 | bytes 32768 | tf_op jit(solution)/shard_map/psum | solution.py:326
  919.2 6.6 collective-permute-done.74
  928.8 30.7 %collective-permute-done.70 = bf16[512,1024]{1,0:T(8,128)(2,1)} collective-permute-done((bf16[512,1024]{1,0:T(8,128)(2,1)}, bf16[512,1024]{1,0:T(8,128)(2,1)}, u32[]{:S(2)}, u32[]{:S(2)}) %collective-permute-start.70) | collective-permute-done | bytes 1048608 | tf_op jit(solution)/shard_map/ppermute | solution.py:58
  961.2 31.9 %collective-permute-done.66 = bf16[512,1024]{1,0:T(8,128)(2,1)S(1)} collective-permute-done((bf16[512,1024]{1,0:T(8,128)(2,1)S(1)}, bf16[512,1024]{1,0:T(8,128)(2,1)S(1)}, u32[]{:S(2)}, u32[]{:S(2)}) %collective-permute-start.66) | collective-permute-done | bytes 1048608 | tf_op jit(solution)/shard_map/ppermute | solution.py:58
  993.7 22.0 %collective-permute-done.62 = bf16[512,1024]{1,0:T(8,128)(2,1)S(1)} collective-permute-done((bf16[512,1024]{1,0:T(8,128)(2,1)S(1)}, bf16[512,1024]{1,0:T(8,128)(2,1)S(1)}, u32[]{:S(2)}, u32[]{:S(2)}) %collective-permute-start.62) | collective-permute-done | bytes 1048608 | tf_op jit(solution)/shard_map/ppermute | solution.py:58
  1024.8 38.0 %collective-permute-done.63 = bf16[256,1024]{1,0:T(8,128)(2,1)S(1)} collective-permute-done((bf16[256,1024]{1,0:T(8,128)(2,1)S(1)}, bf16[256,1024]{1,0:T(8,128)(2,1)S(1)}, u32[]{:S(2)}, u32[]{:S(2)}) %collective-permute-start.63) | collective-permute-done | bytes 524320 | tf_op jit(solution)/shard_map/ppermute | solution.py:58
  (923 shorter events, 492.5 us)
Async XLA Ops:
  37.1 144.8 %collective-permute-start.43 = (bf16[256,2048]{1,0:T(8,128)(2,1)S(1)}, bf16[256,2048]{1,0:T(8,128)(2,1)S(1)}, u32[]{:S(2)}, u32[]{:S(2)}) collective-permute-start(bf16[256,2048]{1,0:T(8,128)(2,1)S(1)} %bitcast.120), channel_id=1, source_target_pairs={{1,8},{3,10},{5,12},{7,14},{8,1},{10,3},{12,5},{14,7},{17,24},{19,... | collective-permute-start | bytes 3145736 | tf_op jit(solution)/shard_map/ppermute | solution.py:58
  40.2 103.7 %collective-permute-start.28 = (bf16[256,1024]{1,0:T(8,128)(2,1)S(1)}, bf16[256,1024]{1,0:T(8,128)(2,1)S(1)}, u32[]{:S(2)}, u32[]{:S(2)}) collective-permute-start(bf16[256,1024]{1,0:T(8,128)(2,1)S(1)} %bitcast.118), channel_id=1, source_target_pairs={{1,8},{3,10},{5,12},{7,14},{8,1},{10,3},{12,5},{14,7},{17,24},{19,... | collective-permute-start | bytes 1572872 | tf_op jit(solution)/shard_map/ppermute | solution.py:58
  48.9 96.6 %collective-permute-start.4 = (bf16[256,1024]{1,0:T(8,128)(2,1)S(1)}, bf16[256,1024]{1,0:T(8,128)(2,1)S(1)}, u32[]{:S(2)}, u32[]{:S(2)}) collective-permute-start(bf16[256,1024]{1,0:T(8,128)(2,1)S(1)} %broadcast_select_fusion.8), channel_id=1, source_target_pairs={{0,4},{1,5},{2,6},{3,7},{4,0},{5,1},{6,2},{7,3},{8,12},{9,13},{10,... | collective-permute-start | bytes 1572872 | tf_op jit(solution)/shard_map/ppermute | solution.py:58
  77.7 69.3 %collective-permute-start.17 = (bf16[256,1024]{1,0:T(8,128)(2,1)S(1)}, bf16[256,1024]{1,0:T(8,128)(2,1)S(1)}, u32[]{:S(2)}, u32[]{:S(2)}) collective-permute-start(bf16[256,1024]{1,0:T(8,128)(2,1)S(1)} %broadcast_select_fusion.5), channel_id=1, source_target_pairs={{0,4},{1,5},{2,6},{3,7},{4,0},{5,1},{6,2},{7,3},{8,12},{9,13},{10,... | collective-permute-start | bytes 1572872 | tf_op jit(solution)/shard_map/ppermute | solution.py:58
  145.5 91.9 %collective-permute-start.10 = (bf16[1024,1024]{1,0:T(8,128)(2,1)S(1)}, bf16[1024,1024]{1,0:T(8,128)(2,1)S(1)}, u32[]{:S(2)}, u32[]{:S(2)}) collective-permute-start(bf16[1024,1024]{1,0:T(8,128)(2,1)S(1)} %pad_maximum_fusion.8), channel_id=1, source_target_pairs={{0,8},{1,9},{2,10},{3,11},{4,12},{5,13},{6,14},{7,15},{8,0},{9,1},... | collective-permute-start | bytes 6291464 | tf_op jit(solution)/shard_map/ppermute | solution.py:58
  177.3 58.1 %collective-permute-start.18 = (bf16[512,1024]{1,0:T(8,128)(2,1)S(1)}, bf16[512,1024]{1,0:T(8,128)(2,1)S(1)}, u32[]{:S(2)}, u32[]{:S(2)}) collective-permute-start(bf16[512,1024]{1,0:T(8,128)(2,1)S(1)} %pad_maximum_fusion.26), channel_id=1, source_target_pairs={{0,2},{1,3},{2,0},{3,1},{4,6},{5,7},{6,4},{7,5},{8,10},{9,11},{10,... | collective-permute-start | bytes 3145736 | tf_op jit(solution)/shard_map/ppermute | solution.py:58
  183.1 53.9 %collective-permute-start.35 = (bf16[256,2048]{1,0:T(8,128)(2,1)S(1)}, bf16[256,2048]{1,0:T(8,128)(2,1)S(1)}, u32[]{:S(2)}, u32[]{:S(2)}) collective-permute-start(bf16[256,2048]{1,0:T(8,128)(2,1)S(1)} %pad_maximum_fusion.30), channel_id=1, source_target_pairs={{0,1},{1,0},{2,3},{3,2},{4,5},{5,4},{6,7},{7,6},{8,9},{9,8},{10,11... | collective-permute-start | bytes 3145736 | tf_op jit(solution)/shard_map/ppermute | solution.py:58
  201.6 105.3 %collective-permute-start.29 = (bf16[256,1024]{1,0:T(8,128)(2,1)}, bf16[256,1024]{1,0:T(8,128)(2,1)}, u32[]{:S(2)}, u32[]{:S(2)}) collective-permute-start(bf16[256,1024]{1,0:T(8,128)(2,1)} %broadcast_select_fusion.3), channel_id=1, source_target_pairs={{0,4},{1,5},{2,6},{3,7},{4,0},{5,1},{6,2},{7,3},{8,12},{9,13},{10,... | collective-permute-start | bytes 1572872 | tf_op jit(solution)/shard_map/ppermute | solution.py:58
  235.3 98.2 %collective-permute-start.26 = (bf16[512,1024]{1,0:T(8,128)(2,1)}, bf16[512,1024]{1,0:T(8,128)(2,1)}, u32[]{:S(2)}, u32[]{:S(2)}) collective-permute-start(bf16[512,1024]{1,0:T(8,128)(2,1)} %pad_maximum_fusion.28), channel_id=1, source_target_pairs={{0,2},{1,3},{2,0},{3,1},{4,6},{5,7},{6,4},{7,5},{8,10},{9,11},{10,... | collective-permute-start | bytes 3145736 | tf_op jit(solution)/shard_map/ppermute | solution.py:58
  336.2 56.9 %collective-permute-start.27 = (bf16[1024,1024]{1,0:T(8,128)(2,1)}, bf16[1024,1024]{1,0:T(8,128)(2,1)}, u32[]{:S(2)}, u32[]{:S(2)}) collective-permute-start(bf16[1024,1024]{1,0:T(8,128)(2,1)} %pad_maximum_fusion.13), channel_id=1, source_target_pairs={{0,8},{1,9},{2,10},{3,11},{4,12},{5,13},{6,14},{7,15},{8,0},{9,1},... | collective-permute-start | bytes 6291464 | tf_op jit(solution)/shard_map/ppermute | solution.py:58
  380.3 69.8 %collective-permute-start.45 = (bf16[256,2048]{1,0:T(8,128)(2,1)S(1)}, bf16[256,2048]{1,0:T(8,128)(2,1)S(1)}, u32[]{:S(2)}, u32[]{:S(2)}) collective-permute-start(bf16[256,2048]{1,0:T(8,128)(2,1)S(1)} %pad_maximum_fusion.32), channel_id=1, source_target_pairs={{0,1},{1,0},{2,3},{3,2},{4,5},{5,4},{6,7},{7,6},{8,9},{9,8},{10,11... | collective-permute-start | bytes 3145736 | tf_op jit(solution)/shard_map/ppermute | solution.py:58
  389.9 70.1 %collective-permute-start.31 = (bf16[1024,1024]{1,0:T(8,128)(2,1)S(1)}, bf16[1024,1024]{1,0:T(8,128)(2,1)}, u32[]{:S(2)}, u32[]{:S(2)}) collective-permute-start(bf16[1024,1024]{1,0:T(8,128)(2,1)S(1)} %pad_maximum_fusion.14), channel_id=1, source_target_pairs={{0,8},{1,9},{2,10},{3,11},{4,12},{5,13},{6,14},{7,15},{8,0},{9,1},... | collective-permute-start | bytes 6291464 | tf_op jit(solution)/shard_map/ppermute | solution.py:58
  393.1 52.4 %collective-permute-start.23 = (bf16[256,2048]{1,0:T(8,128)(2,1)S(1)}, bf16[256,2048]{1,0:T(8,128)(2,1)S(1)}, u32[]{:S(2)}, u32[]{:S(2)}) collective-permute-start(bf16[256,2048]{1,0:T(8,128)(2,1)S(1)} %pad_maximum_fusion.27), channel_id=1, source_target_pairs={{0,1},{1,0},{2,3},{3,2},{4,5},{5,4},{6,7},{7,6},{8,9},{9,8},{10,11... | collective-permute-start | bytes 3145736 | tf_op jit(solution)/shard_map/ppermute | solution.py:58
  454.8 169.8 %collective-permute-start.81 = (bf16[1024,1024]{1,0:T(8,128)(2,1)}, bf16[1024,1024]{1,0:T(8,128)(2,1)}, u32[]{:S(2)}, u32[]{:S(2)}) collective-permute-start(bf16[1024,1024]{1,0:T(8,128)(2,1)} %slice.1052), channel_id=1, source_target_pairs={{0,8},{1,9},{2,10},{3,11},{4,12},{5,13},{6,14},{7,15},{8,0},{9,1},... | collective-permute-start | bytes 6291464 | tf_op jit(solution)/shard_map/ppermute | solution.py:58
  480.8 148.4 %collective-permute-start.77 = (bf16[1024,1024]{1,0:T(8,128)(2,1)}, bf16[1024,1024]{1,0:T(8,128)(2,1)S(1)}, u32[]{:S(2)}, u32[]{:S(2)}) collective-permute-start(bf16[1024,1024]{1,0:T(8,128)(2,1)} %slice.1053), channel_id=1, source_target_pairs={{0,8},{1,9},{2,10},{3,11},{4,12},{5,13},{6,14},{7,15},{8,0},{9,1},... | collective-permute-start | bytes 6291464 | tf_op jit(solution)/shard_map/ppermute | solution.py:58
  487.7 93.5 %collective-permute-start.32 = (bf16[256,2048]{1,0:T(8,128)(2,1)}, bf16[256,2048]{1,0:T(8,128)(2,1)S(1)}, u32[]{:S(2)}, u32[]{:S(2)}) collective-permute-start(bf16[256,2048]{1,0:T(8,128)(2,1)} %slice.1070), channel_id=1, source_target_pairs={{0,1},{1,0},{2,3},{3,2},{4,5},{5,4},{6,7},{7,6},{8,9},{9,8},{10,11... | collective-permute-start | bytes 3145736 | tf_op jit(solution)/shard_map/ppermute | solution.py:58
  627.4 67.2 %collective-permute-start.82 = (bf16[512,1024]{1,0:T(8,128)(2,1)S(1)}, bf16[512,1024]{1,0:T(8,128)(2,1)S(1)}, u32[]{:S(2)}, u32[]{:S(2)}) collective-permute-start(bf16[512,1024]{1,0:T(8,128)(2,1)S(1)} %slice.1058), channel_id=1, source_target_pairs={{0,2},{1,3},{2,0},{3,1},{4,6},{5,7},{6,4},{7,5},{8,10},{9,11},{10,... | collective-permute-start | bytes 3145736 | tf_op jit(solution)/shard_map/ppermute | solution.py:58
  630.5 73.1 %collective-permute-start.78 = (bf16[512,1024]{1,0:T(8,128)(2,1)S(1)}, bf16[512,1024]{1,0:T(8,128)(2,1)S(1)}, u32[]{:S(2)}, u32[]{:S(2)}) collective-permute-start(bf16[512,1024]{1,0:T(8,128)(2,1)S(1)} %slice.1059), channel_id=1, source_target_pairs={{0,2},{1,3},{2,0},{3,1},{4,6},{5,7},{6,4},{7,5},{8,10},{9,11},{10,... | collective-permute-start | bytes 3145736 | tf_op jit(solution)/shard_map/ppermute | solution.py:58
  696.3 95.1 %collective-permute-start.83 = (bf16[256,1024]{1,0:T(8,128)(2,1)}, bf16[256,1024]{1,0:T(8,128)(2,1)S(1)}, u32[]{:S(2)}, u32[]{:S(2)}) collective-permute-start(bf16[256,1024]{1,0:T(8,128)(2,1)} %slice.1072), channel_id=1, source_target_pairs={{0,4},{1,5},{2,6},{3,7},{4,0},{5,1},{6,2},{7,3},{8,12},{9,13},{10,... | collective-permute-start | bytes 1572872 | tf_op jit(solution)/shard_map/ppermute | solution.py:58
  705.6 89.2 %collective-permute-start.79 = (bf16[256,1024]{1,0:T(8,128)(2,1)}, bf16[256,1024]{1,0:T(8,128)(2,1)}, u32[]{:S(2)}, u32[]{:S(2)}) collective-permute-start(bf16[256,1024]{1,0:T(8,128)(2,1)} %slice.1073), channel_id=1, source_target_pairs={{0,4},{1,5},{2,6},{3,7},{4,0},{5,1},{6,2},{7,3},{8,12},{9,13},{10,... | collective-permute-start | bytes 1572872 | tf_op jit(solution)/shard_map/ppermute | solution.py:58
  713.0 183.4 %collective-permute-start.73 = (bf16[1024,1024]{1,0:T(8,128)(2,1)}, bf16[1024,1024]{1,0:T(8,128)(2,1)}, u32[]{:S(2)}, u32[]{:S(2)}) collective-permute-start(bf16[1024,1024]{1,0:T(8,128)(2,1)} %slice.1054), channel_id=1, source_target_pairs={{0,8},{1,9},{2,10},{3,11},{4,12},{5,13},{6,14},{7,15},{8,0},{9,1},... | collective-permute-start | bytes 6291464 | tf_op jit(solution)/shard_map/ppermute | solution.py:58
  723.7 179.3 %collective-permute-start.69 = (bf16[1024,1024]{1,0:T(8,128)(2,1)}, bf16[1024,1024]{1,0:T(8,128)(2,1)}, u32[]{:S(2)}, u32[]{:S(2)}) collective-permute-start(bf16[1024,1024]{1,0:T(8,128)(2,1)} %slice.1055), channel_id=1, source_target_pairs={{0,8},{1,9},{2,10},{3,11},{4,12},{5,13},{6,14},{7,15},{8,0},{9,1},... | collective-permute-start | bytes 6291464 | tf_op jit(solution)/shard_map/ppermute | solution.py:58
  828.1 79.7 %collective-permute-start.65 = (bf16[1024,1024]{1,0:T(8,128)(2,1)}, bf16[1024,1024]{1,0:T(8,128)(2,1)}, u32[]{:S(2)}, u32[]{:S(2)}) collective-permute-start(bf16[1024,1024]{1,0:T(8,128)(2,1)} %slice.1056), channel_id=1, source_target_pairs={{0,8},{1,9},{2,10},{3,11},{4,12},{5,13},{6,14},{7,15},{8,0},{9,1},... | collective-permute-start | bytes 6291464 | tf_op jit(solution)/shard_map/ppermute | solution.py:58
  830.8 81.3 %collective-permute-start.61 = (bf16[1024,1024]{1,0:T(8,128)(2,1)}, bf16[1024,1024]{1,0:T(8,128)(2,1)}, u32[]{:S(2)}, u32[]{:S(2)}) collective-permute-start(bf16[1024,1024]{1,0:T(8,128)(2,1)} %slice.1057), channel_id=1, source_target_pairs={{0,8},{1,9},{2,10},{3,11},{4,12},{5,13},{6,14},{7,15},{8,0},{9,1},... | collective-permute-start | bytes 6291464 | tf_op jit(solution)/shard_map/ppermute | solution.py:58
  846.6 68.6 %collective-permute-start.60 = (bf16[256,2048]{1,0:T(8,128)(2,1)S(1)}, bf16[256,2048]{1,0:T(8,128)(2,1)}, u32[]{:S(2)}, u32[]{:S(2)}) collective-permute-start(bf16[256,2048]{1,0:T(8,128)(2,1)S(1)} %convert_element_type.370), channel_id=1, source_target_pairs={{1,8},{3,10},{5,12},{7,14},{8,1},{10,3},{12,5},{14,7},{17,24},{19,... | collective-permute-start | bytes 3145736 | tf_op jit(solution)/shard_map/ppermute | solution.py:58
  910.8 82.4 %collective-permute-start.66 = (bf16[512,1024]{1,0:T(8,128)(2,1)S(1)}, bf16[512,1024]{1,0:T(8,128)(2,1)S(1)}, u32[]{:S(2)}, u32[]{:S(2)}) collective-permute-start(bf16[512,1024]{1,0:T(8,128)(2,1)S(1)} %slice.1062), channel_id=1, source_target_pairs={{0,2},{1,3},{2,0},{3,1},{4,6},{5,7},{6,4},{7,5},{8,10},{9,11},{10,... | collective-permute-start | bytes 3145736 | tf_op jit(solution)/shard_map/ppermute | solution.py:58
  915.0 100.7 %collective-permute-start.62 = (bf16[512,1024]{1,0:T(8,128)(2,1)S(1)}, bf16[512,1024]{1,0:T(8,128)(2,1)S(1)}, u32[]{:S(2)}, u32[]{:S(2)}) collective-permute-start(bf16[512,1024]{1,0:T(8,128)(2,1)S(1)} %slice.1063), channel_id=1, source_target_pairs={{0,2},{1,3},{2,0},{3,1},{4,6},{5,7},{6,4},{7,5},{8,10},{9,11},{10,... | collective-permute-start | bytes 3145736 | tf_op jit(solution)/shard_map/ppermute | solution.py:58
  927.5 88.8 %collective-permute-start.75 = (bf16[256,1024]{1,0:T(8,128)(2,1)S(1)}, bf16[256,1024]{1,0:T(8,128)(2,1)S(1)}, u32[]{:S(2)}, u32[]{:S(2)}) collective-permute-start(bf16[256,1024]{1,0:T(8,128)(2,1)S(1)} %slice.1074), channel_id=1, source_target_pairs={{0,4},{1,5},{2,6},{3,7},{4,0},{5,1},{6,2},{7,3},{8,12},{9,13},{10,... | collective-permute-start | bytes 1572872 | tf_op jit(solution)/shard_map/ppermute | solution.py:58
  961.2 60.8 %collective-permute-start.71 = (bf16[256,1024]{1,0:T(8,128)(2,1)S(1)}, bf16[256,1024]{1,0:T(8,128)(2,1)S(1)}, u32[]{:S(2)}, u32[]{:S(2)}) collective-permute-start(bf16[256,1024]{1,0:T(8,128)(2,1)S(1)} %slice.1075), channel_id=1, source_target_pairs={{0,4},{1,5},{2,6},{3,7},{4,0},{5,1},{6,2},{7,3},{8,12},{9,13},{10,... | collective-permute-start | bytes 1572872 | tf_op jit(solution)/shard_map/ppermute | solution.py:58
  993.7 72.5 %collective-permute-start.67 = (bf16[256,1024]{1,0:T(8,128)(2,1)S(1)}, bf16[256,1024]{1,0:T(8,128)(2,1)S(1)}, u32[]{:S(2)}, u32[]{:S(2)}) collective-permute-start(bf16[256,1024]{1,0:T(8,128)(2,1)S(1)} %slice.1076), channel_id=1, source_target_pairs={{0,4},{1,5},{2,6},{3,7},{4,0},{5,1},{6,2},{7,3},{8,12},{9,13},{10,... | collective-permute-start | bytes 1572872 | tf_op jit(solution)/shard_map/ppermute | solution.py:58
  1016.5 53.9 %collective-permute-start.76 = (bf16[256,1024]{1,0:T(8,128)(2,1)S(1)}, bf16[256,1024]{1,0:T(8,128)(2,1)S(1)}, u32[]{:S(2)}, u32[]{:S(2)}) collective-permute-start(bf16[256,1024]{1,0:T(8,128)(2,1)S(1)} %fusion.50), channel_id=1, source_target_pairs={{1,8},{3,10},{5,12},{7,14},{8,1},{10,3},{12,5},{14,7},{17,24},{19,... | collective-permute-start | bytes 1572872 | tf_op jit(solution)/shard_map/ppermute | solution.py:58
  1022.9 54.5 %collective-permute-start.72 = (bf16[256,1024]{1,0:T(8,128)(2,1)}, bf16[256,1024]{1,0:T(8,128)(2,1)}, u32[]{:S(2)}, u32[]{:S(2)}) collective-permute-start(bf16[256,1024]{1,0:T(8,128)(2,1)} %fusion.49), channel_id=1, source_target_pairs={{1,8},{3,10},{5,12},{7,14},{8,1},{10,3},{12,5},{14,7},{17,24},{19,... | collective-permute-start | bytes 1572872 | tf_op jit(solution)/shard_map/ppermute | solution.py:58
  (300 other events, 5891.9 us)

commit v2 on v1

v2 whole, which is shorter than its diff:
```python
import functools

import jax
import jax.numpy as jnp
from jax import lax
from jax.experimental import pallas as pl
from jax.experimental.pallas import tpu as pltpu
from jax.sharding import PartitionSpec as P

KEY_HEAD = 256
VAL_HEAD = 512
ROT = KEY_HEAD // 2
eps_norm = 1e-05
eps_group = 1.0
BF = jnp.bfloat16
F32 = jnp.float32
AXES = ("seq", "fsdp")
ANY = pl.BlockSpec(memory_space=pl.ANY)


def nn(left, right):
    return jnp.dot(left, right, preferred_element_type=F32)


def nt(left, right):
    return lax.dot_general(left, right, (((1,), (1,)), ((), ())), preferred_element_type=F32)


def tn(left, right):
    return lax.dot_general(left, right, (((0,), (0,)), ((), ())), preferred_element_type=F32)


def after(value, *first):
    return lax.optimization_barrier((value, *first))[0]


class Grid:
    def __init__(self, n_seq, n_fsdp):
        assert n_seq == 4 and n_fsdp % 2 == 0
        self.n_fsdp, self.nz = n_fsdp, n_fsdp // 2
        self.lines = [[z * 2 + x for z in range(self.nz)] for x in range(2)]

    def send(self, value, move):
        found = []
        for y in range(2):
            for c in range(2):
                for z in range(self.nz):
                    for x in range(2):
                        y2, c2, z2, x2 = move(y, c, z, x)
                        src = (y * 2 + c) * self.n_fsdp + z * 2 + x
                        dst = (y2 * 2 + c2) * self.n_fsdp + z2 * 2 + x2
                        if src != dst:
                            found.append((src, dst))
        return lax.ppermute(value, AXES, found)

    def flip_z(self, value, bit):
        return self.send(value, lambda y, c, z, x: (y, c, z ^ bit, x))

    def flip_c(self, value):
        return self.send(value, lambda y, c, z, x: (y, 1 - c, z, x))

    def flip_y(self, value):
        return self.send(value, lambda y, c, z, x: (1 - y, c, z, x))

    def flip_x(self, value):
        return self.send(value, lambda y, c, z, x: (y, c, z, 1 - x))

    def first(self, b, value):
        return self.flip_y(value) if b == 0 else self.flip_x(value)

    def second(self, b, value):
        return self.flip_x(value) if b == 0 else self.flip_y(value)

    def swap(self, value, same):
        other = self.send(value.astype(BF), lambda y, c, z, x: (y, x, z, c))
        return jnp.where(same, value, other.astype(value.dtype))

    def gather_line(self, shard):
        return lax.all_gather(shard, "fsdp", axis=0, tiled=True, axis_index_groups=self.lines)

    def scatter_line(self, value):
        return lax.psum_scatter(
            value, "fsdp", scatter_dimension=0, tiled=True, axis_index_groups=self.lines
        )

    def gather_tokens(self, b, block):
        other = self.first(b, block)
        return (block, other, self.second(b, jnp.concatenate([block, other], axis=0)))

    def scatter_tokens(self, b, sent, kept):
        n = kept.shape[0] // 2
        got = self.second(b, sent).astype(F32)
        more = self.first(b, (kept[n:] + got[n:]).astype(BF)).astype(F32)
        return kept[:n] + got[:n] + more

    def total(self, value):
        for flip in (self.flip_y, self.flip_x, self.flip_c):
            value = value + flip(value)
        if self.nz & (self.nz - 1):
            return lax.psum(value, "fsdp", axis_index_groups=self.lines)
        bit = 1
        while bit < self.nz:
            value = value + self.flip_z(value, bit)
            bit *= 2
        return value


def call(body, grid, ins, outs, shapes, scratch=(), flops=0, moved=0):
    return pl.pallas_call(
        body,
        out_shape=shapes,
        grid=grid,
        in_specs=ins,
        out_specs=outs,
        scratch_shapes=list(scratch),
        cost_estimate=pl.CostEstimate(flops=flops, bytes_accessed=moved, transcendentals=0),
        compiler_params=pltpu.CompilerParams(vmem_limit_bytes=48 << 20),
    )


def shape(rows, cols, dtype=BF):
    return jax.ShapeDtypeStruct((rows, cols), dtype)


def spec(rows, cols, index):
    return pl.BlockSpec((rows, cols), index)


def fetch(pieces, target, sems):
    copies, row = [], 0
    for i, piece in enumerate(pieces):
        rows = piece.shape[0]
        copies.append(pltpu.make_async_copy(piece, target.at[pl.ds(row, rows)], sems.at[i]))
        row += rows
    for copy in copies:
        copy.start()
    for copy in copies:
        copy.wait()


def assemble(pieces):
    n = len(pieces)

    def body(*refs):
        fetch(refs[:n], refs[n], refs[n + 1])

    rows = sum(p.shape[0] for p in pieces)
    cols = pieces[0].shape[1]
    return pl.pallas_call(
        body,
        out_shape=shape(rows, cols),
        in_specs=[ANY] * n,
        out_specs=ANY,
        scratch_shapes=[pltpu.SemaphoreType.DMA((n,))],
        cost_estimate=pl.CostEstimate(
            flops=0, bytes_accessed=4 * rows * cols, transcendentals=0
        ),
    )(*pieces)


def rotated(first, second, cos_part, sin_part):
    return (first * cos_part - second * sin_part, second * cos_part + first * sin_part)


def project_qkv(pieces, w_own, w_oth, cos_table, sin_table, rotate_cols):
    n = len(pieces)
    rows = sum(p.shape[0] for p in pieces)
    width = pieces[0].shape[1]
    half, cols = w_own.shape
    tile, chunk = 512, 256

    def body(*refs):
        a, b, cos_ref, sin_ref, h_ref, o_ref, sems = refs[n:]
        j = pl.program_id(0)

        @pl.when(j == 0)
        def _():
            fetch(refs[:n], h_ref, sems)

        turn = j * tile < rotate_cols

        def step(i, _):
            at = pl.ds(pl.multiple_of(i * chunk, chunk), chunk)
            acc = nn(h_ref[at, :half], a[...]) + nn(h_ref[at, half:], b[...])
            cos_part = jnp.where(turn, cos_ref[at, :], 1.0)
            sin_part = jnp.where(turn, sin_ref[at, :], 0.0)
            for s in range(0, tile, KEY_HEAD):
                u, v = rotated(
                    acc[:, s : s + ROT], acc[:, s + ROT : s + KEY_HEAD], cos_part, sin_part
                )
                o_ref[at, s : s + ROT] = u.astype(BF)
                o_ref[at, s + ROT : s + KEY_HEAD] = v.astype(BF)
            return 0

        lax.fori_loop(0, rows // chunk, step, 0)

    return call(
        body,
        (cols // tile,),
        [ANY] * n
        + [spec(half, tile, lambda j: (0, j))] * 2
        + [spec(rows, ROT, lambda j: (0, 0))] * 2,
        [spec(rows, width, lambda j: (0, 0)), spec(rows, tile, lambda j: (0, j))],
        [shape(rows, width), shape(rows, cols)],
        [pltpu.SemaphoreType.DMA((n,))],
        2 * rows * width * cols,
        2 * (2 * rows * width + width * cols + rows * cols),
    )(*pieces, w_own, w_oth, cos_table, sin_table)


def decay_chunk(col_ref, row_ref, at, log_gamma):
    pos_n, seg_n = col_ref[at, 0:1], col_ref[at, 1:2]
    pos_m, seg_m = row_ref[0:1, :], row_ref[1:2, :]
    distance = pos_n - pos_m
    allowed = (distance >= 0.0) & (seg_n == seg_m)
    value = jnp.exp(jnp.maximum(distance, 0.0) * log_gamma) * (KEY_HEAD**-0.5)
    return jnp.where(allowed, value, 0.0)


def sigmoid(value):
    return 1.0 / (1.0 + jnp.exp(-value))


def retain(b, h1, qkv, w1_own, w1_oth, col_info, row_info, log_gamma, heads):
    width = h1.shape[1]
    half = width // 2
    rows = h1.shape[0] // 2
    dv = heads * VAL_HEAD
    chunk = 256

    def body(h_ref, ga, gb, oa, ob, q_ref, k_ref, v_ref, col_ref, row_ref, lg_ref,
             gate_ref, gated_ref, sent_ref, kept_ref, acc_ref):
        h = pl.program_id(0)
        log_g = lg_ref[h]

        def step(i, _):
            at = pl.ds(pl.multiple_of(i * chunk, chunk), chunk)
            gate = nn(h_ref[at, :half], ga[...]) + nn(h_ref[at, half:], gb[...])
            gate_ref[at, :] = gate
            decay = decay_chunk(col_ref, row_ref, at, log_g)
            weights = (nt(q_ref[at, :], k_ref[...]) * decay).astype(BF)
            kept = nn(weights, v_ref[...])
            scale = lax.rsqrt(jnp.mean(kept * kept, axis=-1, keepdims=True) + eps_group)
            gated = (gate * sigmoid(gate) * (kept * scale)).astype(BF)
            gated_ref[at, :] = gated
            left, right = nt(gated, oa[...]), nt(gated, ob[...])

            @pl.when(h == 0)
            def _():
                acc_ref[at, :half] = left
                acc_ref[at, half:] = right

            @pl.when(h != 0)
            def _():
                acc_ref[at, :half] = acc_ref[at, :half] + left
                acc_ref[at, half:] = acc_ref[at, half:] + right

            return 0

        lax.fori_loop(0, rows // chunk, step, 0)

        @pl.when(h == heads - 1)
        def _():
            kept_ref[...] = acc_ref[: rows // 2, :]
            sent_ref[...] = acc_ref[rows // 2 :, :].astype(BF)

    gate_spec = spec(half, VAL_HEAD, lambda h: (0, h))
    out_spec = spec(half, VAL_HEAD, lambda h: (0, heads + h))
    return call(
        body,
        (heads,),
        [
            spec(rows, width, lambda h: (b, 0)),
            gate_spec,
            gate_spec,
            out_spec,
            out_spec,
            spec(rows, KEY_HEAD, lambda h: (b, h)),
            spec(rows, KEY_HEAD, lambda h: (b, heads + h)),
            spec(rows, VAL_HEAD, lambda h: (b, heads + h)),
            spec(rows, 128, lambda h: (b, 0)),
            spec(8, rows, lambda h: (b, 0)),
            pl.BlockSpec(memory_space=pltpu.SMEM),
        ],
        [
            spec(rows, VAL_HEAD, lambda h: (0, h)),
            spec(rows, VAL_HEAD, lambda h: (0, h)),
            spec(rows // 2, width, lambda h: (0, 0)),
            spec(rows // 2, width, lambda h: (0, 0)),
        ],
        [
            shape(rows, dv, F32),
            shape(rows, dv),
            shape(rows // 2, width),
            shape(rows // 2, width, F32),
        ],
        [pltpu.VMEM((rows, width), F32)],
        4 * rows * width * dv + 2 * rows * rows * heads * (KEY_HEAD + VAL_HEAD),
        2 * rows * width + 4 * width * dv + 8 * rows * dv + 3 * rows * width,
    )(h1, w1_own, w1_oth, w1_own, w1_oth, qkv, qkv, qkv, col_info, row_info, log_gamma)


ROOT_2_PI = 0.7978845608028654


def feed_up(pieces, w2_own, w2_oth, hidden):
    n = len(pieces)
    rows = sum(p.shape[0] for p in pieces)
    width = pieces[0].shape[1]
    half = width // 2
    tile, chunk = 512, 256

    def body(*refs):
        a, b, h_ref, act_ref, slope_ref, sems = refs[n:]

        @pl.when(pl.program_id(0) == 0)
        def _():
            fetch(refs[:n], h_ref, sems)

        def step(i, _):
            at = pl.ds(pl.multiple_of(i * chunk, chunk), chunk)
            up = nn(h_ref[at, :half], a[...]) + nn(h_ref[at, half:], b[...])
            square = up * up
            bent = jnp.tanh(ROOT_2_PI * (up + 0.044715 * square * up))
            act_ref[at, :] = (0.5 * up * (1.0 + bent)).astype(BF)
            inner = ROOT_2_PI * (1.0 + 3.0 * 0.044715 * square)
            slope = 0.5 * (1.0 + bent) + 0.5 * up * (1.0 - bent * bent) * inner
            slope_ref[at, :] = slope
            return 0

        lax.fori_loop(0, rows // chunk, step, 0)

    return call(
        body,
        (hidden // tile,),
        [ANY] * n + [spec(half, tile, lambda j: (0, j))] * 2,
        [spec(rows, width, lambda j: (0, 0))] + [spec(rows, tile, lambda j: (0, j))] * 2,
        [shape(rows, width), shape(rows, hidden), shape(rows, hidden, F32)],
        [pltpu.SemaphoreType.DMA((n,))],
        2 * rows * width * hidden,
        4 * rows * width + 2 * width * hidden + 6 * rows * hidden,
    )(*pieces, w2_own, w2_oth)


def feed_down(act, w2_own, w2_oth, hidden):
    rows = act.shape[0]
    half = w2_own.shape[0]
    width = 2 * half
    tile, chunk = 512, 256
    steps = hidden // tile

    def body(act_ref, a, b, sent_ref, kept_ref, acc_ref):
        j = pl.program_id(0)

        def step(i, _):
            at = pl.ds(pl.multiple_of(i * chunk, chunk), chunk)
            left, right = nt(act_ref[at, :], a[...]), nt(act_ref[at, :], b[...])

            @pl.when(j == 0)
            def _():
                acc_ref[at, :half] = left
                acc_ref[at, half:] = right

            @pl.when(j != 0)
            def _():
                acc_ref[at, :half] = acc_ref[at, :half] + left
                acc_ref[at, half:] = acc_ref[at, half:] + right

            return 0

        lax.fori_loop(0, rows // chunk, step, 0)

        @pl.when(j == steps - 1)
        def _():
            kept_ref[...] = acc_ref[: rows // 2, :]
            sent_ref[...] = acc_ref[rows // 2 :, :].astype(BF)

    return call(
        body,
        (steps,),
        [spec(rows, tile, lambda j: (0, j))]
        + [spec(half, tile, lambda j: (0, steps + j))] * 2,
        [spec(rows // 2, width, lambda j: (0, 0))] * 2,
        [shape(rows // 2, width), shape(rows // 2, width, F32)],
        [pltpu.VMEM((rows, width), F32)],
        2 * rows * width * hidden,
        2 * rows * hidden + 2 * width * hidden + 3 * rows * width,
    )(act, w2_own, w2_oth)


def feed_back(b, cot, slope, w2_own, w2_oth, hidden):
    width = cot.shape[1]
    half = width // 2
    rows = slope.shape[0]
    tile, chunk = 512, 256
    steps = hidden // tile

    def body(cot_ref, slope_ref, da, db, ua, ub, dup_ref, sent_ref, kept_ref, acc_ref):
        j = pl.program_id(0)

        def step(i, _):
            at = pl.ds(pl.multiple_of(i * chunk, chunk), chunk)
            d_act = nn(cot_ref[at, :half], da[...]) + nn(cot_ref[at, half:], db[...])
            d_up = (d_act * slope_ref[at, :]).astype(BF)
            dup_ref[at, :] = d_up
            left, right = nt(d_up, ua[...]), nt(d_up, ub[...])

            @pl.when(j == 0)
            def _():
                acc_ref[at, :half] = left
                acc_ref[at, half:] = right

            @pl.when(j != 0)
            def _():
                acc_ref[at, :half] = acc_ref[at, :half] + left
                acc_ref[at, half:] = acc_ref[at, half:] + right

            return 0

        lax.fori_loop(0, rows // chunk, step, 0)

        @pl.when(j == steps - 1)
        def _():
            kept_ref[...] = acc_ref[: rows // 2, :]
            sent_ref[...] = acc_ref[rows // 2 :, :].astype(BF)

    return call(
        body,
        (steps,),
        [spec(rows, width, lambda j: (b, 0)), spec(rows, tile, lambda j: (0, j))]
        + [spec(half, tile, lambda j: (0, steps + j))] * 2
        + [spec(half, tile, lambda j: (0, j))] * 2,
        [spec(rows, tile, lambda j: (0, j))] + [spec(rows // 2, width, lambda j: (0, 0))] * 2,
        [shape(rows, hidden), shape(rows // 2, width), shape(rows // 2, width, F32)],
        [pltpu.VMEM((rows, width), F32)],
        4 * rows * width * hidden,
        5 * rows * width + 4 * width * hidden + 6 * rows * hidden,
    )(cot, slope, w2_own, w2_oth, w2_own, w2_oth)


def retain_back(b, pieces, gate, qkv, weights, col_info, row_info, cos_table, sin_table,
                log_gamma, heads):
    w0_own, w0_oth, w1_own, w1_oth = weights
    n = len(pieces)
    rows = sum(p.shape[0] for p in pieces)
    width = pieces[0].shape[1]
    half = width // 2
    dk, dv = heads * KEY_HEAD, heads * VAL_HEAD
    chunk = 256

    def body(*refs):
        (oa, ob, ga, gb, va, vb, qa, qb, ka, kb, gate_ref, q_ref, k_ref, v_ref, col_ref, row_ref,
         cos_ref, sin_ref, lg_ref, mix_ref, dgate_ref, dq_ref, dk_ref, dv_ref, sent_ref, kept_ref,
         acc_ref, dk_acc, dv_acc, sems) = refs[n:]
        h = pl.program_id(0)
        log_g = lg_ref[h]

        @pl.when(h == 0)
        def _():
            fetch(refs[:n], mix_ref, sems)

        def step(i, _):
            at = pl.ds(pl.multiple_of(i * chunk, chunk), chunk)
            d_gated = nn(mix_ref[at, :half], oa[...]) + nn(mix_ref[at, half:], ob[...])
            decay = decay_chunk(col_ref, row_ref, at, log_g)
            weights = (nt(q_ref[at, :], k_ref[...]) * decay).astype(BF)
            kept = nn(weights, v_ref[...])
            scale = lax.rsqrt(jnp.mean(kept * kept, axis=-1, keepdims=True) + eps_group)
            y_norm = kept * scale
            gate = gate_ref[at, :]
            sig = sigmoid(gate)
            d_gate = d_gated * y_norm * sig * (1.0 + gate * (1.0 - sig))
            dgate_ref[at, :] = d_gate.astype(BF)
            d_y = d_gated * (gate * sig)
            d_ret = (
                scale * (d_y - y_norm * jnp.mean(d_y * y_norm, axis=-1, keepdims=True))
            ).astype(BF)
            d_weights = nt(d_ret, v_ref[...])
            d_scores = (d_weights * decay).astype(BF)
            d_v = tn(weights, d_ret)
            d_k = tn(d_scores, q_ref[at, :])
            d_q = nn(d_scores, k_ref[...])
            u, v = rotated(d_q[:, :ROT], d_q[:, ROT:], cos_ref[at, :], -sin_ref[at, :])
            dq_ref[at, :ROT] = u.astype(BF)
            dq_ref[at, ROT:] = v.astype(BF)

            @pl.when(i == 0)
            def _():
                dk_acc[...] = d_k
                dv_acc[...] = d_v

            @pl.when(i != 0)
            def _():
                dk_acc[...] = dk_acc[...] + d_k
                dv_acc[...] = dv_acc[...] + d_v

            return 0

        lax.fori_loop(0, rows // chunk, step, 0)
        dv_ref[...] = dv_acc[...].astype(BF)
        u, v = rotated(dk_acc[:, :ROT], dk_acc[:, ROT:], cos_ref[...], -sin_ref[...])
        dk_ref[:, :ROT] = u.astype(BF)
        dk_ref[:, ROT:] = v.astype(BF)

        def back(i, _):
            at = pl.ds(pl.multiple_of(i * chunk, chunk), chunk)
            pairs = ((qa, ka, va, ga), (qb, kb, vb, gb))
            for side, (wq, wk, wv, wg) in enumerate(pairs):
                cols = slice(side * half, (side + 1) * half)
                part = (
                    nt(dq_ref[at, :], wq[...])
                    + nt(dk_ref[at, :], wk[...])
                    + nt(dv_ref[at, :], wv[...])
                    + nt(dgate_ref[at, :], wg[...])
                )

                @pl.when(h == 0)
                def _():
                    acc_ref[at, cols] = part

                @pl.when(h != 0)
                def _():
                    acc_ref[at, cols] = acc_ref[at, cols] + part

            return 0

        lax.fori_loop(0, rows // chunk, back, 0)

        @pl.when(h == heads - 1)
        def _():
            kept_ref[...] = acc_ref[: rows // 2, :]
            sent_ref[...] = acc_ref[rows // 2 :, :].astype(BF)

    wide = [spec(half, VAL_HEAD, lambda h: (0, heads + h))] * 2
    gate_w = [spec(half, VAL_HEAD, lambda h: (0, h))] * 2
    q_w = [spec(half, KEY_HEAD, lambda h: (0, h))] * 2
    k_w = [spec(half, KEY_HEAD, lambda h: (0, heads + h))] * 2
    per_head = spec(rows, VAL_HEAD, lambda h: (0, h))
    per_key = spec(rows, KEY_HEAD, lambda h: (0, h))
    whole = spec(rows // 2, width, lambda h: (0, 0))
    return call(
        body,
        (heads,),
        [ANY] * n
        + wide
        + gate_w
        + wide
        + q_w
        + k_w
        + [
            per_head,
            spec(rows, KEY_HEAD, lambda h: (b, h)),
            spec(rows, KEY_HEAD, lambda h: (b, heads + h)),
            spec(rows, VAL_HEAD, lambda h: (b, heads + h)),
            spec(rows, 128, lambda h: (b, 0)),
            spec(8, rows, lambda h: (b, 0)),
            spec(rows, ROT, lambda h: (b, 0)),
            spec(rows, ROT, lambda h: (b, 0)),
            pl.BlockSpec(memory_space=pltpu.SMEM),
        ],
        [
            spec(rows, width, lambda h: (0, 0)),
            per_head,
            per_key,
            per_key,
            per_head,
            whole,
            whole,
        ],
        [
            shape(rows, width),
            shape(rows, dv),
            shape(rows, dk),
            shape(rows, dk),
            shape(rows, dv),
            shape(rows // 2, width),
            shape(rows // 2, width, F32),
        ],
        [
            pltpu.VMEM((rows, width), F32),
            pltpu.VMEM((rows, KEY_HEAD), F32),
            pltpu.VMEM((rows, VAL_HEAD), F32),
            pltpu.SemaphoreType.DMA((n,)),
        ],
        2 * rows * width * (2 * dk + 3 * dv) + 2 * rows * rows * heads * 5 * VAL_HEAD,
        2 * width * (2 * dk + 3 * dv) + 12 * rows * dv + 7 * rows * width,
    )(
        *pieces, w1_own, w1_oth, w1_own, w1_oth, w0_own, w0_oth, w0_own, w0_oth, w0_own, w0_oth,
        gate, qkv, qkv, qkv, col_info, row_info, cos_table, sin_table, log_gamma,
    )


def weight_grad(side, lefts, rights, received=None):
    micro = len(lefts)
    groups = len(rights)
    width = lefts[0][0].shape[1]
    half = width // 2
    tile = 512
    tiles = half // tile
    sizes = [r[0].shape[1] for r in rights]
    cols = sum(sizes)
    flat = [r for group in rights for r in group]

    def body(*refs):
        left = refs[:micro]
        right = refs[micro : micro + len(flat)]
        o_ref = refs[-1]
        start = 0
        for g in range(groups):
            at = slice(start, start + sizes[g])
            acc = tn(left[0][...], right[g * micro][...])
            for b in range(1, micro):
                acc = acc + tn(left[b][...], right[g * micro + b][...])
            if received is not None:
                acc = acc + refs[-2][:, at].astype(F32)
            o_ref[:, at] = acc.astype(BF)
            start += sizes[g]

    rows = rights[0][0].shape[0]
    left_args = [array for array, _ in lefts]
    ins = [spec(rows, tile, lambda i, b=b: (b, side * tiles + i)) for _, b in lefts]
    ins = ins + [spec(r.shape[0], r.shape[1], lambda i: (0, 0)) for r in flat]
    args = left_args + flat
    if received is not None:
        ins.append(spec(tile, cols, lambda i: (i, 0)))
        args.append(received)
    return call(
        body,
        (tiles,),
        ins,
        spec(tile, cols, lambda i: (i, 0)),
        shape(half, cols),
        (),
        2 * micro * rows * half * cols,
        2 * (micro * rows * (half + cols) + half * cols),
    )(*args)


def layer_norm_parts(inputs, gain_row):
    center = inputs - jnp.mean(inputs, axis=-1, keepdims=True)
    inverse = lax.rsqrt(jnp.mean(center * center, axis=-1, keepdims=True) + eps_norm)
    scaled = center * inverse
    return (scaled * gain_row, scaled, inverse)


def layer_norm_back(incoming, scaled, inverse, gain_row):
    upstream = incoming * gain_row
    centered_grad = (
        upstream
        - jnp.mean(upstream, axis=-1, keepdims=True)
        - scaled * jnp.mean(upstream * scaled, axis=-1, keepdims=True)
    )
    return (centered_grad * inverse, jnp.sum(incoming * scaled, axis=0))


def make_on_device(grid):
    n_slots = grid.n_fsdp

    def on_device(
        tokens, norm_gains, w_query, w_key, w_value, w_gate, w_out, w_up, w_down, segments, d_output
    ):
        micro, _, piece, width = tokens.shape
        assert micro == 2
        own, length = micro * piece, 4 * piece
        col = width // n_slots
        dk, dv = w_query.shape[1], w_value.shape[1]
        heads = dk // KEY_HEAD
        hidden = w_up.shape[1]
        seq_id = lax.axis_index("seq")
        fsdp_id = lax.axis_index("fsdp")
        y, c = seq_id // 2, seq_id % 2
        x = fsdp_id % 2
        same = x == c
        both = range(micro)

        def to_local(value):
            v = value.reshape(-1, grid.nz, 2, col)
            a, b = v[:, :, 0].reshape(-1, width // 2), v[:, :, 1].reshape(-1, width // 2)
            return jnp.where(
                c == 0, jnp.concatenate([a, b], axis=1), jnp.concatenate([b, a], axis=1)
            )

        def to_natural(value):
            a, b = value[:, : width // 2], value[:, width // 2 :]
            a, b = a.reshape(-1, grid.nz, 1, col), b.reshape(-1, grid.nz, 1, col)
            v = jnp.where(
                c == 0, jnp.concatenate([a, b], axis=2), jnp.concatenate([b, a], axis=2)
            )
            return v.reshape(-1, width)

        w0 = grid.swap(jnp.concatenate([w_query, w_key, w_value], axis=1), same)
        toks = grid.swap(after(tokens.reshape(own, width), w0), same)
        segs = grid.swap(segments.reshape(micro, length).astype(F32), same)
        w0_own = grid.gather_line(w0)
        w1 = grid.swap(after(jnp.concatenate([w_gate, w_out.T], axis=1), toks), same)
        w1_own = grid.gather_line(w1)
        gains = to_local(norm_gains)
        gain_in, gain_mid = gains[0], gains[1]
        xin = to_local(toks).astype(F32)
        normed, scaled_in, inverse_in = layer_norm_parts(xin, gain_in)
        normed = normed.astype(BF)

        def rows(value, b):
            return value[b * piece : (b + 1) * piece]

        h1_pieces = [grid.gather_tokens(b, rows(normed, b)) for b in both]
        w0_oth = grid.flip_c(w0_own)
        w2 = grid.swap(after(jnp.concatenate([w_up, w_down.T], axis=1), w0_oth), same)
        w2_own = grid.gather_line(w2)

        ranks = [
            [2 * (y ^ i) + (x ^ j) for i, j in ((0, 0), (1, 0), (0, 1), (1, 1))],
            [2 * (y ^ i) + (x ^ j) for i, j in ((0, 0), (0, 1), (1, 0), (1, 1))],
        ]
        positions = jnp.stack(
            [jnp.concatenate([r * piece + jnp.arange(piece) for r in ranks[b]]) for b in both]
        ).astype(F32)
        seg_rows = jnp.stack(
            [
                jnp.concatenate(
                    [lax.dynamic_slice_in_dim(segs[b], r * piece, piece) for r in ranks[b]]
                )
                for b in both
            ]
        )
        frequency = jnp.exp(-jnp.log(10000.0) * 2.0 * jnp.arange(ROT, dtype=F32) / KEY_HEAD)
        angles = positions.reshape(-1, 1) * frequency[None, :]
        cos_table, sin_table = jnp.cos(angles), jnp.sin(angles)
        lanes = jnp.arange(128)[None, :]
        col_info = jnp.where(
            lanes == 0,
            positions.reshape(-1, 1),
            jnp.where(lanes == 1, seg_rows.reshape(-1, 1), 0.0),
        )
        row_info = jnp.stack([positions, seg_rows] + [jnp.zeros_like(positions)] * 6, axis=1)
        row_info = row_info.reshape(8 * micro, length)
        head_ids = (y * 2 + x) * heads + jnp.arange(heads, dtype=jnp.int32)
        log_gamma = jnp.log1p(-jnp.exp2(-5.0 - head_ids.astype(F32)))

        h1, qkv = project_qkv(
            [p for b in both for p in h1_pieces[b]], w0_own, w0_oth, cos_table, sin_table, 2 * dk
        )
        cots = grid.swap(after(d_output.reshape(own, width), qkv), same)
        cot_own = to_local(cots)
        cot_pieces = [grid.gather_tokens(b, rows(cot_own, b)) for b in both]
        cot = assemble([p for b in both for p in cot_pieces[b]])
        w1_oth = grid.flip_c(after(w1_own, cot))
        gate, gated, mixed = [], [], []
        for b in both:
            g, d, sent, kept = retain(
                b, h1, qkv, w1_own, w1_oth, col_info, row_info, log_gamma, heads
            )
            gate.append(g)
            gated.append(d)
            mixed.append(grid.scatter_tokens(b, sent, kept))
        x1, scaled_mid, inverse_mid, h2, act, slope = [], [], [], [], [], []
        w2_oth = grid.flip_c(w2_own)
        for b in both:
            x1.append(rows(xin, b) + mixed[b])
            out, scaled, inverse = layer_norm_parts(x1[b], gain_mid)
            scaled_mid.append(scaled)
            inverse_mid.append(inverse)
            h, a, s = feed_up(grid.gather_tokens(b, out.astype(BF)), w2_own, w2_oth, hidden)
            h2.append(h)
            act.append(a)
            slope.append(s)

        cot_rows = [(cot, b) for b in both]
        moved = grid.flip_c(weight_grad(1, cot_rows, [act]))
        d_up, d_h2 = [], []
        for b in both:
            d, sent, kept = feed_back(b, cot, slope[b], w2_own, w2_oth, hidden)
            d_up.append(d)
            d_h2.append(grid.scatter_tokens(b, sent, kept))
        h2_rows = [(h, 0) for h in h2]
        g_down = grid.scatter_line(weight_grad(0, cot_rows, [act], moved))
        moved = grid.flip_c(weight_grad(1, h2_rows, [d_up]))
        g_up = grid.scatter_line(weight_grad(0, h2_rows, [d_up], moved))

        d_x1, mix_pieces, gain_mid_grad = [], [], 0.0
        for b in both:
            d_ln, part = layer_norm_back(d_h2[b], scaled_mid[b], inverse_mid[b], gain_mid)
            gain_mid_grad = gain_mid_grad + part
            d_x1.append(rows(cot_own, b).astype(F32) + d_ln)
            mix_pieces.append(grid.gather_tokens(b, d_x1[b].astype(BF)))

        d_mix, d_gate, d_q, d_k, d_v, d_h1 = [], [], [], [], [], []
        for b in both:
            m, g, q, k, v, sent, kept = retain_back(
                b, mix_pieces[b], gate[b], qkv, (w0_own, w0_oth, w1_own, w1_oth), col_info,
                row_info, cos_table, sin_table, log_gamma, heads,
            )
            d_mix.append(m)
            d_gate.append(g)
            d_q.append(q)
            d_k.append(k)
            d_v.append(v)
            d_h1.append(grid.scatter_tokens(b, sent, kept))
        h1_rows = [(h1, b) for b in both]
        mix_rows = [(m, 0) for m in d_mix]
        moved = grid.flip_c(weight_grad(1, mix_rows, [gated]))
        g_out = grid.scatter_line(weight_grad(0, mix_rows, [gated], moved))
        moved = grid.flip_c(weight_grad(1, h1_rows, [d_gate, d_v]))
        g_gv = grid.scatter_line(weight_grad(0, h1_rows, [d_gate, d_v], moved))
        moved = grid.flip_c(weight_grad(1, h1_rows, [d_q, d_k]))
        g_qk = grid.scatter_line(weight_grad(0, h1_rows, [d_q, d_k], moved))

        outs = []
        for b in both:
            sent, kept = feed_down(act[b], w2_own, w2_oth, hidden)
            outs.append((x1[b] + grid.scatter_tokens(b, sent, kept)).astype(BF))

        d_inputs, gain_in_grad = [], 0.0
        for b in both:
            d_ln, part = layer_norm_back(
                d_h1[b], rows(scaled_in, b), rows(inverse_in, b), gain_in
            )
            gain_in_grad = gain_in_grad + part
            d_inputs.append(d_x1[b] + d_ln)
        grad_norms = grid.total(to_natural(jnp.stack([gain_in_grad, gain_mid_grad])))
        g_down, g_up, g_out, g_gv, g_qk = [
            grid.swap(g, same).astype(F32) for g in (g_down, g_up, g_out, g_gv, g_qk)
        ]
        output = grid.swap(to_natural(jnp.concatenate(outs)), same)
        d_input = grid.swap(to_natural(jnp.concatenate(d_inputs)), same)
        whole = (micro, 1, piece, width)
        return (
            output.reshape(whole),
            d_input.reshape(whole),
            grad_norms,
            g_qk[:, :dk],
            g_qk[:, dk:],
            g_gv[:, dv:],
            g_gv[:, :dv],
            g_out.T,
            g_up,
            g_down.T,
        )

    return on_device


def solution(mesh):
    grid = Grid(mesh.shape["seq"], mesh.shape["fsdp"])
    rows = P("fsdp", "seq")
    cols = P("seq", "fsdp")
    tok = P(None, "fsdp", "seq", None)
    return jax.shard_map(
        make_on_device(grid),
        mesh=mesh,
        in_specs=(tok, P(), rows, rows, rows, rows, cols, rows, cols, P(None, "fsdp", None), tok),
        out_specs=(tok, tok, P(), rows, rows, rows, rows, cols, rows, cols),
        check_vma=False,
    )
```

time: 1090 us -> 1010 us (0.927)
  Pallas kernels: 0 us -> 327 us
  matrix products: 178 us -> 0 us
  waiting for transfers between devices: 530 us -> 432 us
  starting transfers between devices: 143 us -> 79.9 us
  blocking collectives: 44.6 us -> 0 us
  other arithmetic: 102 us -> 71.7 us
    pallas_call x0 -> x22, Pallas kernels: none -> 327 us  [the longest x1 128 us: assemble(): pl.pallas_call(body, out_shape=shape(rows, cols), in_specs=[ANY] * n, out...]
    dot_general x60 -> x0, matrix products: 178 us -> none  [the longest x20 69.6 us: mm_t(): lax.dot_general(left, right, (((1,), (1,)), ((), ())), preferred_element_...]
    ppermute x85 -> x58, waiting for transfers between devices: 530 us -> 355 us  [send(): return lax.ppermute(value, AXES, found)]
    ppermute x85 -> x58, starting transfers between devices: 143 us -> 79.6 us  [send(): return lax.ppermute(value, AXES, found)]
    all_gather x0 -> x3, waiting for transfers between devices: none -> 53.7 us  [gather_line(): lax.all_gather(shard, 'fsdp', axis=0, tiled=True, axis_index_groups=self....]
    psum x1 -> x0, blocking collectives: 44.6 us -> none  [on_device(): grad_norms = lax.psum(pick(gain_grads, block_slot), AXES)]
    add x24 -> x10, other arithmetic: 30 us -> 1.24 us  [the longest x2 0.63 us: total(): value = value + self.flip_z(value, bit)]
    reduce_scatter x0 -> x5, waiting for transfers between devices: none -> 23 us  [scatter_line(): lax.psum_scatter(value, 'fsdp', scatter_dimension=0, tiled=True, axis_ind...]
  transfers between devices with their start and end apart: 85 -> 66, of which waited for: 37 -> 37; matrix products, arithmetic and copies ran while one was open for 30% -> 10% of each run, Pallas kernels for 0% -> 31%
where the time goes in v2:
time: 1010 us; the launch traced here: 998 us
  waiting for transfers between devices  432 us (43%)
  Pallas kernels  327 us (32%)
  starting transfers between devices  79.9 us (8%)
  other arithmetic  71.7 us (7%)
  local copies, waits for them, and re-layouts  70.8 us (7%)
  between operations  16.2 us (2%)
    ppermute x58, waiting for transfers between devices, send(): return lax.ppermute(value, AXES, found)  355 us
    pallas_call x1, Pallas kernels, assemble(): pl.pallas_call(body, out_shape=shape(rows, cols), in_specs=[ANY] * n, out...  128 us
    ppermute x58, starting transfers between devices, send(): return lax.ppermute(value, AXES, found)  79.6 us
    pallas_call x2, Pallas kernels, retain_back(): call(body, (heads,), [ANY] * n + wide + gate_w + wide + q_w + k_w + [per_...  56.3 us
    all_gather x3, waiting for transfers between devices, gather_line(): lax.all_gather(shard, 'fsdp', axis=0, tiled=True, axis_index_groups=self....  53.7 us
    pallas_call x10, Pallas kernels, weight_grad(): call(body, (tiles,), ins, spec(tile, cols, lambda i: (i, 0)), shape(half,...  51.7 us
    unnamed x175, local copies, waits for them, and re-layouts  46.6 us
    pallas_call x2, Pallas kernels, retain(): call(body, (heads,), [spec(rows, width, lambda h: (b, 0)), gate_spec, gat...  28.1 us
  transfers between devices with their start and end apart: 66, of which 37 were waited for; matrix products, arithmetic and copies ran while one was open for 10% of the time, Pallas kernels for 31%

profile of v2, /device:TPU:1, one launch (start us, length us, event | category | flops | bytes accessed | tf_op | source)
XLA Modules:
  0.0 997.8 jit_solution(13697601425632954335)
XLA Ops:
  14.9 12.4 %collective-permute-done = bf16[256,2048]{1,0:T(8,128)(2,1)S(1)} collective-permute-done((bf16[256,2048]{1,0:T(8,128)(2,1)S(1)}, bf16[256,2048]{1,0:T(8,128)(2,1)S(1)}, u32[]{:S(2)}, u32[]{:S(2)}) %collective-permute-start) | collective-permute-done | bytes 1048608 | tf_op jit(solution)/shard_map/ppermute | solution.py:54
  37.6 11.0 %collective-permute-done.1 = bf16[256,2048]{1,0:T(8,128)(2,1)} collective-permute-done((bf16[256,2048]{1,0:T(8,128)(2,1)S(1)}, bf16[256,2048]{1,0:T(8,128)(2,1)}, u32[]{:S(2)}, u32[]{:S(2)}) %collective-permute-start.1) | collective-permute-done | bytes 1048608 | tf_op jit(solution)/shard_map/ppermute | solution.py:54
  56.9 53.7 %all-gather.4.cloned.1.call-done.refs_6_.refs_7_.refs_9_.refs_11_ = bf16[1024,2048]{1,0:T(8,128)(2,1)} async-done(((bf16[256,2048]{1,0:T(8,128)(2,1)}), bf16[1024,2048]{1,0:T(8,128)(2,1)}) %all-gather.4.cloned.1.call-update) | async-done | bytes 4194320 | tf_op jit(solution)/shard_map/all_gather | solution.py:79
  116.2 11.0 %collective-permute-done.4.refs_4_ = bf16[128,2048]{1,0:T(8,128)(2,1)S(1)} collective-permute-done((bf16[128,2048]{1,0:T(8,128)(2,1)S(1)}, bf16[128,2048]{1,0:T(8,128)(2,1)S(1)}, u32[]{:S(2)}, u32[]{:S(2)}) %collective-permute-start.4) | collective-permute-done | bytes 524320 | tf_op jit(solution)/shard_map/ppermute | solution.py:54
  135.2 17.2 %collective-permute-done.5.refs_5_ = bf16[256,2048]{1,0:T(8,128)(2,1)} collective-permute-done((bf16[256,2048]{1,0:T(8,128)(2,1)}, bf16[256,2048]{1,0:T(8,128)(2,1)}, u32[]{:S(2)}, u32[]{:S(2)}) %collective-permute-start.5) | collective-permute-done | bytes 1048608 | tf_op jit(solution)/shard_map/ppermute | solution.py:54
  156.7 17.2 %shard_map.186 = (bf16[1024,2048]{1,0:T(8,128)(2,1)}, bf16[1024,2048]{1,0:T(8,128)(2,1)}) custom-call(bf16[128,2048]{1,0:T(8,128)(2,1)S(1)} %get-tuple-element.171.refs_0_, bf16[128,2048]{1,0:T(8,128)(2,1)S(1)} %copy-done.34, bf16[256,2048]{1,0:T(8,128)(2,1)S(1)} %collective-permute-done.3.refs_2_, bf16[128,2048]{1,0:T(8,128)(2,1)S(1)} %get-tuple-element.170.refs_3_, ...), custom_call_target="tpu_custom_call" | custom-call | flops 8589934592 | bytes 20971520 | tf_op jit(solution)/shard_map/pallas_call | solution.py:197
  184.2 7.6 collective-permute-done.8
  206.2 13.4 %collective-permute-done.11.refs_4_ = bf16[128,2048]{1,0:T(8,128)(2,1)S(1)} collective-permute-done((bf16[128,2048]{1,0:T(8,128)(2,1)S(1)}, bf16[128,2048]{1,0:T(8,128)(2,1)S(1)}, u32[]{:S(2)}, u32[]{:S(2)}) %collective-permute-start.11) | collective-permute-done | bytes 524320 | tf_op jit(solution)/shard_map/ppermute | solution.py:54
  224.6 20.5 %collective-permute-done.12.refs_5_ = bf16[256,2048]{1,0:T(8,128)(2,1)} collective-permute-done((bf16[256,2048]{1,0:T(8,128)(2,1)}, bf16[256,2048]{1,0:T(8,128)(2,1)}, u32[]{:S(2)}, u32[]{:S(2)}) %collective-permute-start.12) | collective-permute-done | bytes 1048608 | tf_op jit(solution)/shard_map/ppermute | solution.py:54
  246.4 128.2 %shard_map.187.cot_ref.refs_0_.refs_1_ = bf16[1024,2048]{1,0:T(8,128)(2,1)} custom-call(bf16[128,2048]{1,0:T(8,128)(2,1)} %copy-done.50, bf16[128,2048]{1,0:T(8,128)(2,1)} %copy-done.65, bf16[256,2048]{1,0:T(8,128)(2,1)} %collective-permute-done.10.refs_2_, bf16[128,2048]{1,0:T(8,128)(2,1)} %copy-done.49, bf16[128,2048]{1,0:T(8,128)(2,1)} %copy-done.64, ...), custom_call_target="tpu_custom_call" | custom-call | bytes 8388608 | tf_op jit(solution)/shard_map/pallas_call | solution.py:149
  383.5 14.1 %shard_map.191 = (f32[512,1024]{1,0:T(8,128)S(1)}, bf16[512,1024]{1,0:T(8,128)(2,1)S(1)}, bf16[256,2048]{1,0:T(8,128)(2,1)}, f32[256,2048]{1,0:T(8,128)}) custom-call(bf16[1024,2048]{1,0:T(8,128)(2,1)} %get-tuple-element.56.h_ref.refs_0_.refs_1_, bf16[1024,2048]{1,0:T(8,128)(2,1)} %all-gather.6.cloned.1.call-done.ga.oa.refs_3_.refs_5_, ...), custom_call_target="tpu_custom_call" | custom-call | flops 5100273664 | bytes 17825792 | tf_op jit(solution)/shard_map/pallas_call | solution.py:269
  401.2 14.0 %shard_map.188 = (f32[512,1024]{1,0:T(8,128)S(1)}, bf16[512,1024]{1,0:T(8,128)(2,1)S(1)}, bf16[256,2048]{1,0:T(8,128)(2,1)S(1)}, f32[256,2048]{1,0:T(8,128)}) custom-call(bf16[1024,2048]{1,0:T(8,128)(2,1)} %get-tuple-element.56.h_ref.refs_0_.refs_1_, bf16[1024,2048]{1,0:T(8,128)(2,1)} %all-gather.6.cloned.1.call-done.ga.oa.refs_3_.refs_5_, ...), custom_call_target="tpu_custom_call" | custom-call | flops 5100273664 | bytes 17825792 | tf_op jit(solution)/shard_map/pallas_call | solution.py:269
  426.3 15.3 %collective-permute-done.15 = bf16[256,2048]{1,0:T(8,128)(2,1)} collective-permute-done((bf16[256,2048]{1,0:T(8,128)(2,1)S(1)}, bf16[256,2048]{1,0:T(8,128)(2,1)}, u32[]{:S(2)}, u32[]{:S(2)}) %collective-permute-start.15) | collective-permute-done | bytes 1048608 | tf_op jit(solution)/shard_map/ppermute | solution.py:54
  444.6 8.1 collective-permute-done.24
  456.2 9.6 collective-permute-done.17.refs_1_
  465.9 20.1 %collective-permute-done.18.refs_2_ = bf16[256,2048]{1,0:T(8,128)(2,1)S(1)} collective-permute-done((bf16[256,2048]{1,0:T(8,128)(2,1)S(1)}, bf16[256,2048]{1,0:T(8,128)(2,1)S(1)}, u32[]{:S(2)}, u32[]{:S(2)}) %collective-permute-start.18) | collective-permute-done | bytes 1048608 | tf_op jit(solution)/shard_map/ppermute | solution.py:54
  501.5 10.7 %shard_map.194 = (bf16[512,1024]{1,0:T(8,128)(2,1)S(1)}, bf16[256,2048]{1,0:T(8,128)(2,1)S(1)}, f32[256,2048]{1,0:T(8,128)S(1)}) custom-call(bf16[1024,2048]{1,0:T(8,128)(2,1)} %shard_map.187.cot_ref.refs_0_.refs_1_, f32[512,1024]{1,0:T(8,128)} %get-tuple-element.72.slope_ref, bf16[1024,2048]{1,0:T(8,128)(2,1)} %all-gather.8.cloned.1.call-done.refs_3_.a.da.ua, ...), custom_call_target="tpu_custom_call" | custom-call | flops 4294967296 | bytes 16777216 | tf_op jit(solution)/shard_map/pallas_call | solution.py:427
  521.4 21.8 %collective-permute-done.30 = bf16[256,2048]{1,0:T(8,128)(2,1)S(1)} collective-permute-done((bf16[256,2048]{1,0:T(8,128)(2,1)S(1)}, bf16[256,2048]{1,0:T(8,128)(2,1)S(1)}, u32[]{:S(2)}, u32[]{:S(2)}) %collective-permute-start.30) | collective-permute-done | bytes 1048608 | tf_op jit(solution)/shard_map/ppermute | solution.py:54
  553.4 8.0 collective-permute-done.25.refs_1_
  561.8 15.7 %collective-permute-done.26.refs_2_ = bf16[256,2048]{1,0:T(8,128)(2,1)S(1)} collective-permute-done((bf16[256,2048]{1,0:T(8,128)(2,1)S(1)}, bf16[256,2048]{1,0:T(8,128)(2,1)S(1)}, u32[]{:S(2)}, u32[]{:S(2)}) %collective-permute-start.26) | collective-permute-done | bytes 1048608 | tf_op jit(solution)/shard_map/ppermute | solution.py:54
  589.5 9.6 collective-permute-start.56
  599.1 10.2 %shard_map.196 = (bf16[512,1024]{1,0:T(8,128)(2,1)S(1)}, bf16[256,2048]{1,0:T(8,128)(2,1)S(1)}, f32[256,2048]{1,0:T(8,128)S(1)}) custom-call(bf16[1024,2048]{1,0:T(8,128)(2,1)} %shard_map.187.cot_ref.refs_0_.refs_1_, f32[512,1024]{1,0:T(8,128)} %get-tuple-element.78.slope_ref, bf16[1024,2048]{1,0:T(8,128)(2,1)} %all-gather.8.cloned.1.call-done.refs_3_.a.da.ua, ...), custom_call_target="tpu_custom_call" | custom-call | flops 4294967296 | bytes 16777216 | tf_op jit(solution)/shard_map/pallas_call | solution.py:427
  618.6 15.6 %collective-permute-done.36 = bf16[256,2048]{1,0:T(8,128)(2,1)S(1)} collective-permute-done((bf16[256,2048]{1,0:T(8,128)(2,1)S(1)}, bf16[256,2048]{1,0:T(8,128)(2,1)S(1)}, u32[]{:S(2)}, u32[]{:S(2)}) %collective-permute-start.36) | collective-permute-done | bytes 1048608 | tf_op jit(solution)/shard_map/ppermute | solution.py:54
  661.7 9.6 collective-permute-done.28
  674.1 11.8 %collective-permute-done.38.refs_1_ = bf16[128,2048]{1,0:T(8,128)(2,1)S(1)} collective-permute-done((bf16[128,2048]{1,0:T(8,128)(2,1)S(1)}, bf16[128,2048]{1,0:T(8,128)(2,1)S(1)}, u32[]{:S(2)}, u32[]{:S(2)}) %collective-permute-start.38) | collective-permute-done | bytes 524320 | tf_op jit(solution)/shard_map/ppermute | solution.py:54
  688.3 32.1 %collective-permute-done.32.refs_1_ = bf16[128,2048]{1,0:T(8,128)(2,1)S(1)} collective-permute-done((bf16[128,2048]{1,0:T(8,128)(2,1)S(1)}, bf16[128,2048]{1,0:T(8,128)(2,1)S(1)}, u32[]{:S(2)}, u32[]{:S(2)}) %collective-permute-start.32) | collective-permute-done | bytes 524320 | tf_op jit(solution)/shard_map/ppermute | solution.py:54
  727.5 28.1 %shard_map.197 = (bf16[512,2048]{1,0:T(8,128)(2,1)}, bf16[512,1024]{1,0:T(8,128)(2,1)S(1)}, bf16[512,512]{1,0:T(8,128)(2,1)S(1)}, bf16[512,512]{1,0:T(8,128)(2,1...) custom-call(bf16[128,2048]{1,0:T(8,128)(2,1)S(1)} %get-tuple-element.156.refs_0_, ...), custom_call_target="tpu_custom_call" | custom-call | flops 11274289152 | bytes 30408704 | tf_op jit(solution)/shard_map/pallas_call | solution.py:541
  757.4 28.2 %shard_map.195 = (bf16[512,2048]{1,0:T(8,128)(2,1)}, bf16[512,1024]{1,0:T(8,128)(2,1)S(1)}, bf16[512,512]{1,0:T(8,128)(2,1)S(1)}, bf16[512,512]{1,0:T(8,128)(2,1...) custom-call(bf16[128,2048]{1,0:T(8,128)(2,1)S(1)} %get-tuple-element.138.refs_0_, ...), custom_call_target="tpu_custom_call" | custom-call | flops 11274289152 | bytes 30408704 | tf_op jit(solution)/shard_map/pallas_call | solution.py:541
  831.5 8.1 shard_map.201
  842.5 23.0 %collective-permute-done.40 = bf16[256,2048]{1,0:T(8,128)(2,1)S(1)} collective-permute-done((bf16[256,2048]{1,0:T(8,128)(2,1)S(1)}, bf16[256,2048]{1,0:T(8,128)(2,1)S(1)}, u32[]{:S(2)}, u32[]{:S(2)}) %collective-permute-start.40) | collective-permute-done | bytes 1048608 | tf_op jit(solution)/shard_map/ppermute | solution.py:54
  908.1 9.0 collective-permute-done.44
  949.5 23.0 %reduce-scatter.8.cloned.1.call-done = bf16[256,2048]{1,0:T(8,128)(2,1)} async-done(((bf16[1024,2048]{1,0:T(8,128)(2,1)}), bf16[256,2048]{1,0:T(8,128)(2,1)}) %reduce-scatter.8.cloned.1.call-update) | async-done | bytes 1048592 | tf_op jit(solution)/shard_map/reduce_scatter | solution.py:82
  (434 shorter events, 343.8 us)
Async XLA Ops:
  7.2 103.3 %all-gather.4.cloned.1.call-start = ((), (), s32[]{:S(2)}) async-start(), calls=%async_computation.5 | async-start | bytes 5242880 | tf_op jit(solution)/shard_map/all_gather | solution.py:79
  28.4 346.2 %all-gather.6.cloned.1.call-start = ((), (), s32[]{:S(2)}) async-start(), calls=%async_computation.6 | async-start | bytes 5242880 | tf_op jit(solution)/shard_map/all_gather | solution.py:79
  28.5 104.7 %collective-permute-start.14 = (bf16[2,512]{1,0:T(2,128)(2,1)S(1)}, bf16[2,512]{1,0:T(2,128)(2,1)S(1)}, u32[]{:S(2)}, u32[]{:S(2)}) collective-permute-start(bf16[2,512]{1,0:T(2,128)(2,1)S(1)} %bitcast.91), channel_id=1, source_target_pairs={{1,8},{3,10},{5,12},{7,14},{8,1},{10,3},{12,5},{14,7},{17,24},{19,... | collective-permute-start | bytes 6152 | tf_op jit(solution)/shard_map/ppermute | solution.py:54
  54.6 74.8 %collective-permute-start.7 = (bf16[256,2048]{1,0:T(8,128)(2,1)}, bf16[256,2048]{1,0:T(8,128)(2,1)}, u32[]{:S(2)}, u32[]{:S(2)}) collective-permute-start(bf16[256,2048]{1,0:T(8,128)(2,1)} %pad_maximum_fusion.3), channel_id=1, source_target_pairs={{1,8},{3,10},{5,12},{7,14},{8,1},{10,3},{12,5},{14,7},{17,24},{19,... | collective-permute-start | bytes 3145736 | tf_op jit(solution)/shard_map/ppermute | solution.py:54
  110.5 45.1 %collective-permute-start.6 = (bf16[1024,2048]{1,0:T(8,128)(2,1)}, bf16[1024,2048]{1,0:T(8,128)(2,1)}, u32[]{:S(2)}, u32[]{:S(2)}) collective-permute-start(bf16[1024,2048]{1,0:T(8,128)(2,1)} %all-gather.4.cloned.1.call-done.refs_6_.refs_7_.refs_9_.refs_11_), channel_id=1, source_target_pairs={{0,8},{1,9},{2,10},{3,11},{4,12},{5,13},{6,14},{7,15},{8,0},{9,1},... | collective-permute-start | bytes 12582920 | tf_op jit(solution)/shard_map/ppermute | solution.py:54
  128.2 24.2 %collective-permute-start.5 = (bf16[256,2048]{1,0:T(8,128)(2,1)}, bf16[256,2048]{1,0:T(8,128)(2,1)}, u32[]{:S(2)}, u32[]{:S(2)}) collective-permute-start(bf16[256,2048]{1,0:T(8,128)(2,1)} %pad_maximum_fusion.2), channel_id=1, source_target_pairs={{0,16},{1,17},{2,18},{3,19},{4,20},{5,21},{6,22},{7,23},{8,24},{9,... | collective-permute-start | bytes 3145736 | tf_op jit(solution)/shard_map/ppermute | solution.py:54
  131.8 285.7 %all-gather.8.cloned.1.call-start = ((), (), s32[]{:S(2)}) async-start(), calls=%async_computation.7 | async-start | bytes 5242880 | tf_op jit(solution)/shard_map/all_gather | solution.py:79
  182.1 40.1 %collective-permute-start.19 = (bf16[256,2048]{1,0:T(8,128)(2,1)}, bf16[256,2048]{1,0:T(8,128)(2,1)}, u32[]{:S(2)}, u32[]{:S(2)}) collective-permute-start(bf16[256,2048]{1,0:T(8,128)(2,1)} %pad_maximum_fusion.7), channel_id=1, source_target_pairs={{1,8},{3,10},{5,12},{7,14},{8,1},{10,3},{12,5},{14,7},{17,24},{19,... | collective-permute-start | bytes 3145736 | tf_op jit(solution)/shard_map/ppermute | solution.py:54
  220.7 24.5 %collective-permute-start.12 = (bf16[256,2048]{1,0:T(8,128)(2,1)}, bf16[256,2048]{1,0:T(8,128)(2,1)}, u32[]{:S(2)}, u32[]{:S(2)}) collective-permute-start(bf16[256,2048]{1,0:T(8,128)(2,1)} %pad_maximum_fusion.5), channel_id=1, source_target_pairs={{0,16},{1,17},{2,18},{3,19},{4,20},{5,21},{6,22},{7,23},{8,24},{9,... | collective-permute-start | bytes 3145736 | tf_op jit(solution)/shard_map/ppermute | solution.py:54
  224.6 708.2 %reduce-scatter.14.cloned.1.call-start = ((), (), s32[]{:S(2)}) async-start(), calls=%async_computation.12 | async-start | bytes 2621440 | tf_op jit(solution)/shard_map/reduce_scatter | solution.py:82
  400.0 24.7 %collective-permute-start.23 = (bf16[256,2048]{1,0:T(8,128)(2,1)}, bf16[256,2048]{1,0:T(8,128)(2,1)}, u32[]{:S(2)}, u32[]{:S(2)}) collective-permute-start(bf16[256,2048]{1,0:T(8,128)(2,1)} %get-tuple-element.68), channel_id=1, source_target_pairs={{0,16},{1,17},{2,18},{3,19},{4,20},{5,21},{6,22},{7,23},{8,24},{9,... | collective-permute-start | bytes 3145736 | tf_op jit(solution)/shard_map/ppermute | solution.py:54
  417.5 68.6 %collective-permute-start.20 = (bf16[1024,2048]{1,0:T(8,128)(2,1)}, bf16[1024,2048]{1,0:T(8,128)(2,1)S(1)}, u32[]{:S(2)}, u32[]{:S(2)}) collective-permute-start(bf16[1024,2048]{1,0:T(8,128)(2,1)} %all-gather.8.cloned.1.call-done.refs_3_.a.da.ua), channel_id=1, source_target_pairs={{0,8},{1,9},{2,10},{3,11},{4,12},{5,13},{6,14},{7,15},{8,0},{9,1},... | collective-permute-start | bytes 12582920 | tf_op jit(solution)/shard_map/ppermute | solution.py:54
  426.3 26.5 %collective-permute-start.24 = (bf16[128,2048]{1,0:T(8,128)(2,1)S(1)}, bf16[128,2048]{1,0:T(8,128)(2,1)S(1)}, u32[]{:S(2)}, u32[]{:S(2)}) collective-permute-start(bf16[128,2048]{1,0:T(8,128)(2,1)S(1)} %fusion.13), channel_id=1, source_target_pairs={{0,1},{1,0},{2,3},{3,2},{4,5},{5,4},{6,7},{7,6},{8,9},{9,8},{10,11... | collective-permute-start | bytes 1572872 | tf_op jit(solution)/shard_map/ppermute | solution.py:54
  512.2 30.9 %collective-permute-start.30 = (bf16[256,2048]{1,0:T(8,128)(2,1)S(1)}, bf16[256,2048]{1,0:T(8,128)(2,1)S(1)}, u32[]{:S(2)}, u32[]{:S(2)}) collective-permute-start(bf16[256,2048]{1,0:T(8,128)(2,1)S(1)} %get-tuple-element.74), channel_id=1, source_target_pairs={{0,1},{1,0},{2,3},{3,2},{4,5},{5,4},{6,7},{7,6},{8,9},{9,8},{10,11... | collective-permute-start | bytes 3145736 | tf_op jit(solution)/shard_map/ppermute | solution.py:54
  589.5 46.3 %collective-permute-start.56 = (bf16[1024,1024]{1,0:T(8,128)(2,1)S(1)}, bf16[1024,1024]{1,0:T(8,128)(2,1)S(1)}, u32[]{:S(2)}, u32[]{:S(2)}) collective-permute-start(bf16[1024,1024]{1,0:T(8,128)(2,1)S(1)} %shard_map.206), channel_id=1, source_target_pairs={{0,8},{1,9},{2,10},{3,11},{4,12},{5,13},{6,14},{7,15},{8,0},{9,1},... | collective-permute-start | bytes 6291464 | tf_op jit(solution)/shard_map/ppermute | solution.py:54
  609.4 24.8 %collective-permute-start.36 = (bf16[256,2048]{1,0:T(8,128)(2,1)S(1)}, bf16[256,2048]{1,0:T(8,128)(2,1)S(1)}, u32[]{:S(2)}, u32[]{:S(2)}) collective-permute-start(bf16[256,2048]{1,0:T(8,128)(2,1)S(1)} %get-tuple-element.80), channel_id=1, source_target_pairs={{0,16},{1,17},{2,18},{3,19},{4,20},{5,21},{6,22},{7,23},{8,24},{9,... | collective-permute-start | bytes 3145736 | tf_op jit(solution)/shard_map/ppermute | solution.py:54
  618.3 38.5 %collective-permute-start.27 = (bf16[256,2048]{1,0:T(8,128)(2,1)}, bf16[256,2048]{1,0:T(8,128)(2,1)}, u32[]{:S(2)}, u32[]{:S(2)}) collective-permute-start(bf16[256,2048]{1,0:T(8,128)(2,1)} %get-tuple-element.71), channel_id=1, source_target_pairs={{0,16},{1,17},{2,18},{3,19},{4,20},{5,21},{6,22},{7,23},{8,24},{9,... | collective-permute-start | bytes 3145736 | tf_op jit(solution)/shard_map/ppermute | solution.py:54
  642.2 294.0 %reduce-scatter.12.cloned.1.call-start = ((), (), s32[]{:S(2)}) async-start(), calls=%async_computation.11 | async-start | bytes 2621440 | tf_op jit(solution)/shard_map/reduce_scatter | solution.py:82
  648.0 74.3 %collective-permute-start.54 = (bf16[1024,1024]{1,0:T(8,128)(2,1)S(1)}, bf16[1024,1024]{1,0:T(8,128)(2,1)}, u32[]{:S(2)}, u32[]{:S(2)}) collective-permute-start(bf16[1024,1024]{1,0:T(8,128)(2,1)S(1)} %shard_map.204), channel_id=1, source_target_pairs={{0,8},{1,9},{2,10},{3,11},{4,12},{5,13},{6,14},{7,15},{8,0},{9,1},... | collective-permute-start | bytes 6291464 | tf_op jit(solution)/shard_map/ppermute | solution.py:54
  686.9 40.7 %collective-permute-start.39 = (bf16[256,2048]{1,0:T(8,128)(2,1)}, bf16[256,2048]{1,0:T(8,128)(2,1)}, u32[]{:S(2)}, u32[]{:S(2)}) collective-permute-start(bf16[256,2048]{1,0:T(8,128)(2,1)} %pad_maximum_fusion.10), channel_id=1, source_target_pairs={{0,16},{1,17},{2,18},{3,19},{4,20},{5,21},{6,22},{7,23},{8,24},{9,... | collective-permute-start | bytes 3145736 | tf_op jit(solution)/shard_map/ppermute | solution.py:54
  687.1 33.3 %collective-permute-start.32 = (bf16[128,2048]{1,0:T(8,128)(2,1)S(1)}, bf16[128,2048]{1,0:T(8,128)(2,1)S(1)}, u32[]{:S(2)}, u32[]{:S(2)}) collective-permute-start(bf16[128,2048]{1,0:T(8,128)(2,1)S(1)} %get-tuple-element.138.refs_0_), channel_id=1, source_target_pairs={{0,16},{1,17},{2,18},{3,19},{4,20},{5,21},{6,22},{7,23},{8,24},{9,... | collective-permute-start | bytes 1572872 | tf_op jit(solution)/shard_map/ppermute | solution.py:54
  722.3 35.1 %collective-permute-start.33 = (bf16[256,2048]{1,0:T(8,128)(2,1)}, bf16[256,2048]{1,0:T(8,128)(2,1)}, u32[]{:S(2)}, u32[]{:S(2)}) collective-permute-start(bf16[256,2048]{1,0:T(8,128)(2,1)} %pad_maximum_fusion.9), channel_id=1, source_target_pairs={{0,1},{1,0},{2,3},{3,2},{4,5},{5,4},{6,7},{7,6},{8,9},{9,8},{10,11... | collective-permute-start | bytes 3145736 | tf_op jit(solution)/shard_map/ppermute | solution.py:54
  727.5 213.8 %reduce-scatter.10.cloned.1.call-start = ((), (), s32[]{:S(2)}) async-start(), calls=%async_computation.10 | async-start | bytes 2621440 | tf_op jit(solution)/shard_map/reduce_scatter | solution.py:82
  806.4 140.8 %reduce-scatter.6.cloned.1.call-start = ((), (), s32[]{:S(2)}) async-start(), calls=%async_computation.8 | async-start | bytes 2621440 | tf_op jit(solution)/shard_map/reduce_scatter | solution.py:82
  829.4 143.1 %reduce-scatter.8.cloned.1.call-start = ((), (), s32[]{:S(2)}) async-start(), calls=%async_computation.9 | async-start | bytes 5242880 | tf_op jit(solution)/shard_map/reduce_scatter | solution.py:82
  840.8 24.7 %collective-permute-start.40 = (bf16[256,2048]{1,0:T(8,128)(2,1)S(1)}, bf16[256,2048]{1,0:T(8,128)(2,1)S(1)}, u32[]{:S(2)}, u32[]{:S(2)}) collective-permute-start(bf16[256,2048]{1,0:T(8,128)(2,1)S(1)} %copy-done.78), channel_id=1, source_target_pairs={{0,16},{1,17},{2,18},{3,19},{4,20},{5,21},{6,22},{7,23},{8,24},{9,... | collective-permute-start | bytes 3145736 | tf_op jit(solution)/shard_map/ppermute | solution.py:54
  841.2 27.0 %collective-permute-start.34 = (bf16[256,2048]{1,0:T(8,128)(2,1)S(1)}, bf16[256,2048]{1,0:T(8,128)(2,1)S(1)}, u32[]{:S(2)}, u32[]{:S(2)}) collective-permute-start(bf16[256,2048]{1,0:T(8,128)(2,1)S(1)} %copy-done.79), channel_id=1, source_target_pairs={{0,1},{1,0},{2,3},{3,2},{4,5},{5,4},{6,7},{7,6},{8,9},{9,8},{10,11... | collective-permute-start | bytes 3145736 | tf_op jit(solution)/shard_map/ppermute | solution.py:54
  881.5 44.4 %collective-permute-start.29 = (bf16[256,2048]{1,0:T(8,128)(2,1)S(1)}, bf16[256,2048]{1,0:T(8,128)(2,1)}, u32[]{:S(2)}, u32[]{:S(2)}) collective-permute-start(bf16[256,2048]{1,0:T(8,128)(2,1)S(1)} %select_n.181), channel_id=1, source_target_pairs={{1,8},{3,10},{5,12},{7,14},{8,1},{10,3},{12,5},{14,7},{17,24},{19,... | collective-permute-start | bytes 3145736 | tf_op jit(solution)/shard_map/ppermute | solution.py:54
  902.2 36.3 %collective-permute-start.42 = (bf16[256,2048]{1,0:T(8,128)(2,1)}, bf16[256,2048]{1,0:T(8,128)(2,1)}, u32[]{:S(2)}, u32[]{:S(2)}) collective-permute-start(bf16[256,2048]{1,0:T(8,128)(2,1)} %convert_element_type.195), channel_id=1, source_target_pairs={{1,8},{3,10},{5,12},{7,14},{8,1},{10,3},{12,5},{14,7},{17,24},{19,... | collective-permute-start | bytes 3145736 | tf_op jit(solution)/shard_map/ppermute | solution.py:54
  936.3 39.8 %collective-permute-start.55 = (bf16[256,1024]{1,0:T(8,128)(2,1)}, bf16[256,1024]{1,0:T(8,128)(2,1)}, u32[]{:S(2)}, u32[]{:S(2)}) collective-permute-start(bf16[256,1024]{1,0:T(8,128)(2,1)} %reduce-scatter.12.cloned.1.call-done), channel_id=1, source_target_pairs={{1,8},{3,10},{5,12},{7,14},{8,1},{10,3},{12,5},{14,7},{17,24},{19,... | collective-permute-start | bytes 1572872 | tf_op jit(solution)/shard_map/ppermute | solution.py:54
  941.3 36.9 %collective-permute-start.53 = (bf16[256,1024]{1,0:T(8,128)(2,1)}, bf16[256,1024]{1,0:T(8,128)(2,1)}, u32[]{:S(2)}, u32[]{:S(2)}) collective-permute-start(bf16[256,1024]{1,0:T(8,128)(2,1)} %reduce-scatter.10.cloned.1.call-done), channel_id=1, source_target_pairs={{1,8},{3,10},{5,12},{7,14},{8,1},{10,3},{12,5},{14,7},{17,24},{19,... | collective-permute-start | bytes 1572872 | tf_op jit(solution)/shard_map/ppermute | solution.py:54
  947.2 33.5 %collective-permute-start.49 = (bf16[256,1024]{1,0:T(8,128)(2,1)}, bf16[256,1024]{1,0:T(8,128)(2,1)}, u32[]{:S(2)}, u32[]{:S(2)}) collective-permute-start(bf16[256,1024]{1,0:T(8,128)(2,1)} %reduce-scatter.6.cloned.1.call-done), channel_id=1, source_target_pairs={{1,8},{3,10},{5,12},{7,14},{8,1},{10,3},{12,5},{14,7},{17,24},{19,... | collective-permute-start | bytes 1572872 | tf_op jit(solution)/shard_map/ppermute | solution.py:54
  (114 other events, 1479.2 us)
Sparse Core Ops, SparseCore 0:
  28.5 81.9 all-gather.3
  131.9 78.7 all-gather.5
  224.7 79.9 all-gather.7
  642.3 40.8 reduce-scatter.13
  727.6 44.4 reduce-scatter.11
  806.5 41.0 reduce-scatter.9
  850.0 43.0 reduce-scatter.5
  895.5 77.0 reduce-scatter.7

commit v3 on v2

v3 whole, which is shorter than its diff:
```python
import jax
import jax.numpy as jnp
from jax import lax
from jax.experimental import pallas as pl
from jax.experimental.pallas import tpu as pltpu
from jax.sharding import PartitionSpec as P

KEY_HEAD = 256
VAL_HEAD = 512
ROT = KEY_HEAD // 2
eps_norm = 1e-05
eps_group = 1.0
BF = jnp.bfloat16
F32 = jnp.float32
AXES = ("seq", "fsdp")
ANY = pl.BlockSpec(memory_space=pl.ANY)


def nn(left, right):
    return jnp.dot(left, right, preferred_element_type=F32)


def nt(left, right):
    return lax.dot_general(left, right, (((1,), (1,)), ((), ())), preferred_element_type=F32)


def tn(left, right):
    return lax.dot_general(left, right, (((0,), (0,)), ((), ())), preferred_element_type=F32)


def after(value, *first):
    return lax.optimization_barrier((value, *first))[0]


class Grid:
    def __init__(self, n_seq, n_fsdp):
        assert n_seq == 4 and n_fsdp % 2 == 0
        self.n_fsdp, self.nz = n_fsdp, n_fsdp // 2
        self.lines = [[z * 2 + x for z in range(self.nz)] for x in range(2)]
        self.groups = [
            [(y * 2 + c) * n_fsdp + z * 2 + x for z in range(self.nz) for c in range(2)]
            for y in range(2)
            for x in range(2)
        ]

    def send(self, value, move):
        found = []
        for y in range(2):
            for c in range(2):
                for z in range(self.nz):
                    for x in range(2):
                        y2, c2, z2, x2 = move(y, c, z, x)
                        src = (y * 2 + c) * self.n_fsdp + z * 2 + x
                        dst = (y2 * 2 + c2) * self.n_fsdp + z2 * 2 + x2
                        if src != dst:
                            found.append((src, dst))
        return lax.ppermute(value, AXES, found)

    def flip_z(self, value, bit):
        return self.send(value, lambda y, c, z, x: (y, c, z ^ bit, x))

    def flip_c(self, value):
        return self.send(value, lambda y, c, z, x: (y, 1 - c, z, x))

    def flip_y(self, value):
        return self.send(value, lambda y, c, z, x: (1 - y, c, z, x))

    def flip_x(self, value):
        return self.send(value, lambda y, c, z, x: (y, c, z, 1 - x))

    def first(self, b, value):
        return self.flip_y(value) if b == 0 else self.flip_x(value)

    def second(self, b, value):
        return self.flip_x(value) if b == 0 else self.flip_y(value)

    def swap(self, value):
        return self.send(value.astype(BF), lambda y, c, z, x: (y, x, z, c))

    def gather_weight(self, shard):
        return lax.all_gather(shard, AXES, axis=0, tiled=True, axis_index_groups=self.groups)

    def scatter_grad(self, value):
        return lax.psum_scatter(
            value, AXES, scatter_dimension=0, tiled=True, axis_index_groups=self.groups
        )

    def total(self, value):
        for flip in (self.flip_y, self.flip_x, self.flip_c):
            value = value + flip(value)
        if self.nz & (self.nz - 1):
            return lax.psum(value, "fsdp", axis_index_groups=self.lines)
        bit = 1
        while bit < self.nz:
            value = value + self.flip_z(value, bit)
            bit *= 2
        return value


def call(body, grid, ins, outs, shapes, scratch=(), flops=0, moved=0):
    return pl.pallas_call(
        body,
        out_shape=shapes,
        grid=grid,
        in_specs=ins,
        out_specs=outs,
        scratch_shapes=list(scratch),
        cost_estimate=pl.CostEstimate(
            flops=flops // 50, bytes_accessed=moved // 50, transcendentals=0
        ),
        compiler_params=pltpu.CompilerParams(vmem_limit_bytes=48 << 20),
    )


def shape(rows, cols, dtype=BF):
    return jax.ShapeDtypeStruct((rows, cols), dtype)


def spec(rows, cols, index):
    return pl.BlockSpec((rows, cols), index)


def fetch(pieces, target, sems):
    copies, row = [], 0
    for i, piece in enumerate(pieces):
        rows = piece.shape[0]
        copies.append(pltpu.make_async_copy(piece, target.at[pl.ds(row, rows)], sems.at[i]))
        row += rows
    for copy in copies:
        copy.start()
    for copy in copies:
        copy.wait()


def assemble(pieces):
    n = len(pieces)

    def body(*refs):
        fetch(refs[:n], refs[n], refs[n + 1])

    rows = sum(p.shape[0] for p in pieces)
    cols = pieces[0].shape[1]
    return pl.pallas_call(
        body,
        out_shape=shape(rows, cols),
        in_specs=[ANY] * n,
        scratch_shapes=[pltpu.SemaphoreType.DMA((n,))],
        cost_estimate=pl.CostEstimate(
            flops=0, bytes_accessed=4 * rows * cols, transcendentals=0
        ),
    )(*pieces)


def rotated(first, second, cos_part, sin_part):
    return (first * cos_part - second * sin_part, second * cos_part + first * sin_part)


def project(pieces, weight, cos_table, sin_table, rotate_cols, gate_cols):
    n = len(pieces)
    rows = sum(p.shape[0] for p in pieces)
    width = pieces[0].shape[1]
    cols = weight.shape[1]
    tile, chunk = 512, 512
    first = (cols - gate_cols) // tile

    def body(*refs):
        w_ref, cos_ref, sin_ref, h_ref, o_ref, gate_ref, sems = refs[n:]
        j = pl.program_id(0)

        @pl.when(j == 0)
        def _():
            fetch(refs[:n], h_ref, sems)

        turn = j * tile < rotate_cols

        def step(i, _):
            at = pl.ds(pl.multiple_of(i * chunk, chunk), chunk)
            acc = nn(h_ref[at, :], w_ref[...])

            @pl.when(j < first)
            def _():
                cos_part = jnp.where(turn, cos_ref[at, :], 1.0)
                sin_part = jnp.where(turn, sin_ref[at, :], 0.0)
                for s in range(0, tile, KEY_HEAD):
                    u, v = rotated(
                        acc[:, s : s + ROT], acc[:, s + ROT : s + KEY_HEAD], cos_part, sin_part
                    )
                    o_ref[at, s : s + ROT] = u.astype(BF)
                    o_ref[at, s + ROT : s + KEY_HEAD] = v.astype(BF)

            @pl.when(j >= first)
            def _():
                gate_ref[at, :] = acc

            return 0

        lax.fori_loop(0, rows // chunk, step, 0)

    return call(
        body,
        (cols // tile,),
        [ANY] * n
        + [spec(width, tile, lambda j: (0, j))]
        + [spec(rows, ROT, lambda j: (0, 0))] * 2,
        [
            spec(rows, width, lambda j: (0, 0)),
            spec(rows, tile, lambda j: (0, jnp.minimum(j, first - 1))),
            spec(rows, tile, lambda j: (0, jnp.maximum(j - first, 0))),
        ],
        [shape(rows, width), shape(rows, cols - gate_cols), shape(rows, gate_cols, F32)],
        [pltpu.SemaphoreType.DMA((n,))],
        2 * rows * width * cols,
        2 * (2 * rows * width + width * cols + rows * cols),
    )(*pieces, weight, cos_table, sin_table)


def decay_chunk(col_ref, row_ref, at, log_gamma):
    pos_n, seg_n = col_ref[at, 0:1], col_ref[at, 1:2]
    pos_m, seg_m = row_ref[0:1, :], row_ref[1:2, :]
    distance = pos_n - pos_m
    allowed = (distance >= 0.0) & (seg_n == seg_m)
    value = jnp.exp(jnp.maximum(distance, 0.0) * log_gamma) * (KEY_HEAD**-0.5)
    return jnp.where(allowed, value, 0.0)


def sigmoid(value):
    return 1.0 / (1.0 + jnp.exp(-value))


def retain(qkv, gate, col_info, row_info, log_gamma, heads, micro):
    rows = qkv.shape[0] // micro
    dv = heads * VAL_HEAD
    chunk = 256

    def body(q_ref, k_ref, v_ref, gate_ref, col_ref, row_ref, lg_ref, gated_ref):
        log_g = lg_ref[pl.program_id(1)]

        def step(i, _):
            at = pl.ds(pl.multiple_of(i * chunk, chunk), chunk)
            decay = decay_chunk(col_ref, row_ref, at, log_g)
            weights = (nt(q_ref[at, :], k_ref[...]) * decay).astype(BF)
            kept = nn(weights, v_ref[...])
            scale = lax.rsqrt(jnp.mean(kept * kept, axis=-1, keepdims=True) + eps_group)
            gate = gate_ref[at, :]
            gated_ref[at, :] = (gate * sigmoid(gate) * (kept * scale)).astype(BF)
            return 0

        lax.fori_loop(0, rows // chunk, step, 0)

    return call(
        body,
        (micro, heads),
        [
            spec(rows, KEY_HEAD, lambda b, h: (b, h)),
            spec(rows, KEY_HEAD, lambda b, h: (b, heads + h)),
            spec(rows, VAL_HEAD, lambda b, h: (b, heads + h)),
            spec(rows, VAL_HEAD, lambda b, h: (b, h)),
            spec(rows, 128, lambda b, h: (b, 0)),
            spec(8, rows, lambda b, h: (b, 0)),
            pl.BlockSpec(memory_space=pltpu.SMEM),
        ],
        spec(rows, VAL_HEAD, lambda b, h: (b, h)),
        shape(micro * rows, dv),
        (),
        2 * micro * rows * rows * heads * (KEY_HEAD + VAL_HEAD),
        10 * micro * rows * dv,
    )(qkv, qkv, qkv, gate, col_info, row_info, log_gamma)


ROOT_2_PI = 0.7978845608028654


def feed_up(pieces, weight, hidden):
    n = len(pieces)
    rows = sum(p.shape[0] for p in pieces)
    width = pieces[0].shape[1]
    tile, chunk = 512, 512

    def body(*refs):
        w_ref, h_ref, act_ref, slope_ref, sems = refs[n:]

        @pl.when(pl.program_id(0) == 0)
        def _():
            fetch(refs[:n], h_ref, sems)

        def step(i, _):
            at = pl.ds(pl.multiple_of(i * chunk, chunk), chunk)
            up = nn(h_ref[at, :], w_ref[...])
            square = up * up
            bent = jnp.tanh(ROOT_2_PI * (up + 0.044715 * square * up))
            act_ref[at, :] = (0.5 * up * (1.0 + bent)).astype(BF)
            inner = ROOT_2_PI * (1.0 + 3.0 * 0.044715 * square)
            slope = 0.5 * (1.0 + bent) + 0.5 * up * (1.0 - bent * bent) * inner
            slope_ref[at, :] = slope
            return 0

        lax.fori_loop(0, rows // chunk, step, 0)

    return call(
        body,
        (hidden // tile,),
        [ANY] * n + [spec(width, tile, lambda j: (0, j))],
        [spec(rows, width, lambda j: (0, 0))] + [spec(rows, tile, lambda j: (0, j))] * 2,
        [shape(rows, width), shape(rows, hidden), shape(rows, hidden, F32)],
        [pltpu.SemaphoreType.DMA((n,))],
        2 * rows * width * hidden,
        4 * rows * width + 2 * width * hidden + 6 * rows * hidden,
    )(*pieces, weight)


def project_back(b, value, rows, weight, first_col):
    hidden = value.shape[1]
    width = weight.shape[0]
    tile, chunk = 512, 512
    steps, first = hidden // tile, first_col // tile

    def body(in_ref, w_ref, sent_ref, kept_ref, acc_ref):
        j = pl.program_id(0)

        def step(i, _):
            at = pl.ds(pl.multiple_of(i * chunk, chunk), chunk)
            add_back(j, acc_ref, at, nt(in_ref[at, :], w_ref[...]))
            return 0

        lax.fori_loop(0, rows // chunk, step, 0)
        hand_out(j == steps - 1, acc_ref, sent_ref, kept_ref)

    return call(
        body,
        (steps,),
        [spec(rows, tile, lambda j: (b, j))]
        + [spec(width, tile, lambda j: (0, first + j))],
        [spec(rows // 2, width, lambda j: (0, 0))] * 2,
        [shape(rows // 2, width), shape(rows // 2, width, F32)],
        [pltpu.VMEM((rows, width), F32)],
        2 * rows * width * hidden,
        2 * rows * hidden + 2 * width * hidden + 3 * rows * width,
    )(value, weight)


def add_back(j, acc_ref, at, part):
    @pl.when(j == 0)
    def _():
        acc_ref[at, :] = part

    @pl.when(j != 0)
    def _():
        acc_ref[at, :] = acc_ref[at, :] + part


def hand_out(last, acc_ref, sent_ref, kept_ref):
    rows = acc_ref.shape[0]

    @pl.when(last)
    def _():
        kept_ref[...] = acc_ref[: rows // 2, :]
        sent_ref[...] = acc_ref[rows // 2 :, :].astype(BF)


def feed_back(b, cot, slope, weight, hidden):
    width = cot.shape[1]
    rows = slope.shape[0]
    tile, chunk = 512, 512
    steps = hidden // tile

    def body(cot_ref, slope_ref, down_ref, up_ref, dup_ref, sent_ref, kept_ref, acc_ref):
        j = pl.program_id(0)

        def step(i, _):
            at = pl.ds(pl.multiple_of(i * chunk, chunk), chunk)
            d_act = nn(cot_ref[at, :], down_ref[...])
            d_up = (d_act * slope_ref[at, :]).astype(BF)
            dup_ref[at, :] = d_up
            add_back(j, acc_ref, at, nt(d_up, up_ref[...]))
            return 0

        lax.fori_loop(0, rows // chunk, step, 0)
        hand_out(j == steps - 1, acc_ref, sent_ref, kept_ref)

    return call(
        body,
        (steps,),
        [spec(rows, width, lambda j: (b, 0)), spec(rows, tile, lambda j: (0, j))]
        + [spec(width, tile, lambda j: (0, steps + j)), spec(width, tile, lambda j: (0, j))],
        [spec(rows, tile, lambda j: (0, j))] + [spec(rows // 2, width, lambda j: (0, 0))] * 2,
        [shape(rows, hidden), shape(rows // 2, width), shape(rows // 2, width, F32)],
        [pltpu.VMEM((rows, width), F32)],
        4 * rows * width * hidden,
        5 * rows * width + 4 * width * hidden + 6 * rows * hidden,
    )(cot, slope, weight, weight)


def retain_back(b, d_mix, gate, qkv, weights, col_info, row_info, cos_table, sin_table,
                log_gamma, heads):
    w0, w1 = weights
    rows = d_mix.shape[0] // 2
    width = d_mix.shape[1]
    dk, dv = heads * KEY_HEAD, heads * VAL_HEAD
    chunk = 256

    def body(mix_ref, wo, wg, wv, wq, wk, gate_ref, q_ref, k_ref, v_ref, col_ref, row_ref,
             cos_ref, sin_ref, lg_ref, dgate_ref, dq_ref, dk_ref, dv_ref, sent_ref, kept_ref,
             acc_ref, dk_acc, dv_acc):
        h = pl.program_id(0)
        log_g = lg_ref[h]

        def step(i, _):
            at = pl.ds(pl.multiple_of(i * chunk, chunk), chunk)
            d_gated = nn(mix_ref[at, :], wo[...])
            decay = decay_chunk(col_ref, row_ref, at, log_g)
            weights = (nt(q_ref[at, :], k_ref[...]) * decay).astype(BF)
            kept = nn(weights, v_ref[...])
            scale = lax.rsqrt(jnp.mean(kept * kept, axis=-1, keepdims=True) + eps_group)
            y_norm = kept * scale
            gate = gate_ref[at, :]
            sig = sigmoid(gate)
            d_gate = d_gated * y_norm * sig * (1.0 + gate * (1.0 - sig))
            dgate_ref[at, :] = d_gate.astype(BF)
            d_y = d_gated * (gate * sig)
            d_ret = (
                scale * (d_y - y_norm * jnp.mean(d_y * y_norm, axis=-1, keepdims=True))
            ).astype(BF)
            d_weights = nt(d_ret, v_ref[...])
            d_scores = (d_weights * decay).astype(BF)
            d_v = tn(weights, d_ret)
            d_k = tn(d_scores, q_ref[at, :])
            d_q = nn(d_scores, k_ref[...])
            u, v = rotated(d_q[:, :ROT], d_q[:, ROT:], cos_ref[at, :], -sin_ref[at, :])
            dq_ref[at, :ROT] = u.astype(BF)
            dq_ref[at, ROT:] = v.astype(BF)

            @pl.when(i == 0)
            def _():
                dk_acc[...] = d_k
                dv_acc[...] = d_v

            @pl.when(i != 0)
            def _():
                dk_acc[...] = dk_acc[...] + d_k
                dv_acc[...] = dv_acc[...] + d_v

            return 0

        lax.fori_loop(0, rows // chunk, step, 0)
        dv_ref[...] = dv_acc[...].astype(BF)
        u, v = rotated(dk_acc[:, :ROT], dk_acc[:, ROT:], cos_ref[...], -sin_ref[...])
        dk_ref[:, :ROT] = u.astype(BF)
        dk_ref[:, ROT:] = v.astype(BF)

        def back(i, _):
            at = pl.ds(pl.multiple_of(i * chunk, chunk), chunk)
            part = (
                nt(dq_ref[at, :], wq[...])
                + nt(dk_ref[at, :], wk[...])
                + nt(dv_ref[at, :], wv[...])
                + nt(dgate_ref[at, :], wg[...])
            )
            add_back(h, acc_ref, at, part)
            return 0

        lax.fori_loop(0, rows // chunk, back, 0)
        hand_out(h == heads - 1, acc_ref, sent_ref, kept_ref)

    per_head = spec(rows, VAL_HEAD, lambda h: (0, h))
    per_key = spec(rows, KEY_HEAD, lambda h: (0, h))
    whole = spec(rows // 2, width, lambda h: (0, 0))
    return call(
        body,
        (heads,),
        [
            spec(rows, width, lambda h: (b, 0)),
            spec(width, VAL_HEAD, lambda h: (0, h)),
            spec(width, VAL_HEAD, lambda h: (0, 2 * heads + h)),
            spec(width, VAL_HEAD, lambda h: (0, heads + h)),
            spec(width, KEY_HEAD, lambda h: (0, h)),
            spec(width, KEY_HEAD, lambda h: (0, heads + h)),
            spec(rows, VAL_HEAD, lambda h: (b, h)),
            spec(rows, KEY_HEAD, lambda h: (b, h)),
            spec(rows, KEY_HEAD, lambda h: (b, heads + h)),
            spec(rows, VAL_HEAD, lambda h: (b, heads + h)),
            spec(rows, 128, lambda h: (b, 0)),
            spec(8, rows, lambda h: (b, 0)),
            spec(rows, ROT, lambda h: (b, 0)),
            spec(rows, ROT, lambda h: (b, 0)),
            pl.BlockSpec(memory_space=pltpu.SMEM),
        ],
        [
            per_head,
            per_key,
            per_key,
            per_head,
            whole,
            whole,
        ],
        [
            shape(rows, dv),
            shape(rows, dk),
            shape(rows, dk),
            shape(rows, dv),
            shape(rows // 2, width),
            shape(rows // 2, width, F32),
        ],
        [
            pltpu.VMEM((rows, width), F32),
            pltpu.VMEM((rows, KEY_HEAD), F32),
            pltpu.VMEM((rows, VAL_HEAD), F32),
        ],
        2 * rows * width * (2 * dk + 3 * dv) + 2 * rows * rows * heads * 5 * VAL_HEAD,
        2 * width * (2 * dk + 3 * dv) + 12 * rows * dv + 7 * rows * width,
    )(
        d_mix, w1, w0, w0, w0, w0,
        gate, qkv, qkv, qkv, col_info, row_info, cos_table, sin_table, log_gamma,
    )


def weight_grad(lefts, rights):
    micro = len(lefts)
    groups = len(rights)
    width = lefts[0][0].shape[1]
    tile = 512
    sizes = [r[0][0].shape[1] for r in rights]
    cols = sum(sizes)
    flat = [r for group in rights for r in group]

    def body(*refs):
        left = refs[:micro]
        right = refs[micro : micro + len(flat)]
        o_ref = refs[-1]
        start = 0
        for g in range(groups):
            at = slice(start, start + sizes[g])
            acc = tn(left[0][...], right[g * micro][...])
            for b in range(1, micro):
                acc = acc + tn(left[b][...], right[g * micro + b][...])
            o_ref[:, at] = acc.astype(BF)
            start += sizes[g]

    rows = lefts[0][2]
    args = [array for array, _, _ in lefts] + [array for array, _, _ in flat]
    ins = [spec(rows, tile, lambda i, b=b: (b, i)) for _, b, _ in lefts]
    ins = ins + [spec(rows, r.shape[1], lambda i, b=b: (b, 0)) for r, b, _ in flat]
    return call(
        body,
        (width // tile,),
        ins,
        spec(tile, cols, lambda i: (i, 0)),
        shape(width, cols),
        (),
        2 * micro * rows * width * cols,
        2 * (micro * rows * (width + cols) + width * cols),
    )(*args)


def layer_norm_parts(inputs, gain_row):
    center = inputs - jnp.mean(inputs, axis=-1, keepdims=True)
    inverse = lax.rsqrt(jnp.mean(center * center, axis=-1, keepdims=True) + eps_norm)
    scaled = center * inverse
    return (scaled * gain_row, scaled, inverse)


def layer_norm_back(incoming, scaled, inverse, gain_row):
    upstream = incoming * gain_row
    centered_grad = (
        upstream
        - jnp.mean(upstream, axis=-1, keepdims=True)
        - scaled * jnp.mean(upstream * scaled, axis=-1, keepdims=True)
    )
    return (centered_grad * inverse, jnp.sum(incoming * scaled, axis=0))


def make_on_device(grid):
    def on_device(
        tokens, norm_gains, w_query, w_key, w_value, w_gate, w_out, w_up, w_down, segments, d_output
    ):
        micro, _, piece, width = tokens.shape
        assert micro == 2
        own, length = micro * piece, 4 * piece
        dk, dv = w_query.shape[1], w_value.shape[1]
        heads = dk // KEY_HEAD
        hidden = w_up.shape[1]
        seq_id = lax.axis_index("seq")
        fsdp_id = lax.axis_index("fsdp")
        y, c = seq_id // 2, seq_id % 2
        x = fsdp_id % 2
        same = x == c
        both = range(micro)

        last = []

        def hold(value):
            return after(value, *last)

        def mark(value):
            last[:] = [value]
            return value

        def settle(value, moved):
            return mark(jnp.where(same, value, hold(moved).astype(value.dtype)))

        def rows(value, b):
            return value[b * piece : (b + 1) * piece]

        def pair(block, moved):
            return mark(jnp.concatenate([block, hold(moved)], axis=0))

        def reduce_second(b, kept, got):
            got = hold(got).astype(F32)
            kept = kept + got
            return kept[:piece], grid.first(b, mark(kept[piece:].astype(BF)))

        w0 = mark(jnp.concatenate([w_query, w_key, w_value, w_gate], axis=1))
        w0_moved = grid.swap(w0)
        toks = tokens.reshape(own, width)
        toks_moved = grid.swap(toks)
        segs = segments.reshape(micro, length).astype(F32)
        segs_moved = grid.swap(segs)
        w1 = mark(hold(w_out).T)
        w2 = mark(jnp.concatenate([w_up, hold(w_down).T], axis=1))

        ranks = [
            [2 * (y ^ i) + (x ^ j) for i, j in ((0, 0), (1, 0), (0, 1), (1, 1))],
            [2 * (y ^ i) + (x ^ j) for i, j in ((0, 0), (0, 1), (1, 0), (1, 1))],
        ]
        positions = jnp.stack(
            [jnp.concatenate([r * piece + jnp.arange(piece) for r in ranks[b]]) for b in both]
        ).astype(F32)
        frequency = jnp.exp(-jnp.log(10000.0) * 2.0 * jnp.arange(ROT, dtype=F32) / KEY_HEAD)
        angles = hold(positions).reshape(-1, 1) * frequency[None, :]
        cos_table, sin_table = jnp.cos(angles), jnp.sin(angles)
        mark(cos_table)
        head_ids = (y * 2 + x) * heads + jnp.arange(heads, dtype=jnp.int32)
        log_gamma = jnp.log1p(-jnp.exp2(-5.0 - head_ids.astype(F32)))
        gain_in, gain_mid = norm_gains[0], norm_gains[1]

        w0 = settle(w0, w0_moved)
        w0_full = grid.gather_weight(w0)
        toks = settle(toks, toks_moved)
        xin = toks.astype(F32)
        normed, scaled_in, inverse_in = layer_norm_parts(xin, gain_in)
        normed = mark(normed.astype(BF))
        h1_own = [rows(normed, b) for b in both]
        h1_first = [grid.first(b, h1_own[b]) for b in both]
        w1_moved = grid.swap(hold(w1))
        segs = settle(segs, segs_moved)
        seg_rows = jnp.stack(
            [
                jnp.concatenate(
                    [lax.dynamic_slice_in_dim(segs[b], r * piece, piece) for r in ranks[b]]
                )
                for b in both
            ]
        )
        lanes = jnp.arange(128)[None, :]
        col_info = jnp.where(
            lanes == 0,
            positions.reshape(-1, 1),
            jnp.where(lanes == 1, seg_rows.reshape(-1, 1), 0.0),
        )
        row_info = jnp.stack([positions, seg_rows] + [jnp.zeros_like(positions)] * 6, axis=1)
        row_info = mark(row_info.reshape(8 * micro, length))
        h1_second = [grid.second(b, pair(h1_own[b], h1_first[b])) for b in both]
        w1 = settle(w1, w1_moved)
        w1_full = grid.gather_weight(w1)
        cots = d_output.reshape(own, width)
        cots_moved = grid.swap(hold(cots))
        w2_moved = grid.swap(hold(w2))
        cots = settle(cots, cots_moved)
        cot_own = [rows(cots, b) for b in both]
        cot_first = [grid.first(b, cot_own[b]) for b in both]
        w2 = settle(w2, w2_moved)
        w2_full = grid.gather_weight(w2)
        cot_second = [grid.second(b, pair(cot_own[b], cot_first[b])) for b in both]

        h1, qkv, gate = project(
            [p for b in both for p in (h1_own[b], h1_first[b], h1_second[b])],
            hold(w0_full), cos_table, sin_table, 2 * dk, dv,
        )
        mark(qkv)
        cot = mark(
            assemble([p for b in both for p in (cot_own[b], cot_first[b], hold(cot_second[b]))])
        )
        gated = mark(retain(hold(qkv), gate, col_info, row_info, log_gamma, heads, micro))
        sums = []
        for b in both:
            sent, kept = project_back(b, hold(gated), length, w1_full, 0)
            mark(sent)
            sums.append((kept, grid.second(b, sent)))
        sums = [reduce_second(b, *sums[b]) for b in both]
        x1, mid, scaled_mid, inverse_mid, mid_first = [], [], [], [], []
        for b in both:
            x1.append(rows(xin, b) + (sums[b][0] + hold(sums[b][1]).astype(F32)))
            out, scaled, inverse = layer_norm_parts(x1[b], gain_mid)
            mid.append(mark(out.astype(BF)))
            scaled_mid.append(scaled)
            inverse_mid.append(inverse)
            mid_first.append(grid.first(b, mid[b]))
        mid_second = [grid.second(b, pair(mid[b], mid_first[b])) for b in both]
        h2, act, slope = [], [], []
        for b in both:
            h, a, s = feed_up(
                (mid[b], mid_first[b], hold(mid_second[b])), w2_full, hidden
            )
            mark(a)
            h2.append(h)
            act.append(a)
            slope.append(s)

        def blocks(value):
            if isinstance(value, list):
                return [(v, 0, length) for v in value]
            return [(value, b, length) for b in both]

        def grad(left, rights):
            left = hold(left) if not isinstance(left, list) else [hold(v) for v in left]
            sent = mark(weight_grad(blocks(left), [blocks(r) for r in rights]))
            return grid.scatter_grad(sent)

        d_up, sums = [], []
        g_down = grad(cot, [act])
        for b in both:
            d, sent, kept = feed_back(b, hold(cot), slope[b], w2_full, hidden)
            mark(sent)
            d_up.append(d)
            sums.append((kept, grid.second(b, sent)))
        g_up = grad(h2, [d_up])
        sums = [reduce_second(b, *sums[b]) for b in both]
        d_x1, mix_first, gain_mid_grad = [], [], 0.0
        for b in both:
            d_h2 = sums[b][0] + hold(sums[b][1]).astype(F32)
            d_ln, part = layer_norm_back(d_h2, scaled_mid[b], inverse_mid[b], gain_mid)
            gain_mid_grad = gain_mid_grad + part
            d_x1.append(cot_own[b].astype(F32) + d_ln)
            mix_first.append((mark(d_x1[b].astype(BF)),))
            mix_first[b] = mix_first[b] + (grid.first(b, mix_first[b][0]),)
        down = []
        sent, kept = project_back(0, hold(act[0]), length, w2_full, hidden)
        mark(sent)
        down.append((kept, sent))
        mix = [(v, f, grid.second(b, pair(v, f))) for b, (v, f) in enumerate(mix_first)]
        sent, kept = project_back(0, hold(act[1]), length, w2_full, hidden)
        mark(sent)
        down.append((kept, sent))
        d_mix = mark(assemble([p for b in both for p in mix[b][:2] + (hold(mix[b][2]),)]))
        g_out = grad(d_mix, [gated])
        g_down_moved = grid.swap(hold(g_down))
        d_gate, d_q, d_k, d_v, sums = [], [], [], [], []
        for b in both:
            g, q, k, v, sent, kept = retain_back(
                b, hold(d_mix), gate, qkv, (w0_full, w1_full), col_info, row_info, cos_table,
                sin_table, log_gamma, heads,
            )
            mark(sent)
            d_gate.append(g)
            d_q.append(q)
            d_k.append(k)
            d_v.append(v)
            sums.append((kept, grid.second(b, sent)))
            if b == 0:
                down = [(kept, grid.second(b, hold(sent))) for b, (kept, sent) in enumerate(down)]
                g_up_moved = grid.swap(hold(g_up))
        g_gv = grad(h1, [d_gate, d_v])
        g_qk = grad(h1, [d_q, d_k])
        down = [reduce_second(b, *down[b]) for b in both]
        sums = [reduce_second(b, *sums[b]) for b in both]
        outs = [
            (x1[b] + (down[b][0] + hold(down[b][1]).astype(F32))).astype(BF) for b in both
        ]
        output = mark(jnp.concatenate(outs))
        output_moved = grid.swap(output)
        d_inputs, gain_in_grad = [], 0.0
        for b in both:
            d_h1 = sums[b][0] + hold(sums[b][1]).astype(F32)
            d_ln, part = layer_norm_back(d_h1, rows(scaled_in, b), rows(inverse_in, b), gain_in)
            gain_in_grad = gain_in_grad + part
            d_inputs.append(mark(d_x1[b] + d_ln))
        d_input = mark(jnp.concatenate(d_inputs))
        d_input_moved = grid.swap(d_input)
        g_out_moved = grid.swap(hold(g_out))
        grad_norms = grid.total(jnp.stack([gain_in_grad, gain_mid_grad]))
        g_gv_moved = grid.swap(mark(hold(g_gv)))
        g_qk_moved = grid.swap(hold(g_qk))
        pairs = (
            (output, output_moved), (d_input, d_input_moved), (g_down, g_down_moved),
            (g_up, g_up_moved), (g_out, g_out_moved), (g_gv, g_gv_moved), (g_qk, g_qk_moved),
        )
        output, d_input, g_down, g_up, g_out, g_gv, g_qk = [
            jnp.where(same, value, moved.astype(value.dtype)) for value, moved in pairs
        ]
        g_down, g_up, g_out, g_gv, g_qk = [
            g.astype(F32) for g in (g_down, g_up, g_out, g_gv, g_qk)
        ]
        whole = (micro, 1, piece, width)
        return (
            output.reshape(whole),
            d_input.reshape(whole),
            grad_norms,
            g_qk[:, :dk],
            g_qk[:, dk:],
            g_gv[:, dv:],
            g_gv[:, :dv],
            g_out.T,
            g_up,
            g_down.T,
        )

    return on_device


def solution(mesh):
    grid = Grid(mesh.shape["seq"], mesh.shape["fsdp"])
    rows = P("fsdp", "seq")
    cols = P("seq", "fsdp")
    tok = P(None, "fsdp", "seq", None)
    return jax.shard_map(
        make_on_device(grid),
        mesh=mesh,
        in_specs=(tok, P(), rows, rows, rows, rows, cols, rows, cols, P(None, "fsdp", None), tok),
        out_specs=(tok, tok, P(), rows, rows, rows, rows, cols, rows, cols),
        check_vma=False,
    )
```

time: 1010 us -> 670 us (0.66)
  Pallas kernels: 327 us -> 189 us
  waiting for transfers between devices: 432 us -> 294 us
  local copies, waits for them, and re-layouts: 70.8 us -> 31.3 us
  other arithmetic: 71.7 us -> 52.7 us
    pallas_call x20 -> x17, Pallas kernels: 307 us -> 169 us  [the longest x2 49.5 us: retain_back(): call(body, (heads,), [spec(rows, width, lambda h: (b, 0)), spec(width, VA...]
    ppermute x58 -> x50, waiting for transfers between devices: 355 us -> 244 us  [send(): return lax.ppermute(value, AXES, found)]
    unnamed x175 -> x149, local copies, waits for them, and re-layouts: 46.6 us -> 24.5 us
    all_gather x3, waiting for transfers between devices: 53.7 us -> 39.5 us  [gather_weight(): lax.all_gather(shard, AXES, axis=0, tiled=True, axis_index_groups=self.gr...]
    reduce_scatter x5, waiting for transfers between devices: 23 us -> 9.84 us  [scatter_grad(): lax.psum_scatter(value, AXES, scatter_dimension=0, tiled=True, axis_index...]
    select_n x13 -> x8, other arithmetic: 24.5 us -> 13 us  [the longest x5 7.28 us: settle(): return mark(jnp.where(same, value, hold(moved).astype(value.dtype)))]
    convert_element_type x24 -> x11, other arithmetic: 19.1 us -> 7.78 us  [the longest x3 3.41 us: on_device(): g.astype(F32)]
    add x1 -> x10, other arithmetic: 0.57 us -> 11 us  [the longest x8 10.3 us: reduce_second(): kept = kept + got]
  transfers between devices with their start and end apart: 66 -> 58, of which waited for: 37 -> 32; matrix products, arithmetic and copies ran while one was open for 10% -> 9% of each run, Pallas kernels for 31% -> 26%
where the time goes in v3:
time: 670 us; the launch traced here: 662 us
  waiting for transfers between devices  294 us (44%)
  Pallas kernels  189 us (28%)
  starting transfers between devices  79.6 us (12%)
  other arithmetic  52.7 us (8%)
  local copies, waits for them, and re-layouts  31.3 us (5%)
  between operations  15.7 us (2%)
    ppermute x50, waiting for transfers between devices, send(): return lax.ppermute(value, AXES, found)  244 us
    ppermute x50, starting transfers between devices, send(): return lax.ppermute(value, AXES, found)  79.2 us
    pallas_call x2, Pallas kernels, retain_back(): call(body, (heads,), [spec(rows, width, lambda h: (b, 0)), spec(width, VA...  49.5 us
    pallas_call x5, Pallas kernels, weight_grad(): call(body, (width // tile,), ins, spec(tile, cols, lambda i: (i, 0)), sha...  43 us
    all_gather x3, waiting for transfers between devices, gather_weight(): lax.all_gather(shard, AXES, axis=0, tiled=True, axis_index_groups=self.gr...  39.5 us
    unnamed x149, local copies, waits for them, and re-layouts  24.5 us
    pallas_call x1, Pallas kernels, project(): call(body, (cols // tile,), [ANY] * n + [spec(width, tile, lambda j: (0,...  23.9 us
    pallas_call x4, Pallas kernels, project_back(): call(body, (steps,), [spec(rows, tile, lambda j: (b, j))] + [spec(width,...  22.5 us
  transfers between devices with their start and end apart: 58, of which 32 were waited for; matrix products, arithmetic and copies ran while one was open for 9% of the time, Pallas kernels for 26%

profile of v3, /device:TPU:1, one launch (start us, length us, event | category | flops | bytes accessed | tf_op | source)
XLA Modules:
  0.0 662.2 jit_solution(12916423627305400978)
XLA Ops:
  20.4 12.8 %collective-permute-done.1 = bf16[256,3072]{1,0:T(8,128)(2,1)} collective-permute-done((bf16[256,3072]{1,0:T(8,128)(2,1)S(1)}, bf16[256,3072]{1,0:T(8,128)(2,1)}, u32[]{:S(2)}, u32[]{:S(2)}) %collective-permute-start.1) | collective-permute-done | bytes 1572896 | tf_op jit(solution)/shard_map/ppermute | solution.py:57
  42.0 10.9 %collective-permute-done = bf16[256,2048]{1,0:T(8,128)(2,1)} collective-permute-done((bf16[256,2048]{1,0:T(8,128)(2,1)}, bf16[256,2048]{1,0:T(8,128)(2,1)}, u32[]{:S(2)}, u32[]{:S(2)}) %collective-permute-start) | collective-permute-done | bytes 1048608 | tf_op jit(solution)/shard_map/ppermute | solution.py:57
  83.2 11.2 %collective-permute-done.8 = bf16[256,2048]{1,0:T(8,128)(2,1)S(1)} collective-permute-done((bf16[256,2048]{1,0:T(8,128)(2,1)}, bf16[256,2048]{1,0:T(8,128)(2,1)S(1)}, u32[]{:S(2)}, u32[]{:S(2)}) %collective-permute-start.8) | collective-permute-done | bytes 1048608 | tf_op jit(solution)/shard_map/ppermute | solution.py:57
  96.6 8.9 %collective-permute-done.11 = bf16[256,2048]{1,0:T(8,128)(2,1)S(1)} collective-permute-done((bf16[256,2048]{1,0:T(8,128)(2,1)}, bf16[256,2048]{1,0:T(8,128)(2,1)S(1)}, u32[]{:S(2)}, u32[]{:S(2)}) %collective-permute-start.11) | collective-permute-done | bytes 1048608 | tf_op jit(solution)/shard_map/ppermute | solution.py:57
  111.3 8.7 %collective-permute-done.10.refs_1_ = bf16[128,2048]{1,0:T(8,128)(2,1)S(1)} collective-permute-done((bf16[128,2048]{1,0:T(8,128)(2,1)S(1)}, bf16[128,2048]{1,0:T(8,128)(2,1)S(1)}, u32[]{:S(2)}, u32[]{:S(2)}) %collective-permute-start.10) | collective-permute-done | bytes 524320 | tf_op jit(solution)/shard_map/ppermute | solution.py:57
  125.6 28.9 %all-gather.4.cloned.1.call-done.refs_6_.wg.wv.wq.wk = bf16[2048,3072]{1,0:T(8,128)(2,1)} async-done(((bf16[256,3072]{1,0:T(8,128)(2,1)}), bf16[2048,3072]{1,0:T(8,128)(2,1)}) %all-gather.4.cloned.1.call-update) | async-done | bytes 12582928 | tf_op jit(solution)/shard_map/all_gather | solution.py:81
  155.5 23.9 %shard_map.186 = (bf16[1024,2048]{1,0:T(8,128)(2,1)}, bf16[1024,2048]{1,0:T(8,128)(2,1)}, f32[1024,1024]{1,0:T(8,128)}) custom-call(bf16[128,2048]{1,0:T(8,128)(2,1)S(1)} %get-tuple-element.253.refs_0_, bf16[128,2048]{1,0:T(8,128)(2,1)S(1)} %copy-done.21, bf16[256,2048]{1,0:T(8,128)(2,1)} %collective-permute-done.4.refs_2_, ...), custom_call_target="tpu_custom_call" | custom-call | flops 257698032 | bytes 545259 | tf_op jit(solution)/shard_map/pallas_call | solution.py:199
  183.8 7.6 %shard_map.188.in_ref.refs_2_.refs_3_ = bf16[1024,1024]{1,0:T(8,128)(2,1)S(1)} custom-call(bf16[1024,2048]{1,0:T(8,128)(2,1)} %get-tuple-element.130.q_ref.k_ref.v_ref, bf16[1024,2048]{1,0:T(8,128)(2,1)} %get-tuple-element.130.q_ref.k_ref.v_ref, bf16[1024,2048]{1,0:T(8,128)(2,1)} %get-tuple-element.130.q_ref.k_ref.v_ref, ...), custom_call_target="tpu_custom_call" | custom-call | flops 32212254 | bytes 209715 | tf_op jit(solution)/shard_map/pallas_call | solution.py:250
  191.4 10.6 %all-gather.6.cloned.1.call-done.w_ref.wo = bf16[2048,1024]{1,0:T(8,128)(2,1)} async-done(((bf16[256,1024]{1,0:T(8,128)(2,1)}), bf16[2048,1024]{1,0:T(8,128)(2,1)}) %all-gather.6.cloned.1.call-update) | async-done | bytes 4194320 | tf_op jit(solution)/shard_map/all_gather | solution.py:81
  215.1 16.7 %collective-permute-done.14 = bf16[256,2048]{1,0:T(8,128)(2,1)S(1)} collective-permute-done((bf16[256,2048]{1,0:T(8,128)(2,1)S(1)}, bf16[256,2048]{1,0:T(8,128)(2,1)S(1)}, u32[]{:S(2)}, u32[]{:S(2)}) %collective-permute-start.14) | collective-permute-done | bytes 1048608 | tf_op jit(solution)/shard_map/ppermute | solution.py:57
  238.6 10.7 %collective-permute-done.15 = bf16[128,2048]{1,0:T(8,128)(2,1)S(1)} collective-permute-done((bf16[128,2048]{1,0:T(8,128)(2,1)S(1)}, bf16[128,2048]{1,0:T(8,128)(2,1)S(1)}, u32[]{:S(2)}, u32[]{:S(2)}) %collective-permute-start.15) | collective-permute-done | bytes 524320 | tf_op jit(solution)/shard_map/ppermute | solution.py:57
  252.3 10.1 %collective-permute-done.17.refs_1_ = bf16[128,2048]{1,0:T(8,128)(2,1)S(1)} collective-permute-done((bf16[128,2048]{1,0:T(8,128)(2,1)S(1)}, bf16[128,2048]{1,0:T(8,128)(2,1)S(1)}, u32[]{:S(2)}, u32[]{:S(2)}) %collective-permute-start.17) | collective-permute-done | bytes 524320 | tf_op jit(solution)/shard_map/ppermute | solution.py:57
  265.0 21.6 %collective-permute-done.19.refs_2_ = bf16[256,2048]{1,0:T(8,128)(2,1)S(1)} collective-permute-done((bf16[256,2048]{1,0:T(8,128)(2,1)S(1)}, bf16[256,2048]{1,0:T(8,128)(2,1)S(1)}, u32[]{:S(2)}, u32[]{:S(2)}) %collective-permute-start.19) | collective-permute-done | bytes 1048608 | tf_op jit(solution)/shard_map/ppermute | solution.py:57
  298.7 8.0 %shard_map.192 = (bf16[512,2048]{1,0:T(8,128)(2,1)S(1)}, bf16[512,1024]{1,0:T(8,128)(2,1)S(1)}, f32[512,1024]{1,0:T(8,128)}) custom-call(bf16[128,2048]{1,0:T(8,128)(2,1)S(1)} %copy-done.5, bf16[128,2048]{1,0:T(8,128)(2,1)S(1)} %copy-done.25, bf16[256,2048]{1,0:T(8,128)(2,1)} %collective-permute-done.21.refs_2_, ...), custom_call_target="tpu_custom_call" | custom-call | flops 42949672 | bytes 230686 | tf_op jit(solution)/shard_map/pallas_call | solution.py:299
  308.0 7.7 %shard_map.193 = bf16[2048,1024]{1,0:T(8,128)(2,1)} custom-call(bf16[1024,2048]{1,0:T(8,128)(2,1)} %shard_map.187.refs_0_.refs_1_.cot_ref, bf16[1024,2048]{1,0:T(8,128)(2,1)} %shard_map.187.refs_0_.refs_1_.cot_ref, bf16[512,1024]{1,0:T(8,128)(2,1)S(1)} %get-tuple-element.167.refs_2_.in_ref, bf16[512,1024]{1,0:T(8,128)(2,1)S(1)} %get-tuple-element.172.refs_3_.in_ref), custom_call_target="tpu_custom_call" | custom-call | flops 85899344 | bytes 209715 | tf_op jit(solution)/shard_map/pallas_call | solution.py:542
  316.8 10.0 %shard_map.194 = (bf16[512,1024]{1,0:T(8,128)(2,1)S(1)}, bf16[256,2048]{1,0:T(8,128)(2,1)S(1)}, f32[256,2048]{1,0:T(8,128)S(1)}) custom-call(bf16[1024,2048]{1,0:T(8,128)(2,1)} %shard_map.187.refs_0_.refs_1_.cot_ref, f32[512,1024]{1,0:T(8,128)} %get-tuple-element.150.slope_ref, bf16[2048,2048]{1,0:T(8,128)(2,1)} %all-gather.8.cloned.1.call-done.refs_3_.down_ref.up_ref.w_ref, ...), custom_call_target="tpu_custom_call" | custom-call | flops 85899344 | bytes 335544 | tf_op jit(solution)/shard_map/pallas_call | solution.py:380
  329.1 9.8 %shard_map.195 = (bf16[512,1024]{1,0:T(8,128)(2,1)S(1)}, bf16[256,2048]{1,0:T(8,128)(2,1)S(1)}, f32[256,2048]{1,0:T(8,128)S(1)}) custom-call(bf16[1024,2048]{1,0:T(8,128)(2,1)} %shard_map.187.refs_0_.refs_1_.cot_ref, f32[512,1024]{1,0:T(8,128)} %get-tuple-element.153.slope_ref, bf16[2048,2048]{1,0:T(8,128)(2,1)} %all-gather.8.cloned.1.call-done.refs_3_.down_ref.up_ref.w_ref, ...), custom_call_target="tpu_custom_call" | custom-call | flops 85899344 | bytes 335544 | tf_op jit(solution)/shard_map/pallas_call | solution.py:380
  341.2 7.4 %shard_map.196 = bf16[2048,1024]{1,0:T(8,128)(2,1)} custom-call(bf16[512,2048]{1,0:T(8,128)(2,1)S(1)} %copy-done.11, bf16[512,2048]{1,0:T(8,128)(2,1)} %copy-done.12, bf16[512,1024]{1,0:T(8,128)(2,1)S(1)} %get-tuple-element.161.refs_2_, bf16[512,1024]{1,0:T(8,128)(2,1)S(1)} %get-tuple-element.162.refs_3_), custom_call_target="tpu_custom_call" | custom-call | flops 85899344 | bytes 209715 | tf_op jit(solution)/shard_map/pallas_call | solution.py:542
  349.3 21.8 %collective-permute-done.23 = bf16[256,2048]{1,0:T(8,128)(2,1)S(1)} collective-permute-done((bf16[256,2048]{1,0:T(8,128)(2,1)}, bf16[256,2048]{1,0:T(8,128)(2,1)S(1)}, u32[]{:S(2)}, u32[]{:S(2)}) %collective-permute-start.23) | collective-permute-done | bytes 1048608 | tf_op jit(solution)/shard_map/ppermute | solution.py:57
  375.3 8.6 %collective-permute-done.25 = bf16[128,2048]{1,0:T(8,128)(2,1)S(1)} collective-permute-done((bf16[128,2048]{1,0:T(8,128)(2,1)S(1)}, bf16[128,2048]{1,0:T(8,128)(2,1)S(1)}, u32[]{:S(2)}, u32[]{:S(2)}) %collective-permute-start.25) | collective-permute-done | bytes 524320 | tf_op jit(solution)/shard_map/ppermute | solution.py:57
  408.7 9.9 %collective-permute-done.29.refs_5_ = bf16[256,2048]{1,0:T(8,128)(2,1)S(1)} collective-permute-done((bf16[256,2048]{1,0:T(8,128)(2,1)S(1)}, bf16[256,2048]{1,0:T(8,128)(2,1)S(1)}, u32[]{:S(2)}, u32[]{:S(2)}) %collective-permute-start.29) | collective-permute-done | bytes 1048608 | tf_op jit(solution)/shard_map/ppermute | solution.py:57
  423.9 7.8 %shard_map.200 = bf16[2048,1024]{1,0:T(8,128)(2,1)} custom-call(bf16[1024,2048]{1,0:T(8,128)(2,1)} %shard_map.199.refs_0_.refs_1_.mix_ref, bf16[1024,2048]{1,0:T(8,128)(2,1)} %shard_map.199.refs_0_.refs_1_.mix_ref, bf16[1024,1024]{1,0:T(8,128)(2,1)S(1)} %shard_map.188.in_ref.refs_2_.refs_3_, bf16[1024,1024]{1,0:T(8,128)(2,1)S(1)} %shard_map.188.in_ref.refs_2_.refs_3_), custom_call_target="tpu_custom_call" | custom-call | flops 85899344 | bytes 209715 | tf_op jit(solution)/shard_map/pallas_call | solution.py:542
  432.7 24.7 %shard_map.201 = (bf16[512,1024]{1,0:T(8,128)(2,1)S(1)}, bf16[512,512]{1,0:T(8,128)(2,1)S(1)}, bf16[512,512]{1,0:T(8,128)(2,1)S(1)}, bf16[512,1024]{1,0:T(8,128)...) custom-call(bf16[1024,2048]{1,0:T(8,128)(2,1)} %shard_map.199.refs_0_.refs_1_.mix_ref, ...), custom_call_target="tpu_custom_call" | custom-call | flops 225485776 | bytes 608174 | tf_op jit(solution)/shard_map/pallas_call | solution.py:467
  457.4 24.8 %shard_map.202 = (bf16[512,1024]{1,0:T(8,128)(2,1)S(1)}, bf16[512,512]{1,0:T(8,128)(2,1)S(1)}, bf16[512,512]{1,0:T(8,128)(2,1)S(1)}, bf16[512,1024]{1,0:T(8,128)...) custom-call(bf16[1024,2048]{1,0:T(8,128)(2,1)} %shard_map.199.refs_0_.refs_1_.mix_ref, ...), custom_call_target="tpu_custom_call" | custom-call | flops 225485776 | bytes 608174 | tf_op jit(solution)/shard_map/pallas_call | solution.py:467
  483.0 12.1 %shard_map.203 = bf16[2048,2048]{1,0:T(8,128)(2,1)} custom-call(bf16[1024,2048]{1,0:T(8,128)(2,1)} %get-tuple-element.188.refs_0_.refs_1_, bf16[1024,2048]{1,0:T(8,128)(2,1)} %get-tuple-element.188.refs_0_.refs_1_, bf16[512,1024]{1,0:T(8,128)(2,1)S(1)} %get-tuple-element.184.refs_2_, bf16[512,1024]{1,0:T(8,128)(2,1)S(1)} %get-tuple-element.185.refs_3_, ...), custom_call_target="tpu_custom_call" | custom-call | flops 171798688 | bytes 335544 | tf_op jit(solution)/shard_map/pallas_call | solution.py:542
  499.2 7.9 %shard_map.204 = bf16[2048,1024]{1,0:T(8,128)(2,1)} custom-call(bf16[1024,2048]{1,0:T(8,128)(2,1)} %get-tuple-element.188.refs_0_.refs_1_, bf16[1024,2048]{1,0:T(8,128)(2,1)} %get-tuple-element.188.refs_0_.refs_1_, bf16[512,512]{1,0:T(8,128)(2,1)S(1)} %get-tuple-element.189.refs_2_, bf16[512,512]{1,0:T(8,128)(2,1)S(1)} %get-tuple-element.190.refs_3_, ...), custom_call_target="tpu_custom_call" | custom-call | flops 85899344 | bytes 209715 | tf_op jit(solution)/shard_map/pallas_call | solution.py:542
  507.2 8.4 %collective-permute-done.30 = bf16[256,2048]{1,0:T(8,128)(2,1)} collective-permute-done((bf16[256,2048]{1,0:T(8,128)(2,1)}, bf16[256,2048]{1,0:T(8,128)(2,1)}, u32[]{:S(2)}, u32[]{:S(2)}) %collective-permute-start.30) | collective-permute-done | bytes 1048608 | tf_op jit(solution)/shard_map/ppermute | solution.py:57
  522.5 15.5 %collective-permute-done.33 = bf16[256,2048]{1,0:T(8,128)(2,1)} collective-permute-done((bf16[256,2048]{1,0:T(8,128)(2,1)}, bf16[256,2048]{1,0:T(8,128)(2,1)}, u32[]{:S(2)}, u32[]{:S(2)}) %collective-permute-start.33) | collective-permute-done | bytes 1048608 | tf_op jit(solution)/shard_map/ppermute | solution.py:57
  551.9 9.7 %collective-permute-done.37 = bf16[128,2048]{1,0:T(8,128)(2,1)S(1)} collective-permute-done((bf16[128,2048]{1,0:T(8,128)(2,1)S(1)}, bf16[128,2048]{1,0:T(8,128)(2,1)S(1)}, u32[]{:S(2)}, u32[]{:S(2)}) %collective-permute-start.37) | collective-permute-done | bytes 524320 | tf_op jit(solution)/shard_map/ppermute | solution.py:57
  565.1 8.5 %collective-permute-start.39 = (bf16[256,2048]{1,0:T(8,128)(2,1)}, bf16[256,2048]{1,0:T(8,128)(2,1)}, u32[]{:S(2)}, u32[]{:S(2)}) collective-permute-start(bf16[256,2048]{1,0:T(8,128)(2,1)} %pad_maximum_fusion), channel_id=1, source_target_pairs={{1,8},{3,10},{5,12},{7,14},{8,1},{10,3},{12,5},{14,7},{17,24},{19,... | collective-permute-start | bytes 3145736 | tf_op jit(solution)/shard_map/ppermute | solution.py:57
  577.5 19.6 %collective-permute-done.41 = f32[2,2048]{1,0:T(2,128)S(1)} collective-permute-done((f32[2,2048]{1,0:T(2,128)S(1)}, f32[2,2048]{1,0:T(2,128)S(1)}, u32[]{:S(2)}, u32[]{:S(2)}) %collective-permute-start.41) | collective-permute-done | bytes 16416 | tf_op jit(solution)/shard_map/ppermute | solution.py:57
  628.4 9.8 %reduce-scatter.6.cloned.1.call-done = bf16[256,1024]{1,0:T(8,128)(2,1)} async-done(((bf16[2048,1024]{1,0:T(8,128)(2,1)}), bf16[256,1024]{1,0:T(8,128)(2,1)}) %reduce-scatter.6.cloned.1.call-update) | async-done | bytes 524304 | tf_op jit(solution)/shard_map/reduce_scatter | solution.py:84
  (373 shorter events, 231.8 us)
Async XLA Ops:
  7.2 147.3 %all-gather.4.cloned.1.call-start = ((), (), s32[]{:S(2)}) async-start(), calls=%async_computation.5 | async-start | bytes 14155776 | tf_op jit(solution)/shard_map/all_gather | solution.py:81
  10.5 22.7 %collective-permute-start.1 = (bf16[256,3072]{1,0:T(8,128)(2,1)S(1)}, bf16[256,3072]{1,0:T(8,128)(2,1)}, u32[]{:S(2)}, u32[]{:S(2)}) collective-permute-start(bf16[256,3072]{1,0:T(8,128)(2,1)S(1)} %constant_dynamic-update-slice_fusion), channel_id=1, source_target_pairs={{1,8},{3,10},{5,12},{7,14},{8,1},{10,3},{12,5},{14,7},{17,24},{19,... | collective-permute-start | bytes 4718600 | tf_op jit(solution)/shard_map/ppermute | solution.py:57
  36.0 166.0 %all-gather.6.cloned.1.call-start = ((), (), s32[]{:S(2)}) async-start(), calls=%async_computation.6 | async-start | bytes 4718592 | tf_op jit(solution)/shard_map/all_gather | solution.py:81
  77.4 210.2 %all-gather.8.cloned.1.call-start = ((), (), s32[]{:S(2)}) async-start(), calls=%async_computation.7 | async-start | bytes 9437184 | tf_op jit(solution)/shard_map/all_gather | solution.py:81
  79.7 25.9 %collective-permute-start.11 = (bf16[256,2048]{1,0:T(8,128)(2,1)}, bf16[256,2048]{1,0:T(8,128)(2,1)S(1)}, u32[]{:S(2)}, u32[]{:S(2)}) collective-permute-start(bf16[256,2048]{1,0:T(8,128)(2,1)} %pad_maximum_fusion.1), channel_id=1, source_target_pairs={{1,8},{3,10},{5,12},{7,14},{8,1},{10,3},{12,5},{14,7},{17,24},{19,... | collective-permute-start | bytes 3145736 | tf_op jit(solution)/shard_map/ppermute | solution.py:57
  106.9 501.4 %reduce-scatter.14.cloned.1.call-start = ((), (), s32[]{:S(2)}) async-start(), calls=%async_computation.12 | async-start | bytes 4718592 | tf_op jit(solution)/shard_map/reduce_scatter | solution.py:84
  109.6 44.9 %collective-permute-start.6 = (bf16[256,2048]{1,0:T(8,128)(2,1)}, bf16[256,2048]{1,0:T(8,128)(2,1)}, u32[]{:S(2)}, u32[]{:S(2)}) collective-permute-start(bf16[256,2048]{1,0:T(8,128)(2,1)} %pad_maximum_fusion.3), channel_id=1, source_target_pairs={{0,16},{1,17},{2,18},{3,19},{4,20},{5,21},{6,22},{7,23},{8,24},{9,... | collective-permute-start | bytes 3145736 | tf_op jit(solution)/shard_map/ppermute | solution.py:57
  109.8 44.7 %collective-permute-start.4 = (bf16[256,2048]{1,0:T(8,128)(2,1)}, bf16[256,2048]{1,0:T(8,128)(2,1)}, u32[]{:S(2)}, u32[]{:S(2)}) collective-permute-start(bf16[256,2048]{1,0:T(8,128)(2,1)} %pad_maximum_fusion.2), channel_id=1, source_target_pairs={{0,1},{1,0},{2,3},{3,2},{4,5},{5,4},{6,7},{7,6},{8,9},{9,8},{10,11... | collective-permute-start | bytes 3145736 | tf_op jit(solution)/shard_map/ppermute | solution.py:57
  124.9 54.5 %collective-permute-start.13 = (bf16[256,2048]{1,0:T(8,128)(2,1)}, bf16[256,2048]{1,0:T(8,128)(2,1)}, u32[]{:S(2)}, u32[]{:S(2)}) collective-permute-start(bf16[256,2048]{1,0:T(8,128)(2,1)} %pad_maximum_fusion.5), channel_id=1, source_target_pairs={{0,16},{1,17},{2,18},{3,19},{4,20},{5,21},{6,22},{7,23},{8,24},{9,... | collective-permute-start | bytes 3145736 | tf_op jit(solution)/shard_map/ppermute | solution.py:57
  125.2 54.2 %collective-permute-start.12 = (bf16[256,2048]{1,0:T(8,128)(2,1)}, bf16[256,2048]{1,0:T(8,128)(2,1)}, u32[]{:S(2)}, u32[]{:S(2)}) collective-permute-start(bf16[256,2048]{1,0:T(8,128)(2,1)} %pad_maximum_fusion.4), channel_id=1, source_target_pairs={{0,1},{1,0},{2,3},{3,2},{4,5},{5,4},{6,7},{7,6},{8,9},{9,8},{10,11... | collective-permute-start | bytes 3145736 | tf_op jit(solution)/shard_map/ppermute | solution.py:57
  207.1 24.7 %collective-permute-start.14 = (bf16[256,2048]{1,0:T(8,128)(2,1)S(1)}, bf16[256,2048]{1,0:T(8,128)(2,1)S(1)}, u32[]{:S(2)}, u32[]{:S(2)}) collective-permute-start(bf16[256,2048]{1,0:T(8,128)(2,1)S(1)} %get-tuple-element.134), channel_id=1, source_target_pairs={{0,1},{1,0},{2,3},{3,2},{4,5},{5,4},{6,7},{7,6},{8,9},{9,8},{10,11... | collective-permute-start | bytes 3145736 | tf_op jit(solution)/shard_map/ppermute | solution.py:57
  213.7 24.3 %collective-permute-start.16 = (bf16[256,2048]{1,0:T(8,128)(2,1)S(1)}, bf16[256,2048]{1,0:T(8,128)(2,1)S(1)}, u32[]{:S(2)}, u32[]{:S(2)}) collective-permute-start(bf16[256,2048]{1,0:T(8,128)(2,1)S(1)} %get-tuple-element.136), channel_id=1, source_target_pairs={{0,16},{1,17},{2,18},{3,19},{4,20},{5,21},{6,22},{7,23},{8,24},{9,... | collective-permute-start | bytes 3145736 | tf_op jit(solution)/shard_map/ppermute | solution.py:57
  262.4 24.2 %collective-permute-start.19 = (bf16[256,2048]{1,0:T(8,128)(2,1)S(1)}, bf16[256,2048]{1,0:T(8,128)(2,1)S(1)}, u32[]{:S(2)}, u32[]{:S(2)}) collective-permute-start(bf16[256,2048]{1,0:T(8,128)(2,1)S(1)} %pad_maximum_fusion.6), channel_id=1, source_target_pairs={{0,1},{1,0},{2,3},{3,2},{4,5},{5,4},{6,7},{7,6},{8,9},{9,8},{10,11... | collective-permute-start | bytes 3145736 | tf_op jit(solution)/shard_map/ppermute | solution.py:57
  264.9 33.8 %collective-permute-start.21 = (bf16[256,2048]{1,0:T(8,128)(2,1)}, bf16[256,2048]{1,0:T(8,128)(2,1)}, u32[]{:S(2)}, u32[]{:S(2)}) collective-permute-start(bf16[256,2048]{1,0:T(8,128)(2,1)} %pad_maximum_fusion.7), channel_id=1, source_target_pairs={{0,16},{1,17},{2,18},{3,19},{4,20},{5,21},{6,22},{7,23},{8,24},{9,... | collective-permute-start | bytes 3145736 | tf_op jit(solution)/shard_map/ppermute | solution.py:57
  316.7 298.9 %reduce-scatter.12.cloned.1.call-start = ((), (), s32[]{:S(2)}) async-start(), calls=%async_computation.11 | async-start | bytes 4718592 | tf_op jit(solution)/shard_map/reduce_scatter | solution.py:84
  348.7 271.6 %reduce-scatter.10.cloned.1.call-start = ((), (), s32[]{:S(2)}) async-start(), calls=%async_computation.10 | async-start | bytes 4718592 | tf_op jit(solution)/shard_map/reduce_scatter | solution.py:84
  348.7 22.3 %collective-permute-start.23 = (bf16[256,2048]{1,0:T(8,128)(2,1)}, bf16[256,2048]{1,0:T(8,128)(2,1)S(1)}, u32[]{:S(2)}, u32[]{:S(2)}) collective-permute-start(bf16[256,2048]{1,0:T(8,128)(2,1)} %copy-done.31), channel_id=1, source_target_pairs={{0,1},{1,0},{2,3},{3,2},{4,5},{5,4},{6,7},{7,6},{8,9},{9,8},{10,11... | collective-permute-start | bytes 3145736 | tf_op jit(solution)/shard_map/ppermute | solution.py:57
  349.3 24.3 %collective-permute-start.22 = (bf16[256,2048]{1,0:T(8,128)(2,1)}, bf16[256,2048]{1,0:T(8,128)(2,1)S(1)}, u32[]{:S(2)}, u32[]{:S(2)}) collective-permute-start(bf16[256,2048]{1,0:T(8,128)(2,1)} %copy-done.30), channel_id=1, source_target_pairs={{0,16},{1,17},{2,18},{3,19},{4,20},{5,21},{6,22},{7,23},{8,24},{9,... | collective-permute-start | bytes 3145736 | tf_op jit(solution)/shard_map/ppermute | solution.py:57
  431.7 194.8 %reduce-scatter.8.cloned.1.call-start = ((), (), s32[]{:S(2)}) async-start(), calls=%async_computation.9 | async-start | bytes 9437184 | tf_op jit(solution)/shard_map/reduce_scatter | solution.py:84
  495.2 143.1 %reduce-scatter.6.cloned.1.call-start = ((), (), s32[]{:S(2)}) async-start(), calls=%async_computation.8 | async-start | bytes 4718592 | tf_op jit(solution)/shard_map/reduce_scatter | solution.py:84
  495.2 20.3 %collective-permute-start.30 = (bf16[256,2048]{1,0:T(8,128)(2,1)}, bf16[256,2048]{1,0:T(8,128)(2,1)}, u32[]{:S(2)}, u32[]{:S(2)}) collective-permute-start(bf16[256,2048]{1,0:T(8,128)(2,1)} %get-tuple-element.179), channel_id=1, source_target_pairs={{0,1},{1,0},{2,3},{3,2},{4,5},{5,4},{6,7},{7,6},{8,9},{9,8},{10,11... | collective-permute-start | bytes 3145736 | tf_op jit(solution)/shard_map/ppermute | solution.py:57
  497.6 21.5 %collective-permute-start.34 = (bf16[256,2048]{1,0:T(8,128)(2,1)}, bf16[256,2048]{1,0:T(8,128)(2,1)}, u32[]{:S(2)}, u32[]{:S(2)}) collective-permute-start(bf16[256,2048]{1,0:T(8,128)(2,1)} %get-tuple-element.197), channel_id=1, source_target_pairs={{0,16},{1,17},{2,18},{3,19},{4,20},{5,21},{6,22},{7,23},{8,24},{9,... | collective-permute-start | bytes 3145736 | tf_op jit(solution)/shard_map/ppermute | solution.py:57
  499.0 42.6 %collective-permute-start.32 = (bf16[256,2048]{1,0:T(8,128)(2,1)}, bf16[256,2048]{1,0:T(8,128)(2,1)}, u32[]{:S(2)}, u32[]{:S(2)}) collective-permute-start(bf16[256,2048]{1,0:T(8,128)(2,1)} %get-tuple-element.182), channel_id=1, source_target_pairs={{0,16},{1,17},{2,18},{3,19},{4,20},{5,21},{6,22},{7,23},{8,24},{9,... | collective-permute-start | bytes 3145736 | tf_op jit(solution)/shard_map/ppermute | solution.py:57
  499.1 38.9 %collective-permute-start.33 = (bf16[256,2048]{1,0:T(8,128)(2,1)}, bf16[256,2048]{1,0:T(8,128)(2,1)}, u32[]{:S(2)}, u32[]{:S(2)}) collective-permute-start(bf16[256,2048]{1,0:T(8,128)(2,1)} %get-tuple-element.178), channel_id=1, source_target_pairs={{0,1},{1,0},{2,3},{3,2},{4,5},{5,4},{6,7},{7,6},{8,9},{9,8},{10,11... | collective-permute-start | bytes 3145736 | tf_op jit(solution)/shard_map/ppermute | solution.py:57
  517.3 33.1 %collective-permute-start.31 = (bf16[128,2048]{1,0:T(8,128)(2,1)S(1)}, bf16[128,2048]{1,0:T(8,128)(2,1)S(1)}, u32[]{:S(2)}, u32[]{:S(2)}) collective-permute-start(bf16[128,2048]{1,0:T(8,128)(2,1)S(1)} %slice.255), channel_id=1, source_target_pairs={{0,16},{1,17},{2,18},{3,19},{4,20},{5,21},{6,22},{7,23},{8,24},{9,... | collective-permute-start | bytes 1572872 | tf_op jit(solution)/shard_map/ppermute | solution.py:57
  520.9 28.3 %collective-permute-start.35 = (bf16[128,2048]{1,0:T(8,128)(2,1)S(1)}, bf16[128,2048]{1,0:T(8,128)(2,1)S(1)}, u32[]{:S(2)}, u32[]{:S(2)}) collective-permute-start(bf16[128,2048]{1,0:T(8,128)(2,1)S(1)} %slice.254), channel_id=1, source_target_pairs={{0,1},{1,0},{2,3},{3,2},{4,5},{5,4},{6,7},{7,6},{8,9},{9,8},{10,11... | collective-permute-start | bytes 1572872 | tf_op jit(solution)/shard_map/ppermute | solution.py:57
  539.8 21.8 %collective-permute-start.37 = (bf16[128,2048]{1,0:T(8,128)(2,1)S(1)}, bf16[128,2048]{1,0:T(8,128)(2,1)S(1)}, u32[]{:S(2)}, u32[]{:S(2)}) collective-permute-start(bf16[128,2048]{1,0:T(8,128)(2,1)S(1)} %slice.253), channel_id=1, source_target_pairs={{0,16},{1,17},{2,18},{3,19},{4,20},{5,21},{6,22},{7,23},{8,24},{9,... | collective-permute-start | bytes 1572872 | tf_op jit(solution)/shard_map/ppermute | solution.py:57
  565.1 47.6 %collective-permute-start.39 = (bf16[256,2048]{1,0:T(8,128)(2,1)}, bf16[256,2048]{1,0:T(8,128)(2,1)}, u32[]{:S(2)}, u32[]{:S(2)}) collective-permute-start(bf16[256,2048]{1,0:T(8,128)(2,1)} %pad_maximum_fusion), channel_id=1, source_target_pairs={{1,8},{3,10},{5,12},{7,14},{8,1},{10,3},{12,5},{14,7},{17,24},{19,... | collective-permute-start | bytes 3145736 | tf_op jit(solution)/shard_map/ppermute | solution.py:57
  575.2 42.5 %collective-permute-start.36 = (bf16[256,2048]{1,0:T(8,128)(2,1)}, bf16[256,2048]{1,0:T(8,128)(2,1)}, u32[]{:S(2)}, u32[]{:S(2)}) collective-permute-start(bf16[256,2048]{1,0:T(8,128)(2,1)} %pad_maximum_fusion.10), channel_id=1, source_target_pairs={{1,8},{3,10},{5,12},{7,14},{8,1},{10,3},{12,5},{14,7},{17,24},{19,... | collective-permute-start | bytes 3145736 | tf_op jit(solution)/shard_map/ppermute | solution.py:57
  615.6 28.5 %collective-permute-start.48 = (bf16[256,1024]{1,0:T(8,128)(2,1)}, bf16[256,1024]{1,0:T(8,128)(2,1)}, u32[]{:S(2)}, u32[]{:S(2)}) collective-permute-start(bf16[256,1024]{1,0:T(8,128)(2,1)} %reduce-scatter.12.cloned.1.call-done), channel_id=1, source_target_pairs={{1,8},{3,10},{5,12},{7,14},{8,1},{10,3},{12,5},{14,7},{17,24},{19,... | collective-permute-start | bytes 1572872 | tf_op jit(solution)/shard_map/ppermute | solution.py:57
  620.3 25.9 %collective-permute-start.47 = (bf16[256,1024]{1,0:T(8,128)(2,1)}, bf16[256,1024]{1,0:T(8,128)(2,1)}, u32[]{:S(2)}, u32[]{:S(2)}) collective-permute-start(bf16[256,1024]{1,0:T(8,128)(2,1)} %reduce-scatter.10.cloned.1.call-done), channel_id=1, source_target_pairs={{1,8},{3,10},{5,12},{7,14},{8,1},{10,3},{12,5},{14,7},{17,24},{19,... | collective-permute-start | bytes 1572872 | tf_op jit(solution)/shard_map/ppermute | solution.py:57
  626.5 26.9 %collective-permute-start.46 = (bf16[256,2048]{1,0:T(8,128)(2,1)}, bf16[256,2048]{1,0:T(8,128)(2,1)S(1)}, u32[]{:S(2)}, u32[]{:S(2)}) collective-permute-start(bf16[256,2048]{1,0:T(8,128)(2,1)} %reduce-scatter.8.cloned.1.call-done), channel_id=1, source_target_pairs={{1,8},{3,10},{5,12},{7,14},{8,1},{10,3},{12,5},{14,7},{17,24},{19,... | collective-permute-start | bytes 3145736 | tf_op jit(solution)/shard_map/ppermute | solution.py:57
  (96 other events, 940.9 us)
Sparse Core Ops, SparseCore 0:
  36.1 118.3 all-gather.3
  156.7 45.2 all-gather.5
  204.2 80.8 all-gather.7
  316.8 46.2 reduce-scatter.13
  365.3 48.1 reduce-scatter.11
  431.8 51.5 reduce-scatter.9
  495.3 91.5 reduce-scatter.7
  589.2 49.0 reduce-scatter.5

commit v4 on v3

v4 whole, which is shorter than its diff:
```python
import jax
import jax.numpy as jnp
from jax import lax
from jax.experimental import pallas as pl
from jax.experimental.pallas import tpu as pltpu
from jax.sharding import PartitionSpec as P

KEY_HEAD = 256
VAL_HEAD = 512
ROT = KEY_HEAD // 2
eps_norm = 1e-05
eps_group = 1.0
BF = jnp.bfloat16
F32 = jnp.float32
AXES = ("seq", "fsdp")
ANY = pl.BlockSpec(memory_space=pl.ANY)


def nn(left, right):
    return jnp.dot(left, right, preferred_element_type=F32)


def nt(left, right):
    return lax.dot_general(left, right, (((1,), (1,)), ((), ())), preferred_element_type=F32)


def tn(left, right):
    return lax.dot_general(left, right, (((0,), (0,)), ((), ())), preferred_element_type=F32)


def after(value, *first):
    return lax.optimization_barrier((value, *first))[0]


class Grid:
    def __init__(self, n_seq, n_fsdp):
        assert n_seq == 4 and n_fsdp % 2 == 0
        self.n_fsdp, self.nz = n_fsdp, n_fsdp // 2
        self.lines = [[z * 2 + x for z in range(self.nz)] for x in range(2)]
        self.groups = [
            [(y * 2 + c) * n_fsdp + z * 2 + x for z in range(self.nz) for c in range(2)]
            for y in range(2)
            for x in range(2)
        ]

    def send(self, value, move):
        found = []
        for y in range(2):
            for c in range(2):
                for z in range(self.nz):
                    for x in range(2):
                        y2, c2, z2, x2 = move(y, c, z, x)
                        src = (y * 2 + c) * self.n_fsdp + z * 2 + x
                        dst = (y2 * 2 + c2) * self.n_fsdp + z2 * 2 + x2
                        if src != dst:
                            found.append((src, dst))
        return lax.ppermute(value, AXES, found)

    def flip_z(self, value, bit):
        return self.send(value, lambda y, c, z, x: (y, c, z ^ bit, x))

    def flip_c(self, value):
        return self.send(value, lambda y, c, z, x: (y, 1 - c, z, x))

    def flip_y(self, value):
        return self.send(value, lambda y, c, z, x: (1 - y, c, z, x))

    def flip_x(self, value):
        return self.send(value, lambda y, c, z, x: (y, c, z, 1 - x))

    def first(self, b, value):
        return self.flip_y(value) if b == 0 else self.flip_x(value)

    def second(self, b, value):
        return self.flip_x(value) if b == 0 else self.flip_y(value)

    def swap(self, value):
        return self.send(value.astype(BF), lambda y, c, z, x: (y, x, z, c))

    def gather_weight(self, shard):
        return lax.all_gather(shard, AXES, axis=0, tiled=True, axis_index_groups=self.groups)

    def scatter_grad(self, value):
        return lax.psum_scatter(
            value, AXES, scatter_dimension=0, tiled=True, axis_index_groups=self.groups
        )

    def gather_line(self, shard):
        return lax.all_gather(shard, "fsdp", axis=0, tiled=True, axis_index_groups=self.lines)

    def scatter_line(self, value):
        return lax.psum_scatter(
            value, "fsdp", scatter_dimension=0, tiled=True, axis_index_groups=self.lines
        )

    def total(self, value):
        for flip in (self.flip_y, self.flip_x, self.flip_c):
            value = value + flip(value)
        if self.nz & (self.nz - 1):
            return lax.psum(value, "fsdp", axis_index_groups=self.lines)
        bit = 1
        while bit < self.nz:
            value = value + self.flip_z(value, bit)
            bit *= 2
        return value


def call(body, grid, ins, outs, shapes, scratch=(), flops=0, moved=0):
    return pl.pallas_call(
        body,
        out_shape=shapes,
        grid=grid,
        in_specs=ins,
        out_specs=outs,
        scratch_shapes=list(scratch),
        cost_estimate=pl.CostEstimate(
            flops=flops, bytes_accessed=moved, transcendentals=0
        ),
        compiler_params=pltpu.CompilerParams(vmem_limit_bytes=60 << 20),
    )


def shape(rows, cols, dtype=BF):
    return jax.ShapeDtypeStruct((rows, cols), dtype)


def spec(rows, cols, index):
    return pl.BlockSpec((rows, cols), index)


def copies_into(pieces, target, sems):
    copies, row = [], 0
    for i, piece in enumerate(pieces):
        rows = piece.shape[0]
        copies.append(pltpu.make_async_copy(piece, target.at[pl.ds(row, rows)], sems.at[i]))
        row += rows
    return copies


def fetch(pieces, target, sems):
    copies = copies_into(pieces, target, sems)
    for copy in copies:
        copy.start()
    for copy in copies:
        copy.wait()


def fetch_and_keep(j, steps, pieces, target, out, sems):
    keep = pltpu.make_async_copy(target, out, sems.at[len(pieces)])

    @pl.when(j == 0)
    def _():
        fetch(pieces, target, sems)
        keep.start()

    return keep


def assemble(pieces):
    n = len(pieces)

    def body(*refs):
        fetch(refs[:n], refs[n], refs[n + 1])

    rows = sum(p.shape[0] for p in pieces)
    cols = pieces[0].shape[1]
    return pl.pallas_call(
        body,
        out_shape=shape(rows, cols),
        in_specs=[ANY] * n,
        scratch_shapes=[pltpu.SemaphoreType.DMA((n,))],
        cost_estimate=pl.CostEstimate(
            flops=0, bytes_accessed=4 * rows * cols, transcendentals=0
        ),
    )(*pieces)


def rotated(first, second, cos_part, sin_part):
    return (first * cos_part - second * sin_part, second * cos_part + first * sin_part)


def project_turned(pieces, weight, cos_table, sin_table):
    n = len(pieces)
    rows = sum(p.shape[0] for p in pieces)
    width = pieces[0].shape[1]
    cols = weight.shape[1]
    tile, chunk = 512, 512
    steps = cols // tile

    def body(*refs):
        w_ref, cos_ref, sin_ref, out_ref, o_ref, h_ref, sems = refs[n:]
        j = pl.program_id(0)
        keep = fetch_and_keep(j, steps, refs[:n], h_ref, out_ref, sems)

        def step(i, _):
            at = pl.ds(pl.multiple_of(i * chunk, chunk), chunk)
            acc = nn(h_ref[at, :], w_ref[...])
            for s in range(0, tile, KEY_HEAD):
                u, v = rotated(
                    acc[:, s : s + ROT],
                    acc[:, s + ROT : s + KEY_HEAD],
                    cos_ref[at, :],
                    sin_ref[at, :],
                )
                o_ref[at, s : s + ROT] = u.astype(BF)
                o_ref[at, s + ROT : s + KEY_HEAD] = v.astype(BF)
            return 0

        lax.fori_loop(0, rows // chunk, step, 0, unroll=True)

        @pl.when(j == steps - 1)
        def _():
            keep.wait()

    return call(
        body,
        (steps,),
        [ANY] * n
        + [spec(width, tile, lambda j: (0, j))]
        + [spec(rows, ROT, lambda j: (0, 0))] * 2,
        [ANY, spec(rows, tile, lambda j: (0, j))],
        [shape(rows, width), shape(rows, cols)],
        [pltpu.VMEM((rows, width), BF), pltpu.SemaphoreType.DMA((n + 1,))],
        2 * rows * width * cols,
        2 * (2 * rows * width + width * cols + rows * cols),
    )(*pieces, weight, cos_table, sin_table)


def project_plain(h1, weight, gate_cols):
    rows, width = h1.shape
    cols = weight.shape[1]
    tile, chunk = 512, 512
    first = (cols - gate_cols) // tile

    def body(h_ref, w_ref, v_ref, gate_ref):
        j = pl.program_id(0)

        def step(i, _):
            at = pl.ds(pl.multiple_of(i * chunk, chunk), chunk)
            acc = nn(h_ref[at, :], w_ref[...])

            @pl.when(j < first)
            def _():
                v_ref[at, :] = acc.astype(BF)

            @pl.when(j >= first)
            def _():
                gate_ref[at, :] = acc

            return 0

        lax.fori_loop(0, rows // chunk, step, 0, unroll=True)

    return call(
        body,
        (cols // tile,),
        [spec(rows, width, lambda j: (0, 0)), spec(width, tile, lambda j: (0, j))],
        [
            spec(rows, tile, lambda j: (0, jnp.minimum(j, first - 1))),
            spec(rows, tile, lambda j: (0, jnp.maximum(j - first, 0))),
        ],
        [shape(rows, cols - gate_cols), shape(rows, gate_cols, F32)],
        (),
        2 * rows * width * cols,
        2 * (rows * width + width * cols + 2 * rows * cols),
    )(h1, weight)


def decay_chunk(col_ref, row_ref, at, log_gamma):
    pos_n, seg_n = col_ref[at, 0:1], col_ref[at, 1:2]
    pos_m, seg_m = row_ref[0:1, :], row_ref[1:2, :]
    distance = pos_n - pos_m
    allowed = (distance >= 0.0) & (seg_n == seg_m)
    value = jnp.exp(jnp.maximum(distance, 0.0) * log_gamma) * (KEY_HEAD**-0.5)
    return jnp.where(allowed, value, 0.0)


def sigmoid(value):
    return 1.0 / (1.0 + jnp.exp(-value))


def retain(qk, values, gate, col_info, row_info, log_gamma, heads, micro):
    rows = qk.shape[0] // micro
    dv = heads * VAL_HEAD
    chunk = 512

    def body(q_ref, k_ref, v_ref, gate_ref, col_ref, row_ref, lg_ref, gated_ref):
        log_g = lg_ref[pl.program_id(1)]

        def step(i, _):
            at = pl.ds(pl.multiple_of(i * chunk, chunk), chunk)
            decay = decay_chunk(col_ref, row_ref, at, log_g)
            weights = (nt(q_ref[at, :], k_ref[...]) * decay).astype(BF)
            kept = nn(weights, v_ref[...])
            scale = lax.rsqrt(jnp.mean(kept * kept, axis=-1, keepdims=True) + eps_group)
            gate = gate_ref[at, :]
            gated_ref[at, :] = (gate * sigmoid(gate) * (kept * scale)).astype(BF)
            return 0

        lax.fori_loop(0, rows // chunk, step, 0, unroll=True)

    return call(
        body,
        (micro, heads),
        [
            spec(rows, KEY_HEAD, lambda b, h: (b, h)),
            spec(rows, KEY_HEAD, lambda b, h: (b, heads + h)),
            spec(rows, VAL_HEAD, lambda b, h: (b, h)),
            spec(rows, VAL_HEAD, lambda b, h: (b, h)),
            spec(rows, 128, lambda b, h: (b, 0)),
            spec(8, rows, lambda b, h: (b, 0)),
            pl.BlockSpec(memory_space=pltpu.SMEM),
        ],
        spec(rows, VAL_HEAD, lambda b, h: (b, h)),
        shape(micro * rows, dv),
        (),
        2 * micro * rows * rows * heads * (KEY_HEAD + VAL_HEAD),
        10 * micro * rows * dv,
    )(qk, qk, values, gate, col_info, row_info, log_gamma)


ROOT_2_PI = 0.7978845608028654


def feed_up(pieces, weight, hidden):
    n = len(pieces)
    rows = sum(p.shape[0] for p in pieces)
    width = pieces[0].shape[1]
    tile, chunk = 512, 512
    steps = hidden // tile

    def body(*refs):
        w_ref, out_ref, act_ref, slope_ref, h_ref, sems = refs[n:]
        j = pl.program_id(0)
        keep = fetch_and_keep(j, steps, refs[:n], h_ref, out_ref, sems)

        def step(i, _):
            at = pl.ds(pl.multiple_of(i * chunk, chunk), chunk)
            up = nn(h_ref[at, :], w_ref[...])
            square = up * up
            bent = jnp.tanh(ROOT_2_PI * (up + 0.044715 * square * up))
            act_ref[at, :] = (0.5 * up * (1.0 + bent)).astype(BF)
            inner = ROOT_2_PI * (1.0 + 3.0 * 0.044715 * square)
            slope = 0.5 * (1.0 + bent) + 0.5 * up * (1.0 - bent * bent) * inner
            slope_ref[at, :] = slope
            return 0

        lax.fori_loop(0, rows // chunk, step, 0, unroll=True)

        @pl.when(j == steps - 1)
        def _():
            keep.wait()

    return call(
        body,
        (steps,),
        [ANY] * n + [spec(width, tile, lambda j: (0, j))],
        [ANY] + [spec(rows, tile, lambda j: (0, j))] * 2,
        [shape(rows, width), shape(rows, hidden), shape(rows, hidden, F32)],
        [pltpu.VMEM((rows, width), BF), pltpu.SemaphoreType.DMA((n + 1,))],
        2 * rows * width * hidden,
        4 * rows * width + 2 * width * hidden + 6 * rows * hidden,
    )(*pieces, weight)


def in_pairs(flat):
    return [tuple(flat[i : i + 2]) for i in range(0, len(flat), 2)]


def hand_out_specs(micro, rows, width, tile, index):
    shapes = [shape(rows // 2, width), shape(rows // 2, width, F32)] * micro
    return [spec(rows // 2, tile, index)] * len(shapes), shapes


def hand_out(acc, b, outs):
    half = acc.shape[0] // 2
    outs[2 * b][...] = acc[half:].astype(BF)
    outs[2 * b + 1][...] = acc[:half]


def project_back(values, weights):
    n = len(values)
    rows = values[0].shape[0]
    width = weights[0][0].shape[0]
    tile = 512
    each = rows // 2
    sizes = [v.shape[1] for v in values]

    def body(*refs):
        outs = refs[2 * n :]
        for b in range(2):
            at = slice(b * each, (b + 1) * each)
            acc = nt(refs[0][at, :], refs[n][...])
            for i in range(1, n):
                acc = acc + nt(refs[i][at, :], refs[n + i][...])
            hand_out(acc, b, outs)

    out_specs, shapes = hand_out_specs(2, each, width, tile, lambda j: (0, j))
    flat = call(
        body,
        (width // tile,),
        [spec(rows, k, lambda j: (0, 0)) for k in sizes]
        + [spec(tile, k, lambda j, i=i: (j, i)) for k, (_, i) in zip(sizes, weights)],
        out_specs,
        shapes,
        (),
        2 * rows * width * sum(sizes),
        2 * (rows + width) * sum(sizes) + 3 * rows * width,
    )(*values, *[w for w, _ in weights])
    return in_pairs(flat)


def feed_back(cot, slope, weight, hidden):
    rows, width = cot.shape
    tile = 512
    micro, each = 2, rows // 2
    first, second = hidden // tile, width // tile

    def body(cot_ref, down_ref, up_ref, slope_ref, dup_ref, *rest):
        *outs, keep_ref = rest
        j = pl.program_id(0)

        for i in range(first):

            @pl.when(j == i)
            def _(i=i):
                for b in range(micro):
                    at = slice(b * each, (b + 1) * each)
                    d_act = nn(cot_ref[at, :], down_ref[...])
                    d_up = (d_act * slope_ref[at, :]).astype(BF)
                    dup_ref[at, :] = d_up
                    keep_ref[at, i * tile : (i + 1) * tile] = d_up

        @pl.when(j >= first)
        def _():
            acc = nt(keep_ref[...], up_ref[...])
            for b in range(micro):
                hand_out(acc[b * each : (b + 1) * each], b, outs)

    def early(j):
        return jnp.minimum(j, first - 1)

    def late(j):
        return jnp.maximum(j - first, 0)

    out_specs, shapes = hand_out_specs(micro, each, width, tile, lambda j: (0, late(j)))
    d_up, *flat = call(
        body,
        (first + second,),
        [
            spec(rows, width, lambda j: (0, 0)),
            spec(width, tile, lambda j: (0, first + early(j))),
            spec(tile, hidden, lambda j: (late(j), 0)),
            spec(rows, tile, lambda j: (0, early(j))),
        ],
        [spec(rows, tile, lambda j: (0, early(j)))] + out_specs,
        [shape(rows, hidden)] + shapes,
        [pltpu.VMEM((rows, hidden), BF)],
        4 * rows * width * hidden,
        5 * rows * width + 4 * width * hidden + 6 * rows * hidden,
    )(cot, weight, weight, slope)
    return d_up, in_pairs(flat)


def retain_back(d_mix, gate, qk, values, w_out, col_info, row_info, cos_table, sin_table,
                log_gamma, heads, micro):
    rows = d_mix.shape[0] // micro
    width = d_mix.shape[1]
    dk, dv = heads * KEY_HEAD, heads * VAL_HEAD

    def body(mix_ref, wo, gate_ref, q_ref, k_ref, v_ref, col_ref, row_ref, cos_ref,
             sin_ref, lg_ref, dv_ref, dg_ref, dq_ref, dk_ref):
        log_g = lg_ref[pl.program_id(0)]
        d_gated = nn(mix_ref[...], wo[...])
        decay = decay_chunk(col_ref, row_ref, slice(None), log_g)
        weights = (nt(q_ref[...], k_ref[...]) * decay).astype(BF)
        kept = nn(weights, v_ref[...])
        scale = lax.rsqrt(jnp.mean(kept * kept, axis=-1, keepdims=True) + eps_group)
        y_norm = kept * scale
        gate = gate_ref[...]
        sig = sigmoid(gate)
        dg_ref[...] = (d_gated * y_norm * sig * (1.0 + gate * (1.0 - sig))).astype(BF)
        d_y = d_gated * (gate * sig)
        d_ret = (
            scale * (d_y - y_norm * jnp.mean(d_y * y_norm, axis=-1, keepdims=True))
        ).astype(BF)
        d_scores = (nt(d_ret, v_ref[...]) * decay).astype(BF)
        dv_ref[...] = tn(weights, d_ret).astype(BF)
        d_k = tn(d_scores, q_ref[...])
        d_q = nn(d_scores, k_ref[...])
        cos_part, sin_part = cos_ref[...], -sin_ref[...]
        for out, part in ((dq_ref, d_q), (dk_ref, d_k)):
            u, v = rotated(part[:, :ROT], part[:, ROT:], cos_part, sin_part)
            out[:, :ROT] = u.astype(BF)
            out[:, ROT:] = v.astype(BF)

    def per_head(cols, start=0):
        return spec(rows, cols, lambda h, b: (b, start + h))

    def per_row(height, cols):
        return spec(height, cols, lambda h, b: (b, 0))

    total = micro * rows
    return call(
        body,
        (heads, micro),
        [
            per_row(rows, width),
            spec(width, VAL_HEAD, lambda h, b: (0, h)),
            per_head(VAL_HEAD),
            per_head(KEY_HEAD),
            per_head(KEY_HEAD, heads),
            per_head(VAL_HEAD),
            per_row(rows, 128),
            per_row(8, rows),
            per_row(rows, ROT),
            per_row(rows, ROT),
            pl.BlockSpec(memory_space=pltpu.SMEM),
        ],
        [per_head(VAL_HEAD), per_head(VAL_HEAD), per_head(KEY_HEAD), per_head(KEY_HEAD)],
        [shape(total, dv), shape(total, dv), shape(total, dk), shape(total, dk)],
        (),
        2 * total * width * dv + 2 * total * rows * heads * 5 * VAL_HEAD,
        2 * width * dv + 20 * total * dv + 2 * total * width,
    )(
        d_mix, w_out, gate, qk, qk, values, col_info, row_info, cos_table, sin_table, log_gamma
    )


def weight_grad(left, rights):
    rows, width = left.shape
    sizes = [v.shape[1] for v in rights]
    cols = sum(sizes)
    tile = 512

    def body(left_ref, *refs):
        start = 0
        for right, size in zip(refs, sizes):
            refs[-1][:, start : start + size] = tn(left_ref[...], right[...]).astype(BF)
            start += size

    return call(
        body,
        (width // tile,),
        [spec(rows, tile, lambda i: (0, i))] + [spec(rows, k, lambda i: (0, 0)) for k in sizes],
        spec(tile, cols, lambda i: (i, 0)),
        shape(width, cols),
        (),
        2 * rows * width * cols,
        2 * (rows * (width + cols) + width * cols),
    )(left, *rights)


def weight_grad_pieces(pieces, right):
    n = len(pieces)
    rows, cols = right.shape
    width = pieces[0].shape[1]
    tile = 512
    steps = width // tile

    def body(*refs):
        right_ref, out_ref, o_ref, left_ref, sems = refs[n:]
        j = pl.program_id(0)
        keep = fetch_and_keep(j, steps, refs[:n], left_ref, out_ref, sems)
        at = pl.ds(pl.multiple_of(j * tile, tile), tile)
        o_ref[...] = tn(left_ref[:, at], right_ref[...]).astype(BF)

        @pl.when(j == steps - 1)
        def _():
            keep.wait()

    return call(
        body,
        (steps,),
        [ANY] * n + [spec(rows, cols, lambda i: (0, 0))],
        [ANY, spec(tile, cols, lambda i: (i, 0))],
        [shape(rows, width), shape(width, cols)],
        [pltpu.VMEM((rows, width), BF), pltpu.SemaphoreType.DMA((n + 1,))],
        2 * rows * width * cols,
        2 * (rows * (width + cols) + width * cols),
    )(*pieces, right)


def layer_norm_parts(inputs, gain_row):
    center = inputs - jnp.mean(inputs, axis=-1, keepdims=True)
    inverse = lax.rsqrt(jnp.mean(center * center, axis=-1, keepdims=True) + eps_norm)
    scaled = center * inverse
    return (scaled * gain_row, scaled, inverse)


def layer_norm_back(incoming, scaled, inverse, gain_row):
    upstream = incoming * gain_row
    centered_grad = (
        upstream
        - jnp.mean(upstream, axis=-1, keepdims=True)
        - scaled * jnp.mean(upstream * scaled, axis=-1, keepdims=True)
    )
    return (centered_grad * inverse, jnp.sum(incoming * scaled, axis=0))


def make_on_device(grid):
    def on_device(
        tokens, norm_gains, w_query, w_key, w_value, w_gate, w_out, w_up, w_down, segments, d_output
    ):
        micro, _, piece, width = tokens.shape
        assert micro == 2
        own, length = micro * piece, 4 * piece
        dk, dv = w_query.shape[1], w_value.shape[1]
        heads = dk // KEY_HEAD
        hidden = w_up.shape[1]
        seq_id = lax.axis_index("seq")
        fsdp_id = lax.axis_index("fsdp")
        y, c = seq_id // 2, seq_id % 2
        x = fsdp_id % 2
        same = x == c
        both = range(micro)

        last = []

        def hold(value):
            return after(value, *last)

        def mark(value):
            last[:] = [value]
            return value

        def settle(value, moved):
            return mark(jnp.where(same, value, hold(moved).astype(value.dtype)))

        def rows(value, b):
            return value[b * piece : (b + 1) * piece]

        def await_(*values):
            waited = lax.optimization_barrier((*values, *last))[: len(values)]
            last[:] = [waited[0]]
            return list(waited)

        def pair(block, moved):
            return mark(jnp.concatenate([block, hold(moved)], axis=0))

        def reduce_second(b, kept, got):
            got = hold(got).astype(F32)
            kept = kept + got
            return kept[:piece], grid.first(b, mark(kept[piece:].astype(BF)))

        line_qk = grid.gather_line(mark(jnp.concatenate([w_query, w_key], axis=1)))
        w_vgo = mark(jnp.concatenate([hold(w_value), w_gate, w_out.T], axis=1))
        vgo_moved = grid.swap(w_vgo)
        toks = tokens.reshape(own, width)
        toks_moved = grid.swap(toks)
        segs = segments.reshape(micro, length).astype(F32)
        segs_moved = grid.swap(segs)
        ud_cot = mark(
            jnp.concatenate(
                [jnp.concatenate([w_up, hold(w_down).T], axis=1), d_output.reshape(own, width)],
                axis=0,
            )
        )

        ranks = [
            [2 * (y ^ i) + (x ^ j) for i, j in ((0, 0), (1, 0), (0, 1), (1, 1))],
            [2 * (y ^ i) + (x ^ j) for i, j in ((0, 0), (0, 1), (1, 0), (1, 1))],
        ]
        positions = jnp.stack(
            [jnp.concatenate([r * piece + jnp.arange(piece) for r in ranks[b]]) for b in both]
        ).astype(F32)
        frequency = jnp.exp(-jnp.log(10000.0) * 2.0 * jnp.arange(ROT, dtype=F32) / KEY_HEAD)
        angles = hold(positions).reshape(-1, 1) * frequency[None, :]
        cos_table, sin_table = jnp.cos(angles), jnp.sin(angles)
        mark(cos_table)
        head_ids = (y * 2 + x) * heads + jnp.arange(heads, dtype=jnp.int32)
        log_gamma = jnp.log1p(-jnp.exp2(-5.0 - head_ids.astype(F32)))
        gain_in, gain_mid = norm_gains[0], norm_gains[1]

        w_vgo = settle(w_vgo, vgo_moved)
        full_vg = grid.gather_weight(w_vgo[:, : 2 * dv])
        full_o = grid.gather_weight(w_vgo[:, 2 * dv :])
        toks = settle(toks, toks_moved)
        xin = toks.astype(F32)
        normed, scaled_in, inverse_in = layer_norm_parts(xin, gain_in)
        normed = mark(normed.astype(BF))
        h1_own = [rows(normed, b) for b in both]
        h1_first = [grid.first(b, h1_own[b]) for b in both]
        segs = settle(segs, segs_moved)
        h1_second = [grid.second(b, pair(h1_own[b], h1_first[b])) for b in both]
        line_qk = await_(line_qk)[0]
        qk_moved = grid.swap(line_qk)
        ud_cot_moved = grid.swap(after(ud_cot, line_qk))
        h1_second = await_(*h1_second)
        line_qk = settle(line_qk, qk_moved)
        line_other = grid.flip_c(line_qk)
        even, odd = [v.reshape(grid.nz, 1, -1, 2 * dk) for v in (line_qk, hold(line_other))]
        full_qk = jnp.where(
            c == 0,
            jnp.concatenate([even, odd], axis=1),
            jnp.concatenate([odd, even], axis=1),
        ).reshape(width, 2 * dk)
        mark(full_qk)
        h1, qk = project_turned(
            [p for b in both for p in (h1_own[b], h1_first[b], h1_second[b])],
            full_qk, cos_table, sin_table,
        )
        mark(qk)
        ud_cot = settle(ud_cot, ud_cot_moved)
        full_ud = grid.gather_weight(ud_cot[:-own])
        cots = ud_cot[-own:]
        cot_own = [rows(cots, b) for b in both]
        cot_first = [grid.first(b, cot_own[b]) for b in both]
        seg_rows = jnp.stack(
            [
                jnp.concatenate(
                    [lax.dynamic_slice_in_dim(hold(segs)[b], r * piece, piece) for r in ranks[b]]
                )
                for b in both
            ]
        )
        lanes = jnp.arange(128)[None, :]
        col_info = jnp.where(
            lanes == 0,
            positions.reshape(-1, 1),
            jnp.where(lanes == 1, seg_rows.reshape(-1, 1), 0.0),
        )
        row_info = jnp.stack([positions, seg_rows] + [jnp.zeros_like(positions)] * 6, axis=1)
        row_info = mark(row_info.reshape(8 * micro, length))

        values, gate = project_plain(hold(h1), hold(full_vg), dv)
        mark(values)
        cot_second = [grid.second(b, pair(cot_own[b], cot_first[b])) for b in both]
        gated = mark(
            retain(qk, hold(values), gate, col_info, row_info, log_gamma, heads, micro)
        )
        outs = project_back([hold(gated)], [(full_o, 0)])
        mark(outs[0][0])
        moved = [grid.second(b, outs[b][0]) for b in both]
        cot = mark(
            assemble([p for b in both for p in (cot_own[b], cot_first[b], hold(cot_second[b]))])
        )
        sums = [reduce_second(b, outs[b][1], moved[b]) for b in both]
        x1, mid, scaled_mid, inverse_mid, mid_first = [], [], [], [], []
        for b in both:
            x1.append(rows(xin, b) + (sums[b][0] + hold(sums[b][1]).astype(F32)))
            out, scaled, inverse = layer_norm_parts(x1[b], gain_mid)
            mid.append(mark(out.astype(BF)))
            scaled_mid.append(scaled)
            inverse_mid.append(inverse)
            mid_first.append(grid.first(b, mid[b]))
        mid_second = [grid.second(b, pair(mid[b], mid_first[b])) for b in both]
        h2, act, slope = feed_up(
            [p for b in both for p in (mid[b], mid_first[b], hold(mid_second[b]))], full_ud, hidden
        )
        mark(act)

        def grad(left, rights):
            return mark(weight_grad(hold(left), rights))

        g_down = grid.scatter_grad(grad(cot, [act]))
        d_up, outs = feed_back(hold(cot), slope, full_ud, hidden)
        mark(d_up)
        moved = [grid.second(b, outs[b][0]) for b in both]
        g_up = grad(h2, [d_up])
        sums = [reduce_second(b, outs[b][1], moved[b]) for b in both]
        g_up = grid.scatter_grad(hold(g_up))
        d_x1, mix_first, gain_mid_grad = [], [], 0.0
        for b in both:
            d_h2 = sums[b][0] + hold(sums[b][1]).astype(F32)
            d_ln, part = layer_norm_back(d_h2, scaled_mid[b], inverse_mid[b], gain_mid)
            gain_mid_grad = gain_mid_grad + part
            d_x1.append(cot_own[b].astype(F32) + d_ln)
            mix_first.append((mark(d_x1[b].astype(BF)),))
            mix_first[b] = mix_first[b] + (grid.first(b, mix_first[b][0]),)
        g_down = await_(g_down)[0]
        g_down_moved = grid.swap(g_down)
        down = project_back([hold(act)], [(full_ud, 1)])
        mark(down[0][0])
        mix = [(v, f, grid.second(b, pair(v, f))) for b, (v, f) in enumerate(mix_first)]
        g_down = settle(g_down, g_down_moved)
        d_mix, g_out = weight_grad_pieces(
            [p for b in both for p in mix[b][:2] + (hold(mix[b][2]),)], gated
        )
        g_out = grid.scatter_grad(mark(g_out))
        g_up = await_(g_up)[0]
        g_up_moved = grid.swap(g_up)
        down_moved = [grid.second(b, hold(down[b][0])) for b in both]
        d_v, d_gate, d_q, d_k = retain_back(
            hold(d_mix), gate, qk, values, full_o, col_info, row_info, cos_table, sin_table,
            log_gamma, heads, micro,
        )
        mark(d_v)
        g_vg = grid.scatter_grad(grad(h1, [d_v, d_gate]))
        down = [reduce_second(b, down[b][1], down_moved[b]) for b in both]
        outs = project_back(
            [d_q, d_k, d_v, hold(d_gate)],
            [(full_qk, 0), (full_qk, 1), (full_vg, 0), (full_vg, 1)],
        )
        mark(outs[0][0])
        moved = [grid.second(b, outs[b][0]) for b in both]
        g_qk = grid.scatter_grad(grad(h1, [d_q, d_k]))
        output = mark(
            jnp.concatenate(
                [x1[b] + (down[b][0] + hold(down[b][1]).astype(F32)) for b in both]
            ).astype(BF)
        )
        output_moved = grid.swap(output)
        g_up = settle(g_up, g_up_moved)
        sums = [reduce_second(b, outs[b][1], moved[b]) for b in both]
        g_out = await_(g_out)[0]
        g_out_moved = grid.swap(g_out)
        output = settle(output, output_moved)
        d_inputs, gain_in_grad = [], 0.0
        for b in both:
            d_h1 = sums[b][0] + hold(sums[b][1]).astype(F32)
            d_ln, part = layer_norm_back(d_h1, rows(scaled_in, b), rows(inverse_in, b), gain_in)
            gain_in_grad = gain_in_grad + part
            d_inputs.append(mark(d_x1[b] + d_ln))
        d_input = jnp.concatenate(d_inputs)
        d_input_moved = grid.swap(hold(d_input))
        g_out = settle(g_out, g_out_moved)
        d_input = settle(d_input, d_input_moved)
        grad_norms = grid.total(hold(jnp.stack([gain_in_grad, gain_mid_grad])))
        mark(grad_norms)
        g_down, g_up, g_out = [hold(g).astype(F32) for g in (g_down.T, g_up, g_out.T)]
        last[:] = [g_down, g_up, g_out]
        g_vg = await_(g_vg)[0]
        g_vg = mark(settle(g_vg, grid.swap(g_vg)).astype(F32))
        g_qk = await_(g_qk)[0]
        g_qk = settle(g_qk, grid.swap(g_qk)).astype(F32)
        whole = (micro, 1, piece, width)
        return (
            output.reshape(whole),
            d_input.reshape(whole),
            grad_norms,
            g_qk[:, :dk],
            g_qk[:, dk:],
            g_vg[:, :dv],
            g_vg[:, dv:],
            g_out,
            g_up,
            g_down,
        )

    return on_device


def solution(mesh):
    grid = Grid(mesh.shape["seq"], mesh.shape["fsdp"])
    rows = P("fsdp", "seq")
    cols = P("seq", "fsdp")
    tok = P(None, "fsdp", "seq", None)
    return jax.shard_map(
        make_on_device(grid),
        mesh=mesh,
        in_specs=(tok, P(), rows, rows, rows, rows, cols, rows, cols, P(None, "fsdp", None), tok),
        out_specs=(tok, tok, P(), rows, rows, rows, rows, cols, rows, cols),
        check_vma=False,
    )
```

time: 670 us -> 649 us (0.969)
  waiting for transfers between devices: 294 us -> 261 us
  Pallas kernels: 189 us -> 168 us
  other arithmetic: 52.7 us -> 71.3 us
  starting transfers between devices: 79.6 us -> 93.5 us
    all_gather x3, waiting for transfers between devices: 39.5 us -> 0.02 us  [gather_weight(): lax.all_gather(shard, AXES, axis=0, tiled=True, axis_index_groups=self.gr...]
    pallas_call x16 -> x13, Pallas kernels: 173 us -> 156 us  [the longest x4 39 us: weight_grad(): call(body, (width // tile,), [spec(rows, tile, lambda i: (0, i))] + [spec...]
    ppermute x50, waiting for transfers between devices: 244 us -> 261 us  [send(): return lax.ppermute(value, AXES, found)]
    ppermute x50, starting transfers between devices: 79.2 us -> 92.3 us  [send(): return lax.ppermute(value, AXES, found)]
    reduce_scatter x5, waiting for transfers between devices: 9.84 us -> 0.04 us  [scatter_grad(): lax.psum_scatter(value, AXES, scatter_dimension=0, tiled=True, axis_index...]
    unnamed x149 -> x118, local copies, waits for them, and re-layouts: 24.5 us -> 20 us
  transfers between devices with their start and end apart: 58 -> 59, of which waited for: 32 -> 29; matrix products, arithmetic and copies ran while one was open for 9% -> 13% of each run, Pallas kernels for 26% -> 23%
where the time goes in v4:
time: 649 us; the launch traced here: 641 us
  waiting for transfers between devices  261 us (40%)
  Pallas kernels  168 us (26%)
  starting transfers between devices  93.5 us (14%)
  other arithmetic  71.3 us (11%)
  local copies, waits for them, and re-layouts  32.1 us (5%)
  between operations  15.2 us (2%)
    ppermute x50, waiting for transfers between devices, send(): return lax.ppermute(value, AXES, found)  261 us
    ppermute x50, starting transfers between devices, send(): return lax.ppermute(value, AXES, found)  92.3 us
    pallas_call x4, Pallas kernels, weight_grad(): call(body, (width // tile,), [spec(rows, tile, lambda i: (0, i))] + [spec...  39 us
    pallas_call x3, Pallas kernels, project_back(): call(body, (width // tile,), [spec(rows, k, lambda j: (0, 0)) for k in si...  35.4 us
    unnamed x118, local copies, waits for them, and re-layouts  20 us
    pallas_call x1, Pallas kernels, retain_back(): call(body, (heads, micro), [per_row(rows, width), spec(width, VAL_HEAD, l...  17.4 us
    pallas_call x1, Pallas kernels, feed_back(): call(body, (first + second,), [spec(rows, width, lambda j: (0, 0)), spec(...  16 us
    pallas_call x1, Pallas kernels, project_plain(): call(body, (cols // tile,), [spec(rows, width, lambda j: (0, 0)), spec(wi...  15.2 us
  transfers between devices with their start and end apart: 59, of which 29 were waited for; matrix products, arithmetic and copies ran while one was open for 13% of the time, Pallas kernels for 23%

profile of v4, /device:TPU:1, one launch (start us, length us, event | category | flops | bytes accessed | tf_op | source)
XLA Modules:
  0.0 641.0 jit_solution(69066338481367597)
XLA Ops:
  24.3 11.6 %collective-permute-done.1 = bf16[256,3072]{1,0:T(8,128)(2,1)} collective-permute-done((bf16[256,3072]{1,0:T(8,128)(2,1)}, bf16[256,3072]{1,0:T(8,128)(2,1)}, u32[]{:S(2)}, u32[]{:S(2)}) %collective-permute-start.1) | collective-permute-done | bytes 1572896 | tf_op jit(solution)/shard_map/ppermute | solution.py:57
  43.7 12.3 %collective-permute-done = bf16[256,2048]{1,0:T(8,128)(2,1)} collective-permute-done((bf16[256,2048]{1,0:T(8,128)(2,1)S(1)}, bf16[256,2048]{1,0:T(8,128)(2,1)}, u32[]{:S(2)}, u32[]{:S(2)}) %collective-permute-start) | collective-permute-done | bytes 1048608 | tf_op jit(solution)/shard_map/ppermute | solution.py:57
  64.7 10.7 %collective-permute-done.3 = bf16[2,512]{1,0:T(2,128)(2,1)S(1)} collective-permute-done((bf16[2,512]{1,0:T(2,128)(2,1)S(1)}, bf16[2,512]{1,0:T(2,128)(2,1)S(1)}, u32[]{:S(2)}, u32[]{:S(2)}) %collective-permute-start.3) | collective-permute-done | bytes 2080 | tf_op jit(solution)/shard_map/ppermute | solution.py:57
  79.4 45.3 %collective-permute-done.4.refs_2_ = bf16[256,2048]{1,0:T(8,128)(2,1)S(1)} collective-permute-done((bf16[256,2048]{1,0:T(8,128)(2,1)S(1)}, bf16[256,2048]{1,0:T(8,128)(2,1)S(1)}, u32[]{:S(2)}, u32[]{:S(2)}) %collective-permute-start.4) | collective-permute-done | bytes 1048608 | tf_op jit(solution)/shard_map/ppermute | solution.py:57
  139.4 10.1 %shard_map.186 = (bf16[1024,2048]{1,0:T(8,128)(2,1)}, bf16[1024,1024]{1,0:T(8,128)(2,1)}) custom-call(bf16[128,2048]{1,0:T(8,128)(2,1)} %copy-done.34, bf16[128,2048]{1,0:T(8,128)(2,1)} %copy-done.43, bf16[256,2048]{1,0:T(8,128)(2,1)} %copy-done.50, bf16[128,2048]{1,0:T(8,128)(2,1)} %copy-done.33, bf16[128,2048]{1,0:T(8,128)(2,1)} %copy-done.44, ...), custom_call_target="tpu_custom_call" | custom-call | flops 4294967296 | bytes 14680064 | tf_op jit(solution)/shard_map/pallas_call | solution.py:215
  149.6 9.3 %collective-permute-done.9 = bf16[512,2048]{1,0:T(8,128)(2,1)} collective-permute-done((bf16[512,2048]{1,0:T(8,128)(2,1)}, bf16[512,2048]{1,0:T(8,128)(2,1)}, u32[]{:S(2)}, u32[]{:S(2)}) %collective-permute-start.9) | collective-permute-done | bytes 2097184 | tf_op jit(solution)/shard_map/ppermute | solution.py:57
  167.1 15.2 %shard_map.187 = (bf16[1024,1024]{1,0:T(8,128)(2,1)}, f32[1024,1024]{1,0:T(8,128)}) custom-call(bf16[1024,2048]{1,0:T(8,128)(2,1)} %get-tuple-element.198.h_ref.left_ref, bf16[2048,2048]{1,0:T(8,128)(2,1)} %all-gather.7.cloned.1.call-done.w_ref.refs_6_.refs_7_), custom_call_target="tpu_custom_call" | custom-call | flops 8589934592 | bytes 20971520 | tf_op jit(solution)/shard_map/pallas_call | solution.py:254
  189.6 7.6 %shard_map.188.refs_0_.refs_6_ = bf16[1024,1024]{1,0:T(8,128)(2,1)} custom-call(bf16[1024,1024]{1,0:T(8,128)(2,1)} %get-tuple-element.129.q_ref.k_ref, bf16[1024,1024]{1,0:T(8,128)(2,1)} %get-tuple-element.129.q_ref.k_ref, bf16[1024,1024]{1,0:T(8,128)(2,1)} %get-tuple-element.139.v_ref, f32[1024,1024]{1,0:T(8,128)} %get-tuple-element.140.gate_ref, ...), custom_call_target="tpu_custom_call" | custom-call | flops 1610612736 | bytes 10485760 | tf_op jit(solution)/shard_map/pallas_call | solution.py:302
  197.2 8.4 %shard_map.189 = (bf16[256,2048]{1,0:T(8,128)(2,1)}, f32[256,2048]{1,0:T(8,128)}, bf16[256,2048]{1,0:T(8,128)(2,1)}, f32[256,2048]{1,0:T(8,128)}) custom-call(bf16[1024,1024]{1,0:T(8,128)(2,1)} %shard_map.188.refs_0_.refs_6_, bf16[2048,1024]{1,0:T(8,128)(2,1)} %all-gather.9.cloned.1.call-done.refs_1_.wo), custom_call_target="tpu_custom_call" | custom-call | flops 4294967296 | bytes 12582912 | tf_op jit(solution)/shard_map/pallas_call | solution.py:399
  218.0 13.5 %collective-permute-done.12 = bf16[256,2048]{1,0:T(8,128)(2,1)} collective-permute-done((bf16[256,2048]{1,0:T(8,128)(2,1)}, bf16[256,2048]{1,0:T(8,128)(2,1)}, u32[]{:S(2)}, u32[]{:S(2)}) %collective-permute-start.12) | collective-permute-done | bytes 1048608 | tf_op jit(solution)/shard_map/ppermute | solution.py:57
  238.9 7.1 %collective-permute-done.15 = bf16[128,2048]{1,0:T(8,128)(2,1)S(1)} collective-permute-done((bf16[128,2048]{1,0:T(8,128)(2,1)S(1)}, bf16[128,2048]{1,0:T(8,128)(2,1)S(1)}, u32[]{:S(2)}, u32[]{:S(2)}) %collective-permute-start.15) | collective-permute-done | bytes 524320 | tf_op jit(solution)/shard_map/ppermute | solution.py:57
  258.3 5.4 collective-permute-start.19
  266.4 21.2 %collective-permute-done.19.refs_2_ = bf16[256,2048]{1,0:T(8,128)(2,1)S(1)} collective-permute-done((bf16[256,2048]{1,0:T(8,128)(2,1)S(1)}, bf16[256,2048]{1,0:T(8,128)(2,1)S(1)}, u32[]{:S(2)}, u32[]{:S(2)}) %collective-permute-start.19) | collective-permute-done | bytes 1048608 | tf_op jit(solution)/shard_map/ppermute | solution.py:57
  288.6 12.5 %shard_map.191 = (bf16[1024,2048]{1,0:T(8,128)(2,1)}, bf16[1024,1024]{1,0:T(8,128)(2,1)}, f32[1024,1024]{1,0:T(8,128)}) custom-call(bf16[128,2048]{1,0:T(8,128)(2,1)} %copy-done.35, bf16[128,2048]{1,0:T(8,128)(2,1)} %copy-done.45, bf16[256,2048]{1,0:T(8,128)(2,1)} %copy-done.53, bf16[128,2048]{1,0:T(8,128)(2,1)} %copy-done.36, bf16[128,2048]{1,0:T(8,128)(2,1)} %copy-done.46, ...), custom_call_target="tpu_custom_call" | custom-call | flops 4294967296 | bytes 18874368 | tf_op jit(solution)/shard_map/pallas_call | solution.py:354
  301.0 8.5 %shard_map.192 = bf16[2048,1024]{1,0:T(8,128)(2,1)} custom-call(bf16[1024,2048]{1,0:T(8,128)(2,1)} %shard_map.190.left_ref.cot_ref, bf16[1024,1024]{1,0:T(8,128)(2,1)} %get-tuple-element.172.refs_0_), custom_call_target="tpu_custom_call" | custom-call | flops 4294967296 | bytes 10485760 | tf_op jit(solution)/shard_map/pallas_call | solution.py:542
  309.8 16.0 %shard_map.193 = (bf16[1024,1024]{1,0:T(8,128)(2,1)}, bf16[256,2048]{1,0:T(8,128)(2,1)}, f32[256,2048]{1,0:T(8,128)}, bf16[256,2048]{1,0:T(8,128)(2,1)}, f32[256,2048]{1,0:T(8,128)}) custom-call(bf16[1024,2048]{1,0:T(8,128)(2,1)} %shard_map.190.left_ref.cot_ref, bf16[2048,2048]{1,0:T(8,128)(2,1)} %all-gather.11.cloned.1.call-done.refs_6_.down_ref.up_ref.refs_1_, ...), custom_call_target="tpu_custom_call" | custom-call | flops 8589934592 | bytes 25165824 | tf_op jit(solution)/shard_map/pallas_call | solution.py:447
  327.8 8.5 %shard_map.194 = bf16[2048,1024]{1,0:T(8,128)(2,1)} custom-call(bf16[1024,2048]{1,0:T(8,128)(2,1)} %get-tuple-element.166.left_ref, bf16[1024,1024]{1,0:T(8,128)(2,1)} %get-tuple-element.165.refs_0_), custom_call_target="tpu_custom_call" | custom-call | flops 4294967296 | bytes 10485760 | tf_op jit(solution)/shard_map/pallas_call | solution.py:542
  336.4 12.4 %collective-permute-done.23 = bf16[256,2048]{1,0:T(8,128)(2,1)} collective-permute-done((bf16[256,2048]{1,0:T(8,128)(2,1)}, bf16[256,2048]{1,0:T(8,128)(2,1)}, u32[]{:S(2)}, u32[]{:S(2)}) %collective-permute-start.23) | collective-permute-done | bytes 1048608 | tf_op jit(solution)/shard_map/ppermute | solution.py:57
  356.8 8.6 %collective-permute-done.25 = bf16[128,2048]{1,0:T(8,128)(2,1)S(1)} collective-permute-done((bf16[128,2048]{1,0:T(8,128)(2,1)S(1)}, bf16[128,2048]{1,0:T(8,128)(2,1)S(1)}, u32[]{:S(2)}, u32[]{:S(2)}) %collective-permute-start.25) | collective-permute-done | bytes 524320 | tf_op jit(solution)/shard_map/ppermute | solution.py:57
  373.9 8.2 %shard_map.195 = (bf16[256,2048]{1,0:T(8,128)(2,1)}, f32[256,2048]{1,0:T(8,128)}, bf16[256,2048]{1,0:T(8,128)(2,1)}, f32[256,2048]{1,0:T(8,128)}) custom-call(bf16[1024,1024]{1,0:T(8,128)(2,1)} %get-tuple-element.172.refs_0_, bf16[2048,2048]{1,0:T(8,128)(2,1)} %all-gather.11.cloned.1.call-done.refs_6_.down_ref.up_ref.refs_1_), custom_call_target="tpu_custom_call" | custom-call | flops 4294967296 | bytes 12582912 | tf_op jit(solution)/shard_map/pallas_call | solution.py:399
  385.9 8.4 %collective-permute-start.28 = (bf16[256,1024]{1,0:T(8,128)(2,1)S(1)}, bf16[256,1024]{1,0:T(8,128)(2,1)S(1)}, u32[]{:S(2)}, u32[]{:S(2)}) collective-permute-start(bf16[256,1024]{1,0:T(8,128)(2,1)S(1)} %copy-done.41), channel_id=1, source_target_pairs={{1,8},{3,10},{5,12},{7,14},{8,1},{10,3},{12,5},{14,7},{17,24},{19,... | collective-permute-start | bytes 1572872 | tf_op jit(solution)/shard_map/ppermute | solution.py:57
  394.3 20.8 %collective-permute-done.28 = bf16[256,1024]{1,0:T(8,128)(2,1)S(1)} collective-permute-done((bf16[256,1024]{1,0:T(8,128)(2,1)S(1)}, bf16[256,1024]{1,0:T(8,128)(2,1)S(1)}, u32[]{:S(2)}, u32[]{:S(2)}) %collective-permute-start.28) | collective-permute-done | bytes 524320 | tf_op jit(solution)/shard_map/ppermute | solution.py:57
  417.9 10.1 %shard_map.196 = (bf16[1024,2048]{1,0:T(8,128)(2,1)}, bf16[2048,1024]{1,0:T(8,128)(2,1)}) custom-call(bf16[128,2048]{1,0:T(8,128)(2,1)} %copy-done.29, bf16[128,2048]{1,0:T(8,128)(2,1)} %collective-permute-done.26.refs_1_, bf16[256,2048]{1,0:T(8,128)(2,1)} %copy-done.52, bf16[128,2048]{1,0:T(8,128)(2,1)} %copy-done.32, ...), custom_call_target="tpu_custom_call" | custom-call | flops 4294967296 | bytes 10485760 | tf_op jit(solution)/shard_map/pallas_call | solution.py:572
  428.5 17.4 %shard_map.197 = (bf16[1024,1024]{1,0:T(8,128)(2,1)}, bf16[1024,1024]{1,0:T(8,128)(2,1)}, bf16[1024,512]{1,0:T(8,128)(2,1)}, bf16[1024,512]{1,0:T(8,128)(2,1)}) custom-call(bf16[1024,2048]{1,0:T(8,128)(2,1)} %get-tuple-element.185.mix_ref, bf16[2048,1024]{1,0:T(8,128)(2,1)} %all-gather.9.cloned.1.call-done.refs_1_.wo, ...), custom_call_target="tpu_custom_call" | custom-call | flops 9663676416 | bytes 29360128 | tf_op jit(solution)/shard_map/pallas_call | solution.py:504
  446.0 13.5 %shard_map.198 = bf16[2048,2048]{1,0:T(8,128)(2,1)} custom-call(bf16[1024,2048]{1,0:T(8,128)(2,1)} %get-tuple-element.198.h_ref.left_ref, bf16[1024,1024]{1,0:T(8,128)(2,1)} %get-tuple-element.186.refs_0_.refs_2_, bf16[1024,1024]{1,0:T(8,128)(2,1)} %get-tuple-element.196.refs_1_.refs_3_), custom_call_target="tpu_custom_call" | custom-call | flops 8589934592 | bytes 16777216 | tf_op jit(solution)/shard_map/pallas_call | solution.py:542
  465.1 20.8 %collective-permute-done.31 = bf16[256,2048]{1,0:T(8,128)(2,1)S(1)} collective-permute-done((bf16[256,2048]{1,0:T(8,128)(2,1)S(1)}, bf16[256,2048]{1,0:T(8,128)(2,1)S(1)}, u32[]{:S(2)}, u32[]{:S(2)}) %collective-permute-start.31) | collective-permute-done | bytes 1048608 | tf_op jit(solution)/shard_map/ppermute | solution.py:57
  490.9 18.8 %shard_map.199 = (bf16[256,2048]{1,0:T(8,128)(2,1)}, f32[256,2048]{1,0:T(8,128)}, bf16[256,2048]{1,0:T(8,128)(2,1)}, f32[256,2048]{1,0:T(8,128)}) custom-call(bf16[1024,512]{1,0:T(8,128)(2,1)} %get-tuple-element.190.refs_0_, bf16[1024,512]{1,0:T(8,128)(2,1)} %get-tuple-element.191.refs_1_, bf16[1024,1024]{1,0:T(8,128)(2,1)} %get-tuple-element.186.refs_0_.refs_2_, ...), custom_call_target="tpu_custom_call" | custom-call | flops 12884901888 | bytes 25165824 | tf_op jit(solution)/shard_map/pallas_call | solution.py:399
  512.4 8.5 %shard_map.200 = bf16[2048,1024]{1,0:T(8,128)(2,1)} custom-call(bf16[1024,2048]{1,0:T(8,128)(2,1)} %get-tuple-element.198.h_ref.left_ref, bf16[1024,512]{1,0:T(8,128)(2,1)} %get-tuple-element.190.refs_0_, bf16[1024,512]{1,0:T(8,128)(2,1)} %get-tuple-element.191.refs_1_), custom_call_target="tpu_custom_call" | custom-call | flops 4294967296 | bytes 10485760 | tf_op jit(solution)/shard_map/pallas_call | solution.py:542
  558.9 5.6 collective-permute-start.41
  566.5 16.5 %collective-permute-done.42 = bf16[256,1024]{1,0:T(8,128)(2,1)S(1)} collective-permute-done((bf16[256,1024]{1,0:T(8,128)(2,1)S(1)}, bf16[256,1024]{1,0:T(8,128)(2,1)S(1)}, u32[]{:S(2)}, u32[]{:S(2)}) %collective-permute-start.42) | collective-permute-done | bytes 524320 | tf_op jit(solution)/shard_map/ppermute | solution.py:57
  603.0 5.4 collective-permute-start.48
  608.4 12.7 %collective-permute-done.48 = bf16[256,2048]{1,0:T(8,128)(2,1)S(1)} collective-permute-done((bf16[256,2048]{1,0:T(8,128)(2,1)}, bf16[256,2048]{1,0:T(8,128)(2,1)S(1)}, u32[]{:S(2)}, u32[]{:S(2)}) %collective-permute-start.48) | collective-permute-done | bytes 1048608 | tf_op jit(solution)/shard_map/ppermute | solution.py:57
  (345 shorter events, 214.8 us)
Async XLA Ops:
  7.2 69.9 %all-gather.5.cloned.1.call-start = ((), (), s32[]{:S(2)}) async-start(), calls=%async_computation.5 | async-start | bytes 2621440 | tf_op jit(solution)/shard_map/all_gather | solution.py:89
  10.1 157.0 %all-gather.7.cloned.1.call-start = ((), (), s32[]{:S(2)}) async-start(), calls=%async_computation.6 | async-start | bytes 9437184 | tf_op jit(solution)/shard_map/all_gather | solution.py:81
  12.7 23.2 %collective-permute-start.1 = (bf16[256,3072]{1,0:T(8,128)(2,1)}, bf16[256,3072]{1,0:T(8,128)(2,1)}, u32[]{:S(2)}, u32[]{:S(2)}) collective-permute-start(bf16[256,3072]{1,0:T(8,128)(2,1)} %pad_maximum_fusion.2), channel_id=1, source_target_pairs={{1,8},{3,10},{5,12},{7,14},{8,1},{10,3},{12,5},{14,7},{17,24},{19,... | collective-permute-start | bytes 4718600 | tf_op jit(solution)/shard_map/ppermute | solution.py:57
  39.0 158.2 %all-gather.9.cloned.1.call-start = ((), (), s32[]{:S(2)}) async-start(), calls=%async_computation.7 | async-start | bytes 4718592 | tf_op jit(solution)/shard_map/all_gather | solution.py:81
  59.9 228.7 %all-gather.11.cloned.1.call-start = ((), (), s32[]{:S(2)}) async-start(), calls=%async_computation.8 | async-start | bytes 9437184 | tf_op jit(solution)/shard_map/all_gather | solution.py:81
  77.1 49.5 %collective-permute-start.7 = (bf16[1024,1024]{1,0:T(8,128)(2,1)}, bf16[1024,1024]{1,0:T(8,128)(2,1)S(1)}, u32[]{:S(2)}, u32[]{:S(2)}) collective-permute-start(bf16[1024,1024]{1,0:T(8,128)(2,1)} %all-gather.5.cloned.1.call-done), channel_id=1, source_target_pairs={{1,8},{3,10},{5,12},{7,14},{8,1},{10,3},{12,5},{14,7},{17,24},{19,... | collective-permute-start | bytes 6291464 | tf_op jit(solution)/shard_map/ppermute | solution.py:57
  79.0 45.6 %collective-permute-start.4 = (bf16[256,2048]{1,0:T(8,128)(2,1)S(1)}, bf16[256,2048]{1,0:T(8,128)(2,1)S(1)}, u32[]{:S(2)}, u32[]{:S(2)}) collective-permute-start(bf16[256,2048]{1,0:T(8,128)(2,1)S(1)} %pad_maximum_fusion.3), channel_id=1, source_target_pairs={{0,1},{1,0},{2,3},{3,2},{4,5},{5,4},{6,7},{7,6},{8,9},{9,8},{10,11... | collective-permute-start | bytes 3145736 | tf_op jit(solution)/shard_map/ppermute | solution.py:57
  79.1 45.6 %collective-permute-start.6 = (bf16[256,2048]{1,0:T(8,128)(2,1)S(1)}, bf16[256,2048]{1,0:T(8,128)(2,1)S(1)}, u32[]{:S(2)}, u32[]{:S(2)}) collective-permute-start(bf16[256,2048]{1,0:T(8,128)(2,1)S(1)} %pad_maximum_fusion.4), channel_id=1, source_target_pairs={{0,16},{1,17},{2,18},{3,19},{4,20},{5,21},{6,22},{7,23},{8,24},{9,... | collective-permute-start | bytes 3145736 | tf_op jit(solution)/shard_map/ppermute | solution.py:57
  131.0 28.0 %collective-permute-start.9 = (bf16[512,2048]{1,0:T(8,128)(2,1)}, bf16[512,2048]{1,0:T(8,128)(2,1)}, u32[]{:S(2)}, u32[]{:S(2)}) collective-permute-start(bf16[512,2048]{1,0:T(8,128)(2,1)} %pad_maximum_fusion), channel_id=1, source_target_pairs={{1,8},{3,10},{5,12},{7,14},{8,1},{10,3},{12,5},{14,7},{17,24},{19,... | collective-permute-start | bytes 6291464 | tf_op jit(solution)/shard_map/ppermute | solution.py:57
  163.0 210.9 %reduce-scatter.6.cloned.1.call-start = ((), (), s32[]{:S(2)}) async-start(), calls=%async_computation.9 | async-start | bytes 4718592 | tf_op jit(solution)/shard_map/reduce_scatter | solution.py:84
  184.6 24.6 %collective-permute-start.13 = (bf16[256,2048]{1,0:T(8,128)(2,1)}, bf16[256,2048]{1,0:T(8,128)(2,1)}, u32[]{:S(2)}, u32[]{:S(2)}) collective-permute-start(bf16[256,2048]{1,0:T(8,128)(2,1)} %pad_maximum_fusion.5), channel_id=1, source_target_pairs={{0,1},{1,0},{2,3},{3,2},{4,5},{5,4},{6,7},{7,6},{8,9},{9,8},{10,11... | collective-permute-start | bytes 3145736 | tf_op jit(solution)/shard_map/ppermute | solution.py:57
  188.3 25.4 %collective-permute-start.14 = (bf16[256,2048]{1,0:T(8,128)(2,1)}, bf16[256,2048]{1,0:T(8,128)(2,1)}, u32[]{:S(2)}, u32[]{:S(2)}) collective-permute-start(bf16[256,2048]{1,0:T(8,128)(2,1)} %pad_maximum_fusion.6), channel_id=1, source_target_pairs={{0,16},{1,17},{2,18},{3,19},{4,20},{5,21},{6,22},{7,23},{8,24},{9,... | collective-permute-start | bytes 3145736 | tf_op jit(solution)/shard_map/ppermute | solution.py:57
  205.6 25.9 %collective-permute-start.12 = (bf16[256,2048]{1,0:T(8,128)(2,1)}, bf16[256,2048]{1,0:T(8,128)(2,1)}, u32[]{:S(2)}, u32[]{:S(2)}) collective-permute-start(bf16[256,2048]{1,0:T(8,128)(2,1)} %get-tuple-element.143), channel_id=1, source_target_pairs={{0,1},{1,0},{2,3},{3,2},{4,5},{5,4},{6,7},{7,6},{8,9},{9,8},{10,11... | collective-permute-start | bytes 3145736 | tf_op jit(solution)/shard_map/ppermute | solution.py:57
  206.0 29.9 %collective-permute-start.16 = (bf16[256,2048]{1,0:T(8,128)(2,1)}, bf16[256,2048]{1,0:T(8,128)(2,1)}, u32[]{:S(2)}, u32[]{:S(2)}) collective-permute-start(bf16[256,2048]{1,0:T(8,128)(2,1)} %get-tuple-element.148), channel_id=1, source_target_pairs={{0,16},{1,17},{2,18},{3,19},{4,20},{5,21},{6,22},{7,23},{8,24},{9,... | collective-permute-start | bytes 3145736 | tf_op jit(solution)/shard_map/ppermute | solution.py:57
  258.3 29.3 %collective-permute-start.19 = (bf16[256,2048]{1,0:T(8,128)(2,1)S(1)}, bf16[256,2048]{1,0:T(8,128)(2,1)S(1)}, u32[]{:S(2)}, u32[]{:S(2)}) collective-permute-start(bf16[256,2048]{1,0:T(8,128)(2,1)S(1)} %pad_maximum_fusion.7), channel_id=1, source_target_pairs={{0,1},{1,0},{2,3},{3,2},{4,5},{5,4},{6,7},{7,6},{8,9},{9,8},{10,11... | collective-permute-start | bytes 3145736 | tf_op jit(solution)/shard_map/ppermute | solution.py:57
  264.6 24.0 %collective-permute-start.21 = (bf16[256,2048]{1,0:T(8,128)(2,1)S(1)}, bf16[256,2048]{1,0:T(8,128)(2,1)}, u32[]{:S(2)}, u32[]{:S(2)}) collective-permute-start(bf16[256,2048]{1,0:T(8,128)(2,1)S(1)} %pad_maximum_fusion.8), channel_id=1, source_target_pairs={{0,16},{1,17},{2,18},{3,19},{4,20},{5,21},{6,22},{7,23},{8,24},{9,... | collective-permute-start | bytes 3145736 | tf_op jit(solution)/shard_map/ppermute | solution.py:57
  309.5 119.0 %reduce-scatter.8.cloned.1.call-start = ((), (), s32[]{:S(2)}) async-start(), calls=%async_computation.10 | async-start | bytes 4718592 | tf_op jit(solution)/shard_map/reduce_scatter | solution.py:84
  325.8 22.9 %collective-permute-start.23 = (bf16[256,2048]{1,0:T(8,128)(2,1)}, bf16[256,2048]{1,0:T(8,128)(2,1)}, u32[]{:S(2)}, u32[]{:S(2)}) collective-permute-start(bf16[256,2048]{1,0:T(8,128)(2,1)} %get-tuple-element.163), channel_id=1, source_target_pairs={{0,1},{1,0},{2,3},{3,2},{4,5},{5,4},{6,7},{7,6},{8,9},{9,8},{10,11... | collective-permute-start | bytes 3145736 | tf_op jit(solution)/shard_map/ppermute | solution.py:57
  327.2 24.8 %collective-permute-start.22 = (bf16[256,2048]{1,0:T(8,128)(2,1)}, bf16[256,2048]{1,0:T(8,128)(2,1)S(1)}, u32[]{:S(2)}, u32[]{:S(2)}) collective-permute-start(bf16[256,2048]{1,0:T(8,128)(2,1)} %get-tuple-element.161), channel_id=1, source_target_pairs={{0,16},{1,17},{2,18},{3,19},{4,20},{5,21},{6,22},{7,23},{8,24},{9,... | collective-permute-start | bytes 3145736 | tf_op jit(solution)/shard_map/ppermute | solution.py:57
  354.0 189.1 %reduce-scatter.10.cloned.1.call-start = ((), (), s32[]{:S(2)}) async-start(), calls=%async_computation.11 | async-start | bytes 4718592 | tf_op jit(solution)/shard_map/reduce_scatter | solution.py:84
  383.2 32.7 %collective-permute-start.27 = (bf16[256,2048]{1,0:T(8,128)(2,1)S(1)}, bf16[256,2048]{1,0:T(8,128)(2,1)S(1)}, u32[]{:S(2)}, u32[]{:S(2)}) collective-permute-start(bf16[256,2048]{1,0:T(8,128)(2,1)S(1)} %pad_maximum_fusion.9), channel_id=1, source_target_pairs={{0,1},{1,0},{2,3},{3,2},{4,5},{5,4},{6,7},{7,6},{8,9},{9,8},{10,11... | collective-permute-start | bytes 3145736 | tf_op jit(solution)/shard_map/ppermute | solution.py:57
  385.4 31.5 %collective-permute-start.30 = (bf16[256,2048]{1,0:T(8,128)(2,1)S(1)}, bf16[256,2048]{1,0:T(8,128)(2,1)S(1)}, u32[]{:S(2)}, u32[]{:S(2)}) collective-permute-start(bf16[256,2048]{1,0:T(8,128)(2,1)S(1)} %pad_maximum_fusion.10), channel_id=1, source_target_pairs={{0,16},{1,17},{2,18},{3,19},{4,20},{5,21},{6,22},{7,23},{8,24},{9,... | collective-permute-start | bytes 3145736 | tf_op jit(solution)/shard_map/ppermute | solution.py:57
  385.9 29.2 %collective-permute-start.28 = (bf16[256,1024]{1,0:T(8,128)(2,1)S(1)}, bf16[256,1024]{1,0:T(8,128)(2,1)S(1)}, u32[]{:S(2)}, u32[]{:S(2)}) collective-permute-start(bf16[256,1024]{1,0:T(8,128)(2,1)S(1)} %copy-done.41), channel_id=1, source_target_pairs={{1,8},{3,10},{5,12},{7,14},{8,1},{10,3},{12,5},{14,7},{17,24},{19,... | collective-permute-start | bytes 1572872 | tf_op jit(solution)/shard_map/ppermute | solution.py:57
  428.0 174.9 %reduce-scatter.14.cloned.1.call-start = ((), (), s32[]{:S(2)}) async-start(), calls=%async_computation.13 | async-start | bytes 9437184 | tf_op jit(solution)/shard_map/reduce_scatter | solution.py:84
  459.5 161.7 %reduce-scatter.12.cloned.1.call-start = ((), (), s32[]{:S(2)}) async-start(), calls=%async_computation.12 | async-start | bytes 4718592 | tf_op jit(solution)/shard_map/reduce_scatter | solution.py:84
  460.7 25.2 %collective-permute-start.31 = (bf16[256,2048]{1,0:T(8,128)(2,1)S(1)}, bf16[256,2048]{1,0:T(8,128)(2,1)S(1)}, u32[]{:S(2)}, u32[]{:S(2)}) collective-permute-start(bf16[256,2048]{1,0:T(8,128)(2,1)S(1)} %copy-done.49), channel_id=1, source_target_pairs={{0,1},{1,0},{2,3},{3,2},{4,5},{5,4},{6,7},{7,6},{8,9},{9,8},{10,11... | collective-permute-start | bytes 3145736 | tf_op jit(solution)/shard_map/ppermute | solution.py:57
  460.7 27.3 %collective-permute-start.33 = (bf16[256,2048]{1,0:T(8,128)(2,1)}, bf16[256,2048]{1,0:T(8,128)(2,1)S(1)}, u32[]{:S(2)}, u32[]{:S(2)}) collective-permute-start(bf16[256,2048]{1,0:T(8,128)(2,1)} %get-tuple-element.194), channel_id=1, source_target_pairs={{0,16},{1,17},{2,18},{3,19},{4,20},{5,21},{6,22},{7,23},{8,24},{9,... | collective-permute-start | bytes 3145736 | tf_op jit(solution)/shard_map/ppermute | solution.py:57
  461.1 69.5 %collective-permute-start.38 = (bf16[256,1024]{1,0:T(8,128)(2,1)}, bf16[256,1024]{1,0:T(8,128)(2,1)}, u32[]{:S(2)}, u32[]{:S(2)}) collective-permute-start(bf16[256,1024]{1,0:T(8,128)(2,1)} %reduce-scatter.8.cloned.1.call-done), channel_id=1, source_target_pairs={{1,8},{3,10},{5,12},{7,14},{8,1},{10,3},{12,5},{14,7},{17,24},{19,... | collective-permute-start | bytes 1572872 | tf_op jit(solution)/shard_map/ppermute | solution.py:57
  490.6 30.3 %collective-permute-start.34 = (bf16[128,2048]{1,0:T(8,128)(2,1)S(1)}, bf16[128,2048]{1,0:T(8,128)(2,1)}, u32[]{:S(2)}, u32[]{:S(2)}) collective-permute-start(bf16[128,2048]{1,0:T(8,128)(2,1)S(1)} %slice.270), channel_id=1, source_target_pairs={{0,1},{1,0},{2,3},{3,2},{4,5},{5,4},{6,7},{7,6},{8,9},{9,8},{10,11... | collective-permute-start | bytes 1572872 | tf_op jit(solution)/shard_map/ppermute | solution.py:57
  490.6 32.1 %collective-permute-start.32 = (bf16[128,2048]{1,0:T(8,128)(2,1)S(1)}, bf16[128,2048]{1,0:T(8,128)(2,1)}, u32[]{:S(2)}, u32[]{:S(2)}) collective-permute-start(bf16[128,2048]{1,0:T(8,128)(2,1)S(1)} %slice.271), channel_id=1, source_target_pairs={{0,16},{1,17},{2,18},{3,19},{4,20},{5,21},{6,22},{7,23},{8,24},{9,... | collective-permute-start | bytes 1572872 | tf_op jit(solution)/shard_map/ppermute | solution.py:57
  511.2 25.8 %collective-permute-start.36 = (bf16[256,2048]{1,0:T(8,128)(2,1)}, bf16[256,2048]{1,0:T(8,128)(2,1)}, u32[]{:S(2)}, u32[]{:S(2)}) collective-permute-start(bf16[256,2048]{1,0:T(8,128)(2,1)} %get-tuple-element.202), channel_id=1, source_target_pairs={{0,16},{1,17},{2,18},{3,19},{4,20},{5,21},{6,22},{7,23},{8,24},{9,... | collective-permute-start | bytes 3145736 | tf_op jit(solution)/shard_map/ppermute | solution.py:57
  558.9 24.1 %collective-permute-start.41 = (bf16[256,2048]{1,0:T(8,128)(2,1)S(1)}, bf16[256,2048]{1,0:T(8,128)(2,1)S(1)}, u32[]{:S(2)}, u32[]{:S(2)}) collective-permute-start(bf16[256,2048]{1,0:T(8,128)(2,1)S(1)} %pad_maximum_fusion.1), channel_id=1, source_target_pairs={{1,8},{3,10},{5,12},{7,14},{8,1},{10,3},{12,5},{14,7},{17,24},{19,... | collective-permute-start | bytes 3145736 | tf_op jit(solution)/shard_map/ppermute | solution.py:57
  (82 other events, 704.9 us)
Sparse Core Ops, SparseCore 0:
  10.2 48.0 all-gather.4
  60.5 81.1 all-gather.6
  143.9 45.6 all-gather.8
  191.6 80.7 all-gather.10
  309.7 49.8 reduce-scatter.5
  361.7 48.1 reduce-scatter.7
  428.1 47.7 reduce-scatter.9
  478.3 87.7 reduce-scatter.13
  568.3 49.0 reduce-scatter.11

commit v5 on v4

--- a/solution.py
+++ b/solution.py
@@ -94,15 +94,16 @@
         )
 
     def total(self, value):
-        for flip in (self.flip_y, self.flip_x, self.flip_c):
+        for flip in (self.flip_y, self.flip_c):
             value = value + flip(value)
         if self.nz & (self.nz - 1):
-            return lax.psum(value, "fsdp", axis_index_groups=self.lines)
-        bit = 1
-        while bit < self.nz:
-            value = value + self.flip_z(value, bit)
-            bit *= 2
-        return value
+            value = lax.psum(value, "fsdp", axis_index_groups=self.lines)
+        else:
+            bit = 1
+            while bit < self.nz:
+                value = value + self.flip_z(value, bit)
+                bit *= 2
+        return value + self.flip_x(value)
 
 
 def call(body, grid, ins, outs, shapes, scratch=(), flops=0, moved=0):
@@ -116,7 +117,7 @@
         cost_estimate=pl.CostEstimate(
             flops=flops, bytes_accessed=moved, transcendentals=0
         ),
-        compiler_params=pltpu.CompilerParams(vmem_limit_bytes=60 << 20),
+        compiler_params=pltpu.CompilerParams(vmem_limit_bytes=63 << 20),
     )
 
 
@@ -639,9 +640,9 @@
             return mark(jnp.concatenate([block, hold(moved)], axis=0))
 
         def reduce_second(b, kept, got):
-            got = hold(got).astype(F32)
-            kept = kept + got
-            return kept[:piece], grid.first(b, mark(kept[piece:].astype(BF)))
+            got = hold(got)
+            sent = (kept[piece:] + got[piece:].astype(F32)).astype(BF)
+            return kept[:piece] + got[:piece].astype(F32), grid.first(b, mark(sent))
 
         line_qk = grid.gather_line(mark(jnp.concatenate([w_query, w_key], axis=1)))
         w_vgo = mark(jnp.concatenate([hold(w_value), w_gate, w_out.T], axis=1))
@@ -681,10 +682,26 @@
         normed = mark(normed.astype(BF))
         h1_own = [rows(normed, b) for b in both]
         h1_first = [grid.first(b, h1_own[b]) for b in both]
-        segs = settle(segs, segs_moved)
-        h1_second = [grid.second(b, pair(h1_own[b], h1_first[b])) for b in both]
         line_qk = await_(line_qk)[0]
         qk_moved = grid.swap(line_qk)
+        segs = settle(segs, segs_moved)
+        seg_rows = jnp.stack(
+            [
+                jnp.concatenate(
+                    [lax.dynamic_slice_in_dim(segs[b], r * piece, piece) for r in ranks[b]]
+                )
+                for b in both
+            ]
+        )
+        lanes = jnp.arange(128)[None, :]
+        col_info = jnp.where(
+            lanes == 0,
+            positions.reshape(-1, 1),
+            jnp.where(lanes == 1, seg_rows.reshape(-1, 1), 0.0),
+        )
+        row_info = jnp.stack([positions, seg_rows] + [jnp.zeros_like(positions)] * 6, axis=1)
+        row_info = mark(row_info.reshape(8 * micro, length))
+        h1_second = [grid.second(b, pair(h1_own[b], h1_first[b])) for b in both]
         ud_cot_moved = grid.swap(after(ud_cot, line_qk))
         h1_second = await_(*h1_second)
         line_qk = settle(line_qk, qk_moved)
@@ -706,23 +723,6 @@
         cots = ud_cot[-own:]
         cot_own = [rows(cots, b) for b in both]
         cot_first = [grid.first(b, cot_own[b]) for b in both]
-        seg_rows = jnp.stack(
-            [
-                jnp.concatenate(
-                    [lax.dynamic_slice_in_dim(hold(segs)[b], r * piece, piece) for r in ranks[b]]
-                )
-                for b in both
-            ]
-        )
-        lanes = jnp.arange(128)[None, :]
-        col_info = jnp.where(
-            lanes == 0,
-            positions.reshape(-1, 1),
-            jnp.where(lanes == 1, seg_rows.reshape(-1, 1), 0.0),
-        )
-        row_info = jnp.stack([positions, seg_rows] + [jnp.zeros_like(positions)] * 6, axis=1)
-        row_info = mark(row_info.reshape(8 * micro, length))
-
         values, gate = project_plain(hold(h1), hold(full_vg), dv)
         mark(values)
         cot_second = [grid.second(b, pair(cot_own[b], cot_first[b])) for b in both]
@@ -769,17 +769,15 @@
             mix_first.append((mark(d_x1[b].astype(BF)),))
             mix_first[b] = mix_first[b] + (grid.first(b, mix_first[b][0]),)
         g_down = await_(g_down)[0]
-        g_down_moved = grid.swap(g_down)
         down = project_back([hold(act)], [(full_ud, 1)])
         mark(down[0][0])
         mix = [(v, f, grid.second(b, pair(v, f))) for b, (v, f) in enumerate(mix_first)]
-        g_down = settle(g_down, g_down_moved)
         d_mix, g_out = weight_grad_pieces(
             [p for b in both for p in mix[b][:2] + (hold(mix[b][2]),)], gated
         )
         g_out = grid.scatter_grad(mark(g_out))
-        g_up = await_(g_up)[0]
-        g_up_moved = grid.swap(g_up)
+        g_ud = mark(jnp.concatenate([hold(g_up), g_down], axis=1))
+        g_ud_moved = grid.swap(g_ud)
         down_moved = [grid.second(b, hold(down[b][0])) for b in both]
         d_v, d_gate, d_q, d_k = retain_back(
             hold(d_mix), gate, qk, values, full_o, col_info, row_info, cos_table, sin_table,
@@ -801,7 +799,7 @@
             ).astype(BF)
         )
         output_moved = grid.swap(output)
-        g_up = settle(g_up, g_up_moved)
+        g_ud = settle(g_ud, g_ud_moved)
         sums = [reduce_second(b, outs[b][1], moved[b]) for b in both]
         g_out = await_(g_out)[0]
         g_out_moved = grid.swap(g_out)
@@ -815,10 +813,12 @@
         d_input = jnp.concatenate(d_inputs)
         d_input_moved = grid.swap(hold(d_input))
         g_out = settle(g_out, g_out_moved)
-        d_input = settle(d_input, d_input_moved)
         grad_norms = grid.total(hold(jnp.stack([gain_in_grad, gain_mid_grad])))
         mark(grad_norms)
-        g_down, g_up, g_out = [hold(g).astype(F32) for g in (g_down.T, g_up, g_out.T)]
+        d_input = settle(d_input, d_input_moved)
+        g_down, g_up, g_out = [
+            hold(g).astype(F32) for g in (g_ud[:, hidden:].T, g_ud[:, :hidden], g_out.T)
+        ]
         last[:] = [g_down, g_up, g_out]
         g_vg = await_(g_vg)[0]
         g_vg = mark(settle(g_vg, grid.swap(g_vg)).astype(F32))

time: 649 us -> 628 us (0.968)
  waiting for transfers between devices: 261 us -> 250 us
  local copies, waits for them, and re-layouts: 32.1 us -> 22.7 us
    ppermute x50 -> x49, waiting for transfers between devices: 261 us -> 231 us  [send(): return lax.ppermute(value, AXES, found)]
    reduce_scatter x5, waiting for transfers between devices: 0.04 us -> 17.6 us  [scatter_grad(): lax.psum_scatter(value, AXES, scatter_dimension=0, tiled=True, axis_index...]
    add x8 -> x1, other arithmetic: 12.3 us -> 0.61 us  [total(): return value + self.flip_x(value)]
    convert_element_type x0 -> x8, other arithmetic: none -> 11.5 us  [reduce_second(): sent = (kept[piece:] + got[piece:].astype(F32)).astype(BF)]
    unnamed x118 -> x111, local copies, waits for them, and re-layouts: 20 us -> 12.9 us
    ppermute x50 -> x49, starting transfers between devices: 92.3 us -> 90.5 us  [send(): return lax.ppermute(value, AXES, found)]
  transfers between devices with their start and end apart: 59 -> 58, of which waited for: 29 -> 33; matrix products, arithmetic and copies ran while one was open for 13% -> 14% of each run, Pallas kernels for 23% -> 24%
where the time goes in v5:
time: 628 us; the launch traced here: 620 us
  waiting for transfers between devices  250 us (40%)
  Pallas kernels  168 us (27%)
  starting transfers between devices  91.5 us (15%)
  other arithmetic  72.5 us (12%)
  local copies, waits for them, and re-layouts  22.7 us (4%)
  between operations  15.4 us (2%)
    ppermute x49, waiting for transfers between devices, send(): return lax.ppermute(value, AXES, found)  231 us
    ppermute x49, starting transfers between devices, send(): return lax.ppermute(value, AXES, found)  90.5 us
    pallas_call x4, Pallas kernels, weight_grad(): call(body, (width // tile,), [spec(rows, tile, lambda i: (0, i))] + [spec...  38.9 us
    pallas_call x3, Pallas kernels, project_back(): call(body, (width // tile,), [spec(rows, k, lambda j: (0, 0)) for k in si...  35.6 us
    reduce_scatter x5, waiting for transfers between devices, scatter_grad(): lax.psum_scatter(value, AXES, scatter_dimension=0, tiled=True, axis_index...  17.6 us
    pallas_call x1, Pallas kernels, retain_back(): call(body, (heads, micro), [per_row(rows, width), spec(width, VAL_HEAD, l...  17.4 us
    pallas_call x1, Pallas kernels, feed_back(): call(body, (first + second,), [spec(rows, width, lambda j: (0, 0)), spec(...  16 us
    pallas_call x1, Pallas kernels, project_plain(): call(body, (cols // tile,), [spec(rows, width, lambda j: (0, 0)), spec(wi...  15.2 us
  transfers between devices with their start and end apart: 58, of which 33 were waited for; matrix products, arithmetic and copies ran while one was open for 14% of the time, Pallas kernels for 24%

profile of v5, /device:TPU:1, one launch (start us, length us, event | category | flops | bytes accessed | tf_op | source)
XLA Modules:
  0.0 619.5 jit_solution(5932078662446627736)
XLA Ops:
  24.2 11.7 %collective-permute-done.1 = bf16[256,3072]{1,0:T(8,128)(2,1)} collective-permute-done((bf16[256,3072]{1,0:T(8,128)(2,1)}, bf16[256,3072]{1,0:T(8,128)(2,1)}, u32[]{:S(2)}, u32[]{:S(2)}) %collective-permute-start.1) | collective-permute-done | bytes 1572896 | tf_op jit(solution)/shard_map/ppermute | solution.py:57
  46.0 10.1 %collective-permute-done = bf16[256,2048]{1,0:T(8,128)(2,1)} collective-permute-done((bf16[256,2048]{1,0:T(8,128)(2,1)}, bf16[256,2048]{1,0:T(8,128)(2,1)}, u32[]{:S(2)}, u32[]{:S(2)}) %collective-permute-start) | collective-permute-done | bytes 1048608 | tf_op jit(solution)/shard_map/ppermute | solution.py:57
  77.0 41.4 %collective-permute-done.4.refs_2_ = bf16[256,2048]{1,0:T(8,128)(2,1)S(1)} collective-permute-done((bf16[256,2048]{1,0:T(8,128)(2,1)S(1)}, bf16[256,2048]{1,0:T(8,128)(2,1)S(1)}, u32[]{:S(2)}, u32[]{:S(2)}) %collective-permute-start.4) | collective-permute-done | bytes 1048608 | tf_op jit(solution)/shard_map/ppermute | solution.py:57
  131.7 10.1 %shard_map.186 = (bf16[1024,2048]{1,0:T(8,128)(2,1)}, bf16[1024,1024]{1,0:T(8,128)(2,1)}) custom-call(bf16[128,2048]{1,0:T(8,128)(2,1)} %copy-done.30, bf16[128,2048]{1,0:T(8,128)(2,1)} %collective-permute-done.2.refs_1_, bf16[256,2048]{1,0:T(8,128)(2,1)} %copy-done.47, bf16[128,2048]{1,0:T(8,128)(2,1)} %copy-done.29, ...), custom_call_target="tpu_custom_call" | custom-call | flops 4294967296 | bytes 14680064 | tf_op jit(solution)/shard_map/pallas_call | solution.py:216
  141.8 9.1 %collective-permute-done.9 = bf16[512,2048]{1,0:T(8,128)(2,1)} collective-permute-done((bf16[512,2048]{1,0:T(8,128)(2,1)}, bf16[512,2048]{1,0:T(8,128)(2,1)}, u32[]{:S(2)}, u32[]{:S(2)}) %collective-permute-start.9) | collective-permute-done | bytes 2097184 | tf_op jit(solution)/shard_map/ppermute | solution.py:57
  158.3 15.2 %shard_map.187 = (bf16[1024,1024]{1,0:T(8,128)(2,1)}, f32[1024,1024]{1,0:T(8,128)}) custom-call(bf16[1024,2048]{1,0:T(8,128)(2,1)} %get-tuple-element.194.h_ref.left_ref, bf16[2048,2048]{1,0:T(8,128)(2,1)} %all-gather.7.cloned.1.call-done.w_ref.refs_6_.refs_7_), custom_call_target="tpu_custom_call" | custom-call | flops 8589934592 | bytes 20971520 | tf_op jit(solution)/shard_map/pallas_call | solution.py:255
  180.2 7.6 %shard_map.188.refs_0_.refs_6_ = bf16[1024,1024]{1,0:T(8,128)(2,1)} custom-call(bf16[1024,1024]{1,0:T(8,128)(2,1)} %get-tuple-element.127.q_ref.k_ref, bf16[1024,1024]{1,0:T(8,128)(2,1)} %get-tuple-element.127.q_ref.k_ref, bf16[1024,1024]{1,0:T(8,128)(2,1)} %get-tuple-element.136.v_ref, f32[1024,1024]{1,0:T(8,128)} %get-tuple-element.137.gate_ref, ...), custom_call_target="tpu_custom_call" | custom-call | flops 1610612736 | bytes 10485760 | tf_op jit(solution)/shard_map/pallas_call | solution.py:303
  189.0 8.1 %shard_map.189 = (bf16[256,2048]{1,0:T(8,128)(2,1)}, f32[256,2048]{1,0:T(8,128)}, bf16[256,2048]{1,0:T(8,128)(2,1)}, f32[256,2048]{1,0:T(8,128)}) custom-call(bf16[1024,1024]{1,0:T(8,128)(2,1)} %shard_map.188.refs_0_.refs_6_, bf16[2048,1024]{1,0:T(8,128)(2,1)} %all-gather.9.cloned.1.call-done.refs_1_.wo), custom_call_target="tpu_custom_call" | custom-call | flops 4294967296 | bytes 12582912 | tf_op jit(solution)/shard_map/pallas_call | solution.py:400
  209.0 13.6 %collective-permute-done.12 = bf16[256,2048]{1,0:T(8,128)(2,1)} collective-permute-done((bf16[256,2048]{1,0:T(8,128)(2,1)}, bf16[256,2048]{1,0:T(8,128)(2,1)}, u32[]{:S(2)}, u32[]{:S(2)}) %collective-permute-start.12) | collective-permute-done | bytes 1048608 | tf_op jit(solution)/shard_map/ppermute | solution.py:57
  227.5 9.1 %collective-permute-done.15 = bf16[128,2048]{1,0:T(8,128)(2,1)S(1)} collective-permute-done((bf16[128,2048]{1,0:T(8,128)(2,1)S(1)}, bf16[128,2048]{1,0:T(8,128)(2,1)S(1)}, u32[]{:S(2)}, u32[]{:S(2)}) %collective-permute-start.15) | collective-permute-done | bytes 524320 | tf_op jit(solution)/shard_map/ppermute | solution.py:57
  243.2 7.2 %collective-permute-done.17.refs_1_ = bf16[128,2048]{1,0:T(8,128)(2,1)S(1)} collective-permute-done((bf16[128,2048]{1,0:T(8,128)(2,1)S(1)}, bf16[128,2048]{1,0:T(8,128)(2,1)S(1)}, u32[]{:S(2)}, u32[]{:S(2)}) %collective-permute-start.17) | collective-permute-done | bytes 524320 | tf_op jit(solution)/shard_map/ppermute | solution.py:57
  255.7 21.5 %collective-permute-done.19.refs_2_ = bf16[256,2048]{1,0:T(8,128)(2,1)S(1)} collective-permute-done((bf16[256,2048]{1,0:T(8,128)(2,1)S(1)}, bf16[256,2048]{1,0:T(8,128)(2,1)S(1)}, u32[]{:S(2)}, u32[]{:S(2)}) %collective-permute-start.19) | collective-permute-done | bytes 1048608 | tf_op jit(solution)/shard_map/ppermute | solution.py:57
  278.2 12.5 %shard_map.191 = (bf16[1024,2048]{1,0:T(8,128)(2,1)}, bf16[1024,1024]{1,0:T(8,128)(2,1)}, f32[1024,1024]{1,0:T(8,128)}) custom-call(bf16[128,2048]{1,0:T(8,128)(2,1)} %copy-done.31, bf16[128,2048]{1,0:T(8,128)(2,1)} %copy-done.42, bf16[256,2048]{1,0:T(8,128)(2,1)} %copy-done.49, bf16[128,2048]{1,0:T(8,128)(2,1)} %copy-done.32, bf16[128,2048]{1,0:T(8,128)(2,1)} %copy-done.43, ...), custom_call_target="tpu_custom_call" | custom-call | flops 4294967296 | bytes 18874368 | tf_op jit(solution)/shard_map/pallas_call | solution.py:355
  290.7 8.5 %shard_map.192 = bf16[2048,1024]{1,0:T(8,128)(2,1)} custom-call(bf16[1024,2048]{1,0:T(8,128)(2,1)} %shard_map.190.left_ref.cot_ref, bf16[1024,1024]{1,0:T(8,128)(2,1)} %get-tuple-element.169.refs_0_), custom_call_target="tpu_custom_call" | custom-call | flops 4294967296 | bytes 10485760 | tf_op jit(solution)/shard_map/pallas_call | solution.py:543
  299.5 16.0 %shard_map.193 = (bf16[1024,1024]{1,0:T(8,128)(2,1)}, bf16[256,2048]{1,0:T(8,128)(2,1)}, f32[256,2048]{1,0:T(8,128)}, bf16[256,2048]{1,0:T(8,128)(2,1)}, f32[256,2048]{1,0:T(8,128)}) custom-call(bf16[1024,2048]{1,0:T(8,128)(2,1)} %shard_map.190.left_ref.cot_ref, bf16[2048,2048]{1,0:T(8,128)(2,1)} %all-gather.11.cloned.1.call-done.refs_6_.down_ref.up_ref.refs_1_, ...), custom_call_target="tpu_custom_call" | custom-call | flops 8589934592 | bytes 25165824 | tf_op jit(solution)/shard_map/pallas_call | solution.py:448
  317.6 8.5 %shard_map.194 = bf16[2048,1024]{1,0:T(8,128)(2,1)} custom-call(bf16[1024,2048]{1,0:T(8,128)(2,1)} %get-tuple-element.163.left_ref, bf16[1024,1024]{1,0:T(8,128)(2,1)} %get-tuple-element.162.refs_0_), custom_call_target="tpu_custom_call" | custom-call | flops 4294967296 | bytes 10485760 | tf_op jit(solution)/shard_map/pallas_call | solution.py:543
  326.1 12.5 %collective-permute-done.23 = bf16[256,2048]{1,0:T(8,128)(2,1)} collective-permute-done((bf16[256,2048]{1,0:T(8,128)(2,1)}, bf16[256,2048]{1,0:T(8,128)(2,1)}, u32[]{:S(2)}, u32[]{:S(2)}) %collective-permute-start.23) | collective-permute-done | bytes 1048608 | tf_op jit(solution)/shard_map/ppermute | solution.py:57
  344.7 9.2 %collective-permute-done.25 = bf16[128,2048]{1,0:T(8,128)(2,1)S(1)} collective-permute-done((bf16[128,2048]{1,0:T(8,128)(2,1)}, bf16[128,2048]{1,0:T(8,128)(2,1)S(1)}, u32[]{:S(2)}, u32[]{:S(2)}) %collective-permute-start.25) | collective-permute-done | bytes 524320 | tf_op jit(solution)/shard_map/ppermute | solution.py:57
  362.8 8.2 %shard_map.195 = (bf16[256,2048]{1,0:T(8,128)(2,1)}, f32[256,2048]{1,0:T(8,128)}, bf16[256,2048]{1,0:T(8,128)(2,1)}, f32[256,2048]{1,0:T(8,128)}) custom-call(bf16[1024,1024]{1,0:T(8,128)(2,1)} %get-tuple-element.169.refs_0_, bf16[2048,2048]{1,0:T(8,128)(2,1)} %all-gather.11.cloned.1.call-done.refs_6_.down_ref.up_ref.refs_1_), custom_call_target="tpu_custom_call" | custom-call | flops 4294967296 | bytes 12582912 | tf_op jit(solution)/shard_map/pallas_call | solution.py:400
  374.8 19.2 %collective-permute-done.27.refs_2_ = bf16[256,2048]{1,0:T(8,128)(2,1)S(1)} collective-permute-done((bf16[256,2048]{1,0:T(8,128)(2,1)S(1)}, bf16[256,2048]{1,0:T(8,128)(2,1)S(1)}, u32[]{:S(2)}, u32[]{:S(2)}) %collective-permute-start.27) | collective-permute-done | bytes 1048608 | tf_op jit(solution)/shard_map/ppermute | solution.py:57
  394.9 10.1 %shard_map.196 = (bf16[1024,2048]{1,0:T(8,128)(2,1)}, bf16[2048,1024]{1,0:T(8,128)(2,1)}) custom-call(bf16[128,2048]{1,0:T(8,128)(2,1)} %get-tuple-element.245.refs_0_, bf16[128,2048]{1,0:T(8,128)(2,1)} %collective-permute-done.26.refs_1_, bf16[256,2048]{1,0:T(8,128)(2,1)} %copy-done.50, bf16[128,2048]{1,0:T(8,128)(2,1)} %copy-done.33, ...), custom_call_target="tpu_custom_call" | custom-call | flops 4294967296 | bytes 10485760 | tf_op jit(solution)/shard_map/pallas_call | solution.py:573
  408.2 17.4 %shard_map.197 = (bf16[1024,1024]{1,0:T(8,128)(2,1)}, bf16[1024,1024]{1,0:T(8,128)(2,1)}, bf16[1024,512]{1,0:T(8,128)(2,1)}, bf16[1024,512]{1,0:T(8,128)(2,1)}) custom-call(bf16[1024,2048]{1,0:T(8,128)(2,1)} %get-tuple-element.181.mix_ref, bf16[2048,1024]{1,0:T(8,128)(2,1)} %all-gather.9.cloned.1.call-done.refs_1_.wo, ...), custom_call_target="tpu_custom_call" | custom-call | flops 9663676416 | bytes 29360128 | tf_op jit(solution)/shard_map/pallas_call | solution.py:505
  425.6 13.5 %shard_map.198 = bf16[2048,2048]{1,0:T(8,128)(2,1)} custom-call(bf16[1024,2048]{1,0:T(8,128)(2,1)} %get-tuple-element.194.h_ref.left_ref, bf16[1024,1024]{1,0:T(8,128)(2,1)} %get-tuple-element.182.refs_0_.refs_2_, bf16[1024,1024]{1,0:T(8,128)(2,1)} %get-tuple-element.192.refs_1_.refs_3_), custom_call_target="tpu_custom_call" | custom-call | flops 8589934592 | bytes 16777216 | tf_op jit(solution)/shard_map/pallas_call | solution.py:543
  441.9 7.1 %collective-permute-start.37 = (bf16[256,2048]{1,0:T(8,128)(2,1)}, bf16[256,2048]{1,0:T(8,128)(2,1)}, u32[]{:S(2)}, u32[]{:S(2)}) collective-permute-start(bf16[256,2048]{1,0:T(8,128)(2,1)} %constant_dynamic-update-slice_fusion.2), channel_id=1, source_target_pairs={{1,8},{3,10},{5,12},{7,14},{8,1},{10,3},{12,5},{14,7},{17,24},{19,... | collective-permute-start | bytes 3145736 | tf_op jit(solution)/shard_map/ppermute | solution.py:57
  449.0 11.0 %collective-permute-done.30 = bf16[256,2048]{1,0:T(8,128)(2,1)S(1)} collective-permute-done((bf16[256,2048]{1,0:T(8,128)(2,1)}, bf16[256,2048]{1,0:T(8,128)(2,1)S(1)}, u32[]{:S(2)}, u32[]{:S(2)}) %collective-permute-start.30) | collective-permute-done | bytes 1048608 | tf_op jit(solution)/shard_map/ppermute | solution.py:57
  464.9 19.3 %shard_map.199 = (bf16[256,2048]{1,0:T(8,128)(2,1)}, f32[256,2048]{1,0:T(8,128)}, bf16[256,2048]{1,0:T(8,128)(2,1)}, f32[256,2048]{1,0:T(8,128)}) custom-call(bf16[1024,512]{1,0:T(8,128)(2,1)} %get-tuple-element.186.refs_0_, bf16[1024,512]{1,0:T(8,128)(2,1)} %get-tuple-element.187.refs_1_, bf16[1024,1024]{1,0:T(8,128)(2,1)} %get-tuple-element.182.refs_0_.refs_2_, ...), custom_call_target="tpu_custom_call" | custom-call | flops 12884901888 | bytes 25165824 | tf_op jit(solution)/shard_map/pallas_call | solution.py:400
  485.2 8.5 %shard_map.200 = bf16[2048,1024]{1,0:T(8,128)(2,1)} custom-call(bf16[1024,2048]{1,0:T(8,128)(2,1)} %get-tuple-element.194.h_ref.left_ref, bf16[1024,512]{1,0:T(8,128)(2,1)} %get-tuple-element.186.refs_0_, bf16[1024,512]{1,0:T(8,128)(2,1)} %get-tuple-element.187.refs_1_), custom_call_target="tpu_custom_call" | custom-call | flops 4294967296 | bytes 10485760 | tf_op jit(solution)/shard_map/pallas_call | solution.py:543
  499.2 13.2 %collective-permute-start.34 = (bf16[256,2048]{1,0:T(8,128)(2,1)}, bf16[256,2048]{1,0:T(8,128)(2,1)}, u32[]{:S(2)}, u32[]{:S(2)}) collective-permute-start(bf16[256,2048]{1,0:T(8,128)(2,1)} %pad_maximum_fusion.11), channel_id=1, source_target_pairs={{1,8},{3,10},{5,12},{7,14},{8,1},{10,3},{12,5},{14,7},{17,24},{19,... | collective-permute-start | bytes 3145736 | tf_op jit(solution)/shard_map/ppermute | solution.py:57
  521.7 6.9 %collective-permute-done.34 = bf16[256,2048]{1,0:T(8,128)(2,1)} collective-permute-done((bf16[256,2048]{1,0:T(8,128)(2,1)}, bf16[256,2048]{1,0:T(8,128)(2,1)}, u32[]{:S(2)}, u32[]{:S(2)}) %collective-permute-start.34) | collective-permute-done | bytes 1048608 | tf_op jit(solution)/shard_map/ppermute | solution.py:57
  559.8 6.7 %collective-permute-start.47 = (bf16[256,2048]{1,0:T(8,128)(2,1)}, bf16[256,2048]{1,0:T(8,128)(2,1)S(1)}, u32[]{:S(2)}, u32[]{:S(2)}) collective-permute-start(bf16[256,2048]{1,0:T(8,128)(2,1)} %reduce-scatter.14.cloned.1.call-done), channel_id=1, source_target_pairs={{1,8},{3,10},{5,12},{7,14},{8,1},{10,3},{12,5},{14,7},{17,24},{19,... | collective-permute-start | bytes 3145736 | tf_op jit(solution)/shard_map/ppermute | solution.py:57
  566.5 13.1 %collective-permute-done.47 = bf16[256,2048]{1,0:T(8,128)(2,1)S(1)} collective-permute-done((bf16[256,2048]{1,0:T(8,128)(2,1)}, bf16[256,2048]{1,0:T(8,128)(2,1)S(1)}, u32[]{:S(2)}, u32[]{:S(2)}) %collective-permute-start.47) | collective-permute-done | bytes 1048608 | tf_op jit(solution)/shard_map/ppermute | solution.py:57
  579.7 17.6 %reduce-scatter.12.cloned.1.call-done = bf16[256,1024]{1,0:T(8,128)(2,1)} async-done(((bf16[2048,1024]{1,0:T(8,128)(2,1)}), bf16[256,1024]{1,0:T(8,128)(2,1)}) %reduce-scatter.12.cloned.1.call-update) | async-done | bytes 524304 | tf_op jit(solution)/shard_map/reduce_scatter | solution.py:84
  (329 shorter events, 200.6 us)
Async XLA Ops:
  7.2 54.5 %all-gather.5.cloned.1.call-start = ((), (), s32[]{:S(2)}) async-start(), calls=%async_computation.5 | async-start | bytes 2621440 | tf_op jit(solution)/shard_map/all_gather | solution.py:89
  10.1 148.1 %all-gather.7.cloned.1.call-start = ((), (), s32[]{:S(2)}) async-start(), calls=%async_computation.6 | async-start | bytes 9437184 | tf_op jit(solution)/shard_map/all_gather | solution.py:81
  12.7 23.2 %collective-permute-start.1 = (bf16[256,3072]{1,0:T(8,128)(2,1)}, bf16[256,3072]{1,0:T(8,128)(2,1)}, u32[]{:S(2)}, u32[]{:S(2)}) collective-permute-start(bf16[256,3072]{1,0:T(8,128)(2,1)} %pad_maximum_fusion.2), channel_id=1, source_target_pairs={{1,8},{3,10},{5,12},{7,14},{8,1},{10,3},{12,5},{14,7},{17,24},{19,... | collective-permute-start | bytes 4718600 | tf_op jit(solution)/shard_map/ppermute | solution.py:57
  39.3 149.7 %all-gather.9.cloned.1.call-start = ((), (), s32[]{:S(2)}) async-start(), calls=%async_computation.7 | async-start | bytes 4718592 | tf_op jit(solution)/shard_map/all_gather | solution.py:81
  42.7 22.3 %collective-permute-start.3 = (bf16[2,512]{1,0:T(2,128)(2,1)S(1)}, bf16[2,512]{1,0:T(2,128)(2,1)S(1)}, u32[]{:S(2)}, u32[]{:S(2)}) collective-permute-start(bf16[2,512]{1,0:T(2,128)(2,1)S(1)} %bitcast.99), channel_id=1, source_target_pairs={{1,8},{3,10},{5,12},{7,14},{8,1},{10,3},{12,5},{14,7},{17,24},{19,... | collective-permute-start | bytes 6152 | tf_op jit(solution)/shard_map/ppermute | solution.py:57
  58.5 219.7 %all-gather.11.cloned.1.call-start = ((), (), s32[]{:S(2)}) async-start(), calls=%async_computation.8 | async-start | bytes 9437184 | tf_op jit(solution)/shard_map/all_gather | solution.py:81
  61.7 58.6 %collective-permute-start.7 = (bf16[1024,1024]{1,0:T(8,128)(2,1)}, bf16[1024,1024]{1,0:T(8,128)(2,1)S(1)}, u32[]{:S(2)}, u32[]{:S(2)}) collective-permute-start(bf16[1024,1024]{1,0:T(8,128)(2,1)} %all-gather.5.cloned.1.call-done), channel_id=1, source_target_pairs={{1,8},{3,10},{5,12},{7,14},{8,1},{10,3},{12,5},{14,7},{17,24},{19,... | collective-permute-start | bytes 6291464 | tf_op jit(solution)/shard_map/ppermute | solution.py:57
  70.1 48.3 %collective-permute-start.4 = (bf16[256,2048]{1,0:T(8,128)(2,1)S(1)}, bf16[256,2048]{1,0:T(8,128)(2,1)S(1)}, u32[]{:S(2)}, u32[]{:S(2)}) collective-permute-start(bf16[256,2048]{1,0:T(8,128)(2,1)S(1)} %pad_maximum_fusion.3), channel_id=1, source_target_pairs={{0,1},{1,0},{2,3},{3,2},{4,5},{5,4},{6,7},{7,6},{8,9},{9,8},{10,11... | collective-permute-start | bytes 3145736 | tf_op jit(solution)/shard_map/ppermute | solution.py:57
  76.7 41.7 %collective-permute-start.6 = (bf16[256,2048]{1,0:T(8,128)(2,1)S(1)}, bf16[256,2048]{1,0:T(8,128)(2,1)S(1)}, u32[]{:S(2)}, u32[]{:S(2)}) collective-permute-start(bf16[256,2048]{1,0:T(8,128)(2,1)S(1)} %pad_maximum_fusion.4), channel_id=1, source_target_pairs={{0,16},{1,17},{2,18},{3,19},{4,20},{5,21},{6,22},{7,23},{8,24},{9,... | collective-permute-start | bytes 3145736 | tf_op jit(solution)/shard_map/ppermute | solution.py:57
  123.2 27.7 %collective-permute-start.9 = (bf16[512,2048]{1,0:T(8,128)(2,1)}, bf16[512,2048]{1,0:T(8,128)(2,1)}, u32[]{:S(2)}, u32[]{:S(2)}) collective-permute-start(bf16[512,2048]{1,0:T(8,128)(2,1)} %pad_maximum_fusion), channel_id=1, source_target_pairs={{1,8},{3,10},{5,12},{7,14},{8,1},{10,3},{12,5},{14,7},{17,24},{19,... | collective-permute-start | bytes 6291464 | tf_op jit(solution)/shard_map/ppermute | solution.py:57
  154.8 207.9 %reduce-scatter.6.cloned.1.call-start = ((), (), s32[]{:S(2)}) async-start(), calls=%async_computation.9 | async-start | bytes 4718592 | tf_op jit(solution)/shard_map/reduce_scatter | solution.py:84
  175.6 24.5 %collective-permute-start.13 = (bf16[256,2048]{1,0:T(8,128)(2,1)}, bf16[256,2048]{1,0:T(8,128)(2,1)}, u32[]{:S(2)}, u32[]{:S(2)}) collective-permute-start(bf16[256,2048]{1,0:T(8,128)(2,1)} %pad_maximum_fusion.5), channel_id=1, source_target_pairs={{0,1},{1,0},{2,3},{3,2},{4,5},{5,4},{6,7},{7,6},{8,9},{9,8},{10,11... | collective-permute-start | bytes 3145736 | tf_op jit(solution)/shard_map/ppermute | solution.py:57
  179.3 25.5 %collective-permute-start.14 = (bf16[256,2048]{1,0:T(8,128)(2,1)}, bf16[256,2048]{1,0:T(8,128)(2,1)}, u32[]{:S(2)}, u32[]{:S(2)}) collective-permute-start(bf16[256,2048]{1,0:T(8,128)(2,1)} %pad_maximum_fusion.6), channel_id=1, source_target_pairs={{0,16},{1,17},{2,18},{3,19},{4,20},{5,21},{6,22},{7,23},{8,24},{9,... | collective-permute-start | bytes 3145736 | tf_op jit(solution)/shard_map/ppermute | solution.py:57
  197.1 25.5 %collective-permute-start.12 = (bf16[256,2048]{1,0:T(8,128)(2,1)}, bf16[256,2048]{1,0:T(8,128)(2,1)}, u32[]{:S(2)}, u32[]{:S(2)}) collective-permute-start(bf16[256,2048]{1,0:T(8,128)(2,1)} %get-tuple-element.140), channel_id=1, source_target_pairs={{0,1},{1,0},{2,3},{3,2},{4,5},{5,4},{6,7},{7,6},{8,9},{9,8},{10,11... | collective-permute-start | bytes 3145736 | tf_op jit(solution)/shard_map/ppermute | solution.py:57
  198.3 28.7 %collective-permute-start.16 = (bf16[256,2048]{1,0:T(8,128)(2,1)}, bf16[256,2048]{1,0:T(8,128)(2,1)S(1)}, u32[]{:S(2)}, u32[]{:S(2)}) collective-permute-start(bf16[256,2048]{1,0:T(8,128)(2,1)} %get-tuple-element.145), channel_id=1, source_target_pairs={{0,16},{1,17},{2,18},{3,19},{4,20},{5,21},{6,22},{7,23},{8,24},{9,... | collective-permute-start | bytes 3145736 | tf_op jit(solution)/shard_map/ppermute | solution.py:57
  250.5 26.8 %collective-permute-start.19 = (bf16[256,2048]{1,0:T(8,128)(2,1)S(1)}, bf16[256,2048]{1,0:T(8,128)(2,1)S(1)}, u32[]{:S(2)}, u32[]{:S(2)}) collective-permute-start(bf16[256,2048]{1,0:T(8,128)(2,1)S(1)} %pad_maximum_fusion.7), channel_id=1, source_target_pairs={{0,1},{1,0},{2,3},{3,2},{4,5},{5,4},{6,7},{7,6},{8,9},{9,8},{10,11... | collective-permute-start | bytes 3145736 | tf_op jit(solution)/shard_map/ppermute | solution.py:57
  254.3 23.9 %collective-permute-start.21 = (bf16[256,2048]{1,0:T(8,128)(2,1)S(1)}, bf16[256,2048]{1,0:T(8,128)(2,1)}, u32[]{:S(2)}, u32[]{:S(2)}) collective-permute-start(bf16[256,2048]{1,0:T(8,128)(2,1)S(1)} %pad_maximum_fusion.8), channel_id=1, source_target_pairs={{0,16},{1,17},{2,18},{3,19},{4,20},{5,21},{6,22},{7,23},{8,24},{9,... | collective-permute-start | bytes 3145736 | tf_op jit(solution)/shard_map/ppermute | solution.py:57
  299.2 106.3 %reduce-scatter.8.cloned.1.call-start = ((), (), s32[]{:S(2)}) async-start(), calls=%async_computation.10 | async-start | bytes 4718592 | tf_op jit(solution)/shard_map/reduce_scatter | solution.py:84
  315.5 23.1 %collective-permute-start.23 = (bf16[256,2048]{1,0:T(8,128)(2,1)}, bf16[256,2048]{1,0:T(8,128)(2,1)}, u32[]{:S(2)}, u32[]{:S(2)}) collective-permute-start(bf16[256,2048]{1,0:T(8,128)(2,1)} %get-tuple-element.160), channel_id=1, source_target_pairs={{0,1},{1,0},{2,3},{3,2},{4,5},{5,4},{6,7},{7,6},{8,9},{9,8},{10,11... | collective-permute-start | bytes 3145736 | tf_op jit(solution)/shard_map/ppermute | solution.py:57
  316.6 24.2 %collective-permute-start.22 = (bf16[256,2048]{1,0:T(8,128)(2,1)}, bf16[256,2048]{1,0:T(8,128)(2,1)}, u32[]{:S(2)}, u32[]{:S(2)}) collective-permute-start(bf16[256,2048]{1,0:T(8,128)(2,1)} %get-tuple-element.158), channel_id=1, source_target_pairs={{0,16},{1,17},{2,18},{3,19},{4,20},{5,21},{6,22},{7,23},{8,24},{9,... | collective-permute-start | bytes 3145736 | tf_op jit(solution)/shard_map/ppermute | solution.py:57
  342.9 176.4 %reduce-scatter.10.cloned.1.call-start = ((), (), s32[]{:S(2)}) async-start(), calls=%async_computation.11 | async-start | bytes 4718592 | tf_op jit(solution)/shard_map/reduce_scatter | solution.py:84
  372.3 21.7 %collective-permute-start.27 = (bf16[256,2048]{1,0:T(8,128)(2,1)S(1)}, bf16[256,2048]{1,0:T(8,128)(2,1)S(1)}, u32[]{:S(2)}, u32[]{:S(2)}) collective-permute-start(bf16[256,2048]{1,0:T(8,128)(2,1)S(1)} %pad_maximum_fusion.9), channel_id=1, source_target_pairs={{0,1},{1,0},{2,3},{3,2},{4,5},{5,4},{6,7},{7,6},{8,9},{9,8},{10,11... | collective-permute-start | bytes 3145736 | tf_op jit(solution)/shard_map/ppermute | solution.py:57
  373.8 21.1 %collective-permute-start.29 = (bf16[256,2048]{1,0:T(8,128)(2,1)S(1)}, bf16[256,2048]{1,0:T(8,128)(2,1)}, u32[]{:S(2)}, u32[]{:S(2)}) collective-permute-start(bf16[256,2048]{1,0:T(8,128)(2,1)S(1)} %pad_maximum_fusion.10), channel_id=1, source_target_pairs={{0,16},{1,17},{2,18},{3,19},{4,20},{5,21},{6,22},{7,23},{8,24},{9,... | collective-permute-start | bytes 3145736 | tf_op jit(solution)/shard_map/ppermute | solution.py:57
  405.1 154.6 %reduce-scatter.14.cloned.1.call-start = ((), (), s32[]{:S(2)}) async-start(), calls=%async_computation.13 | async-start | bytes 9437184 | tf_op jit(solution)/shard_map/reduce_scatter | solution.py:84
  439.1 158.2 %reduce-scatter.12.cloned.1.call-start = ((), (), s32[]{:S(2)}) async-start(), calls=%async_computation.12 | async-start | bytes 4718592 | tf_op jit(solution)/shard_map/reduce_scatter | solution.py:84
  441.9 70.5 %collective-permute-start.37 = (bf16[256,2048]{1,0:T(8,128)(2,1)}, bf16[256,2048]{1,0:T(8,128)(2,1)}, u32[]{:S(2)}, u32[]{:S(2)}) collective-permute-start(bf16[256,2048]{1,0:T(8,128)(2,1)} %constant_dynamic-update-slice_fusion.2), channel_id=1, source_target_pairs={{1,8},{3,10},{5,12},{7,14},{8,1},{10,3},{12,5},{14,7},{17,24},{19,... | collective-permute-start | bytes 3145736 | tf_op jit(solution)/shard_map/ppermute | solution.py:57
  462.5 31.2 %collective-permute-start.33 = (bf16[128,2048]{1,0:T(8,128)(2,1)}, bf16[128,2048]{1,0:T(8,128)(2,1)S(1)}, u32[]{:S(2)}, u32[]{:S(2)}) collective-permute-start(bf16[128,2048]{1,0:T(8,128)(2,1)} %add_convert_fusion.4), channel_id=1, source_target_pairs={{0,1},{1,0},{2,3},{3,2},{4,5},{5,4},{6,7},{7,6},{8,9},{9,8},{10,11... | collective-permute-start | bytes 1572872 | tf_op jit(solution)/shard_map/ppermute | solution.py:57
  464.1 32.5 %collective-permute-start.31 = (bf16[128,2048]{1,0:T(8,128)(2,1)}, bf16[128,2048]{1,0:T(8,128)(2,1)}, u32[]{:S(2)}, u32[]{:S(2)}) collective-permute-start(bf16[128,2048]{1,0:T(8,128)(2,1)} %add_convert_fusion.5), channel_id=1, source_target_pairs={{0,16},{1,17},{2,18},{3,19},{4,20},{5,21},{6,22},{7,23},{8,24},{9,... | collective-permute-start | bytes 1572872 | tf_op jit(solution)/shard_map/ppermute | solution.py:57
  484.1 30.6 %collective-permute-start.36 = (bf16[256,2048]{1,0:T(8,128)(2,1)}, bf16[256,2048]{1,0:T(8,128)(2,1)}, u32[]{:S(2)}, u32[]{:S(2)}) collective-permute-start(bf16[256,2048]{1,0:T(8,128)(2,1)} %get-tuple-element.193), channel_id=1, source_target_pairs={{0,1},{1,0},{2,3},{3,2},{4,5},{5,4},{6,7},{7,6},{8,9},{9,8},{10,11... | collective-permute-start | bytes 3145736 | tf_op jit(solution)/shard_map/ppermute | solution.py:57
  484.5 32.8 %collective-permute-start.35 = (bf16[256,2048]{1,0:T(8,128)(2,1)}, bf16[256,2048]{1,0:T(8,128)(2,1)}, u32[]{:S(2)}, u32[]{:S(2)}) collective-permute-start(bf16[256,2048]{1,0:T(8,128)(2,1)} %get-tuple-element.198), channel_id=1, source_target_pairs={{0,16},{1,17},{2,18},{3,19},{4,20},{5,21},{6,22},{7,23},{8,24},{9,... | collective-permute-start | bytes 3145736 | tf_op jit(solution)/shard_map/ppermute | solution.py:57
  499.2 29.3 %collective-permute-start.34 = (bf16[256,2048]{1,0:T(8,128)(2,1)}, bf16[256,2048]{1,0:T(8,128)(2,1)}, u32[]{:S(2)}, u32[]{:S(2)}) collective-permute-start(bf16[256,2048]{1,0:T(8,128)(2,1)} %pad_maximum_fusion.11), channel_id=1, source_target_pairs={{1,8},{3,10},{5,12},{7,14},{8,1},{10,3},{12,5},{14,7},{17,24},{19,... | collective-permute-start | bytes 3145736 | tf_op jit(solution)/shard_map/ppermute | solution.py:57
  519.3 23.0 %collective-permute-start.41 = (bf16[256,1024]{1,0:T(8,128)(2,1)}, bf16[256,1024]{1,0:T(8,128)(2,1)S(1)}, u32[]{:S(2)}, u32[]{:S(2)}) collective-permute-start(bf16[256,1024]{1,0:T(8,128)(2,1)} %reduce-scatter.10.cloned.1.call-done), channel_id=1, source_target_pairs={{1,8},{3,10},{5,12},{7,14},{8,1},{10,3},{12,5},{14,7},{17,24},{19,... | collective-permute-start | bytes 1572872 | tf_op jit(solution)/shard_map/ppermute | solution.py:57
  (77 other events, 777.4 us)
Sparse Core Ops, SparseCore 0:
  10.2 48.0 all-gather.4
  60.5 81.1 all-gather.6
  143.3 45.6 all-gather.8
  191.0 80.7 all-gather.10
  299.3 50.4 reduce-scatter.5
  352.0 48.1 reduce-scatter.7
  405.3 51.2 reduce-scatter.9
  458.8 87.7 reduce-scatter.13
  548.9 48.3 reduce-scatter.11

commit v6 on v5

--- a/solution.py
+++ b/solution.py
@@ -364,79 +364,63 @@
     )(*pieces, weight)
 
 
-def in_pairs(flat):
-    return [tuple(flat[i : i + 2]) for i in range(0, len(flat), 2)]
-
-
-def hand_out_specs(micro, rows, width, tile, index):
-    shapes = [shape(rows // 2, width), shape(rows // 2, width, F32)] * micro
-    return [spec(rows // 2, tile, index)] * len(shapes), shapes
-
-
-def hand_out(acc, b, outs):
-    half = acc.shape[0] // 2
-    outs[2 * b][...] = acc[half:].astype(BF)
-    outs[2 * b + 1][...] = acc[:half]
-
-
-def project_back(values, weights):
-    n = len(values)
+def project_back(values, weights, cuts, dtype):
+    n, m = len(values), len(cuts)
     rows = values[0].shape[0]
     width = weights[0][0].shape[0]
     tile = 512
-    each = rows // 2
     sizes = [v.shape[1] for v in values]
 
     def body(*refs):
-        outs = refs[2 * n :]
-        for b in range(2):
-            at = slice(b * each, (b + 1) * each)
-            acc = nt(refs[0][at, :], refs[n][...])
-            for i in range(1, n):
-                acc = acc + nt(refs[i][at, :], refs[n + i][...])
-            hand_out(acc, b, outs)
-
-    out_specs, shapes = hand_out_specs(2, each, width, tile, lambda j: (0, j))
-    flat = call(
+        acc = 0.0
+        for i in range(n):
+            some = jnp.concatenate([refs[i][at : at + k, :] for at, k in cuts], axis=0)
+            acc = acc + nt(some, refs[n + i][...])
+        start = 0
+        for out, (_, k) in zip(refs[2 * n :], cuts):
+            out[...] = acc[start : start + k].astype(dtype)
+            start += k
+
+    taken = sum(k for _, k in cuts)
+    return call(
         body,
         (width // tile,),
         [spec(rows, k, lambda j: (0, 0)) for k in sizes]
         + [spec(tile, k, lambda j, i=i: (j, i)) for k, (_, i) in zip(sizes, weights)],
-        out_specs,
-        shapes,
+        [spec(k, tile, lambda j: (0, j)) for _, k in cuts],
+        [shape(k, width, dtype) for _, k in cuts],
         (),
-        2 * rows * width * sum(sizes),
-        2 * (rows + width) * sum(sizes) + 3 * rows * width,
+        2 * taken * width * sum(sizes),
+        2 * (rows + width) * sum(sizes) + 3 * taken * width,
     )(*values, *[w for w, _ in weights])
-    return in_pairs(flat)
-
-
-def feed_back(cot, slope, weight, hidden):
+
+
+def feed_back(cot, slopes, w_up, w_down):
     rows, width = cot.shape
+    hidden = w_up.shape[1]
     tile = 512
-    micro, each = 2, rows // 2
+    half = rows // 2
     first, second = hidden // tile, width // tile
 
-    def body(cot_ref, down_ref, up_ref, slope_ref, dup_ref, *rest):
-        *outs, keep_ref = rest
+    def body(cot_ref, down_ref, up_ref, slope_a, slope_b, dup_ref, sent_0, sent_1, keep_ref):
         j = pl.program_id(0)
 
         for i in range(first):
 
             @pl.when(j == i)
             def _(i=i):
-                for b in range(micro):
-                    at = slice(b * each, (b + 1) * each)
-                    d_act = nn(cot_ref[at, :], down_ref[...])
-                    d_up = (d_act * slope_ref[at, :]).astype(BF)
-                    dup_ref[at, :] = d_up
-                    keep_ref[at, i * tile : (i + 1) * tile] = d_up
+                for at, slope_ref in ((0, slope_a), (half, slope_b)):
+                    d_act = nn(cot_ref[at : at + half, :], down_ref[...])
+                    d_up = (d_act * slope_ref[...]).astype(BF)
+                    dup_ref[at : at + half, :] = d_up
+                    if at:
+                        keep_ref[:, i * tile : (i + 1) * tile] = d_up
 
         @pl.when(j >= first)
         def _():
-            acc = nt(keep_ref[...], up_ref[...])
-            for b in range(micro):
-                hand_out(acc[b * each : (b + 1) * each], b, outs)
+            acc = nt(keep_ref[...], up_ref[...]).astype(BF)
+            sent_0[...] = acc[: half // 2]
+            sent_1[...] = acc[half // 2 :]
 
     def early(j):
         return jnp.minimum(j, first - 1)
@@ -444,23 +428,23 @@
     def late(j):
         return jnp.maximum(j - first, 0)
 
-    out_specs, shapes = hand_out_specs(micro, each, width, tile, lambda j: (0, late(j)))
-    d_up, *flat = call(
+    return call(
         body,
         (first + second,),
         [
             spec(rows, width, lambda j: (0, 0)),
-            spec(width, tile, lambda j: (0, first + early(j))),
+            spec(width, tile, lambda j: (0, early(j))),
             spec(tile, hidden, lambda j: (late(j), 0)),
-            spec(rows, tile, lambda j: (0, early(j))),
+            spec(half, tile, lambda j: (0, early(j))),
+            spec(half, tile, lambda j: (0, early(j))),
         ],
-        [spec(rows, tile, lambda j: (0, early(j)))] + out_specs,
-        [shape(rows, hidden)] + shapes,
-        [pltpu.VMEM((rows, hidden), BF)],
-        4 * rows * width * hidden,
-        5 * rows * width + 4 * width * hidden + 6 * rows * hidden,
-    )(cot, weight, weight, slope)
-    return d_up, in_pairs(flat)
+        [spec(rows, tile, lambda j: (0, early(j)))]
+        + [spec(half // 2, tile, lambda j: (0, late(j)))] * 2,
+        [shape(rows, hidden), shape(half // 2, width), shape(half // 2, width)],
+        [pltpu.VMEM((half, hidden), BF)],
+        3 * rows * width * hidden,
+        4 * rows * width + 4 * width * hidden + 6 * rows * hidden,
+    )(cot, w_down, w_up, *slopes)
 
 
 def retain_back(d_mix, gate, qk, values, w_out, col_info, row_info, cos_table, sin_table,
@@ -552,6 +536,30 @@
     )(left, *rights)
 
 
+def weight_grad_rows(rows, pairs):
+    n = len(pairs)
+    width, cols = pairs[0][0][0].shape[1], pairs[0][1][0].shape[1]
+    tile = 512
+
+    def body(*refs):
+        acc = tn(refs[0][...], refs[n][...])
+        for i in range(1, n):
+            acc = acc + tn(refs[i][...], refs[n + i][...])
+        refs[-1][...] = acc.astype(BF)
+
+    return call(
+        body,
+        (width // tile,),
+        [spec(rows, tile, lambda i, b=b: (b, i)) for (_, b), _ in pairs]
+        + [spec(rows, cols, lambda i, b=b: (b, 0)) for _, (_, b) in pairs],
+        spec(tile, cols, lambda i: (i, 0)),
+        shape(width, cols),
+        (),
+        2 * n * rows * width * cols,
+        2 * (n * rows * (width + cols) + width * cols),
+    )(*[left for (left, _), _ in pairs], *[right for _, (right, _) in pairs])
+
+
 def weight_grad_pieces(pieces, right):
     n = len(pieces)
     rows, cols = right.shape
@@ -719,7 +727,8 @@
         )
         mark(qk)
         ud_cot = settle(ud_cot, ud_cot_moved)
-        full_ud = grid.gather_weight(ud_cot[:-own])
+        full_u = grid.gather_weight(ud_cot[:-own, :hidden])
+        full_d = grid.gather_weight(ud_cot[:-own, hidden:])
         cots = ud_cot[-own:]
         cot_own = [rows(cots, b) for b in both]
         cot_first = [grid.first(b, cot_own[b]) for b in both]
@@ -729,13 +738,24 @@
         gated = mark(
             retain(qk, hold(values), gate, col_info, row_info, log_gamma, heads, micro)
         )
-        outs = project_back([hold(gated)], [(full_o, 0)])
-        mark(outs[0][0])
-        moved = [grid.second(b, outs[b][0]) for b in both]
+        halves = [[(b * length + i * 2 * piece, 2 * piece) for b in both] for i in range(2)]
+
+        def exchange_rows(values, weights):
+            sent = project_back(values, weights, halves[1], BF)
+            mark(sent[0])
+            moved = [grid.second(b, sent[b]) for b in both]
+            kept = project_back([hold(values[0]), *values[1:]], weights, halves[0], F32)
+            mark(kept[0])
+            return kept, moved
+
+        kept, moved = exchange_rows([hold(gated)], [(full_o, 0)])
         cot = mark(
-            assemble([p for b in both for p in (cot_own[b], cot_first[b], hold(cot_second[b]))])
-        )
-        sums = [reduce_second(b, outs[b][1], moved[b]) for b in both]
+            assemble(
+                [p for b in both for p in (cot_own[b], cot_first[b])]
+                + [hold(cot_second[b]) for b in both]
+            )
+        )
+        sums = [reduce_second(b, kept[b], moved[b]) for b in both]
         x1, mid, scaled_mid, inverse_mid, mid_first = [], [], [], [], []
         for b in both:
             x1.append(rows(xin, b) + (sums[b][0] + hold(sums[b][1]).astype(F32)))
@@ -745,20 +765,30 @@
             inverse_mid.append(inverse)
             mid_first.append(grid.first(b, mid[b]))
         mid_second = [grid.second(b, pair(mid[b], mid_first[b])) for b in both]
-        h2, act, slope = feed_up(
-            [p for b in both for p in (mid[b], mid_first[b], hold(mid_second[b]))], full_ud, hidden
-        )
-        mark(act)
+        h2, act, slope = [], [], []
+        for some in ([v for b in both for v in (mid[b], mid_first[b])], mid_second):
+            out = feed_up([hold(v) for v in some], full_u, hidden)
+            mark(out[1])
+            for held, value in zip((h2, act, slope), out):
+                held.append(value)
 
         def grad(left, rights):
             return mark(weight_grad(hold(left), rights))
 
-        g_down = grid.scatter_grad(grad(cot, [act]))
-        d_up, outs = feed_back(hold(cot), slope, full_ud, hidden)
+        def grad_rows(lefts, rights):
+            return mark(weight_grad_rows(length, list(zip(lefts, rights))))
+
+        g_down = grid.scatter_grad(
+            grad_rows([(hold(cot), 0), (cot, 1)], [(act[0], 0), (act[1], 0)])
+        )
+        d_up, *sent = feed_back(hold(cot), slope, full_u, full_d)
         mark(d_up)
-        moved = [grid.second(b, outs[b][0]) for b in both]
-        g_up = grad(h2, [d_up])
-        sums = [reduce_second(b, outs[b][1], moved[b]) for b in both]
+        moved = [grid.second(b, sent[b]) for b in both]
+        quarters = [(0, 2 * piece), (2 * piece, 2 * piece)]
+        kept = project_back([hold(d_up)], [(full_u, 0)], quarters, F32)
+        mark(kept[0])
+        g_up = grad_rows([(hold(h2[0]), 0), (h2[1], 0)], [(d_up, 0), (d_up, 1)])
+        sums = [reduce_second(b, kept[b], moved[b]) for b in both]
         g_up = grid.scatter_grad(hold(g_up))
         d_x1, mix_first, gain_mid_grad = [], [], 0.0
         for b in both:
@@ -769,29 +799,30 @@
             mix_first.append((mark(d_x1[b].astype(BF)),))
             mix_first[b] = mix_first[b] + (grid.first(b, mix_first[b][0]),)
         g_down = await_(g_down)[0]
-        down = project_back([hold(act)], [(full_ud, 1)])
-        mark(down[0][0])
         mix = [(v, f, grid.second(b, pair(v, f))) for b, (v, f) in enumerate(mix_first)]
+        down = [
+            project_back([hold(v)], [(full_d, 0)], quarters, dtype)
+            for v, dtype in ((act[0], F32), (act[1], BF))
+        ]
+        last[:] = [down[0][0], down[1][0]]
         d_mix, g_out = weight_grad_pieces(
             [p for b in both for p in mix[b][:2] + (hold(mix[b][2]),)], gated
         )
         g_out = grid.scatter_grad(mark(g_out))
         g_ud = mark(jnp.concatenate([hold(g_up), g_down], axis=1))
         g_ud_moved = grid.swap(g_ud)
-        down_moved = [grid.second(b, hold(down[b][0])) for b in both]
+        down_moved = [grid.second(b, hold(down[1][b])) for b in both]
         d_v, d_gate, d_q, d_k = retain_back(
             hold(d_mix), gate, qk, values, full_o, col_info, row_info, cos_table, sin_table,
             log_gamma, heads, micro,
         )
         mark(d_v)
         g_vg = grid.scatter_grad(grad(h1, [d_v, d_gate]))
-        down = [reduce_second(b, down[b][1], down_moved[b]) for b in both]
-        outs = project_back(
-            [d_q, d_k, d_v, hold(d_gate)],
+        down = [reduce_second(b, down[0][b], down_moved[b]) for b in both]
+        kept, moved = exchange_rows(
+            [hold(d_q), d_k, d_v, d_gate],
             [(full_qk, 0), (full_qk, 1), (full_vg, 0), (full_vg, 1)],
         )
-        mark(outs[0][0])
-        moved = [grid.second(b, outs[b][0]) for b in both]
         g_qk = grid.scatter_grad(grad(h1, [d_q, d_k]))
         output = mark(
             jnp.concatenate(
@@ -800,7 +831,7 @@
         )
         output_moved = grid.swap(output)
         g_ud = settle(g_ud, g_ud_moved)
-        sums = [reduce_second(b, outs[b][1], moved[b]) for b in both]
+        sums = [reduce_second(b, kept[b], moved[b]) for b in both]
         g_out = await_(g_out)[0]
         g_out_moved = grid.swap(g_out)
         output = settle(output, output_moved)

time: 628 us -> 624 us (level)
  waiting for transfers between devices: 250 us -> 212 us
  Pallas kernels: 168 us -> 192 us
  starting transfers between devices: 91.5 us -> 98.7 us
    ppermute x49, waiting for transfers between devices: 231 us -> 193 us  [send(): return lax.ppermute(value, AXES, found)]
    pallas_call x3 -> x7, Pallas kernels: 35.6 us -> 57.9 us  [project_back(): call(body, (width // tile,), [spec(rows, k, lambda j: (0, 0)) for k in si...]
    pallas_call x4 -> x2, Pallas kernels: 38.9 us -> 22 us  [weight_grad(): call(body, (width // tile,), [spec(rows, tile, lambda i: (0, i))] + [spec...]
    pallas_call x0 -> x2, Pallas kernels: none -> 16.8 us  [weight_grad_rows(): call(body, (width // tile,), [spec(rows, tile, lambda i, b=b: (b, i)) for...]
    ppermute x49, starting transfers between devices: 90.5 us -> 97.7 us  [send(): return lax.ppermute(value, AXES, found)]
    pallas_call x1 -> x2, Pallas kernels: 12.5 us -> 16.1 us  [feed_up(): call(body, (steps,), [ANY] * n + [spec(width, tile, lambda j: (0, j))], [...]
    unnamed x111 -> x109, local copies, waits for them, and re-layouts: 12.9 us -> 10.4 us
  transfers between devices with their start and end apart: 58 -> 59, of which waited for: 33 -> 35; matrix products, arithmetic and copies ran while one was open for 14% -> 15% of each run, Pallas kernels for 24% -> 31%
where the time goes in v6:
time: 624 us; the launch traced here: 616 us
  waiting for transfers between devices  212 us (34%)
  Pallas kernels  192 us (31%)
  starting transfers between devices  98.7 us (16%)
  other arithmetic  77.5 us (12%)
  local copies, waits for them, and re-layouts  20.2 us (3%)
  between operations  15.8 us (3%)
    ppermute x49, waiting for transfers between devices, send(): return lax.ppermute(value, AXES, found)  193 us
    ppermute x49, starting transfers between devices, send(): return lax.ppermute(value, AXES, found)  97.7 us
    pallas_call x7, Pallas kernels, project_back(): call(body, (width // tile,), [spec(rows, k, lambda j: (0, 0)) for k in si...  57.9 us
    pallas_call x2, Pallas kernels, weight_grad(): call(body, (width // tile,), [spec(rows, tile, lambda i: (0, i))] + [spec...  22 us
    pallas_call x1, Pallas kernels, retain_back(): call(body, (heads, micro), [per_row(rows, width), spec(width, VAL_HEAD, l...  17.5 us
    pallas_call x2, Pallas kernels, weight_grad_rows(): call(body, (width // tile,), [spec(rows, tile, lambda i, b=b: (b, i)) for...  16.8 us
    pallas_call x2, Pallas kernels, feed_up(): call(body, (steps,), [ANY] * n + [spec(width, tile, lambda j: (0, j))], [...  16.1 us
    pallas_call x1, Pallas kernels, project_plain(): call(body, (cols // tile,), [spec(rows, width, lambda j: (0, 0)), spec(wi...  15.2 us
  transfers between devices with their start and end apart: 59, of which 35 were waited for; matrix products, arithmetic and copies ran while one was open for 15% of the time, Pallas kernels for 31%

profile of v6, /device:TPU:1, one launch (start us, length us, event | category | flops | bytes accessed | tf_op | source)
XLA Modules:
  0.0 615.9 jit_solution(3249134435157006718)
XLA Ops:
  24.3 11.6 %collective-permute-done.1 = bf16[256,3072]{1,0:T(8,128)(2,1)} collective-permute-done((bf16[256,3072]{1,0:T(8,128)(2,1)}, bf16[256,3072]{1,0:T(8,128)(2,1)}, u32[]{:S(2)}, u32[]{:S(2)}) %collective-permute-start.1) | collective-permute-done | bytes 1572896 | tf_op jit(solution)/shard_map/ppermute | solution.py:57
  45.7 10.1 %collective-permute-done = bf16[256,2048]{1,0:T(8,128)(2,1)} collective-permute-done((bf16[256,2048]{1,0:T(8,128)(2,1)}, bf16[256,2048]{1,0:T(8,128)(2,1)}, u32[]{:S(2)}, u32[]{:S(2)}) %collective-permute-start) | collective-permute-done | bytes 1048608 | tf_op jit(solution)/shard_map/ppermute | solution.py:57
  65.7 6.7 %collective-permute-done.2.refs_1_ = bf16[128,2048]{1,0:T(8,128)(2,1)} collective-permute-done((bf16[128,2048]{1,0:T(8,128)(2,1)S(1)}, bf16[128,2048]{1,0:T(8,128)(2,1)}, u32[]{:S(2)}, u32[]{:S(2)}) %collective-permute-start.2) | collective-permute-done | bytes 524320 | tf_op jit(solution)/shard_map/ppermute | solution.py:57
  79.0 19.6 %collective-permute-done.6.refs_5_ = bf16[256,2048]{1,0:T(8,128)(2,1)S(1)} collective-permute-done((bf16[256,2048]{1,0:T(8,128)(2,1)S(1)}, bf16[256,2048]{1,0:T(8,128)(2,1)S(1)}, u32[]{:S(2)}, u32[]{:S(2)}) %collective-permute-start.6) | collective-permute-done | bytes 1048608 | tf_op jit(solution)/shard_map/ppermute | solution.py:57
  98.6 18.3 %collective-permute-done.4.refs_2_ = bf16[256,2048]{1,0:T(8,128)(2,1)S(1)} collective-permute-done((bf16[256,2048]{1,0:T(8,128)(2,1)S(1)}, bf16[256,2048]{1,0:T(8,128)(2,1)S(1)}, u32[]{:S(2)}, u32[]{:S(2)}) %collective-permute-start.4) | collective-permute-done | bytes 1048608 | tf_op jit(solution)/shard_map/ppermute | solution.py:57
  129.1 10.0 %shard_map.186 = (bf16[1024,2048]{1,0:T(8,128)(2,1)}, bf16[1024,1024]{1,0:T(8,128)(2,1)}) custom-call(bf16[128,2048]{1,0:T(8,128)(2,1)} %copy-done.32, bf16[128,2048]{1,0:T(8,128)(2,1)} %collective-permute-done.2.refs_1_, bf16[256,2048]{1,0:T(8,128)(2,1)} %copy-done.49, bf16[128,2048]{1,0:T(8,128)(2,1)} %copy-done.31, ...), custom_call_target="tpu_custom_call" | custom-call | flops 4294967296 | bytes 14680064 | tf_op jit(solution)/shard_map/pallas_call | solution.py:216
  139.1 9.3 %collective-permute-done.9 = bf16[512,2048]{1,0:T(8,128)(2,1)} collective-permute-done((bf16[512,2048]{1,0:T(8,128)(2,1)}, bf16[512,2048]{1,0:T(8,128)(2,1)}, u32[]{:S(2)}, u32[]{:S(2)}) %collective-permute-start.9) | collective-permute-done | bytes 2097184 | tf_op jit(solution)/shard_map/ppermute | solution.py:57
  156.6 15.2 %shard_map.187 = (bf16[1024,1024]{1,0:T(8,128)(2,1)}, f32[1024,1024]{1,0:T(8,128)}) custom-call(bf16[1024,2048]{1,0:T(8,128)(2,1)} %get-tuple-element.217.h_ref.left_ref, bf16[2048,2048]{1,0:T(8,128)(2,1)} %all-gather.8.cloned.1.call-done.w_ref.refs_6_.refs_7_), custom_call_target="tpu_custom_call" | custom-call | flops 8589934592 | bytes 20971520 | tf_op jit(solution)/shard_map/pallas_call | solution.py:255
  177.9 7.6 %shard_map.188.refs_0_.refs_6_ = bf16[1024,1024]{1,0:T(8,128)(2,1)} custom-call(bf16[1024,1024]{1,0:T(8,128)(2,1)} %get-tuple-element.138.q_ref.k_ref, bf16[1024,1024]{1,0:T(8,128)(2,1)} %get-tuple-element.138.q_ref.k_ref, bf16[1024,1024]{1,0:T(8,128)(2,1)} %get-tuple-element.147.v_ref, f32[1024,1024]{1,0:T(8,128)} %get-tuple-element.148.gate_ref, ...), custom_call_target="tpu_custom_call" | custom-call | flops 1610612736 | bytes 10485760 | tf_op jit(solution)/shard_map/pallas_call | solution.py:303
  198.4 6.8 %shard_map.190 = (f32[256,2048]{1,0:T(8,128)}, f32[256,2048]{1,0:T(8,128)}) custom-call(bf16[1024,1024]{1,0:T(8,128)(2,1)} %shard_map.188.refs_0_.refs_6_, bf16[2048,1024]{1,0:T(8,128)(2,1)} %all-gather.10.cloned.1.call-done.refs_1_.wo), custom_call_target="tpu_custom_call" | custom-call | flops 2147483648 | bytes 9437184 | tf_op jit(solution)/shard_map/pallas_call | solution.py:385
  209.5 13.8 %collective-permute-done.12 = bf16[256,2048]{1,0:T(8,128)(2,1)} collective-permute-done((bf16[256,2048]{1,0:T(8,128)(2,1)}, bf16[256,2048]{1,0:T(8,128)(2,1)}, u32[]{:S(2)}, u32[]{:S(2)}) %collective-permute-start.12) | collective-permute-done | bytes 1048608 | tf_op jit(solution)/shard_map/ppermute | solution.py:57
  229.6 6.9 %collective-permute-done.15 = bf16[128,2048]{1,0:T(8,128)(2,1)S(1)} collective-permute-done((bf16[128,2048]{1,0:T(8,128)(2,1)S(1)}, bf16[128,2048]{1,0:T(8,128)(2,1)S(1)}, u32[]{:S(2)}, u32[]{:S(2)}) %collective-permute-start.15) | collective-permute-done | bytes 524320 | tf_op jit(solution)/shard_map/ppermute | solution.py:57
  259.9 8.1 %shard_map.192 = (bf16[512,2048]{1,0:T(8,128)(2,1)}, bf16[512,1024]{1,0:T(8,128)(2,1)}, f32[512,1024]{1,0:T(8,128)}) custom-call(bf16[128,2048]{1,0:T(8,128)(2,1)} %copy-done.33, bf16[128,2048]{1,0:T(8,128)(2,1)} %copy-done.42, bf16[128,2048]{1,0:T(8,128)(2,1)} %copy-done.34, bf16[128,2048]{1,0:T(8,128)(2,1)} %copy-done.44, ...), custom_call_target="tpu_custom_call" | custom-call | flops 2147483648 | bytes 11534336 | tf_op jit(solution)/shard_map/pallas_call | solution.py:355
  268.1 12.8 %collective-permute-done.21.refs_1_ = bf16[256,2048]{1,0:T(8,128)(2,1)} collective-permute-done((bf16[256,2048]{1,0:T(8,128)(2,1)}, bf16[256,2048]{1,0:T(8,128)(2,1)}, u32[]{:S(2)}, u32[]{:S(2)}) %collective-permute-start.21) | collective-permute-done | bytes 1048608 | tf_op jit(solution)/shard_map/ppermute | solution.py:57
  281.4 8.0 %shard_map.193 = (bf16[512,2048]{1,0:T(8,128)(2,1)}, bf16[512,1024]{1,0:T(8,128)(2,1)}, f32[512,1024]{1,0:T(8,128)}) custom-call(bf16[256,2048]{1,0:T(8,128)(2,1)} %collective-permute-done.20.refs_0_, bf16[256,2048]{1,0:T(8,128)(2,1)} %collective-permute-done.21.refs_1_, bf16[2048,1024]{1,0:T(8,128)(2,1)} %all-gather.12.cloned.1.call-done.refs_4_.refs_2_.up_ref.refs_1_), custom_call_target="tpu_custom_call" | custom-call | flops 2147483648 | bytes 11534336 | tf_op jit(solution)/shard_map/pallas_call | solution.py:355
  289.5 8.4 %shard_map.194 = bf16[2048,1024]{1,0:T(8,128)(2,1)} custom-call(bf16[1024,2048]{1,0:T(8,128)(2,1)} %shard_map.191.refs_0_.refs_1_.cot_ref, bf16[1024,2048]{1,0:T(8,128)(2,1)} %shard_map.191.refs_0_.refs_1_.cot_ref, bf16[512,1024]{1,0:T(8,128)(2,1)} %get-tuple-element.191.refs_2_.refs_0_, bf16[512,1024]{1,0:T(8,128)(2,1)} %get-tuple-element.193.refs_3_.refs_0_), custom_call_target="tpu_custom_call" | custom-call | flops 4294967296 | bytes 10485760 | tf_op jit(solution)/shard_map/pallas_call | solution.py:550
  298.2 14.2 %shard_map.195 = (bf16[1024,1024]{1,0:T(8,128)(2,1)}, bf16[256,2048]{1,0:T(8,128)(2,1)}, bf16[256,2048]{1,0:T(8,128)(2,1)}) custom-call(bf16[1024,2048]{1,0:T(8,128)(2,1)} %shard_map.191.refs_0_.refs_1_.cot_ref, bf16[2048,1024]{1,0:T(8,128)(2,1)} %all-gather.14.cloned.1.call-done.down_ref.refs_1_, ...), custom_call_target="tpu_custom_call" | custom-call | flops 6442450944 | bytes 23068672 | tf_op jit(solution)/shard_map/pallas_call | solution.py:431
  314.0 6.8 %shard_map.196 = (f32[256,2048]{1,0:T(8,128)}, f32[256,2048]{1,0:T(8,128)}) custom-call(bf16[1024,1024]{1,0:T(8,128)(2,1)} %get-tuple-element.176.refs_0_.refs_2_.refs_3_, bf16[2048,1024]{1,0:T(8,128)(2,1)} %all-gather.12.cloned.1.call-done.refs_4_.refs_2_.up_ref.refs_1_), custom_call_target="tpu_custom_call" | custom-call | flops 2147483648 | bytes 9437184 | tf_op jit(solution)/shard_map/pallas_call | solution.py:385
  320.8 8.4 %shard_map.197 = bf16[2048,1024]{1,0:T(8,128)(2,1)} custom-call(bf16[512,2048]{1,0:T(8,128)(2,1)} %get-tuple-element.182.refs_0_, bf16[512,2048]{1,0:T(8,128)(2,1)} %get-tuple-element.183.refs_1_, bf16[1024,1024]{1,0:T(8,128)(2,1)} %get-tuple-element.176.refs_0_.refs_2_.refs_3_, bf16[1024,1024]{1,0:T(8,128)(2,1)} %get-tuple-element.176.refs_0_.refs_2_.refs_3_), custom_call_target="tpu_custom_call" | custom-call | flops 4294967296 | bytes 10485760 | tf_op jit(solution)/shard_map/pallas_call | solution.py:550
  340.5 8.6 %collective-permute-done.25 = bf16[128,2048]{1,0:T(8,128)(2,1)S(1)} collective-permute-done((bf16[128,2048]{1,0:T(8,128)(2,1)}, bf16[128,2048]{1,0:T(8,128)(2,1)S(1)}, u32[]{:S(2)}, u32[]{:S(2)}) %collective-permute-start.25) | collective-permute-done | bytes 524320 | tf_op jit(solution)/shard_map/ppermute | solution.py:57
  387.0 10.1 %shard_map.200 = (bf16[1024,2048]{1,0:T(8,128)(2,1)}, bf16[2048,1024]{1,0:T(8,128)(2,1)}) custom-call(bf16[128,2048]{1,0:T(8,128)(2,1)} %get-tuple-element.267.refs_0_, bf16[128,2048]{1,0:T(8,128)(2,1)} %collective-permute-done.27.refs_1_, bf16[256,2048]{1,0:T(8,128)(2,1)} %collective-permute-done.28.refs_2_, bf16[128,2048]{1,0:T(8,128)(2,1)} %copy-done.35, ...), custom_call_target="tpu_custom_call" | custom-call | flops 4294967296 | bytes 10485760 | tf_op jit(solution)/shard_map/pallas_call | solution.py:581
  402.3 17.5 %shard_map.201 = (bf16[1024,1024]{1,0:T(8,128)(2,1)}, bf16[1024,1024]{1,0:T(8,128)(2,1)}, bf16[1024,512]{1,0:T(8,128)(2,1)}, bf16[1024,512]{1,0:T(8,128)(2,1)}) custom-call(bf16[1024,2048]{1,0:T(8,128)(2,1)} %get-tuple-element.202.mix_ref, bf16[2048,1024]{1,0:T(8,128)(2,1)} %all-gather.10.cloned.1.call-done.refs_1_.wo, ...), custom_call_target="tpu_custom_call" | custom-call | flops 9663676416 | bytes 29360128 | tf_op jit(solution)/shard_map/pallas_call | solution.py:489
  419.8 13.5 %shard_map.202 = bf16[2048,2048]{1,0:T(8,128)(2,1)} custom-call(bf16[1024,2048]{1,0:T(8,128)(2,1)} %get-tuple-element.217.h_ref.left_ref, bf16[1024,1024]{1,0:T(8,128)(2,1)} %get-tuple-element.203.refs_0_.refs_2_, bf16[1024,1024]{1,0:T(8,128)(2,1)} %get-tuple-element.205.refs_1_.refs_3_), custom_call_target="tpu_custom_call" | custom-call | flops 8589934592 | bytes 16777216 | tf_op jit(solution)/shard_map/pallas_call | solution.py:527
  435.9 7.6 %collective-permute-start.37 = (bf16[256,2048]{1,0:T(8,128)(2,1)}, bf16[256,2048]{1,0:T(8,128)(2,1)}, u32[]{:S(2)}, u32[]{:S(2)}) collective-permute-start(bf16[256,2048]{1,0:T(8,128)(2,1)} %constant_dynamic-update-slice_fusion.2), channel_id=1, source_target_pairs={{1,8},{3,10},{5,12},{7,14},{8,1},{10,3},{12,5},{14,7},{17,24},{19,... | collective-permute-start | bytes 3145736 | tf_op jit(solution)/shard_map/ppermute | solution.py:57
  443.4 10.4 %collective-permute-done.30 = bf16[256,2048]{1,0:T(8,128)(2,1)S(1)} collective-permute-done((bf16[256,2048]{1,0:T(8,128)(2,1)}, bf16[256,2048]{1,0:T(8,128)(2,1)S(1)}, u32[]{:S(2)}, u32[]{:S(2)}) %collective-permute-start.30) | collective-permute-done | bytes 1048608 | tf_op jit(solution)/shard_map/ppermute | solution.py:57
  458.3 12.9 %shard_map.203 = (bf16[256,2048]{1,0:T(8,128)(2,1)}, bf16[256,2048]{1,0:T(8,128)(2,1)}) custom-call(bf16[1024,512]{1,0:T(8,128)(2,1)} %get-tuple-element.215.refs_0_, bf16[1024,512]{1,0:T(8,128)(2,1)} %get-tuple-element.213.refs_1_, bf16[1024,1024]{1,0:T(8,128)(2,1)} %get-tuple-element.203.refs_0_.refs_2_, ...), custom_call_target="tpu_custom_call" | custom-call | flops 6442450944 | bytes 22020096 | tf_op jit(solution)/shard_map/pallas_call | solution.py:385
  471.3 12.7 %shard_map.204 = (f32[256,2048]{1,0:T(8,128)}, f32[256,2048]{1,0:T(8,128)}) custom-call(bf16[1024,512]{1,0:T(8,128)(2,1)} %get-tuple-element.215.refs_0_, bf16[1024,512]{1,0:T(8,128)(2,1)} %get-tuple-element.213.refs_1_, bf16[1024,1024]{1,0:T(8,128)(2,1)} %get-tuple-element.203.refs_0_.refs_2_, bf16[1024,1024]{1,0:T(8,128)(2,1)} %get-tuple-element.205.refs_1_.refs_3_, ...), custom_call_target="tpu_custom_call" | custom-call | flops 6442450944 | bytes 22020096 | tf_op jit(solution)/shard_map/pallas_call | solution.py:385
  484.0 8.5 %shard_map.205 = bf16[2048,1024]{1,0:T(8,128)(2,1)} custom-call(bf16[1024,2048]{1,0:T(8,128)(2,1)} %get-tuple-element.217.h_ref.left_ref, bf16[1024,512]{1,0:T(8,128)(2,1)} %get-tuple-element.215.refs_0_, bf16[1024,512]{1,0:T(8,128)(2,1)} %get-tuple-element.213.refs_1_), custom_call_target="tpu_custom_call" | custom-call | flops 4294967296 | bytes 10485760 | tf_op jit(solution)/shard_map/pallas_call | solution.py:527
  498.0 14.7 %collective-permute-start.34 = (bf16[256,2048]{1,0:T(8,128)(2,1)}, bf16[256,2048]{1,0:T(8,128)(2,1)}, u32[]{:S(2)}, u32[]{:S(2)}) collective-permute-start(bf16[256,2048]{1,0:T(8,128)(2,1)} %pad_maximum_fusion.11), channel_id=1, source_target_pairs={{1,8},{3,10},{5,12},{7,14},{8,1},{10,3},{12,5},{14,7},{17,24},{19,... | collective-permute-start | bytes 3145736 | tf_op jit(solution)/shard_map/ppermute | solution.py:57
  560.6 6.4 %collective-permute-start.47 = (bf16[256,2048]{1,0:T(8,128)(2,1)}, bf16[256,2048]{1,0:T(8,128)(2,1)S(1)}, u32[]{:S(2)}, u32[]{:S(2)}) collective-permute-start(bf16[256,2048]{1,0:T(8,128)(2,1)} %reduce-scatter.14.cloned.1.call-done), channel_id=1, source_target_pairs={{1,8},{3,10},{5,12},{7,14},{8,1},{10,3},{12,5},{14,7},{17,24},{19,... | collective-permute-start | bytes 3145736 | tf_op jit(solution)/shard_map/ppermute | solution.py:57
  567.0 13.1 %collective-permute-done.47 = bf16[256,2048]{1,0:T(8,128)(2,1)S(1)} collective-permute-done((bf16[256,2048]{1,0:T(8,128)(2,1)}, bf16[256,2048]{1,0:T(8,128)(2,1)S(1)}, u32[]{:S(2)}, u32[]{:S(2)}) %collective-permute-start.47) | collective-permute-done | bytes 1048608 | tf_op jit(solution)/shard_map/ppermute | solution.py:57
  580.3 12.7 %reduce-scatter.12.cloned.1.call-done = bf16[256,1024]{1,0:T(8,128)(2,1)} async-done(((bf16[2048,1024]{1,0:T(8,128)(2,1)}), bf16[256,1024]{1,0:T(8,128)(2,1)}) %reduce-scatter.12.cloned.1.call-update) | async-done | bytes 524304 | tf_op jit(solution)/shard_map/reduce_scatter | solution.py:84
  (335 shorter events, 248.7 us)
Async XLA Ops:
  7.2 54.3 %all-gather.6.cloned.1.call-start = ((), (), s32[]{:S(2)}) async-start(), calls=%async_computation.5 | async-start | bytes 2621440 | tf_op jit(solution)/shard_map/all_gather | solution.py:89
  10.1 146.5 %all-gather.8.cloned.1.call-start = ((), (), s32[]{:S(2)}) async-start(), calls=%async_computation.6 | async-start | bytes 9437184 | tf_op jit(solution)/shard_map/all_gather | solution.py:81
  12.7 23.2 %collective-permute-start.1 = (bf16[256,3072]{1,0:T(8,128)(2,1)}, bf16[256,3072]{1,0:T(8,128)(2,1)}, u32[]{:S(2)}, u32[]{:S(2)}) collective-permute-start(bf16[256,3072]{1,0:T(8,128)(2,1)} %pad_maximum_fusion.2), channel_id=1, source_target_pairs={{1,8},{3,10},{5,12},{7,14},{8,1},{10,3},{12,5},{14,7},{17,24},{19,... | collective-permute-start | bytes 4718600 | tf_op jit(solution)/shard_map/ppermute | solution.py:57
  39.0 150.5 %all-gather.10.cloned.1.call-start = ((), (), s32[]{:S(2)}) async-start(), calls=%async_computation.7 | async-start | bytes 4718592 | tf_op jit(solution)/shard_map/all_gather | solution.py:81
  42.5 22.4 %collective-permute-start.3 = (bf16[2,512]{1,0:T(2,128)(2,1)S(1)}, bf16[2,512]{1,0:T(2,128)(2,1)S(1)}, u32[]{:S(2)}, u32[]{:S(2)}) collective-permute-start(bf16[2,512]{1,0:T(2,128)(2,1)S(1)} %bitcast.101), channel_id=1, source_target_pairs={{1,8},{3,10},{5,12},{7,14},{8,1},{10,3},{12,5},{14,7},{17,24},{19,... | collective-permute-start | bytes 6152 | tf_op jit(solution)/shard_map/ppermute | solution.py:57
  58.2 201.7 %all-gather.12.cloned.1.call-start = ((), (), s32[]{:S(2)}) async-start(), calls=%async_computation.8 | async-start | bytes 4718592 | tf_op jit(solution)/shard_map/all_gather | solution.py:81
  61.5 56.3 %collective-permute-start.7 = (bf16[1024,1024]{1,0:T(8,128)(2,1)}, bf16[1024,1024]{1,0:T(8,128)(2,1)S(1)}, u32[]{:S(2)}, u32[]{:S(2)}) collective-permute-start(bf16[1024,1024]{1,0:T(8,128)(2,1)} %all-gather.6.cloned.1.call-done), channel_id=1, source_target_pairs={{1,8},{3,10},{5,12},{7,14},{8,1},{10,3},{12,5},{14,7},{17,24},{19,... | collective-permute-start | bytes 6291464 | tf_op jit(solution)/shard_map/ppermute | solution.py:57
  75.4 23.2 %collective-permute-start.6 = (bf16[256,2048]{1,0:T(8,128)(2,1)S(1)}, bf16[256,2048]{1,0:T(8,128)(2,1)S(1)}, u32[]{:S(2)}, u32[]{:S(2)}) collective-permute-start(bf16[256,2048]{1,0:T(8,128)(2,1)S(1)} %pad_maximum_fusion.4), channel_id=1, source_target_pairs={{0,16},{1,17},{2,18},{3,19},{4,20},{5,21},{6,22},{7,23},{8,24},{9,... | collective-permute-start | bytes 3145736 | tf_op jit(solution)/shard_map/ppermute | solution.py:57
  76.7 40.2 %collective-permute-start.4 = (bf16[256,2048]{1,0:T(8,128)(2,1)S(1)}, bf16[256,2048]{1,0:T(8,128)(2,1)S(1)}, u32[]{:S(2)}, u32[]{:S(2)}) collective-permute-start(bf16[256,2048]{1,0:T(8,128)(2,1)S(1)} %pad_maximum_fusion.3), channel_id=1, source_target_pairs={{0,1},{1,0},{2,3},{3,2},{4,5},{5,4},{6,7},{7,6},{8,9},{9,8},{10,11... | collective-permute-start | bytes 3145736 | tf_op jit(solution)/shard_map/ppermute | solution.py:57
  120.7 27.7 %collective-permute-start.9 = (bf16[512,2048]{1,0:T(8,128)(2,1)}, bf16[512,2048]{1,0:T(8,128)(2,1)}, u32[]{:S(2)}, u32[]{:S(2)}) collective-permute-start(bf16[512,2048]{1,0:T(8,128)(2,1)} %pad_maximum_fusion), channel_id=1, source_target_pairs={{1,8},{3,10},{5,12},{7,14},{8,1},{10,3},{12,5},{14,7},{17,24},{19,... | collective-permute-start | bytes 6291464 | tf_op jit(solution)/shard_map/ppermute | solution.py:57
  152.6 145.6 %all-gather.14.cloned.1.call-start = ((), (), s32[]{:S(2)}) async-start(), calls=%async_computation.9 | async-start | bytes 4718592 | tf_op jit(solution)/shard_map/all_gather | solution.py:81
  176.3 28.9 %collective-permute-start.14 = (bf16[256,2048]{1,0:T(8,128)(2,1)}, bf16[256,2048]{1,0:T(8,128)(2,1)}, u32[]{:S(2)}, u32[]{:S(2)}) collective-permute-start(bf16[256,2048]{1,0:T(8,128)(2,1)} %pad_maximum_fusion.6), channel_id=1, source_target_pairs={{0,16},{1,17},{2,18},{3,19},{4,20},{5,21},{6,22},{7,23},{8,24},{9,... | collective-permute-start | bytes 3145736 | tf_op jit(solution)/shard_map/ppermute | solution.py:57
  176.5 28.7 %collective-permute-start.13 = (bf16[256,2048]{1,0:T(8,128)(2,1)}, bf16[256,2048]{1,0:T(8,128)(2,1)}, u32[]{:S(2)}, u32[]{:S(2)}) collective-permute-start(bf16[256,2048]{1,0:T(8,128)(2,1)} %pad_maximum_fusion.5), channel_id=1, source_target_pairs={{0,1},{1,0},{2,3},{3,2},{4,5},{5,4},{6,7},{7,6},{8,9},{9,8},{10,11... | collective-permute-start | bytes 3145736 | tf_op jit(solution)/shard_map/ppermute | solution.py:57
  195.9 27.5 %collective-permute-start.12 = (bf16[256,2048]{1,0:T(8,128)(2,1)}, bf16[256,2048]{1,0:T(8,128)(2,1)}, u32[]{:S(2)}, u32[]{:S(2)}) collective-permute-start(bf16[256,2048]{1,0:T(8,128)(2,1)} %get-tuple-element.150), channel_id=1, source_target_pairs={{0,1},{1,0},{2,3},{3,2},{4,5},{5,4},{6,7},{7,6},{8,9},{9,8},{10,11... | collective-permute-start | bytes 3145736 | tf_op jit(solution)/shard_map/ppermute | solution.py:57
  197.1 161.1 %reduce-scatter.6.cloned.1.call-start = ((), (), s32[]{:S(2)}) async-start(), calls=%async_computation.10 | async-start | bytes 4718592 | tf_op jit(solution)/shard_map/reduce_scatter | solution.py:84
  197.2 28.9 %collective-permute-start.16 = (bf16[256,2048]{1,0:T(8,128)(2,1)}, bf16[256,2048]{1,0:T(8,128)(2,1)}, u32[]{:S(2)}, u32[]{:S(2)}) collective-permute-start(bf16[256,2048]{1,0:T(8,128)(2,1)} %get-tuple-element.157), channel_id=1, source_target_pairs={{0,16},{1,17},{2,18},{3,19},{4,20},{5,21},{6,22},{7,23},{8,24},{9,... | collective-permute-start | bytes 3145736 | tf_op jit(solution)/shard_map/ppermute | solution.py:57
  257.7 23.2 %collective-permute-start.21 = (bf16[256,2048]{1,0:T(8,128)(2,1)}, bf16[256,2048]{1,0:T(8,128)(2,1)}, u32[]{:S(2)}, u32[]{:S(2)}) collective-permute-start(bf16[256,2048]{1,0:T(8,128)(2,1)} %pad_maximum_fusion.8), channel_id=1, source_target_pairs={{0,16},{1,17},{2,18},{3,19},{4,20},{5,21},{6,22},{7,23},{8,24},{9,... | collective-permute-start | bytes 3145736 | tf_op jit(solution)/shard_map/ppermute | solution.py:57
  258.5 22.9 %collective-permute-start.20 = (bf16[256,2048]{1,0:T(8,128)(2,1)}, bf16[256,2048]{1,0:T(8,128)(2,1)}, u32[]{:S(2)}, u32[]{:S(2)}) collective-permute-start(bf16[256,2048]{1,0:T(8,128)(2,1)} %pad_maximum_fusion.7), channel_id=1, source_target_pairs={{0,1},{1,0},{2,3},{3,2},{4,5},{5,4},{6,7},{7,6},{8,9},{9,8},{10,11... | collective-permute-start | bytes 3145736 | tf_op jit(solution)/shard_map/ppermute | solution.py:57
  297.9 101.6 %reduce-scatter.8.cloned.1.call-start = ((), (), s32[]{:S(2)}) async-start(), calls=%async_computation.11 | async-start | bytes 4718592 | tf_op jit(solution)/shard_map/reduce_scatter | solution.py:84
  312.4 22.2 %collective-permute-start.23 = (bf16[256,2048]{1,0:T(8,128)(2,1)}, bf16[256,2048]{1,0:T(8,128)(2,1)}, u32[]{:S(2)}, u32[]{:S(2)}) collective-permute-start(bf16[256,2048]{1,0:T(8,128)(2,1)} %get-tuple-element.180), channel_id=1, source_target_pairs={{0,1},{1,0},{2,3},{3,2},{4,5},{5,4},{6,7},{7,6},{8,9},{9,8},{10,11... | collective-permute-start | bytes 3145736 | tf_op jit(solution)/shard_map/ppermute | solution.py:57
  313.9 23.1 %collective-permute-start.22 = (bf16[256,2048]{1,0:T(8,128)(2,1)}, bf16[256,2048]{1,0:T(8,128)(2,1)}, u32[]{:S(2)}, u32[]{:S(2)}) collective-permute-start(bf16[256,2048]{1,0:T(8,128)(2,1)} %get-tuple-element.178), channel_id=1, source_target_pairs={{0,16},{1,17},{2,18},{3,19},{4,20},{5,21},{6,22},{7,23},{8,24},{9,... | collective-permute-start | bytes 3145736 | tf_op jit(solution)/shard_map/ppermute | solution.py:57
  338.9 181.0 %reduce-scatter.10.cloned.1.call-start = ((), (), s32[]{:S(2)}) async-start(), calls=%async_computation.12 | async-start | bytes 4718592 | tf_op jit(solution)/shard_map/reduce_scatter | solution.py:84
  397.2 163.4 %reduce-scatter.14.cloned.1.call-start = ((), (), s32[]{:S(2)}) async-start(), calls=%async_computation.14 | async-start | bytes 9437184 | tf_op jit(solution)/shard_map/reduce_scatter | solution.py:84
  433.3 159.7 %reduce-scatter.12.cloned.1.call-start = ((), (), s32[]{:S(2)}) async-start(), calls=%async_computation.13 | async-start | bytes 4718592 | tf_op jit(solution)/shard_map/reduce_scatter | solution.py:84
  434.7 21.7 %collective-permute-start.32 = (bf16[256,2048]{1,0:T(8,128)(2,1)S(1)}, bf16[256,2048]{1,0:T(8,128)(2,1)S(1)}, u32[]{:S(2)}, u32[]{:S(2)}) collective-permute-start(bf16[256,2048]{1,0:T(8,128)(2,1)S(1)} %copy-done.47), channel_id=1, source_target_pairs={{0,16},{1,17},{2,18},{3,19},{4,20},{5,21},{6,22},{7,23},{8,24},{9,... | collective-permute-start | bytes 3145736 | tf_op jit(solution)/shard_map/ppermute | solution.py:57
  435.9 76.9 %collective-permute-start.37 = (bf16[256,2048]{1,0:T(8,128)(2,1)}, bf16[256,2048]{1,0:T(8,128)(2,1)}, u32[]{:S(2)}, u32[]{:S(2)}) collective-permute-start(bf16[256,2048]{1,0:T(8,128)(2,1)} %constant_dynamic-update-slice_fusion.2), channel_id=1, source_target_pairs={{1,8},{3,10},{5,12},{7,14},{8,1},{10,3},{12,5},{14,7},{17,24},{19,... | collective-permute-start | bytes 3145736 | tf_op jit(solution)/shard_map/ppermute | solution.py:57
  454.8 40.6 %collective-permute-start.31 = (bf16[128,2048]{1,0:T(8,128)(2,1)}, bf16[128,2048]{1,0:T(8,128)(2,1)}, u32[]{:S(2)}, u32[]{:S(2)}) collective-permute-start(bf16[128,2048]{1,0:T(8,128)(2,1)} %add_convert_fusion.5), channel_id=1, source_target_pairs={{0,16},{1,17},{2,18},{3,19},{4,20},{5,21},{6,22},{7,23},{8,24},{9,... | collective-permute-start | bytes 1572872 | tf_op jit(solution)/shard_map/ppermute | solution.py:57
  457.4 35.1 %collective-permute-start.33 = (bf16[128,2048]{1,0:T(8,128)(2,1)}, bf16[128,2048]{1,0:T(8,128)(2,1)S(1)}, u32[]{:S(2)}, u32[]{:S(2)}) collective-permute-start(bf16[128,2048]{1,0:T(8,128)(2,1)} %add_convert_fusion.4), channel_id=1, source_target_pairs={{0,1},{1,0},{2,3},{3,2},{4,5},{5,4},{6,7},{7,6},{8,9},{9,8},{10,11... | collective-permute-start | bytes 1572872 | tf_op jit(solution)/shard_map/ppermute | solution.py:57
  471.3 43.8 %collective-permute-start.36 = (bf16[256,2048]{1,0:T(8,128)(2,1)}, bf16[256,2048]{1,0:T(8,128)(2,1)}, u32[]{:S(2)}, u32[]{:S(2)}) collective-permute-start(bf16[256,2048]{1,0:T(8,128)(2,1)} %get-tuple-element.214), channel_id=1, source_target_pairs={{0,1},{1,0},{2,3},{3,2},{4,5},{5,4},{6,7},{7,6},{8,9},{9,8},{10,11... | collective-permute-start | bytes 3145736 | tf_op jit(solution)/shard_map/ppermute | solution.py:57
  484.0 33.9 %collective-permute-start.35 = (bf16[256,2048]{1,0:T(8,128)(2,1)}, bf16[256,2048]{1,0:T(8,128)(2,1)}, u32[]{:S(2)}, u32[]{:S(2)}) collective-permute-start(bf16[256,2048]{1,0:T(8,128)(2,1)} %get-tuple-element.221), channel_id=1, source_target_pairs={{0,16},{1,17},{2,18},{3,19},{4,20},{5,21},{6,22},{7,23},{8,24},{9,... | collective-permute-start | bytes 3145736 | tf_op jit(solution)/shard_map/ppermute | solution.py:57
  498.0 30.5 %collective-permute-start.34 = (bf16[256,2048]{1,0:T(8,128)(2,1)}, bf16[256,2048]{1,0:T(8,128)(2,1)}, u32[]{:S(2)}, u32[]{:S(2)}) collective-permute-start(bf16[256,2048]{1,0:T(8,128)(2,1)} %pad_maximum_fusion.11), channel_id=1, source_target_pairs={{1,8},{3,10},{5,12},{7,14},{8,1},{10,3},{12,5},{14,7},{17,24},{19,... | collective-permute-start | bytes 3145736 | tf_op jit(solution)/shard_map/ppermute | solution.py:57
  519.9 22.7 %collective-permute-start.41 = (bf16[256,1024]{1,0:T(8,128)(2,1)}, bf16[256,1024]{1,0:T(8,128)(2,1)S(1)}, u32[]{:S(2)}, u32[]{:S(2)}) collective-permute-start(bf16[256,1024]{1,0:T(8,128)(2,1)} %reduce-scatter.10.cloned.1.call-done), channel_id=1, source_target_pairs={{1,8},{3,10},{5,12},{7,14},{8,1},{10,3},{12,5},{14,7},{17,24},{19,... | collective-permute-start | bytes 1572872 | tf_op jit(solution)/shard_map/ppermute | solution.py:57
  (77 other events, 798.1 us)
Sparse Core Ops, SparseCore 0:
  10.2 48.0 all-gather.5
  60.5 81.1 all-gather.7
  143.9 45.6 all-gather.9
  191.0 45.8 all-gather.11
  238.4 45.8 all-gather.13
  298.0 50.9 reduce-scatter.5
  351.3 48.1 reduce-scatter.7
  401.8 50.5 reduce-scatter.9
  454.7 87.7 reduce-scatter.13
  544.6 48.3 reduce-scatter.11

commit v7 on v6

--- a/solution.py
+++ b/solution.py
@@ -534,6 +534,43 @@
         2 * rows * width * cols,
         2 * (rows * (width + cols) + width * cols),
     )(left, *rights)
+
+
+def weight_grad_part(index, left, rights, blocks, received=None):
+    rows, width = left.shape
+    sizes = [v.shape[1] for v in rights]
+    cols, tile = sum(sizes), width // (2 * blocks)
+    more = [] if received is None else [received]
+
+    def body(_, left_ref, *refs):
+        o_ref = refs[-1]
+        start = 0
+        for right, size in zip(refs, sizes):
+            at = slice(start, start + size)
+            acc = tn(left_ref[...], right[...])
+            if more:
+                acc = acc + refs[-2][:, at].astype(F32)
+            o_ref[:, at] = acc.astype(BF)
+            start += size
+
+    return pl.pallas_call(
+        body,
+        out_shape=shape(blocks * tile, cols),
+        grid_spec=pltpu.PrefetchScalarGridSpec(
+            num_scalar_prefetch=1,
+            grid=(blocks,),
+            in_specs=[spec(rows, tile, lambda i, at: (0, 2 * i + at[0]))]
+            + [spec(rows, k, lambda i, at: (0, 0)) for k in sizes]
+            + [spec(tile, cols, lambda i, at: (i, 0)) for _ in more],
+            out_specs=spec(tile, cols, lambda i, at: (i, 0)),
+        ),
+        cost_estimate=pl.CostEstimate(
+            flops=rows * width * cols,
+            bytes_accessed=2 * rows * (width + cols) + 2 * width * cols,
+            transcendentals=0,
+        ),
+        compiler_params=pltpu.CompilerParams(vmem_limit_bytes=63 << 20),
+    )(index, left, *rights, *more)
 
 
 def weight_grad_rows(rows, pairs):
@@ -810,49 +847,75 @@
         )
         g_out = grid.scatter_grad(mark(g_out))
         g_ud = mark(jnp.concatenate([hold(g_up), g_down], axis=1))
-        g_ud_moved = grid.swap(g_ud)
         down_moved = [grid.second(b, hold(down[1][b])) for b in both]
         d_v, d_gate, d_q, d_k = retain_back(
             hold(d_mix), gate, qk, values, full_o, col_info, row_info, cos_table, sin_table,
             log_gamma, heads, micro,
         )
         mark(d_v)
-        g_vg = grid.scatter_grad(grad(h1, [d_v, d_gate]))
+        def line_part(index, left, rights, received=None):
+            if width // grid.n_fsdp % 128 == 0:
+                index = index.astype(jnp.int32).reshape(1)
+                return weight_grad_part(index, left, rights, grid.nz, received)
+            value = weight_grad(left, rights)
+            value = value.reshape(grid.nz, 2, -1, value.shape[-1])
+            value = lax.dynamic_index_in_dim(value, index, 1, False)
+            value = value.reshape(-1, value.shape[-1]).astype(F32)
+            return (value if received is None else value + received.astype(F32)).astype(BF)
+
+        def line_start(rights):
+            return grid.flip_c(mark(line_part(1 - c, hold(h1), rights)))
+
+        def line_finish(rights, moved):
+            return grid.scatter_line(mark(line_part(c, h1, rights, hold(moved))))
+
+        down_moved = await_(*down_moved)
+        vg_moved = line_start([d_v, d_gate])
         down = [reduce_second(b, down[0][b], down_moved[b]) for b in both]
-        kept, moved = exchange_rows(
-            [hold(d_q), d_k, d_v, d_gate],
-            [(full_qk, 0), (full_qk, 1), (full_vg, 0), (full_vg, 1)],
-        )
-        g_qk = grid.scatter_grad(grad(h1, [d_q, d_k]))
+        g_ud_moved = grid.swap(hold(g_ud))
+        g_vg = line_finish([d_v, d_gate], vg_moved)
+        back = [d_q, d_k, d_v, d_gate]
+        back_weights = [(full_qk, 0), (full_qk, 1), (full_vg, 0), (full_vg, 1)]
+        sent = project_back([hold(back[0]), *back[1:]], back_weights, halves[1], BF)
+        mark(sent[0])
+        g_ud_moved = await_(g_ud_moved)[0]
+        moved = [grid.second(b, hold(sent[b])) for b in both]
+        kept = project_back([hold(back[0]), *back[1:]], back_weights, halves[0], F32)
+        mark(kept[0])
+        *moved, g_out = await_(*moved, g_out)
+        qk_moved = line_start([d_q, d_k])
+        sums = [reduce_second(b, kept[b], moved[b]) for b in both]
+        g_qk = line_finish([d_q, d_k], qk_moved)
         output = mark(
             jnp.concatenate(
                 [x1[b] + (down[b][0] + hold(down[b][1]).astype(F32)) for b in both]
             ).astype(BF)
         )
         output_moved = grid.swap(output)
-        g_ud = settle(g_ud, g_ud_moved)
-        sums = [reduce_second(b, kept[b], moved[b]) for b in both]
-        g_out = await_(g_out)[0]
-        g_out_moved = grid.swap(g_out)
-        output = settle(output, output_moved)
         d_inputs, gain_in_grad = [], 0.0
         for b in both:
             d_h1 = sums[b][0] + hold(sums[b][1]).astype(F32)
-            d_ln, part = layer_norm_back(d_h1, rows(scaled_in, b), rows(inverse_in, b), gain_in)
-            gain_in_grad = gain_in_grad + part
+            d_ln, part_grad = layer_norm_back(
+                d_h1, rows(scaled_in, b), rows(inverse_in, b), gain_in
+            )
+            gain_in_grad = gain_in_grad + part_grad
             d_inputs.append(mark(d_x1[b] + d_ln))
         d_input = jnp.concatenate(d_inputs)
         d_input_moved = grid.swap(hold(d_input))
-        g_out = settle(g_out, g_out_moved)
+        g_vg = await_(g_vg)[0]
+        vg_moved = grid.swap(g_vg)
+        output = settle(output, output_moved)
         grad_norms = grid.total(hold(jnp.stack([gain_in_grad, gain_mid_grad])))
         mark(grad_norms)
+        g_out_moved = grid.swap(hold(g_out))
+        g_ud = settle(g_ud, g_ud_moved)
         d_input = settle(d_input, d_input_moved)
+        g_out = settle(g_out, g_out_moved)
         g_down, g_up, g_out = [
             hold(g).astype(F32) for g in (g_ud[:, hidden:].T, g_ud[:, :hidden], g_out.T)
         ]
         last[:] = [g_down, g_up, g_out]
-        g_vg = await_(g_vg)[0]
-        g_vg = mark(settle(g_vg, grid.swap(g_vg)).astype(F32))
+        g_vg = mark(settle(g_vg, vg_moved).astype(F32))
         g_qk = await_(g_qk)[0]
         g_qk = settle(g_qk, grid.swap(g_qk)).astype(F32)
         whole = (micro, 1, piece, width)

time: 624 us -> 614 us (0.984)
  starting transfers between devices: 98.7 us -> 78.4 us
  Pallas kernels: 192 us -> 201 us
    ppermute x49 -> x51, starting transfers between devices: 97.7 us -> 77.3 us  [send(): return lax.ppermute(value, AXES, found)]
    reduce_scatter x5 -> x3, waiting for transfers between devices: 14.8 us -> 2.15 us  [scatter_grad(): lax.psum_scatter(value, AXES, scatter_dimension=0, tiled=True, axis_index...]
    ppermute x49 -> x51, waiting for transfers between devices: 193 us -> 202 us  [send(): return lax.ppermute(value, AXES, found)]
    pallas_call x2 -> x4, Pallas kernels: 22 us -> 31 us  [weight_grad_part(): pl.pallas_call(body, out_shape=shape(blocks * tile, cols), grid_spec=pltp...]
    unnamed x109 -> x111, local copies, waits for them, and re-layouts: 10.4 us -> 12.8 us
  transfers between devices with their start and end apart: 59 -> 61, of which waited for: 35 -> 38; matrix products, arithmetic and copies ran while one was open for 15% -> 15% of each run, Pallas kernels for 31% -> 33%
where the time goes in v7:
time: 614 us; the launch traced here: 605 us
  waiting for transfers between devices  206 us (34%)
  Pallas kernels  201 us (33%)
  other arithmetic  80.9 us (13%)
  starting transfers between devices  78.4 us (13%)
  local copies, waits for them, and re-layouts  22.7 us (4%)
  between operations  15.4 us (3%)
    ppermute x51, waiting for transfers between devices, send(): return lax.ppermute(value, AXES, found)  202 us
    ppermute x51, starting transfers between devices, send(): return lax.ppermute(value, AXES, found)  77.3 us
    pallas_call x7, Pallas kernels, project_back(): call(body, (width // tile,), [spec(rows, k, lambda j: (0, 0)) for k in si...  58 us
    pallas_call x4, Pallas kernels, weight_grad_part(): pl.pallas_call(body, out_shape=shape(blocks * tile, cols), grid_spec=pltp...  31 us
    pallas_call x1, Pallas kernels, retain_back(): call(body, (heads, micro), [per_row(rows, width), spec(width, VAL_HEAD, l...  17.5 us
    pallas_call x2, Pallas kernels, weight_grad_rows(): call(body, (width // tile,), [spec(rows, tile, lambda i, b=b: (b, i)) for...  16.9 us
    pallas_call x2, Pallas kernels, feed_up(): call(body, (steps,), [ANY] * n + [spec(width, tile, lambda j: (0, j))], [...  16.2 us
    pallas_call x1, Pallas kernels, project_plain(): call(body, (cols // tile,), [spec(rows, width, lambda j: (0, 0)), spec(wi...  15.3 us
  transfers between devices with their start and end apart: 61, of which 38 were waited for; matrix products, arithmetic and copies ran while one was open for 15% of the time, Pallas kernels for 33%

profile of v7, /device:TPU:1, one launch (start us, length us, event | category | flops | bytes accessed | tf_op | source)
XLA Modules:
  0.0 604.7 jit_solution(3856649273681780774)
XLA Ops:
  24.2 11.7 %collective-permute-done.1 = bf16[256,3072]{1,0:T(8,128)(2,1)} collective-permute-done((bf16[256,3072]{1,0:T(8,128)(2,1)}, bf16[256,3072]{1,0:T(8,128)(2,1)}, u32[]{:S(2)}, u32[]{:S(2)}) %collective-permute-start.1) | collective-permute-done | bytes 1572896 | tf_op jit(solution)/shard_map/ppermute | solution.py:57
  46.0 10.1 %collective-permute-done = bf16[256,2048]{1,0:T(8,128)(2,1)} collective-permute-done((bf16[256,2048]{1,0:T(8,128)(2,1)}, bf16[256,2048]{1,0:T(8,128)(2,1)}, u32[]{:S(2)}, u32[]{:S(2)}) %collective-permute-start) | collective-permute-done | bytes 1048608 | tf_op jit(solution)/shard_map/ppermute | solution.py:57
  69.4 6.6 %collective-permute-done.5.refs_4_ = bf16[128,2048]{1,0:T(8,128)(2,1)S(1)} collective-permute-done((bf16[128,2048]{1,0:T(8,128)(2,1)S(1)}, bf16[128,2048]{1,0:T(8,128)(2,1)S(1)}, u32[]{:S(2)}, u32[]{:S(2)}) %collective-permute-start.5) | collective-permute-done | bytes 524320 | tf_op jit(solution)/shard_map/ppermute | solution.py:57
  76.4 24.1 %collective-permute-done.6.refs_5_ = bf16[256,2048]{1,0:T(8,128)(2,1)S(1)} collective-permute-done((bf16[256,2048]{1,0:T(8,128)(2,1)S(1)}, bf16[256,2048]{1,0:T(8,128)(2,1)S(1)}, u32[]{:S(2)}, u32[]{:S(2)}) %collective-permute-start.6) | collective-permute-done | bytes 1048608 | tf_op jit(solution)/shard_map/ppermute | solution.py:57
  100.5 18.4 %collective-permute-done.4.refs_2_ = bf16[256,2048]{1,0:T(8,128)(2,1)S(1)} collective-permute-done((bf16[256,2048]{1,0:T(8,128)(2,1)S(1)}, bf16[256,2048]{1,0:T(8,128)(2,1)S(1)}, u32[]{:S(2)}, u32[]{:S(2)}) %collective-permute-start.4) | collective-permute-done | bytes 1048608 | tf_op jit(solution)/shard_map/ppermute | solution.py:57
  131.1 10.0 %shard_map.186 = (bf16[1024,2048]{1,0:T(8,128)(2,1)}, bf16[1024,1024]{1,0:T(8,128)(2,1)}) custom-call(bf16[128,2048]{1,0:T(8,128)(2,1)} %copy-done.32, bf16[128,2048]{1,0:T(8,128)(2,1)} %copy-done.42, bf16[256,2048]{1,0:T(8,128)(2,1)} %copy-done.50, bf16[128,2048]{1,0:T(8,128)(2,1)} %copy-done.31, bf16[128,2048]{1,0:T(8,128)(2,1)} %copy-done.43, ...), custom_call_target="tpu_custom_call" | custom-call | flops 4294967296 | bytes 14680064 | tf_op jit(solution)/shard_map/pallas_call | solution.py:216
  141.1 9.3 %collective-permute-done.9 = bf16[512,2048]{1,0:T(8,128)(2,1)} collective-permute-done((bf16[512,2048]{1,0:T(8,128)(2,1)}, bf16[512,2048]{1,0:T(8,128)(2,1)}, u32[]{:S(2)}, u32[]{:S(2)}) %collective-permute-start.9) | collective-permute-done | bytes 2097184 | tf_op jit(solution)/shard_map/ppermute | solution.py:57
  157.9 15.3 %shard_map.187 = (bf16[1024,1024]{1,0:T(8,128)(2,1)}, f32[1024,1024]{1,0:T(8,128)}) custom-call(bf16[1024,2048]{1,0:T(8,128)(2,1)} %get-tuple-element.237.h_ref.left_ref, bf16[2048,2048]{1,0:T(8,128)(2,1)} %all-gather.8.cloned.1.call-done.w_ref.refs_6_.refs_7_), custom_call_target="tpu_custom_call" | custom-call | flops 8589934592 | bytes 20971520 | tf_op jit(solution)/shard_map/pallas_call | solution.py:255
  179.9 7.5 %shard_map.188.refs_0_.refs_6_ = bf16[1024,1024]{1,0:T(8,128)(2,1)} custom-call(bf16[1024,1024]{1,0:T(8,128)(2,1)} %get-tuple-element.149.q_ref.k_ref, bf16[1024,1024]{1,0:T(8,128)(2,1)} %get-tuple-element.149.q_ref.k_ref, bf16[1024,1024]{1,0:T(8,128)(2,1)} %get-tuple-element.158.v_ref, f32[1024,1024]{1,0:T(8,128)} %get-tuple-element.159.gate_ref, ...), custom_call_target="tpu_custom_call" | custom-call | flops 1610612736 | bytes 10485760 | tf_op jit(solution)/shard_map/pallas_call | solution.py:303
  189.0 6.3 %shard_map.189 = (bf16[256,2048]{1,0:T(8,128)(2,1)}, bf16[256,2048]{1,0:T(8,128)(2,1)}) custom-call(bf16[1024,1024]{1,0:T(8,128)(2,1)} %shard_map.188.refs_0_.refs_6_, bf16[2048,1024]{1,0:T(8,128)(2,1)} %all-gather.10.cloned.1.call-done.refs_1_.wo), custom_call_target="tpu_custom_call" | custom-call | flops 2147483648 | bytes 9437184 | tf_op jit(solution)/shard_map/pallas_call | solution.py:385
  197.8 6.7 %shard_map.190 = (f32[256,2048]{1,0:T(8,128)}, f32[256,2048]{1,0:T(8,128)}) custom-call(bf16[1024,1024]{1,0:T(8,128)(2,1)} %shard_map.188.refs_0_.refs_6_, bf16[2048,1024]{1,0:T(8,128)(2,1)} %all-gather.10.cloned.1.call-done.refs_1_.wo), custom_call_target="tpu_custom_call" | custom-call | flops 2147483648 | bytes 9437184 | tf_op jit(solution)/shard_map/pallas_call | solution.py:385
  208.9 16.5 %collective-permute-done.12 = bf16[256,2048]{1,0:T(8,128)(2,1)} collective-permute-done((bf16[256,2048]{1,0:T(8,128)(2,1)}, bf16[256,2048]{1,0:T(8,128)(2,1)}, u32[]{:S(2)}, u32[]{:S(2)}) %collective-permute-start.12) | collective-permute-done | bytes 1048608 | tf_op jit(solution)/shard_map/ppermute | solution.py:57
  231.6 7.0 %collective-permute-done.15 = bf16[128,2048]{1,0:T(8,128)(2,1)S(1)} collective-permute-done((bf16[128,2048]{1,0:T(8,128)(2,1)S(1)}, bf16[128,2048]{1,0:T(8,128)(2,1)S(1)}, u32[]{:S(2)}, u32[]{:S(2)}) %collective-permute-start.15) | collective-permute-done | bytes 524320 | tf_op jit(solution)/shard_map/ppermute | solution.py:57
  260.6 8.1 %shard_map.192 = (bf16[512,2048]{1,0:T(8,128)(2,1)}, bf16[512,1024]{1,0:T(8,128)(2,1)}, f32[512,1024]{1,0:T(8,128)}) custom-call(bf16[128,2048]{1,0:T(8,128)(2,1)} %copy-done.33, bf16[128,2048]{1,0:T(8,128)(2,1)} %copy-done.44, bf16[128,2048]{1,0:T(8,128)(2,1)} %copy-done.34, bf16[128,2048]{1,0:T(8,128)(2,1)} %copy-done.46, ...), custom_call_target="tpu_custom_call" | custom-call | flops 2147483648 | bytes 11534336 | tf_op jit(solution)/shard_map/pallas_call | solution.py:355
  268.7 13.3 %collective-permute-done.21.refs_1_ = bf16[256,2048]{1,0:T(8,128)(2,1)} collective-permute-done((bf16[256,2048]{1,0:T(8,128)(2,1)}, bf16[256,2048]{1,0:T(8,128)(2,1)}, u32[]{:S(2)}, u32[]{:S(2)}) %collective-permute-start.21) | collective-permute-done | bytes 1048608 | tf_op jit(solution)/shard_map/ppermute | solution.py:57
  282.0 8.1 %shard_map.193 = (bf16[512,2048]{1,0:T(8,128)(2,1)}, bf16[512,1024]{1,0:T(8,128)(2,1)}, f32[512,1024]{1,0:T(8,128)}) custom-call(bf16[256,2048]{1,0:T(8,128)(2,1)} %collective-permute-done.20.refs_0_, bf16[256,2048]{1,0:T(8,128)(2,1)} %collective-permute-done.21.refs_1_, bf16[2048,1024]{1,0:T(8,128)(2,1)} %all-gather.12.cloned.1.call-done.refs_4_.refs_2_.up_ref.refs_1_), custom_call_target="tpu_custom_call" | custom-call | flops 2147483648 | bytes 11534336 | tf_op jit(solution)/shard_map/pallas_call | solution.py:355
  290.1 8.4 %shard_map.194 = bf16[2048,1024]{1,0:T(8,128)(2,1)} custom-call(bf16[1024,2048]{1,0:T(8,128)(2,1)} %shard_map.191.refs_0_.refs_1_.cot_ref, bf16[1024,2048]{1,0:T(8,128)(2,1)} %shard_map.191.refs_0_.refs_1_.cot_ref, bf16[512,1024]{1,0:T(8,128)(2,1)} %get-tuple-element.202.refs_2_.refs_0_, bf16[512,1024]{1,0:T(8,128)(2,1)} %get-tuple-element.204.refs_3_.refs_0_), custom_call_target="tpu_custom_call" | custom-call | flops 4294967296 | bytes 10485760 | tf_op jit(solution)/shard_map/pallas_call | solution.py:587
  298.8 14.1 %shard_map.195 = (bf16[1024,1024]{1,0:T(8,128)(2,1)}, bf16[256,2048]{1,0:T(8,128)(2,1)}, bf16[256,2048]{1,0:T(8,128)(2,1)}) custom-call(bf16[1024,2048]{1,0:T(8,128)(2,1)} %shard_map.191.refs_0_.refs_1_.cot_ref, bf16[2048,1024]{1,0:T(8,128)(2,1)} %all-gather.14.cloned.1.call-done.down_ref.refs_1_, ...), custom_call_target="tpu_custom_call" | custom-call | flops 6442450944 | bytes 23068672 | tf_op jit(solution)/shard_map/pallas_call | solution.py:431
  315.7 6.8 %shard_map.196 = (f32[256,2048]{1,0:T(8,128)}, f32[256,2048]{1,0:T(8,128)}) custom-call(bf16[1024,1024]{1,0:T(8,128)(2,1)} %get-tuple-element.187.refs_0_.refs_2_.refs_3_, bf16[2048,1024]{1,0:T(8,128)(2,1)} %all-gather.12.cloned.1.call-done.refs_4_.refs_2_.up_ref.refs_1_), custom_call_target="tpu_custom_call" | custom-call | flops 2147483648 | bytes 9437184 | tf_op jit(solution)/shard_map/pallas_call | solution.py:385
  322.5 8.4 %shard_map.197 = bf16[2048,1024]{1,0:T(8,128)(2,1)} custom-call(bf16[512,2048]{1,0:T(8,128)(2,1)} %get-tuple-element.193.refs_0_, bf16[512,2048]{1,0:T(8,128)(2,1)} %get-tuple-element.194.refs_1_, bf16[1024,1024]{1,0:T(8,128)(2,1)} %get-tuple-element.187.refs_0_.refs_2_.refs_3_, bf16[1024,1024]{1,0:T(8,128)(2,1)} %get-tuple-element.187.refs_0_.refs_2_.refs_3_), custom_call_target="tpu_custom_call" | custom-call | flops 4294967296 | bytes 10485760 | tf_op jit(solution)/shard_map/pallas_call | solution.py:587
  342.1 7.5 %collective-permute-done.25 = bf16[128,2048]{1,0:T(8,128)(2,1)S(1)} collective-permute-done((bf16[128,2048]{1,0:T(8,128)(2,1)}, bf16[128,2048]{1,0:T(8,128)(2,1)S(1)}, u32[]{:S(2)}, u32[]{:S(2)}) %collective-permute-start.25) | collective-permute-done | bytes 524320 | tf_op jit(solution)/shard_map/ppermute | solution.py:57
  375.4 6.4 %shard_map.198 = (f32[256,2048]{1,0:T(8,128)}, f32[256,2048]{1,0:T(8,128)}) custom-call(bf16[512,1024]{1,0:T(8,128)(2,1)} %get-tuple-element.202.refs_2_.refs_0_, bf16[2048,1024]{1,0:T(8,128)(2,1)} %all-gather.14.cloned.1.call-done.down_ref.refs_1_), custom_call_target="tpu_custom_call" | custom-call | flops 2147483648 | bytes 8388608 | tf_op jit(solution)/shard_map/pallas_call | solution.py:385
  387.9 10.1 %shard_map.200 = (bf16[1024,2048]{1,0:T(8,128)(2,1)}, bf16[2048,1024]{1,0:T(8,128)(2,1)}) custom-call(bf16[128,2048]{1,0:T(8,128)(2,1)} %get-tuple-element.289.refs_0_, bf16[128,2048]{1,0:T(8,128)(2,1)} %collective-permute-done.27.refs_1_, bf16[256,2048]{1,0:T(8,128)(2,1)} %collective-permute-done.28.refs_2_, bf16[128,2048]{1,0:T(8,128)(2,1)} %copy-done.35, ...), custom_call_target="tpu_custom_call" | custom-call | flops 4294967296 | bytes 10485760 | tf_op jit(solution)/shard_map/pallas_call | solution.py:618
  405.6 17.5 %shard_map.201 = (bf16[1024,1024]{1,0:T(8,128)(2,1)}, bf16[1024,1024]{1,0:T(8,128)(2,1)}, bf16[1024,512]{1,0:T(8,128)(2,1)}, bf16[1024,512]{1,0:T(8,128)(2,1)}) custom-call(bf16[1024,2048]{1,0:T(8,128)(2,1)} %get-tuple-element.215.mix_ref, bf16[2048,1024]{1,0:T(8,128)(2,1)} %all-gather.10.cloned.1.call-done.refs_1_.wo, ...), custom_call_target="tpu_custom_call" | custom-call | flops 9663676416 | bytes 29360128 | tf_op jit(solution)/shard_map/pallas_call | solution.py:489
  425.1 8.8 %shard_map.202 = bf16[1024,2048]{1,0:T(8,128)(2,1)} custom-call(s32[1]{0:T(128)} %bitcast.28._, bf16[1024,2048]{1,0:T(8,128)(2,1)} %get-tuple-element.237.h_ref.left_ref, bf16[1024,1024]{1,0:T(8,128)(2,1)} %get-tuple-element.216.refs_0_.refs_2_, bf16[1024,1024]{1,0:T(8,128)(2,1)} %get-tuple-element.219.refs_1_.refs_3_), custom_call_target="tpu_custom_call" | custom-call | flops 4294967296 | bytes 16777216 | tf_op jit(solution)/shard_map/pallas_call | solution.py:556
  446.3 9.7 %shard_map.203 = bf16[1024,2048]{1,0:T(8,128)(2,1)} custom-call(s32[1]{0:T(128)} %bitcast.29._, bf16[1024,2048]{1,0:T(8,128)(2,1)} %get-tuple-element.237.h_ref.left_ref, bf16[1024,1024]{1,0:T(8,128)(2,1)} %get-tuple-element.216.refs_0_.refs_2_, bf16[1024,1024]{1,0:T(8,128)(2,1)} %get-tuple-element.219.refs_1_.refs_3_, ...), custom_call_target="tpu_custom_call" | custom-call | flops 4294967296 | bytes 16777216 | tf_op jit(solution)/shard_map/pallas_call | solution.py:556
  459.3 13.0 %shard_map.204 = (bf16[256,2048]{1,0:T(8,128)(2,1)}, bf16[256,2048]{1,0:T(8,128)(2,1)}) custom-call(bf16[1024,512]{1,0:T(8,128)(2,1)} %get-tuple-element.234.refs_0_, bf16[1024,512]{1,0:T(8,128)(2,1)} %get-tuple-element.222.refs_1_, bf16[1024,1024]{1,0:T(8,128)(2,1)} %get-tuple-element.216.refs_0_.refs_2_, ...), custom_call_target="tpu_custom_call" | custom-call | flops 6442450944 | bytes 22020096 | tf_op jit(solution)/shard_map/pallas_call | solution.py:385
  473.0 12.8 %shard_map.205 = (f32[256,2048]{1,0:T(8,128)}, f32[256,2048]{1,0:T(8,128)}) custom-call(bf16[1024,512]{1,0:T(8,128)(2,1)} %get-tuple-element.234.refs_0_, bf16[1024,512]{1,0:T(8,128)(2,1)} %get-tuple-element.222.refs_1_, bf16[1024,1024]{1,0:T(8,128)(2,1)} %get-tuple-element.216.refs_0_.refs_2_, bf16[1024,1024]{1,0:T(8,128)(2,1)} %get-tuple-element.219.refs_1_.refs_3_, ...), custom_call_target="tpu_custom_call" | custom-call | flops 6442450944 | bytes 22020096 | tf_op jit(solution)/shard_map/pallas_call | solution.py:385
  485.8 10.3 %collective-permute-done.36 = bf16[256,2048]{1,0:T(8,128)(2,1)} collective-permute-done((bf16[256,2048]{1,0:T(8,128)(2,1)}, bf16[256,2048]{1,0:T(8,128)(2,1)}, u32[]{:S(2)}, u32[]{:S(2)}) %collective-permute-start.36) | collective-permute-done | bytes 1048608 | tf_op jit(solution)/shard_map/ppermute | solution.py:57
  498.3 6.1 %shard_map.206 = bf16[1024,1024]{1,0:T(8,128)(2,1)} custom-call(s32[1]{0:T(128)} %bitcast.28._, bf16[1024,2048]{1,0:T(8,128)(2,1)} %get-tuple-element.237.h_ref.left_ref, bf16[1024,512]{1,0:T(8,128)(2,1)} %get-tuple-element.234.refs_0_, bf16[1024,512]{1,0:T(8,128)(2,1)} %get-tuple-element.222.refs_1_), custom_call_target="tpu_custom_call" | custom-call | flops 2147483648 | bytes 10485760 | tf_op jit(solution)/shard_map/pallas_call | solution.py:556
  512.1 6.4 %shard_map.207 = bf16[1024,1024]{1,0:T(8,128)(2,1)} custom-call(s32[1]{0:T(128)} %bitcast.29._, bf16[1024,2048]{1,0:T(8,128)(2,1)} %get-tuple-element.237.h_ref.left_ref, bf16[1024,512]{1,0:T(8,128)(2,1)} %get-tuple-element.234.refs_0_, bf16[1024,512]{1,0:T(8,128)(2,1)} %get-tuple-element.222.refs_1_, bf16[1024,1024]{1,0:T(8,128)(2,1)} %collective-permute-done.37.refs_2_), custom_call_target="tpu_custom_call" | custom-call | flops 2147483648 | bytes 10485760 | tf_op jit(solution)/shard_map/pallas_call | solution.py:556
  572.6 10.7 %collective-permute-done.49 = bf16[256,1024]{1,0:T(8,128)(2,1)S(1)} collective-permute-done((bf16[256,1024]{1,0:T(8,128)(2,1)S(1)}, bf16[256,1024]{1,0:T(8,128)(2,1)S(1)}, u32[]{:S(2)}, u32[]{:S(2)}) %collective-permute-start.49) | collective-permute-done | bytes 524320 | tf_op jit(solution)/shard_map/ppermute | solution.py:57
  (343 shorter events, 253.0 us)
Async XLA Ops:
  7.2 55.0 %all-gather.6.cloned.1.call-start = ((), (), s32[]{:S(2)}) async-start(), calls=%async_computation.5 | async-start | bytes 2621440 | tf_op jit(solution)/shard_map/all_gather | solution.py:89
  10.1 147.8 %all-gather.8.cloned.1.call-start = ((), (), s32[]{:S(2)}) async-start(), calls=%async_computation.6 | async-start | bytes 9437184 | tf_op jit(solution)/shard_map/all_gather | solution.py:81
  12.7 23.2 %collective-permute-start.1 = (bf16[256,3072]{1,0:T(8,128)(2,1)}, bf16[256,3072]{1,0:T(8,128)(2,1)}, u32[]{:S(2)}, u32[]{:S(2)}) collective-permute-start(bf16[256,3072]{1,0:T(8,128)(2,1)} %pad_maximum_fusion.2), channel_id=1, source_target_pairs={{1,8},{3,10},{5,12},{7,14},{8,1},{10,3},{12,5},{14,7},{17,24},{19,... | collective-permute-start | bytes 4718600 | tf_op jit(solution)/shard_map/ppermute | solution.py:57
  39.3 149.7 %all-gather.10.cloned.1.call-start = ((), (), s32[]{:S(2)}) async-start(), calls=%async_computation.7 | async-start | bytes 4718592 | tf_op jit(solution)/shard_map/all_gather | solution.py:81
  42.7 22.8 %collective-permute-start.3 = (bf16[2,512]{1,0:T(2,128)(2,1)S(1)}, bf16[2,512]{1,0:T(2,128)(2,1)S(1)}, u32[]{:S(2)}, u32[]{:S(2)}) collective-permute-start(bf16[2,512]{1,0:T(2,128)(2,1)S(1)} %bitcast.103), channel_id=1, source_target_pairs={{1,8},{3,10},{5,12},{7,14},{8,1},{10,3},{12,5},{14,7},{17,24},{19,... | collective-permute-start | bytes 6152 | tf_op jit(solution)/shard_map/ppermute | solution.py:57
  60.7 199.8 %all-gather.12.cloned.1.call-start = ((), (), s32[]{:S(2)}) async-start(), calls=%async_computation.8 | async-start | bytes 4718592 | tf_op jit(solution)/shard_map/all_gather | solution.py:81
  62.2 57.7 %collective-permute-start.7 = (bf16[1024,1024]{1,0:T(8,128)(2,1)}, bf16[1024,1024]{1,0:T(8,128)(2,1)S(1)}, u32[]{:S(2)}, u32[]{:S(2)}) collective-permute-start(bf16[1024,1024]{1,0:T(8,128)(2,1)} %all-gather.6.cloned.1.call-done), channel_id=1, source_target_pairs={{1,8},{3,10},{5,12},{7,14},{8,1},{10,3},{12,5},{14,7},{17,24},{19,... | collective-permute-start | bytes 6291464 | tf_op jit(solution)/shard_map/ppermute | solution.py:57
  76.1 24.4 %collective-permute-start.6 = (bf16[256,2048]{1,0:T(8,128)(2,1)S(1)}, bf16[256,2048]{1,0:T(8,128)(2,1)S(1)}, u32[]{:S(2)}, u32[]{:S(2)}) collective-permute-start(bf16[256,2048]{1,0:T(8,128)(2,1)S(1)} %pad_maximum_fusion.4), channel_id=1, source_target_pairs={{0,16},{1,17},{2,18},{3,19},{4,20},{5,21},{6,22},{7,23},{8,24},{9,... | collective-permute-start | bytes 3145736 | tf_op jit(solution)/shard_map/ppermute | solution.py:57
  76.4 42.5 %collective-permute-start.4 = (bf16[256,2048]{1,0:T(8,128)(2,1)S(1)}, bf16[256,2048]{1,0:T(8,128)(2,1)S(1)}, u32[]{:S(2)}, u32[]{:S(2)}) collective-permute-start(bf16[256,2048]{1,0:T(8,128)(2,1)S(1)} %pad_maximum_fusion.3), channel_id=1, source_target_pairs={{0,1},{1,0},{2,3},{3,2},{4,5},{5,4},{6,7},{7,6},{8,9},{9,8},{10,11... | collective-permute-start | bytes 3145736 | tf_op jit(solution)/shard_map/ppermute | solution.py:57
  122.8 27.7 %collective-permute-start.9 = (bf16[512,2048]{1,0:T(8,128)(2,1)}, bf16[512,2048]{1,0:T(8,128)(2,1)}, u32[]{:S(2)}, u32[]{:S(2)}) collective-permute-start(bf16[512,2048]{1,0:T(8,128)(2,1)} %pad_maximum_fusion), channel_id=1, source_target_pairs={{1,8},{3,10},{5,12},{7,14},{8,1},{10,3},{12,5},{14,7},{17,24},{19,... | collective-permute-start | bytes 6291464 | tf_op jit(solution)/shard_map/ppermute | solution.py:57
  154.4 144.4 %all-gather.14.cloned.1.call-start = ((), (), s32[]{:S(2)}) async-start(), calls=%async_computation.9 | async-start | bytes 4718592 | tf_op jit(solution)/shard_map/all_gather | solution.py:81
  177.6 27.0 %collective-permute-start.14 = (bf16[256,2048]{1,0:T(8,128)(2,1)}, bf16[256,2048]{1,0:T(8,128)(2,1)}, u32[]{:S(2)}, u32[]{:S(2)}) collective-permute-start(bf16[256,2048]{1,0:T(8,128)(2,1)} %pad_maximum_fusion.6), channel_id=1, source_target_pairs={{0,16},{1,17},{2,18},{3,19},{4,20},{5,21},{6,22},{7,23},{8,24},{9,... | collective-permute-start | bytes 3145736 | tf_op jit(solution)/shard_map/ppermute | solution.py:57
  178.4 26.1 %collective-permute-start.13 = (bf16[256,2048]{1,0:T(8,128)(2,1)}, bf16[256,2048]{1,0:T(8,128)(2,1)}, u32[]{:S(2)}, u32[]{:S(2)}) collective-permute-start(bf16[256,2048]{1,0:T(8,128)(2,1)} %pad_maximum_fusion.5), channel_id=1, source_target_pairs={{0,1},{1,0},{2,3},{3,2},{4,5},{5,4},{6,7},{7,6},{8,9},{9,8},{10,11... | collective-permute-start | bytes 3145736 | tf_op jit(solution)/shard_map/ppermute | solution.py:57
  195.3 30.1 %collective-permute-start.12 = (bf16[256,2048]{1,0:T(8,128)(2,1)}, bf16[256,2048]{1,0:T(8,128)(2,1)}, u32[]{:S(2)}, u32[]{:S(2)}) collective-permute-start(bf16[256,2048]{1,0:T(8,128)(2,1)} %get-tuple-element.161), channel_id=1, source_target_pairs={{0,1},{1,0},{2,3},{3,2},{4,5},{5,4},{6,7},{7,6},{8,9},{9,8},{10,11... | collective-permute-start | bytes 3145736 | tf_op jit(solution)/shard_map/ppermute | solution.py:57
  196.5 162.5 %reduce-scatter.6.cloned.1.call-start = ((), (), s32[]{:S(2)}) async-start(), calls=%async_computation.10 | async-start | bytes 4718592 | tf_op jit(solution)/shard_map/reduce_scatter | solution.py:84
  196.6 30.9 %collective-permute-start.16 = (bf16[256,2048]{1,0:T(8,128)(2,1)}, bf16[256,2048]{1,0:T(8,128)(2,1)}, u32[]{:S(2)}, u32[]{:S(2)}) collective-permute-start(bf16[256,2048]{1,0:T(8,128)(2,1)} %get-tuple-element.168), channel_id=1, source_target_pairs={{0,16},{1,17},{2,18},{3,19},{4,20},{5,21},{6,22},{7,23},{8,24},{9,... | collective-permute-start | bytes 3145736 | tf_op jit(solution)/shard_map/ppermute | solution.py:57
  259.0 23.0 %collective-permute-start.21 = (bf16[256,2048]{1,0:T(8,128)(2,1)}, bf16[256,2048]{1,0:T(8,128)(2,1)}, u32[]{:S(2)}, u32[]{:S(2)}) collective-permute-start(bf16[256,2048]{1,0:T(8,128)(2,1)} %pad_maximum_fusion.8), channel_id=1, source_target_pairs={{0,16},{1,17},{2,18},{3,19},{4,20},{5,21},{6,22},{7,23},{8,24},{9,... | collective-permute-start | bytes 3145736 | tf_op jit(solution)/shard_map/ppermute | solution.py:57
  259.0 23.0 %collective-permute-start.20 = (bf16[256,2048]{1,0:T(8,128)(2,1)}, bf16[256,2048]{1,0:T(8,128)(2,1)}, u32[]{:S(2)}, u32[]{:S(2)}) collective-permute-start(bf16[256,2048]{1,0:T(8,128)(2,1)} %pad_maximum_fusion.7), channel_id=1, source_target_pairs={{0,1},{1,0},{2,3},{3,2},{4,5},{5,4},{6,7},{7,6},{8,9},{9,8},{10,11... | collective-permute-start | bytes 3145736 | tf_op jit(solution)/shard_map/ppermute | solution.py:57
  298.5 101.9 %reduce-scatter.8.cloned.1.call-start = ((), (), s32[]{:S(2)}) async-start(), calls=%async_computation.11 | async-start | bytes 4718592 | tf_op jit(solution)/shard_map/reduce_scatter | solution.py:84
  312.9 22.2 %collective-permute-start.23 = (bf16[256,2048]{1,0:T(8,128)(2,1)}, bf16[256,2048]{1,0:T(8,128)(2,1)}, u32[]{:S(2)}, u32[]{:S(2)}) collective-permute-start(bf16[256,2048]{1,0:T(8,128)(2,1)} %get-tuple-element.191), channel_id=1, source_target_pairs={{0,1},{1,0},{2,3},{3,2},{4,5},{5,4},{6,7},{7,6},{8,9},{9,8},{10,11... | collective-permute-start | bytes 3145736 | tf_op jit(solution)/shard_map/ppermute | solution.py:57
  314.5 23.0 %collective-permute-start.22 = (bf16[256,2048]{1,0:T(8,128)(2,1)}, bf16[256,2048]{1,0:T(8,128)(2,1)}, u32[]{:S(2)}, u32[]{:S(2)}) collective-permute-start(bf16[256,2048]{1,0:T(8,128)(2,1)} %get-tuple-element.189), channel_id=1, source_target_pairs={{0,16},{1,17},{2,18},{3,19},{4,20},{5,21},{6,22},{7,23},{8,24},{9,... | collective-permute-start | bytes 3145736 | tf_op jit(solution)/shard_map/ppermute | solution.py:57
  339.5 158.8 %reduce-scatter.10.cloned.1.call-start = ((), (), s32[]{:S(2)}) async-start(), calls=%async_computation.12 | async-start | bytes 4718592 | tf_op jit(solution)/shard_map/reduce_scatter | solution.py:84
  398.0 143.8 %reduce-scatter.12.cloned.1.call-start = ((), (), s32[]{:S(2)}) async-start(), calls=%async_computation.13 | async-start | bytes 5242880 | tf_op jit(solution)/shard_map/reduce_scatter | solution.py:92
  403.2 20.4 %collective-permute-start.31 = (bf16[256,2048]{1,0:T(8,128)(2,1)}, bf16[256,2048]{1,0:T(8,128)(2,1)}, u32[]{:S(2)}, u32[]{:S(2)}) collective-permute-start(bf16[256,2048]{1,0:T(8,128)(2,1)} %get-tuple-element.213), channel_id=1, source_target_pairs={{0,16},{1,17},{2,18},{3,19},{4,20},{5,21},{6,22},{7,23},{8,24},{9,... | collective-permute-start | bytes 3145736 | tf_op jit(solution)/shard_map/ppermute | solution.py:57
  404.4 20.7 %collective-permute-start.30 = (bf16[256,2048]{1,0:T(8,128)(2,1)}, bf16[256,2048]{1,0:T(8,128)(2,1)}, u32[]{:S(2)}, u32[]{:S(2)}) collective-permute-start(bf16[256,2048]{1,0:T(8,128)(2,1)} %get-tuple-element.211), channel_id=1, source_target_pairs={{0,1},{1,0},{2,3},{3,2},{4,5},{5,4},{6,7},{7,6},{8,9},{9,8},{10,11... | collective-permute-start | bytes 3145736 | tf_op jit(solution)/shard_map/ppermute | solution.py:57
  455.9 128.7 %reduce-scatter.14.cloned.1.call-start = ((), (), s32[]{:S(2)}) async-start(), calls=%async_computation.14 | async-start | bytes 2621440 | tf_op jit(solution)/shard_map/reduce_scatter | solution.py:92
  472.7 23.4 %collective-permute-start.36 = (bf16[256,2048]{1,0:T(8,128)(2,1)}, bf16[256,2048]{1,0:T(8,128)(2,1)}, u32[]{:S(2)}, u32[]{:S(2)}) collective-permute-start(bf16[256,2048]{1,0:T(8,128)(2,1)} %get-tuple-element.233), channel_id=1, source_target_pairs={{0,16},{1,17},{2,18},{3,19},{4,20},{5,21},{6,22},{7,23},{8,24},{9,... | collective-permute-start | bytes 3145736 | tf_op jit(solution)/shard_map/ppermute | solution.py:57
  473.0 25.2 %collective-permute-start.35 = (bf16[256,2048]{1,0:T(8,128)(2,1)}, bf16[256,2048]{1,0:T(8,128)(2,1)}, u32[]{:S(2)}, u32[]{:S(2)}) collective-permute-start(bf16[256,2048]{1,0:T(8,128)(2,1)} %get-tuple-element.231), channel_id=1, source_target_pairs={{0,1},{1,0},{2,3},{3,2},{4,5},{5,4},{6,7},{7,6},{8,9},{9,8},{10,11... | collective-permute-start | bytes 3145736 | tf_op jit(solution)/shard_map/ppermute | solution.py:57
  508.4 21.6 %collective-permute-start.41 = (bf16[128,2048]{1,0:T(8,128)(2,1)}, bf16[128,2048]{1,0:T(8,128)(2,1)}, u32[]{:S(2)}, u32[]{:S(2)}) collective-permute-start(bf16[128,2048]{1,0:T(8,128)(2,1)} %add_convert_fusion.3), channel_id=1, source_target_pairs={{0,16},{1,17},{2,18},{3,19},{4,20},{5,21},{6,22},{7,23},{8,24},{9,... | collective-permute-start | bytes 1572872 | tf_op jit(solution)/shard_map/ppermute | solution.py:57
  510.7 21.5 %collective-permute-start.40 = (bf16[128,2048]{1,0:T(8,128)(2,1)}, bf16[128,2048]{1,0:T(8,128)(2,1)}, u32[]{:S(2)}, u32[]{:S(2)}) collective-permute-start(bf16[128,2048]{1,0:T(8,128)(2,1)} %add_convert_fusion.2), channel_id=1, source_target_pairs={{0,1},{1,0},{2,3},{3,2},{4,5},{5,4},{6,7},{7,6},{8,9},{9,8},{10,11... | collective-permute-start | bytes 1572872 | tf_op jit(solution)/shard_map/ppermute | solution.py:57
  539.1 30.6 %collective-permute-start.42 = (bf16[256,2048]{1,0:T(8,128)(2,1)S(1)}, bf16[256,2048]{1,0:T(8,128)(2,1)}, u32[]{:S(2)}, u32[]{:S(2)}) collective-permute-start(bf16[256,2048]{1,0:T(8,128)(2,1)S(1)} %pad_maximum_fusion.1), channel_id=1, source_target_pairs={{1,8},{3,10},{5,12},{7,14},{8,1},{10,3},{12,5},{14,7},{17,24},{19,... | collective-permute-start | bytes 3145736 | tf_op jit(solution)/shard_map/ppermute | solution.py:57
  561.6 22.9 %collective-permute-start.48 = (bf16[256,2048]{1,0:T(8,128)(2,1)S(1)}, bf16[256,2048]{1,0:T(8,128)(2,1)S(1)}, u32[]{:S(2)}, u32[]{:S(2)}) collective-permute-start(bf16[256,2048]{1,0:T(8,128)(2,1)S(1)} %copy-done.37), channel_id=1, source_target_pairs={{1,8},{3,10},{5,12},{7,14},{8,1},{10,3},{12,5},{14,7},{17,24},{19,... | collective-permute-start | bytes 3145736 | tf_op jit(solution)/shard_map/ppermute | solution.py:57
  (80 other events, 788.4 us)
Sparse Core Ops, SparseCore 0:
  10.2 48.0 all-gather.5
  60.5 81.1 all-gather.7
  143.3 45.6 all-gather.9
  190.4 45.8 all-gather.11
  237.8 45.8 all-gather.13
  298.6 51.2 reduce-scatter.5
  352.2 48.1 reduce-scatter.7
  402.7 48.1 reduce-scatter.9
  456.1 76.3 reduce-scatter.11
  536.1 44.3 reduce-scatter.13

commit v8 on v7

--- a/solution.py
+++ b/solution.py
@@ -93,7 +93,7 @@
             value, "fsdp", scatter_dimension=0, tiled=True, axis_index_groups=self.lines
         )
 
-    def total(self, value):
+    def total_but_x(self, value):
         for flip in (self.flip_y, self.flip_c):
             value = value + flip(value)
         if self.nz & (self.nz - 1):
@@ -103,7 +103,7 @@
             while bit < self.nz:
                 value = value + self.flip_z(value, bit)
                 bit *= 2
-        return value + self.flip_x(value)
+        return value
 
 
 def call(body, grid, ins, outs, shapes, scratch=(), flops=0, moved=0):
@@ -573,28 +573,32 @@
     )(index, left, *rights, *more)
 
 
-def weight_grad_rows(rows, pairs):
+def weight_grad_rows(rows, pairs, earlier=None):
     n = len(pairs)
     width, cols = pairs[0][0][0].shape[1], pairs[0][1][0].shape[1]
     tile = 512
+    more = [] if earlier is None else [earlier]
 
     def body(*refs):
         acc = tn(refs[0][...], refs[n][...])
         for i in range(1, n):
             acc = acc + tn(refs[i][...], refs[n + i][...])
+        if more:
+            acc = acc + refs[-2][...].astype(F32)
         refs[-1][...] = acc.astype(BF)
 
     return call(
         body,
         (width // tile,),
         [spec(rows, tile, lambda i, b=b: (b, i)) for (_, b), _ in pairs]
-        + [spec(rows, cols, lambda i, b=b: (b, 0)) for _, (_, b) in pairs],
+        + [spec(rows, cols, lambda i, b=b: (b, 0)) for _, (_, b) in pairs]
+        + [spec(tile, cols, lambda i: (i, 0)) for _ in more],
         spec(tile, cols, lambda i: (i, 0)),
         shape(width, cols),
         (),
         2 * n * rows * width * cols,
         2 * (n * rows * (width + cols) + width * cols),
-    )(*[left for (left, _), _ in pairs], *[right for _, (right, _) in pairs])
+    )(*[left for (left, _), _ in pairs], *[right for _, (right, _) in pairs], *more)
 
 
 def weight_grad_pieces(pieces, right):
@@ -696,12 +700,8 @@
         toks_moved = grid.swap(toks)
         segs = segments.reshape(micro, length).astype(F32)
         segs_moved = grid.swap(segs)
-        ud_cot = mark(
-            jnp.concatenate(
-                [jnp.concatenate([w_up, hold(w_down).T], axis=1), d_output.reshape(own, width)],
-                axis=0,
-            )
-        )
+        w_ud = mark(jnp.concatenate([w_up, hold(w_down).T], axis=1))
+        cots = d_output.reshape(own, width)
 
         ranks = [
             [2 * (y ^ i) + (x ^ j) for i, j in ((0, 0), (1, 0), (0, 1), (1, 1))],
@@ -747,7 +747,8 @@
         row_info = jnp.stack([positions, seg_rows] + [jnp.zeros_like(positions)] * 6, axis=1)
         row_info = mark(row_info.reshape(8 * micro, length))
         h1_second = [grid.second(b, pair(h1_own[b], h1_first[b])) for b in both]
-        ud_cot_moved = grid.swap(after(ud_cot, line_qk))
+        cots_moved = grid.swap(after(cots, line_qk))
+        ud_moved = grid.swap(after(w_ud, line_qk))
         h1_second = await_(*h1_second)
         line_qk = settle(line_qk, qk_moved)
         line_other = grid.flip_c(line_qk)
@@ -763,15 +764,15 @@
             full_qk, cos_table, sin_table,
         )
         mark(qk)
-        ud_cot = settle(ud_cot, ud_cot_moved)
-        full_u = grid.gather_weight(ud_cot[:-own, :hidden])
-        full_d = grid.gather_weight(ud_cot[:-own, hidden:])
-        cots = ud_cot[-own:]
+        cots = settle(cots, cots_moved)
         cot_own = [rows(cots, b) for b in both]
         cot_first = [grid.first(b, cot_own[b]) for b in both]
+        w_ud = settle(w_ud, ud_moved)
+        full_u = grid.gather_weight(w_ud[:, :hidden])
+        full_d = grid.gather_weight(w_ud[:, hidden:])
+        cot_second = [grid.second(b, pair(cot_own[b], cot_first[b])) for b in both]
         values, gate = project_plain(hold(h1), hold(full_vg), dv)
         mark(values)
-        cot_second = [grid.second(b, pair(cot_own[b], cot_first[b])) for b in both]
         gated = mark(
             retain(qk, hold(values), gate, col_info, row_info, log_gamma, heads, micro)
         )
@@ -803,11 +804,15 @@
             mid_first.append(grid.first(b, mid[b]))
         mid_second = [grid.second(b, pair(mid[b], mid_first[b])) for b in both]
         h2, act, slope = [], [], []
-        for some in ([v for b in both for v in (mid[b], mid_first[b])], mid_second):
+        g_down = None
+        for i, some in enumerate(
+            ([v for b in both for v in (mid[b], mid_first[b])], mid_second)
+        ):
             out = feed_up([hold(v) for v in some], full_u, hidden)
             mark(out[1])
             for held, value in zip((h2, act, slope), out):
                 held.append(value)
+            g_down = mark(weight_grad_rows(length, [((hold(cot), i), (act[i], 0))], g_down))
 
         def grad(left, rights):
             return mark(weight_grad(hold(left), rights))
@@ -815,9 +820,7 @@
         def grad_rows(lefts, rights):
             return mark(weight_grad_rows(length, list(zip(lefts, rights))))
 
-        g_down = grid.scatter_grad(
-            grad_rows([(hold(cot), 0), (cot, 1)], [(act[0], 0), (act[1], 0)])
-        )
+        g_down = grid.scatter_grad(g_down)
         d_up, *sent = feed_back(hold(cot), slope, full_u, full_d)
         mark(d_up)
         moved = [grid.second(b, sent[b]) for b in both]
@@ -846,7 +849,7 @@
             [p for b in both for p in mix[b][:2] + (hold(mix[b][2]),)], gated
         )
         g_out = grid.scatter_grad(mark(g_out))
-        g_ud = mark(jnp.concatenate([hold(g_up), g_down], axis=1))
+        g_up = await_(g_up)[0]
         down_moved = [grid.second(b, hold(down[1][b])) for b in both]
         d_v, d_gate, d_q, d_k = retain_back(
             hold(d_mix), gate, qk, values, full_o, col_info, row_info, cos_table, sin_table,
@@ -872,8 +875,9 @@
         down_moved = await_(*down_moved)
         vg_moved = line_start([d_v, d_gate])
         down = [reduce_second(b, down[0][b], down_moved[b]) for b in both]
-        g_ud_moved = grid.swap(hold(g_ud))
         g_vg = line_finish([d_v, d_gate], vg_moved)
+        g_ud = mark(jnp.concatenate([hold(g_up), g_down], axis=1))
+        g_ud_moved = grid.swap(g_ud)
         back = [d_q, d_k, d_v, d_gate]
         back_weights = [(full_qk, 0), (full_qk, 1), (full_vg, 0), (full_vg, 1)]
         sent = project_back([hold(back[0]), *back[1:]], back_weights, halves[1], BF)
@@ -905,8 +909,9 @@
         g_vg = await_(g_vg)[0]
         vg_moved = grid.swap(g_vg)
         output = settle(output, output_moved)
-        grad_norms = grid.total(hold(jnp.stack([gain_in_grad, gain_mid_grad])))
-        mark(grad_norms)
+        norms = mark(grid.total_but_x(hold(jnp.stack([gain_in_grad, gain_mid_grad]))))
+        g_vg = settle(g_vg, vg_moved)
+        grad_norms = mark(norms + grid.flip_x(hold(norms)))
         g_out_moved = grid.swap(hold(g_out))
         g_ud = settle(g_ud, g_ud_moved)
         d_input = settle(d_input, d_input_moved)
@@ -915,7 +920,7 @@
             hold(g).astype(F32) for g in (g_ud[:, hidden:].T, g_ud[:, :hidden], g_out.T)
         ]
         last[:] = [g_down, g_up, g_out]
-        g_vg = mark(settle(g_vg, vg_moved).astype(F32))
+        g_vg = mark(hold(g_vg).astype(F32))
         g_qk = await_(g_qk)[0]
         g_qk = settle(g_qk, grid.swap(g_qk)).astype(F32)
         whole = (micro, 1, piece, width)

time: 614 us -> 610 us (level)
  starting transfers between devices: 78.4 us -> 67.8 us
  waiting for transfers between devices: 206 us -> 216 us
  other arithmetic: 80.9 us -> 74.7 us
    ppermute x51 -> x52, starting transfers between devices: 77.3 us -> 66.8 us  [send(): return lax.ppermute(value, AXES, found)]
    ppermute x51 -> x52, waiting for transfers between devices: 202 us -> 212 us  [send(): return lax.ppermute(value, AXES, found)]
    pallas_call x2 -> x3, Pallas kernels: 16.9 us -> 21.5 us  [weight_grad_rows(): call(body, (width // tile,), [spec(rows, tile, lambda i, b=b: (b, i)) for...]
    unnamed x111 -> x117, local copies, waits for them, and re-layouts: 12.8 us -> 10.4 us
  transfers between devices with their start and end apart: 61 -> 62, of which waited for: 38 -> 38; matrix products, arithmetic and copies ran while one was open for 15% -> 15% of each run, Pallas kernels for 33% -> 34%
where the time goes in v8:
time: 610 us; the launch traced here: 601 us
  waiting for transfers between devices  216 us (35%)
  Pallas kernels  206 us (34%)
  other arithmetic  74.7 us (12%)
  starting transfers between devices  67.8 us (11%)
  local copies, waits for them, and re-layouts  21.1 us (3%)
  between operations  15.8 us (3%)
    ppermute x52, waiting for transfers between devices, send(): return lax.ppermute(value, AXES, found)  212 us
    ppermute x52, starting transfers between devices, send(): return lax.ppermute(value, AXES, found)  66.8 us
    pallas_call x7, Pallas kernels, project_back(): call(body, (width // tile,), [spec(rows, k, lambda j: (0, 0)) for k in si...  58.3 us
    pallas_call x4, Pallas kernels, weight_grad_part(): pl.pallas_call(body, out_shape=shape(blocks * tile, cols), grid_spec=pltp...  31 us
    pallas_call x3, Pallas kernels, weight_grad_rows(): call(body, (width // tile,), [spec(rows, tile, lambda i, b=b: (b, i)) for...  21.5 us
    pallas_call x1, Pallas kernels, retain_back(): call(body, (heads, micro), [per_row(rows, width), spec(width, VAL_HEAD, l...  17.4 us
    pallas_call x2, Pallas kernels, feed_up(): call(body, (steps,), [ANY] * n + [spec(width, tile, lambda j: (0, j))], [...  16.2 us
    pallas_call x1, Pallas kernels, project_plain(): call(body, (cols // tile,), [spec(rows, width, lambda j: (0, 0)), spec(wi...  15.2 us
  transfers between devices with their start and end apart: 62, of which 38 were waited for; matrix products, arithmetic and copies ran while one was open for 15% of the time, Pallas kernels for 34%

profile of v8, /device:TPU:1, one launch (start us, length us, event | category | flops | bytes accessed | tf_op | source)
XLA Modules:
  0.0 600.9 jit_solution(17414475217413156728)
XLA Ops:
  22.7 13.2 %collective-permute-done.1 = bf16[256,3072]{1,0:T(8,128)(2,1)} collective-permute-done((bf16[256,3072]{1,0:T(8,128)(2,1)}, bf16[256,3072]{1,0:T(8,128)(2,1)}, u32[]{:S(2)}, u32[]{:S(2)}) %collective-permute-start.1) | collective-permute-done | bytes 1572896 | tf_op jit(solution)/shard_map/ppermute | solution.py:57
  45.2 10.9 %collective-permute-done = bf16[256,2048]{1,0:T(8,128)(2,1)} collective-permute-done((bf16[256,2048]{1,0:T(8,128)(2,1)}, bf16[256,2048]{1,0:T(8,128)(2,1)}, u32[]{:S(2)}, u32[]{:S(2)}) %collective-permute-start) | collective-permute-done | bytes 1048608 | tf_op jit(solution)/shard_map/ppermute | solution.py:57
  78.5 23.9 %collective-permute-done.6.refs_5_ = bf16[256,2048]{1,0:T(8,128)(2,1)S(1)} collective-permute-done((bf16[256,2048]{1,0:T(8,128)(2,1)S(1)}, bf16[256,2048]{1,0:T(8,128)(2,1)S(1)}, u32[]{:S(2)}, u32[]{:S(2)}) %collective-permute-start.6) | collective-permute-done | bytes 1048608 | tf_op jit(solution)/shard_map/ppermute | solution.py:57
  102.4 17.5 %collective-permute-done.4.refs_2_ = bf16[256,2048]{1,0:T(8,128)(2,1)S(1)} collective-permute-done((bf16[256,2048]{1,0:T(8,128)(2,1)S(1)}, bf16[256,2048]{1,0:T(8,128)(2,1)S(1)}, u32[]{:S(2)}, u32[]{:S(2)}) %collective-permute-start.4) | collective-permute-done | bytes 1048608 | tf_op jit(solution)/shard_map/ppermute | solution.py:57
  133.7 10.1 %shard_map.186 = (bf16[1024,2048]{1,0:T(8,128)(2,1)}, bf16[1024,1024]{1,0:T(8,128)(2,1)}) custom-call(bf16[128,2048]{1,0:T(8,128)(2,1)} %get-tuple-element.321.refs_0_, bf16[128,2048]{1,0:T(8,128)(2,1)} %copy-done.45, bf16[256,2048]{1,0:T(8,128)(2,1)} %copy-done.53, bf16[128,2048]{1,0:T(8,128)(2,1)} %copy-done.33, ...), custom_call_target="tpu_custom_call" | custom-call | flops 4294967296 | bytes 14680064 | tf_op jit(solution)/shard_map/pallas_call | solution.py:216
  156.7 6.3 %collective-permute-done.11.refs_1_ = bf16[128,2048]{1,0:T(8,128)(2,1)S(1)} collective-permute-done((bf16[128,2048]{1,0:T(8,128)(2,1)S(1)}, bf16[128,2048]{1,0:T(8,128)(2,1)S(1)}, u32[]{:S(2)}, u32[]{:S(2)}) %collective-permute-start.11) | collective-permute-done | bytes 524320 | tf_op jit(solution)/shard_map/ppermute | solution.py:57
  171.2 15.2 %shard_map.187 = (bf16[1024,1024]{1,0:T(8,128)(2,1)}, f32[1024,1024]{1,0:T(8,128)}) custom-call(bf16[1024,2048]{1,0:T(8,128)(2,1)} %get-tuple-element.245.h_ref.left_ref, bf16[2048,2048]{1,0:T(8,128)(2,1)} %all-gather.8.cloned.1.call-done.w_ref.refs_6_.refs_7_), custom_call_target="tpu_custom_call" | custom-call | flops 8589934592 | bytes 20971520 | tf_op jit(solution)/shard_map/pallas_call | solution.py:255
  186.4 7.6 %shard_map.188.refs_0_.refs_6_ = bf16[1024,1024]{1,0:T(8,128)(2,1)} custom-call(bf16[1024,1024]{1,0:T(8,128)(2,1)} %get-tuple-element.154.q_ref.k_ref, bf16[1024,1024]{1,0:T(8,128)(2,1)} %get-tuple-element.154.q_ref.k_ref, bf16[1024,1024]{1,0:T(8,128)(2,1)} %get-tuple-element.165.v_ref, f32[1024,1024]{1,0:T(8,128)} %get-tuple-element.166.gate_ref, ...), custom_call_target="tpu_custom_call" | custom-call | flops 1610612736 | bytes 10485760 | tf_op jit(solution)/shard_map/pallas_call | solution.py:303
  194.0 6.6 %shard_map.189 = (bf16[256,2048]{1,0:T(8,128)(2,1)}, bf16[256,2048]{1,0:T(8,128)(2,1)}) custom-call(bf16[1024,1024]{1,0:T(8,128)(2,1)} %shard_map.188.refs_0_.refs_6_, bf16[2048,1024]{1,0:T(8,128)(2,1)} %all-gather.10.cloned.1.call-done.refs_1_.wo), custom_call_target="tpu_custom_call" | custom-call | flops 2147483648 | bytes 9437184 | tf_op jit(solution)/shard_map/pallas_call | solution.py:385
  200.7 6.8 %shard_map.190 = (f32[256,2048]{1,0:T(8,128)}, f32[256,2048]{1,0:T(8,128)}) custom-call(bf16[1024,1024]{1,0:T(8,128)(2,1)} %shard_map.188.refs_0_.refs_6_, bf16[2048,1024]{1,0:T(8,128)(2,1)} %all-gather.10.cloned.1.call-done.refs_1_.wo), custom_call_target="tpu_custom_call" | custom-call | flops 2147483648 | bytes 9437184 | tf_op jit(solution)/shard_map/pallas_call | solution.py:385
  211.8 14.1 %collective-permute-done.13 = bf16[256,2048]{1,0:T(8,128)(2,1)} collective-permute-done((bf16[256,2048]{1,0:T(8,128)(2,1)}, bf16[256,2048]{1,0:T(8,128)(2,1)}, u32[]{:S(2)}, u32[]{:S(2)}) %collective-permute-start.13) | collective-permute-done | bytes 1048608 | tf_op jit(solution)/shard_map/ppermute | solution.py:57
  229.9 10.2 %collective-permute-done.16 = bf16[128,2048]{1,0:T(8,128)(2,1)S(1)} collective-permute-done((bf16[128,2048]{1,0:T(8,128)(2,1)S(1)}, bf16[128,2048]{1,0:T(8,128)(2,1)S(1)}, u32[]{:S(2)}, u32[]{:S(2)}) %collective-permute-start.16) | collective-permute-done | bytes 524320 | tf_op jit(solution)/shard_map/ppermute | solution.py:57
  245.0 9.3 %collective-permute-done.20.refs_1_ = bf16[128,2048]{1,0:T(8,128)(2,1)S(1)} collective-permute-done((bf16[128,2048]{1,0:T(8,128)(2,1)S(1)}, bf16[128,2048]{1,0:T(8,128)(2,1)S(1)}, u32[]{:S(2)}, u32[]{:S(2)}) %collective-permute-start.20) | collective-permute-done | bytes 524320 | tf_op jit(solution)/shard_map/ppermute | solution.py:57
  259.0 8.1 %shard_map.192 = (bf16[512,2048]{1,0:T(8,128)(2,1)}, bf16[512,1024]{1,0:T(8,128)(2,1)}, f32[512,1024]{1,0:T(8,128)}) custom-call(bf16[128,2048]{1,0:T(8,128)(2,1)} %copy-done.34, bf16[128,2048]{1,0:T(8,128)(2,1)} %copy-done.47, bf16[128,2048]{1,0:T(8,128)(2,1)} %copy-done.35, bf16[128,2048]{1,0:T(8,128)(2,1)} %copy-done.49, ...), custom_call_target="tpu_custom_call" | custom-call | flops 2147483648 | bytes 11534336 | tf_op jit(solution)/shard_map/pallas_call | solution.py:355
  267.1 6.1 %shard_map.193.refs_2_ = bf16[2048,1024]{1,0:T(8,128)(2,1)} custom-call(bf16[1024,2048]{1,0:T(8,128)(2,1)} %shard_map.191.refs_0_.cot_ref, bf16[512,1024]{1,0:T(8,128)(2,1)} %get-tuple-element.210.refs_1_.refs_0_), custom_call_target="tpu_custom_call" | custom-call | flops 2147483648 | bytes 7340032 | tf_op jit(solution)/shard_map/pallas_call | solution.py:590
  273.3 7.8 %collective-permute-done.22.refs_1_ = bf16[256,2048]{1,0:T(8,128)(2,1)} collective-permute-done((bf16[256,2048]{1,0:T(8,128)(2,1)}, bf16[256,2048]{1,0:T(8,128)(2,1)}, u32[]{:S(2)}, u32[]{:S(2)}) %collective-permute-start.22) | collective-permute-done | bytes 1048608 | tf_op jit(solution)/shard_map/ppermute | solution.py:57
  281.1 8.1 %shard_map.194 = (bf16[512,2048]{1,0:T(8,128)(2,1)}, bf16[512,1024]{1,0:T(8,128)(2,1)}, f32[512,1024]{1,0:T(8,128)}) custom-call(bf16[256,2048]{1,0:T(8,128)(2,1)} %collective-permute-done.21.refs_0_, bf16[256,2048]{1,0:T(8,128)(2,1)} %collective-permute-done.22.refs_1_, bf16[2048,1024]{1,0:T(8,128)(2,1)} %all-gather.12.cloned.1.call-done.refs_4_.refs_2_.up_ref.refs_1_), custom_call_target="tpu_custom_call" | custom-call | flops 2147483648 | bytes 11534336 | tf_op jit(solution)/shard_map/pallas_call | solution.py:355
  289.2 7.0 %shard_map.195 = bf16[2048,1024]{1,0:T(8,128)(2,1)} custom-call(bf16[1024,2048]{1,0:T(8,128)(2,1)} %shard_map.191.refs_0_.cot_ref, bf16[512,1024]{1,0:T(8,128)(2,1)} %get-tuple-element.212.refs_1_.refs_0_, bf16[2048,1024]{1,0:T(8,128)(2,1)} %shard_map.193.refs_2_), custom_call_target="tpu_custom_call" | custom-call | flops 2147483648 | bytes 7340032 | tf_op jit(solution)/shard_map/pallas_call | solution.py:590
  296.4 14.0 %shard_map.196 = (bf16[1024,1024]{1,0:T(8,128)(2,1)}, bf16[256,2048]{1,0:T(8,128)(2,1)}, bf16[256,2048]{1,0:T(8,128)(2,1)}) custom-call(bf16[1024,2048]{1,0:T(8,128)(2,1)} %shard_map.191.refs_0_.cot_ref, bf16[2048,1024]{1,0:T(8,128)(2,1)} %all-gather.14.cloned.1.call-done.down_ref.refs_1_, ...), custom_call_target="tpu_custom_call" | custom-call | flops 6442450944 | bytes 23068672 | tf_op jit(solution)/shard_map/pallas_call | solution.py:431
  311.8 6.7 %shard_map.197 = (f32[256,2048]{1,0:T(8,128)}, f32[256,2048]{1,0:T(8,128)}) custom-call(bf16[1024,1024]{1,0:T(8,128)(2,1)} %get-tuple-element.195.refs_0_.refs_2_.refs_3_, bf16[2048,1024]{1,0:T(8,128)(2,1)} %all-gather.12.cloned.1.call-done.refs_4_.refs_2_.up_ref.refs_1_), custom_call_target="tpu_custom_call" | custom-call | flops 2147483648 | bytes 9437184 | tf_op jit(solution)/shard_map/pallas_call | solution.py:385
  318.5 8.4 %shard_map.198 = bf16[2048,1024]{1,0:T(8,128)(2,1)} custom-call(bf16[512,2048]{1,0:T(8,128)(2,1)} %get-tuple-element.201.refs_0_, bf16[512,2048]{1,0:T(8,128)(2,1)} %get-tuple-element.202.refs_1_, bf16[1024,1024]{1,0:T(8,128)(2,1)} %get-tuple-element.195.refs_0_.refs_2_.refs_3_, bf16[1024,1024]{1,0:T(8,128)(2,1)} %get-tuple-element.195.refs_0_.refs_2_.refs_3_), custom_call_target="tpu_custom_call" | custom-call | flops 4294967296 | bytes 10485760 | tf_op jit(solution)/shard_map/pallas_call | solution.py:590
  336.9 7.8 %collective-permute-done.26 = bf16[128,2048]{1,0:T(8,128)(2,1)S(1)} collective-permute-done((bf16[128,2048]{1,0:T(8,128)(2,1)S(1)}, bf16[128,2048]{1,0:T(8,128)(2,1)S(1)}, u32[]{:S(2)}, u32[]{:S(2)}) %collective-permute-start.26) | collective-permute-done | bytes 524320 | tf_op jit(solution)/shard_map/ppermute | solution.py:57
  369.7 6.4 %shard_map.199 = (f32[256,2048]{1,0:T(8,128)}, f32[256,2048]{1,0:T(8,128)}) custom-call(bf16[512,1024]{1,0:T(8,128)(2,1)} %get-tuple-element.210.refs_1_.refs_0_, bf16[2048,1024]{1,0:T(8,128)(2,1)} %all-gather.14.cloned.1.call-done.down_ref.refs_1_), custom_call_target="tpu_custom_call" | custom-call | flops 2147483648 | bytes 8388608 | tf_op jit(solution)/shard_map/pallas_call | solution.py:385
  383.5 10.1 %shard_map.201 = (bf16[1024,2048]{1,0:T(8,128)(2,1)}, bf16[2048,1024]{1,0:T(8,128)(2,1)}) custom-call(bf16[128,2048]{1,0:T(8,128)(2,1)} %copy-done.36, bf16[128,2048]{1,0:T(8,128)(2,1)} %copy-done.46, bf16[256,2048]{1,0:T(8,128)(2,1)} %collective-permute-done.29.refs_2_, bf16[128,2048]{1,0:T(8,128)(2,1)} %copy-done.37, bf16[128,2048]{1,0:T(8,128)(2,1)} %copy-done.48, ...), custom_call_target="tpu_custom_call" | custom-call | flops 4294967296 | bytes 10485760 | tf_op jit(solution)/shard_map/pallas_call | solution.py:622
  399.3 17.4 %shard_map.202 = (bf16[1024,1024]{1,0:T(8,128)(2,1)}, bf16[1024,1024]{1,0:T(8,128)(2,1)}, bf16[1024,512]{1,0:T(8,128)(2,1)}, bf16[1024,512]{1,0:T(8,128)(2,1)}) custom-call(bf16[1024,2048]{1,0:T(8,128)(2,1)} %get-tuple-element.223.mix_ref, bf16[2048,1024]{1,0:T(8,128)(2,1)} %all-gather.10.cloned.1.call-done.refs_1_.wo, ...), custom_call_target="tpu_custom_call" | custom-call | flops 9663676416 | bytes 29360128 | tf_op jit(solution)/shard_map/pallas_call | solution.py:489
  419.7 8.8 %shard_map.203 = bf16[1024,2048]{1,0:T(8,128)(2,1)} custom-call(s32[1]{0:T(128)} %bitcast.28._, bf16[1024,2048]{1,0:T(8,128)(2,1)} %get-tuple-element.245.h_ref.left_ref, bf16[1024,1024]{1,0:T(8,128)(2,1)} %get-tuple-element.224.refs_0_.refs_2_, bf16[1024,1024]{1,0:T(8,128)(2,1)} %get-tuple-element.227.refs_1_.refs_3_), custom_call_target="tpu_custom_call" | custom-call | flops 4294967296 | bytes 16777216 | tf_op jit(solution)/shard_map/pallas_call | solution.py:556
  440.0 9.7 %shard_map.204 = bf16[1024,2048]{1,0:T(8,128)(2,1)} custom-call(s32[1]{0:T(128)} %bitcast.29._, bf16[1024,2048]{1,0:T(8,128)(2,1)} %get-tuple-element.245.h_ref.left_ref, bf16[1024,1024]{1,0:T(8,128)(2,1)} %get-tuple-element.224.refs_0_.refs_2_, bf16[1024,1024]{1,0:T(8,128)(2,1)} %get-tuple-element.227.refs_1_.refs_3_, ...), custom_call_target="tpu_custom_call" | custom-call | flops 4294967296 | bytes 16777216 | tf_op jit(solution)/shard_map/pallas_call | solution.py:556
  455.7 13.0 %shard_map.205 = (bf16[256,2048]{1,0:T(8,128)(2,1)}, bf16[256,2048]{1,0:T(8,128)(2,1)}) custom-call(bf16[1024,512]{1,0:T(8,128)(2,1)} %get-tuple-element.242.refs_0_, bf16[1024,512]{1,0:T(8,128)(2,1)} %get-tuple-element.230.refs_1_, bf16[1024,1024]{1,0:T(8,128)(2,1)} %get-tuple-element.224.refs_0_.refs_2_, ...), custom_call_target="tpu_custom_call" | custom-call | flops 6442450944 | bytes 22020096 | tf_op jit(solution)/shard_map/pallas_call | solution.py:385
  469.6 12.8 %shard_map.206 = (f32[256,2048]{1,0:T(8,128)}, f32[256,2048]{1,0:T(8,128)}) custom-call(bf16[1024,512]{1,0:T(8,128)(2,1)} %get-tuple-element.242.refs_0_, bf16[1024,512]{1,0:T(8,128)(2,1)} %get-tuple-element.230.refs_1_, bf16[1024,1024]{1,0:T(8,128)(2,1)} %get-tuple-element.224.refs_0_.refs_2_, bf16[1024,1024]{1,0:T(8,128)(2,1)} %get-tuple-element.227.refs_1_.refs_3_, ...), custom_call_target="tpu_custom_call" | custom-call | flops 6442450944 | bytes 22020096 | tf_op jit(solution)/shard_map/pallas_call | solution.py:385
  482.4 11.0 %collective-permute-done.37 = bf16[256,2048]{1,0:T(8,128)(2,1)} collective-permute-done((bf16[256,2048]{1,0:T(8,128)(2,1)}, bf16[256,2048]{1,0:T(8,128)(2,1)}, u32[]{:S(2)}, u32[]{:S(2)}) %collective-permute-start.37) | collective-permute-done | bytes 1048608 | tf_op jit(solution)/shard_map/ppermute | solution.py:57
  508.8 6.5 %shard_map.208 = bf16[1024,1024]{1,0:T(8,128)(2,1)} custom-call(s32[1]{0:T(128)} %bitcast.29._, bf16[1024,2048]{1,0:T(8,128)(2,1)} %get-tuple-element.245.h_ref.left_ref, bf16[1024,512]{1,0:T(8,128)(2,1)} %get-tuple-element.242.refs_0_, bf16[1024,512]{1,0:T(8,128)(2,1)} %get-tuple-element.230.refs_1_, bf16[1024,1024]{1,0:T(8,128)(2,1)} %collective-permute-done.38.refs_2_), custom_call_target="tpu_custom_call" | custom-call | flops 2147483648 | bytes 10485760 | tf_op jit(solution)/shard_map/pallas_call | solution.py:556
  558.9 10.6 %collective-permute-done.49 = f32[2,2048]{1,0:T(2,128)S(1)} collective-permute-done((f32[2,2048]{1,0:T(2,128)S(1)}, f32[2,2048]{1,0:T(2,128)S(1)}, u32[]{:S(2)}, u32[]{:S(2)}) %collective-permute-start.49) | collective-permute-done | bytes 16416 | tf_op jit(solution)/shard_map/ppermute | solution.py:57
  (353 shorter events, 252.9 us)
Async XLA Ops:
  7.2 56.1 %all-gather.6.cloned.1.call-start = ((), (), s32[]{:S(2)}) async-start(), calls=%async_computation.5 | async-start | bytes 2621440 | tf_op jit(solution)/shard_map/all_gather | solution.py:89
  10.1 161.1 %all-gather.8.cloned.1.call-start = ((), (), s32[]{:S(2)}) async-start(), calls=%async_computation.6 | async-start | bytes 9437184 | tf_op jit(solution)/shard_map/all_gather | solution.py:81
  12.7 23.2 %collective-permute-start.1 = (bf16[256,3072]{1,0:T(8,128)(2,1)}, bf16[256,3072]{1,0:T(8,128)(2,1)}, u32[]{:S(2)}, u32[]{:S(2)}) collective-permute-start(bf16[256,3072]{1,0:T(8,128)(2,1)} %pad_maximum_fusion.1), channel_id=1, source_target_pairs={{1,8},{3,10},{5,12},{7,14},{8,1},{10,3},{12,5},{14,7},{17,24},{19,... | collective-permute-start | bytes 4718600 | tf_op jit(solution)/shard_map/ppermute | solution.py:57
  39.3 154.7 %all-gather.10.cloned.1.call-start = ((), (), s32[]{:S(2)}) async-start(), calls=%async_computation.7 | async-start | bytes 4718592 | tf_op jit(solution)/shard_map/all_gather | solution.py:81
  42.7 23.9 %collective-permute-start.3 = (bf16[2,512]{1,0:T(2,128)(2,1)S(1)}, bf16[2,512]{1,0:T(2,128)(2,1)S(1)}, u32[]{:S(2)}, u32[]{:S(2)}) collective-permute-start(bf16[2,512]{1,0:T(2,128)(2,1)S(1)} %bitcast.102), channel_id=1, source_target_pairs={{1,8},{3,10},{5,12},{7,14},{8,1},{10,3},{12,5},{14,7},{17,24},{19,... | collective-permute-start | bytes 6152 | tf_op jit(solution)/shard_map/ppermute | solution.py:57
  63.2 195.8 %all-gather.12.cloned.1.call-start = ((), (), s32[]{:S(2)}) async-start(), calls=%async_computation.8 | async-start | bytes 4718592 | tf_op jit(solution)/shard_map/all_gather | solution.py:81
  63.3 57.6 %collective-permute-start.7 = (bf16[1024,1024]{1,0:T(8,128)(2,1)}, bf16[1024,1024]{1,0:T(8,128)(2,1)S(1)}, u32[]{:S(2)}, u32[]{:S(2)}) collective-permute-start(bf16[1024,1024]{1,0:T(8,128)(2,1)} %all-gather.6.cloned.1.call-done), channel_id=1, source_target_pairs={{1,8},{3,10},{5,12},{7,14},{8,1},{10,3},{12,5},{14,7},{17,24},{19,... | collective-permute-start | bytes 6291464 | tf_op jit(solution)/shard_map/ppermute | solution.py:57
  78.2 24.2 %collective-permute-start.6 = (bf16[256,2048]{1,0:T(8,128)(2,1)S(1)}, bf16[256,2048]{1,0:T(8,128)(2,1)S(1)}, u32[]{:S(2)}, u32[]{:S(2)}) collective-permute-start(bf16[256,2048]{1,0:T(8,128)(2,1)S(1)} %pad_maximum_fusion.4), channel_id=1, source_target_pairs={{0,16},{1,17},{2,18},{3,19},{4,20},{5,21},{6,22},{7,23},{8,24},{9,... | collective-permute-start | bytes 3145736 | tf_op jit(solution)/shard_map/ppermute | solution.py:57
  78.5 41.4 %collective-permute-start.4 = (bf16[256,2048]{1,0:T(8,128)(2,1)S(1)}, bf16[256,2048]{1,0:T(8,128)(2,1)S(1)}, u32[]{:S(2)}, u32[]{:S(2)}) collective-permute-start(bf16[256,2048]{1,0:T(8,128)(2,1)S(1)} %pad_maximum_fusion.3), channel_id=1, source_target_pairs={{0,1},{1,0},{2,3},{3,2},{4,5},{5,4},{6,7},{7,6},{8,9},{9,8},{10,11... | collective-permute-start | bytes 3145736 | tf_op jit(solution)/shard_map/ppermute | solution.py:57
  125.8 25.8 %collective-permute-start.12 = (bf16[256,2048]{1,0:T(8,128)(2,1)}, bf16[256,2048]{1,0:T(8,128)(2,1)}, u32[]{:S(2)}, u32[]{:S(2)}) collective-permute-start(bf16[256,2048]{1,0:T(8,128)(2,1)} %pad_maximum_fusion.2), channel_id=1, source_target_pairs={{1,8},{3,10},{5,12},{7,14},{8,1},{10,3},{12,5},{14,7},{17,24},{19,... | collective-permute-start | bytes 3145736 | tf_op jit(solution)/shard_map/ppermute | solution.py:57
  154.3 142.1 %all-gather.14.cloned.1.call-start = ((), (), s32[]{:S(2)}) async-start(), calls=%async_computation.9 | async-start | bytes 4718592 | tf_op jit(solution)/shard_map/all_gather | solution.py:81
  156.5 196.9 %reduce-scatter.6.cloned.1.call-start = ((), (), s32[]{:S(2)}) async-start(), calls=%async_computation.10 | async-start | bytes 4718592 | tf_op jit(solution)/shard_map/reduce_scatter | solution.py:84
  164.1 43.4 %collective-permute-start.14 = (bf16[256,2048]{1,0:T(8,128)(2,1)}, bf16[256,2048]{1,0:T(8,128)(2,1)}, u32[]{:S(2)}, u32[]{:S(2)}) collective-permute-start(bf16[256,2048]{1,0:T(8,128)(2,1)} %pad_maximum_fusion.5), channel_id=1, source_target_pairs={{0,1},{1,0},{2,3},{3,2},{4,5},{5,4},{6,7},{7,6},{8,9},{9,8},{10,11... | collective-permute-start | bytes 3145736 | tf_op jit(solution)/shard_map/ppermute | solution.py:57
  170.0 37.5 %collective-permute-start.15 = (bf16[256,2048]{1,0:T(8,128)(2,1)}, bf16[256,2048]{1,0:T(8,128)(2,1)}, u32[]{:S(2)}, u32[]{:S(2)}) collective-permute-start(bf16[256,2048]{1,0:T(8,128)(2,1)} %pad_maximum_fusion.6), channel_id=1, source_target_pairs={{0,16},{1,17},{2,18},{3,19},{4,20},{5,21},{6,22},{7,23},{8,24},{9,... | collective-permute-start | bytes 3145736 | tf_op jit(solution)/shard_map/ppermute | solution.py:57
  200.6 25.4 %collective-permute-start.13 = (bf16[256,2048]{1,0:T(8,128)(2,1)}, bf16[256,2048]{1,0:T(8,128)(2,1)}, u32[]{:S(2)}, u32[]{:S(2)}) collective-permute-start(bf16[256,2048]{1,0:T(8,128)(2,1)} %get-tuple-element.168), channel_id=1, source_target_pairs={{0,1},{1,0},{2,3},{3,2},{4,5},{5,4},{6,7},{7,6},{8,9},{9,8},{10,11... | collective-permute-start | bytes 3145736 | tf_op jit(solution)/shard_map/ppermute | solution.py:57
  200.6 27.0 %collective-permute-start.17 = (bf16[256,2048]{1,0:T(8,128)(2,1)}, bf16[256,2048]{1,0:T(8,128)(2,1)}, u32[]{:S(2)}, u32[]{:S(2)}) collective-permute-start(bf16[256,2048]{1,0:T(8,128)(2,1)} %get-tuple-element.175), channel_id=1, source_target_pairs={{0,16},{1,17},{2,18},{3,19},{4,20},{5,21},{6,22},{7,23},{8,24},{9,... | collective-permute-start | bytes 3145736 | tf_op jit(solution)/shard_map/ppermute | solution.py:57
  258.3 22.8 %collective-permute-start.22 = (bf16[256,2048]{1,0:T(8,128)(2,1)}, bf16[256,2048]{1,0:T(8,128)(2,1)}, u32[]{:S(2)}, u32[]{:S(2)}) collective-permute-start(bf16[256,2048]{1,0:T(8,128)(2,1)} %pad_maximum_fusion.8), channel_id=1, source_target_pairs={{0,16},{1,17},{2,18},{3,19},{4,20},{5,21},{6,22},{7,23},{8,24},{9,... | collective-permute-start | bytes 3145736 | tf_op jit(solution)/shard_map/ppermute | solution.py:57
  258.7 22.4 %collective-permute-start.21 = (bf16[256,2048]{1,0:T(8,128)(2,1)}, bf16[256,2048]{1,0:T(8,128)(2,1)}, u32[]{:S(2)}, u32[]{:S(2)}) collective-permute-start(bf16[256,2048]{1,0:T(8,128)(2,1)} %pad_maximum_fusion.7), channel_id=1, source_target_pairs={{0,1},{1,0},{2,3},{3,2},{4,5},{5,4},{6,7},{7,6},{8,9},{9,8},{10,11... | collective-permute-start | bytes 3145736 | tf_op jit(solution)/shard_map/ppermute | solution.py:57
  296.2 100.8 %reduce-scatter.8.cloned.1.call-start = ((), (), s32[]{:S(2)}) async-start(), calls=%async_computation.11 | async-start | bytes 4718592 | tf_op jit(solution)/shard_map/reduce_scatter | solution.py:84
  310.5 21.5 %collective-permute-start.24 = (bf16[256,2048]{1,0:T(8,128)(2,1)}, bf16[256,2048]{1,0:T(8,128)(2,1)}, u32[]{:S(2)}, u32[]{:S(2)}) collective-permute-start(bf16[256,2048]{1,0:T(8,128)(2,1)} %get-tuple-element.199), channel_id=1, source_target_pairs={{0,1},{1,0},{2,3},{3,2},{4,5},{5,4},{6,7},{7,6},{8,9},{9,8},{10,11... | collective-permute-start | bytes 3145736 | tf_op jit(solution)/shard_map/ppermute | solution.py:57
  311.0 22.4 %collective-permute-start.23 = (bf16[256,2048]{1,0:T(8,128)(2,1)}, bf16[256,2048]{1,0:T(8,128)(2,1)}, u32[]{:S(2)}, u32[]{:S(2)}) collective-permute-start(bf16[256,2048]{1,0:T(8,128)(2,1)} %get-tuple-element.197), channel_id=1, source_target_pairs={{0,16},{1,17},{2,18},{3,19},{4,20},{5,21},{6,22},{7,23},{8,24},{9,... | collective-permute-start | bytes 3145736 | tf_op jit(solution)/shard_map/ppermute | solution.py:57
  335.5 159.4 %reduce-scatter.10.cloned.1.call-start = ((), (), s32[]{:S(2)}) async-start(), calls=%async_computation.12 | async-start | bytes 4718592 | tf_op jit(solution)/shard_map/reduce_scatter | solution.py:84
  393.7 138.5 %reduce-scatter.12.cloned.1.call-start = ((), (), s32[]{:S(2)}) async-start(), calls=%async_computation.13 | async-start | bytes 5242880 | tf_op jit(solution)/shard_map/reduce_scatter | solution.py:92
  396.9 21.1 %collective-permute-start.32 = (bf16[256,2048]{1,0:T(8,128)(2,1)}, bf16[256,2048]{1,0:T(8,128)(2,1)}, u32[]{:S(2)}, u32[]{:S(2)}) collective-permute-start(bf16[256,2048]{1,0:T(8,128)(2,1)} %get-tuple-element.221), channel_id=1, source_target_pairs={{0,16},{1,17},{2,18},{3,19},{4,20},{5,21},{6,22},{7,23},{8,24},{9,... | collective-permute-start | bytes 3145736 | tf_op jit(solution)/shard_map/ppermute | solution.py:57
  398.1 21.6 %collective-permute-start.31 = (bf16[256,2048]{1,0:T(8,128)(2,1)}, bf16[256,2048]{1,0:T(8,128)(2,1)}, u32[]{:S(2)}, u32[]{:S(2)}) collective-permute-start(bf16[256,2048]{1,0:T(8,128)(2,1)} %get-tuple-element.219), channel_id=1, source_target_pairs={{0,1},{1,0},{2,3},{3,2},{4,5},{5,4},{6,7},{7,6},{8,9},{9,8},{10,11... | collective-permute-start | bytes 3145736 | tf_op jit(solution)/shard_map/ppermute | solution.py:57
  449.7 132.1 %reduce-scatter.14.cloned.1.call-start = ((), (), s32[]{:S(2)}) async-start(), calls=%async_computation.14 | async-start | bytes 2621440 | tf_op jit(solution)/shard_map/reduce_scatter | solution.py:92
  469.1 24.3 %collective-permute-start.37 = (bf16[256,2048]{1,0:T(8,128)(2,1)}, bf16[256,2048]{1,0:T(8,128)(2,1)}, u32[]{:S(2)}, u32[]{:S(2)}) collective-permute-start(bf16[256,2048]{1,0:T(8,128)(2,1)} %get-tuple-element.241), channel_id=1, source_target_pairs={{0,16},{1,17},{2,18},{3,19},{4,20},{5,21},{6,22},{7,23},{8,24},{9,... | collective-permute-start | bytes 3145736 | tf_op jit(solution)/shard_map/ppermute | solution.py:57
  469.6 25.3 %collective-permute-start.36 = (bf16[256,2048]{1,0:T(8,128)(2,1)}, bf16[256,2048]{1,0:T(8,128)(2,1)}, u32[]{:S(2)}, u32[]{:S(2)}) collective-permute-start(bf16[256,2048]{1,0:T(8,128)(2,1)} %get-tuple-element.239), channel_id=1, source_target_pairs={{0,1},{1,0},{2,3},{3,2},{4,5},{5,4},{6,7},{7,6},{8,9},{9,8},{10,11... | collective-permute-start | bytes 3145736 | tf_op jit(solution)/shard_map/ppermute | solution.py:57
  504.9 21.7 %collective-permute-start.42 = (bf16[128,2048]{1,0:T(8,128)(2,1)}, bf16[128,2048]{1,0:T(8,128)(2,1)}, u32[]{:S(2)}, u32[]{:S(2)}) collective-permute-start(bf16[128,2048]{1,0:T(8,128)(2,1)} %add_convert_fusion.3), channel_id=1, source_target_pairs={{0,16},{1,17},{2,18},{3,19},{4,20},{5,21},{6,22},{7,23},{8,24},{9,... | collective-permute-start | bytes 1572872 | tf_op jit(solution)/shard_map/ppermute | solution.py:57
  507.3 21.5 %collective-permute-start.41 = (bf16[128,2048]{1,0:T(8,128)(2,1)}, bf16[128,2048]{1,0:T(8,128)(2,1)}, u32[]{:S(2)}, u32[]{:S(2)}) collective-permute-start(bf16[128,2048]{1,0:T(8,128)(2,1)} %add_convert_fusion.2), channel_id=1, source_target_pairs={{0,1},{1,0},{2,3},{3,2},{4,5},{5,4},{6,7},{7,6},{8,9},{9,8},{10,11... | collective-permute-start | bytes 1572872 | tf_op jit(solution)/shard_map/ppermute | solution.py:57
  532.2 25.3 %collective-permute-start.48 = (bf16[256,2048]{1,0:T(8,128)(2,1)}, bf16[256,2048]{1,0:T(8,128)(2,1)S(1)}, u32[]{:S(2)}, u32[]{:S(2)}) collective-permute-start(bf16[256,2048]{1,0:T(8,128)(2,1)} %reduce-scatter.12.cloned.1.call-done), channel_id=1, source_target_pairs={{1,8},{3,10},{5,12},{7,14},{8,1},{10,3},{12,5},{14,7},{17,24},{19,... | collective-permute-start | bytes 3145736 | tf_op jit(solution)/shard_map/ppermute | solution.py:57
  552.8 21.2 %collective-permute-start.43 = (bf16[256,2048]{1,0:T(8,128)(2,1)S(1)}, bf16[256,2048]{1,0:T(8,128)(2,1)S(1)}, u32[]{:S(2)}, u32[]{:S(2)}) collective-permute-start(bf16[256,2048]{1,0:T(8,128)(2,1)S(1)} %pad_maximum_fusion), channel_id=1, source_target_pairs={{1,8},{3,10},{5,12},{7,14},{8,1},{10,3},{12,5},{14,7},{17,24},{19,... | collective-permute-start | bytes 3145736 | tf_op jit(solution)/shard_map/ppermute | solution.py:57
  (84 other events, 788.8 us)
Sparse Core Ops, SparseCore 0:
  10.2 47.9 all-gather.5
  60.4 81.1 all-gather.7
  143.2 45.6 all-gather.9
  190.4 45.8 all-gather.11
  237.7 46.0 all-gather.13
  296.3 50.1 reduce-scatter.5
  348.7 48.1 reduce-scatter.7
  399.2 48.3 reduce-scatter.9
  449.9 77.5 reduce-scatter.11
  529.7 44.8 reduce-scatter.13
